TPU v7x, 32 devices: a whole 2x2x4 slice. The times are simulated.
32 devices in a mesh: ev: 4 (over z), mesh: 8 (over y, x, core).
Axes of the slice: x: 2, y: 2, z: 4, core: 2. Of those that a mesh axis runs over, the one named last changes fastest.
Arguments:
- kernels: bfloat16 [8, 12, 2048, 128], P('ev', None, 'mesh'), may hold values from -6 to 6
- tile_owner: int32 [8, 4096, 1], P('ev', 'mesh'), may hold values from 0 to 7; in each aligned block of 512 rows (0 to 511, 512 to 1023, ..., all dimensions but the last counted through in order) at most 64 rows name the same one
- tile_source: int32 [8, 4096], P('ev', 'mesh'), may hold values from 0 to 255
- tile_target: int32 [8, 4096], P('ev', 'mesh'), may hold values from 0 to 31
- tile_seed: int32 [8, 4096], P('ev', 'mesh'), may hold values from 0 to 83
- tile_count: int32 [8, 8], P('ev', 'mesh'), may hold values from 256 to 512
- prev_gradient: float32 [12, 8, 32, 128], P(None, 'mesh', 'ev'), may hold values from -18 to 18
- prev_step: float32 [12, 8, 32, 128], P(None, 'mesh', 'ev'), may hold values from -18 to 18, as said below
- precond: float32 [12, 8, 32, 128], P(None, 'mesh', 'ev'), may hold values from 0.2 to 2
Outputs:
- inversion_direction: float32 [12, 8, 32, 128], P(None, 'mesh', 'ev')
- event_direction: float32 [8, 12, 2048, 128], P('ev', None, 'mesh')
Inputs may be any that keep to these rules, and one draw needn't show every extreme that they name: `tile_owner`: in every aligned block of 512 rows (one event's list for one partition) no partition is named by more than 64 rows, a bound that some block reaches. Rows of a list at positions tile_count or later are padding. prev_step = -c * prev_gradient cell by cell, with c between 0.1 and 1.
All inputs are finite; a program needn't handle non-finite values.
Results may differ from a plain program's by a relative error of at most 0.0003.
The roundings to bfloat16 on the way count: a program that leaves them out, or rounds other values in their place, can miss the bound.
Values may be sent and summed in bfloat16 or wider, within the bound.
No kernel may reach another device: no remote copies, remote signals or barrier semaphores. Data moves between devices by JAX's collectives and lax.ppermute only.
A program may use at most 128 MiB of HBM per device.

v0:
```python
import math

import jax
import jax.numpy as jnp
from jax import lax
from jax.sharding import PartitionSpec as P


def make_tiles(seed_ids, node_count):
    node_pos = jnp.arange(node_count).astype(jnp.float32)
    offset = (seed_ids % 7 - 3).astype(jnp.float32)
    spread = 0.55 + 0.1 * (seed_ids // 7 % 3).astype(jnp.float32)
    weight = 0.1 + 0.1 * (seed_ids // 21).astype(jnp.float32)
    distance = node_pos[None, :, None] - node_pos[None, None, :] - offset[:, None, None]
    values = weight[:, None, None] * jnp.exp(
        -distance * distance / (2.0 * spread * spread)[:, None, None]
    )
    return values.astype(jnp.bfloat16)


def body(
    kernels,
    tile_owner,
    tile_source,
    tile_target,
    tile_seed,
    tile_count,
    prev_gradient,
    prev_step,
    precond,
):
    event_local, components, event_blocks, node_count = kernels.shape
    tiles_local = tile_source.shape[1]
    partitions = lax.axis_size("mesh")
    event_groups = lax.axis_size("ev")
    owned_blocks = precond.shape[2]
    sub_blocks = owned_blocks * event_groups
    capacity = tiles_local // 8
    total_tiles = event_local * tiles_local
    block_rows = math.gcd(total_tiles, 512)
    block_count = total_tiles // block_rows
    row_width = components * node_count
    list_pos = lax.broadcasted_iota(jnp.int32, (event_local, tiles_local), 1)
    event_of = lax.broadcasted_iota(jnp.int32, (event_local, tiles_local), 0).reshape(total_tiles)
    live_mask = (list_pos < tile_count).astype(jnp.float32).reshape(total_tiles)
    owner_ids = tile_owner.reshape(total_tiles)
    target_ids = tile_target.reshape(total_tiles)
    seed_ids = tile_seed.reshape(total_tiles)
    source_row = event_of * event_blocks + tile_source.reshape(total_tiles)
    kernel_rows = jnp.transpose(kernels, (0, 2, 1, 3)).reshape(
        event_local * event_blocks, components, node_count
    )

    def forward_block(inputs):
        block_seeds, block_rows_idx, block_live = inputs
        tile_mats = make_tiles(block_seeds, node_count)
        picked = kernel_rows[block_rows_idx]
        product = jnp.einsum("tcn,tnm->tcm", picked, tile_mats, preferred_element_type=jnp.float32)
        return (product * block_live[:, None, None]).astype(jnp.bfloat16)

    contribution = lax.map(
        forward_block,
        (
            seed_ids.reshape(block_count, block_rows),
            source_row.reshape(block_count, block_rows),
            live_mask.reshape(block_count, block_rows),
        ),
    )
    contribution = contribution.reshape(total_tiles, components, node_count)
    owner_hits = (
        owner_ids.reshape(event_local, tiles_local, 1)
        == jnp.arange(partitions, dtype=jnp.int32)[None, None, :]
    ).astype(jnp.float32)
    row_iota = lax.broadcasted_iota(jnp.int32, (tiles_local, tiles_local), 0)
    col_iota = lax.broadcasted_iota(jnp.int32, (tiles_local, tiles_local), 1)
    upper_ones = (row_iota <= col_iota).astype(jnp.float32)
    running = jnp.einsum("etp,ts->esp", owner_hits, upper_ones, precision=lax.Precision.HIGHEST)
    slot_index = (
        jnp.sum(owner_hits * (running - 1.0), axis=2).astype(jnp.int32).reshape(total_tiles)
    )
    slot_place = (owner_ids * event_local + event_of) * capacity + slot_index
    buffer_rows = partitions * event_local * capacity
    tile_number = jnp.arange(total_tiles, dtype=jnp.int32)
    slot_tile = jnp.zeros((buffer_rows,), jnp.int32).at[slot_place].set(tile_number + 1)
    slot_filled = slot_tile > 0
    fill_from = jnp.maximum(slot_tile - 1, 0)
    outgoing = jnp.where(
        slot_filled[:, None, None], contribution[fill_from], jnp.zeros((), jnp.bfloat16)
    )
    labels = jnp.where(slot_filled, target_ids[fill_from], 0)
    arrived, arrived_labels = (
        lax.all_to_all(
            outgoing.reshape(partitions, event_local * capacity, components, node_count),
            "mesh",
            split_axis=0,
            concat_axis=0,
            tiled=True,
        ),
        lax.all_to_all(
            labels.reshape(partitions, event_local * capacity),
            "mesh",
            split_axis=0,
            concat_axis=0,
            tiled=True,
        ),
    )
    flat_labels = arrived_labels.reshape(buffer_rows)
    label_hits = (jnp.arange(sub_blocks, dtype=jnp.int32)[:, None] == flat_labels[None, :]).astype(
        jnp.bfloat16
    )
    partial_sum = jnp.dot(
        label_hits, arrived.reshape(buffer_rows, row_width), preferred_element_type=jnp.float32
    ).reshape(sub_blocks, components, node_count)
    owned = lax.psum_scatter(partial_sum, "ev", scatter_dimension=0, tiled=True)
    gradient = jnp.transpose(owned, (1, 0, 2))[:, None, :, :]
    change = gradient - prev_gradient
    weighted = precond * change
    curvature, slope, cross_term, self_term = lax.psum(
        (
            jnp.sum(prev_step * change),
            jnp.sum(prev_step * gradient),
            jnp.sum(weighted * gradient),
            jnp.sum(weighted * change),
        ),
        ("ev", "mesh"),
    )
    alpha = slope / curvature
    scaled = precond * (gradient - alpha * change)
    bend = cross_term - alpha * self_term
    beta = bend / curvature
    inversion_direction = -(scaled + (alpha - beta) * prev_step)
    local_direction = jnp.transpose(inversion_direction.astype(jnp.bfloat16)[:, 0], (1, 0, 2))
    partition_rows = lax.all_gather(local_direction, "ev", axis=0, tiled=True)
    requested = jnp.einsum(
        "sr,sk->rk",
        label_hits,
        partition_rows.reshape(sub_blocks, row_width),
        preferred_element_type=jnp.float32,
    ).astype(jnp.bfloat16)
    returned = lax.all_to_all(
        requested.reshape(partitions, event_local * capacity, components, node_count),
        "mesh",
        split_axis=0,
        concat_axis=0,
        tiled=True,
    )
    tile_rows = returned.reshape(buffer_rows, components, node_count)[slot_place]
    event_rows = event_local * event_blocks
    event_row_ids = jnp.arange(event_rows, dtype=jnp.int32)

    def backward_block(total, inputs):
        block_seeds, block_dirs, block_live, block_sources = inputs
        tile_mats = make_tiles(block_seeds, node_count)
        product = jnp.einsum(
            "tcm,tnm->tcn", block_dirs, tile_mats, preferred_element_type=jnp.float32
        )
        product = (product * block_live[:, None, None]).reshape(block_sources.shape[0], row_width)
        hits = (event_row_ids[:, None] == block_sources[None, :]).astype(jnp.float32)
        return (
            total
            + jnp.dot(
                hits, product, precision=lax.Precision.HIGHEST, preferred_element_type=jnp.float32
            ),
            None,
        )

    back_start = jnp.zeros((event_rows, row_width), jnp.float32)
    summed, _ = lax.scan(
        backward_block,
        back_start,
        (
            seed_ids.reshape(block_count, block_rows),
            tile_rows.reshape(block_count, block_rows, components, node_count),
            live_mask.reshape(block_count, block_rows),
            source_row.reshape(block_count, block_rows),
        ),
    )
    event_direction = jnp.transpose(
        summed.reshape(event_local, event_blocks, components, node_count), (0, 2, 1, 3)
    )
    return (inversion_direction, event_direction)


def solution(mesh):
    in_specs = (
        P("ev", None, "mesh", None),
        P("ev", "mesh", None),
        P("ev", "mesh"),
        P("ev", "mesh"),
        P("ev", "mesh"),
        P("ev", "mesh"),
        P(None, "mesh", "ev", None),
        P(None, "mesh", "ev", None),
        P(None, "mesh", "ev", None),
    )
    out_specs = (P(None, "mesh", "ev", None), P("ev", None, "mesh", None))
    return jax.shard_map(body, mesh=mesh, in_specs=in_specs, out_specs=out_specs, check_vma=False)
```

profile of v0, /device:TPU:0, one launch (start us, length us, event | category | flops | bytes accessed | tf_op | source)
XLA Modules:
  0.0 326.0 jit_solution(17244777554216144490)
XLA Ops:
  7.2 0.0 copy-start.10
  7.2 0.0 copy-start.8
  7.2 0.0 copy-start
  7.2 0.7 copy.115
  7.9 0.7 broadcast_multiply_fusion.1
  8.6 0.2 fusion.47
  8.9 0.0 copy-start.6
  8.9 4.3 %scatter_custom_fusion = s32[1024]{0:T(1024)S(1)} fusion(s32[1024]{0:T(1024)S(1)} %bitcast.201, s32[1024]{0:T(1024)S(1)} %iota_add_fusion, s32[]{:T(128)} %constant.198.clone.1), kind=kCustom, calls=%fused_computation.125 | custom fusion | bytes 4100 | tf_op jit(solution)/shard_map/scatter | solution.py:84
  13.2 0.0 copy-start.4
  13.2 0.7 copy.106
  13.9 4.5 %gather_fusion.1 = s32[1024]{0:T(1024)S(1)} fusion(s32[1024]{0:T(1024)S(1)} %bitcast.175, s32[1024]{0:T(1024)S(1)} %maximum_clamp_fusion), kind=kCustom, calls=%fused_computation.1 | custom fusion | bytes 12288 | tf_op jit(solution)/shard_map/gather | solution.py:90
  18.4 0.6 broadcast_select_fusion.1
  19.0 0.1 compare_convert_fusion
  19.1 0.0 copy-done.8
  19.1 2.5 copy.83
  21.6 0.0 copy-done
  21.6 0.0 copy-start.5
  21.7 29.3 %while.27 = (s32[]{:T(128)}, bf16[2,512,12,128]{3,2,1,0:T(8,128)(2,1)}, s32[2,512]{1,0:T(2,128)S(1)}, bf16[512,12,128]{2,1,0:T(8,128)(2,1)S(1)}, s32[2,512]{1,0:T(2,128)S(1)}, /*index=5*/f32[2,512]{1,0:T(2,128)S(1)}, s32[]{:T(128)}) while((s32[]{:T(128)}, bf16[2,512,12,128]{3,2,1,0:T(8,128)(2,1)}, s32[2,512]{1,0:T(2,128)S(1)}, ...), condition=%wide.region_3.4_spmd, body=%wide.region_2.3_spmd.sunk | while | flops 253268096 | bytes 7523933 | solution.py:61
  21.8 2.7 gather_fusion
  24.6 0.1 broadcast_subtract_fusion.4
  24.6 11.7 %fusion.85 = bf16[2,512,12,128]{3,2,1,0:T(8,128)(2,1)} fusion(bf16[2,512,12,128]{3,2,1,0:T(8,128)(2,1)} %get-tuple-element.449, s32[]{:T(128)} %get-tuple-element.448, f32[512]{0:T(512)S(1)} %bitcast.196, bf16[512,12,128]{2,1,0:T(8,128)(2,1)} %gather_fusion, f32[512]{0:T(512)S(1)} %get-tuple-element.425, f32[512]{0:T(512)S(1)} %fusion.84, ...), kind=kOutput, calls=%fused_computation.14.clone.1 | convolution fusion | flops 253231104 | bytes 4268544 | tf_op jit(solution)/shard_map/while/body/eval_jaxpr/tcn,tnm->tcm/dot_general | solution.py:58
  36.4 2.7 gather_fusion
  39.2 0.1 broadcast_subtract_fusion.4
  39.3 11.7 %fusion.85 = bf16[2,512,12,128]{3,2,1,0:T(8,128)(2,1)} fusion(bf16[2,512,12,128]{3,2,1,0:T(8,128)(2,1)} %get-tuple-element.449, s32[]{:T(128)} %get-tuple-element.448, f32[512]{0:T(512)S(1)} %bitcast.196, bf16[512,12,128]{2,1,0:T(8,128)(2,1)} %gather_fusion, f32[512]{0:T(512)S(1)} %get-tuple-element.425, f32[512]{0:T(512)S(1)} %fusion.84, ...), kind=kOutput, calls=%fused_computation.14.clone.1 | convolution fusion | flops 253231104 | bytes 4268544 | tf_op jit(solution)/shard_map/while/body/eval_jaxpr/tcn,tnm->tcm/dot_general | solution.py:58
  50.9 10.6 %gather_fusion.2 = bf16[1024,12,128]{2,1,0:T(8,128)(2,1)} fusion(bf16[1024,12,128]{2,1,0:T(8,128)(2,1)} %bitcast.184, s32[1024]{0:T(1024)S(1)} %copy-done.5), kind=kCustom, calls=%fused_computation.2 | custom fusion | bytes 6295552 | tf_op jit(solution)/shard_map/gather | solution.py:88
  61.5 3.0 copy.84
  64.5 0.0 copy-done.9
  64.5 0.3 broadcast_select_fusion
  64.9 2.8 copy.85
  67.6 43.0 %all_to_all.19 = bf16[8,128,12,128]{1,3,2,0:T(8,128)(2,1)S(1)} all-to-all(bf16[8,128,12,128]{1,3,2,0:T(8,128)(2,1)} %copy.85), channel_id=1, replica_groups=mesh['ev'=4,'mesh'=8] {'mesh'}, dimensions={0} | all-to-all | bytes 6291456 | tf_op jit(solution)/shard_map/all_to_all | solution.py:92
  110.6 3.3 %all-to-all-start = ((s32[8,1,128]{2,1,0:T(1,128)}), s32[8,1,128]{2,1,0:T(1,128)S(1)}, u32[]{:S(2)}, u32[]{:S(2)}) async-start(s32[8,1,128]{2,1,0:T(1,128)} %bitcast.14), calls=%async_computation | async-start | bytes 8192 | tf_op jit(solution)/shard_map/all_to_all | solution.py:99
  113.9 0.0 reduce-scatter.2.cloned.1.call-start
  113.9 2.4 copy.86
  116.4 0.0 copy-start.1
  116.4 0.0 copy-start.2
  116.4 0.0 copy-start.3
  116.4 0.8 copy.114
  117.3 1.2 all-to-all-done
  118.5 1.7 fusion.49
  120.2 0.0 reduce-scatter.2.cloned.1.call-update
  120.2 20.1 %reduce-scatter.2.cloned.1.call-done = f32[8,12,128]{2,0,1:T(8,128)} async-done(((f32[32,12,128]{2,0,1:T(8,128)}), f32[8,12,128]{2,0,1:T(8,128)}) %reduce-scatter.2.cloned.1.call-update) | async-done | bytes 49168 | tf_op jit(solution)/shard_map/reduce_scatter | solution.py:114
  140.4 1.5 multiply_reduce_fusion
  141.9 39.0 %all-reduce = (f32[]{:T(128)}, f32[]{:T(128)}, f32[]{:T(128)}, f32[]{:T(128)}) all-reduce(f32[]{:T(128)} %get-tuple-element.291, f32[]{:T(128)} %get-tuple-element.292, f32[]{:T(128)} %get-tuple-element.290, f32[]{:T(128)} %get-tuple-element.289), channel_id=1, replica_groups=mesh['ev'=4,'mesh'=8] {'ev','mesh'}, use_global_device_ids=true, to_apply=%region_6.7 | all-reduce | flops 4 | bytes 32 | tf_op jit(solution)/shard_map/psum | solution.py:118
  184.0 1.4 convert_bitcast_fusion
  185.4 12.1 %all_gather.3 = bf16[32,12,128]{2,0,1:T(8,128)(2,1)S(1)} all-gather(bf16[8,12,128]{2,0,1:T(8,128)(2,1)S(1)} %get-tuple-element.321), channel_id=1, replica_groups=mesh['ev'=4,'mesh'=8] {'ev'}, dimensions={0}, use_global_device_ids=true | all-gather | bytes 122880 | tf_op jit(solution)/shard_map/all_gather | solution.py:133
  197.5 1.0 convolution_convert_fusion
  198.5 3.7 %reshape.473 = bf16[8,128,12,128]{3,2,1,0:T(8,128)(2,1)} reshape(bf16[1024,1536]{1,0:T(8,128)(2,1)S(1)} %convolution_convert_fusion) | data formatting | bytes 6291456 | tf_op jit(solution)/shard_map/reshape | solution.py:141
  202.2 6.6 %copy.95 = bf16[8,128,12,128]{1,3,2,0:T(8,128)(2,1)} copy(bf16[8,128,12,128]{3,2,1,0:T(8,128)(2,1)} %reshape.473) | data formatting | bytes 6291456 | tf_op jit(solution)/shard_map/reshape | solution.py:141
  208.8 4.1 %all-to-all-start.2 = ((bf16[8,128,12,128]{1,3,2,0:T(8,128)(2,1)}), bf16[8,128,12,128]{1,3,2,0:T(8,128)(2,1)S(1)}, u32[]{:S(2)}, u32[]{:S(2)}) async-start(bf16[8,128,12,128]{1,3,2,0:T(8,128)(2,1)} %copy.95), calls=%async_computation.3 | async-start | bytes 6291456 | tf_op jit(solution)/shard_map/all_to_all | solution.py:140
  212.9 37.8 %all-to-all-done.2 = bf16[8,128,12,128]{1,3,2,0:T(8,128)(2,1)S(1)} async-done(((bf16[8,128,12,128]{1,3,2,0:T(8,128)(2,1)}), bf16[8,128,12,128]{1,3,2,0:T(8,128)(2,1)S(1)}, u32[]{:S(2)}, u32[]{:S(2)}) %all-to-all-start.2) | async-done | bytes 3145760 | tf_op jit(solution)/shard_map/all_to_all | solution.py:140
  250.8 4.9 %copy.96 = bf16[8,128,12,128]{3,2,1,0:T(8,128)(2,1)} copy(bf16[8,128,12,128]{1,3,2,0:T(8,128)(2,1)S(1)} %all-to-all-done.2) | data formatting | bytes 6291456 | tf_op jit(solution)/shard_map/all_to_all | solution.py:140
  255.6 10.6 %gather_fusion.3 = bf16[1024,12,128]{2,1,0:T(8,128)(2,1)} fusion(bf16[1024,12,128]{2,1,0:T(8,128)(2,1)} %bitcast.178, s32[1024]{0:T(1024)S(1)} %broadcast_clamp_fusion), kind=kCustom, calls=%fused_computation.3 | custom fusion | bytes 6295552 | tf_op jit(solution)/shard_map/gather | solution.py:147
  266.2 41.6 %while.28 = (s32[]{:T(128)}, f32[512,1536]{1,0:T(8,128)}, s32[2,512]{1,0:T(2,128)S(1)}, bf16[2,512,12,128]{3,2,1,0:T(8,128)(2,1)}, s32[2,512]{1,0:T(2,128)S(1)}, /*index=5*/f32[2,512]{1,0:T(2,128)S(1)}, s32[]{:T(128)}, s32[]{:T(128)}) while((s32[]{:T(128)}, f32[512,1536]{1,0:T(8,128)}, s32[2,512]{1,0:T(2,128)S(1)}, ...), condition=%wide.region_14.15_spmd.clone, body=%wide.region_13.14_spmd.clone.sunk | while | flops 5086152192 | bytes 21149292 | solution.py:168
  266.3 0.1 broadcast_subtract_fusion.5
  266.4 12.0 %broadcast_multiply_fusion.3 = f32[512,12,128]{2,1,0:T(8,128)} fusion(f32[512]{0:T(512)S(1)} %bitcast.197, f32[512]{0:T(512)S(1)} %get-tuple-element.438, f32[512]{0:T(512)S(1)} %fusion.90, f32[128,128]{1,0:T(8,128)S(1)} %broadcast_subtract_fusion.5, f32[512]{0:T(512)S(1)} %get-tuple-element.439, bf16[2,512,12,128]{3,2,1,0:T(8,128)(2,1)} %get-tuple-element.481, ...), kind=kOutput, calls=%fused_computation.49.clone.1 | convolution fusion | flops 252444672 | bytes 5317120 | tf_op jit(solution)/shard_map/while/body/eval_jaxpr/tcm,tnm->tcn/dot_general | solution.py:154
  278.5 3.4 %copy.117 = f32[512,12,128]{0,2,1:T(8,128)S(1)} copy(f32[512,12,128]{2,1,0:T(8,128)} %broadcast_multiply_fusion.3) | data formatting | bytes 6291456 | tf_op jit(solution)/shard_map/while/body/eval_jaxpr/mul | solution.py:157
  281.9 4.4 %convolution_add_fusion.2 = f32[512,1536]{1,0:T(8,128)} fusion(f32[512,1536]{0,1:T(8,128)S(1)} %bitcast.176, f32[512,1536]{1,0:T(8,128)} %get-tuple-element.471, pred[]{:T(512)S(6)} %compare.3, s32[512]{0:T(512)S(1)} %bitcast.195), kind=kOutput, calls=%fused_computation.47.clone.1 | convolution fusion | flops 4833673216 | bytes 9439233 | tf_op jit(solution)/shard_map/while/body/eval_jaxpr/dot_general | solution.py:161
  286.4 0.1 broadcast_subtract_fusion.5
  286.5 12.0 %broadcast_multiply_fusion.3 = f32[512,12,128]{2,1,0:T(8,128)} fusion(f32[512]{0:T(512)S(1)} %bitcast.197, f32[512]{0:T(512)S(1)} %get-tuple-element.438, f32[512]{0:T(512)S(1)} %fusion.90, f32[128,128]{1,0:T(8,128)S(1)} %broadcast_subtract_fusion.5, f32[512]{0:T(512)S(1)} %get-tuple-element.439, bf16[2,512,12,128]{3,2,1,0:T(8,128)(2,1)} %get-tuple-element.481, ...), kind=kOutput, calls=%fused_computation.49.clone.1 | convolution fusion | flops 252444672 | bytes 5317120 | tf_op jit(solution)/shard_map/while/body/eval_jaxpr/tcm,tnm->tcn/dot_general | solution.py:154
  298.6 3.4 %copy.117 = f32[512,12,128]{0,2,1:T(8,128)S(1)} copy(f32[512,12,128]{2,1,0:T(8,128)} %broadcast_multiply_fusion.3) | data formatting | bytes 6291456 | tf_op jit(solution)/shard_map/while/body/eval_jaxpr/mul | solution.py:157
  302.0 5.8 %convolution_add_fusion.2 = f32[512,1536]{1,0:T(8,128)} fusion(f32[512,1536]{0,1:T(8,128)S(1)} %bitcast.176, f32[512,1536]{1,0:T(8,128)} %get-tuple-element.471, pred[]{:T(512)S(6)} %compare.3, s32[512]{0:T(512)S(1)} %bitcast.195), kind=kOutput, calls=%fused_computation.47.clone.1 | convolution fusion | flops 4833673216 | bytes 9439233 | tf_op jit(solution)/shard_map/while/body/eval_jaxpr/dot_general | solution.py:161
  307.8 2.4 copy.97
  310.2 3.3 %reshape.426 = f32[2,256,12,128]{1,0,3,2:T(2,128)} reshape(f32[512,1536]{0,1:T(8,128)S(1)} %copy.97) | data formatting | bytes 6291456 | tf_op jit(solution)/shard_map/reshape | solution.py:179
  313.5 5.7 %copy.99 = f32[2,12,256,128]{3,2,1,0:T(8,128)} copy(f32[2,12,256,128]{2,0,3,1:T(2,128)} %bitcast.182) | data formatting | bytes 6291456
  (49 shorter events, 0.5 us)
Async XLA Ops:
  7.2 11.9 %copy-start.10 = (s32[2,1]{0,1:T(1,128)S(1)}, s32[2,1]{0,1:T(1,128)}, u32[]{:S(2)}) copy-start(s32[2,1]{0,1:T(1,128)} %param.18) | copy-start | bytes 28
  7.2 11.9 %copy-start.8 = (s32[2,512]{1,0:T(2,128)S(1)}, s32[2,512]{1,0:T(2,128)}, u32[]{:S(2)}) copy-start(s32[2,512]{1,0:T(2,128)} %param.15) | copy-start | bytes 12292
  7.2 14.5 %copy-start = (s32[2,512]{1,0:T(2,128)S(1)}, s32[2,512]{1,0:T(2,128)}, u32[]{:S(2)}) copy-start(s32[2,512]{1,0:T(2,128)} %param.17) | copy-start | bytes 12292
  8.9 4.3 %copy-start.6 = (s32[1024,1]{0,1:T(1,128)}, s32[1024,1]{0,1:T(1,128)S(1)}, u32[]{:S(2)}) copy-start(s32[1024,1]{0,1:T(1,128)S(1)} %compare_select_fusion.1) | copy-start | bytes 12292
  13.2 5.9 %copy-start.4 = (s32[1024]{0:T(1024)}, s32[1024]{0:T(1024)S(1)}, u32[]{:S(2)}) copy-start(s32[1024]{0:T(1024)S(1)} %maximum_clamp_fusion) | copy-start | bytes 12292
  21.6 29.3 %copy-start.5 = (s32[1024]{0:T(1024)S(1)}, s32[1024]{0:T(1024)}, u32[]{:S(2)}) copy-start(s32[1024]{0:T(1024)} %copy-done.4) | copy-start | bytes 12292
  61.5 3.0 copy-start.9
  110.6 7.9 %all-to-all-start = ((s32[8,1,128]{2,1,0:T(1,128)}), s32[8,1,128]{2,1,0:T(1,128)S(1)}, u32[]{:S(2)}, u32[]{:S(2)}) async-start(s32[8,1,128]{2,1,0:T(1,128)} %bitcast.14), calls=%async_computation | async-start | bytes 8192 | tf_op jit(solution)/shard_map/all_to_all | solution.py:99
  113.9 26.5 %reduce-scatter.2.cloned.1.call-start = ((), (), s32[]{:S(2)}) async-start(), calls=%async_computation.4 | async-start | bytes 245760 | tf_op jit(solution)/shard_map/reduce_scatter | solution.py:114
  116.4 24.0 %copy-start.1 = (f32[12,1,8,128]{3,2,1,0:T(8,128)S(1)}, f32[12,1,8,128]{3,2,1,0:T(8,128)}, u32[]{:S(2)}) copy-start(f32[12,1,8,128]{3,2,1,0:T(8,128)} %param.20) | copy-start | bytes 147460
  116.4 24.0 %copy-start.2 = (f32[12,1,8,128]{3,2,1,0:T(8,128)S(1)}, f32[12,1,8,128]{3,2,1,0:T(8,128)}, u32[]{:S(2)}) copy-start(f32[12,1,8,128]{3,2,1,0:T(8,128)} %param.21) | copy-start | bytes 147460
  116.4 24.0 %copy-start.3 = (f32[12,1,8,128]{3,2,1,0:T(8,128)S(1)}, f32[12,1,8,128]{3,2,1,0:T(8,128)}, u32[]{:S(2)}) copy-start(f32[12,1,8,128]{3,2,1,0:T(8,128)} %param.19) | copy-start | bytes 147460
  208.8 4.1 %copy-start.7 = (s32[1024,1]{0,1:T(1,128)S(1)}, s32[1024,1]{0,1:T(1,128)}, u32[]{:S(2)}) copy-start(s32[1024,1]{0,1:T(1,128)} %copy-done.6) | copy-start | bytes 12292
  208.8 42.0 %all-to-all-start.2 = ((bf16[8,128,12,128]{1,3,2,0:T(8,128)(2,1)}), bf16[8,128,12,128]{1,3,2,0:T(8,128)(2,1)S(1)}, u32[]{:S(2)}, u32[]{:S(2)}) async-start(bf16[8,128,12,128]{1,3,2,0:T(8,128)(2,1)} %copy.95), calls=%async_computation.3 | async-start | bytes 6291456 | tf_op jit(solution)/shard_map/all_to_all | solution.py:140
Sparse Core Ops, SparseCore 0:
  120.4 19.9 reduce-scatter.1
where the time goes:
time: 327 us; the launch traced here: 326 us
  blocking collectives  94.1 us (29%)
  local copies, waits for them, and re-layouts  81.9 us (25%)
  matrix products  60.5 us (19%)
  waiting for transfers between devices  59.2 us (18%)
  between operations  17.4 us (5%)
  starting transfers between devices  7.42 us (2%)
  other arithmetic  5.42 us (2%)
    all_to_all x1, blocking collectives, body(): lax.all_to_all(outgoing.reshape(partitions, event_local * capacity, compo...  43 us
    psum x1, blocking collectives, body(): lax.psum((jnp.sum(prev_step * change), jnp.sum(prev_step * gradient), jnp...  39 us
    all_to_all x1, waiting for transfers between devices, body(): lax.all_to_all(requested.reshape(partitions, event_local * capacity, comp...  37.8 us
    dot_general x2, matrix products, backward_block(): jnp.einsum('tcm,tnm->tcn', block_dirs, tile_mats, preferred_element_type=...  24.1 us
    dot_general x2, matrix products, forward_block(): jnp.einsum('tcn,tnm->tcm', picked, tile_mats, preferred_element_type=jnp....  23.3 us
    reduce_scatter x1, waiting for transfers between devices, body(): owned = lax.psum_scatter(partial_sum, 'ev', scatter_dimension=0, tiled=True)  20.1 us
    gather x2, local copies, waits for them, and re-layouts, body(): contribution[fill_from]  13.6 us
    all_gather x1, blocking collectives, body(): partition_rows = lax.all_gather(local_direction, 'ev', axis=0, tiled=True)  12.1 us
  transfers between devices with their start and end apart: 3, of which 3 were waited for; matrix products, arithmetic and copies ran while one was open for 1% of the time, Pallas kernels for 0%

commit v1 on v0

v1 whole, which is shorter than its diff:
```python
import functools

import jax
import jax.numpy as jnp
import numpy as np
from jax import lax
from jax.experimental import pallas as pl
from jax.experimental.pallas import tpu as pltpu
from jax.sharding import PartitionSpec as P

OFFSETS = 7
SPREADS = 3
WEIGHTS = 4
SHAPES = OFFSETS * SPREADS * WEIGHTS
ROW = 16
UNROLL = 8


def fill_table(tab_ref, nodes):
    row = lax.broadcasted_iota(jnp.int32, (nodes, nodes), 0)
    col = lax.broadcasted_iota(jnp.int32, (nodes, nodes), 1)
    gap = (row - col).astype(jnp.float32)

    def one(k, carry):
        offset = (k % OFFSETS - OFFSETS // 2).astype(jnp.float32)
        spread = 0.55 + 0.1 * (k // OFFSETS).astype(jnp.float32)
        distance = gap - offset
        bell = jnp.exp(-distance * distance / (2.0 * spread * spread))
        for w in range(WEIGHTS):
            weight = np.float32(0.1) + np.float32(0.1) * np.float32(w)
            at = pl.multiple_of((w * OFFSETS * SPREADS + k) * nodes, nodes)
            tab_ref[pl.ds(at, nodes), :] = (weight * bell).astype(jnp.bfloat16)
        return carry

    lax.fori_loop(0, OFFSETS * SPREADS, one, 0)


def tile_loop(count, unroll, one):
    def group(i, carry):
        for u in range(unroll):
            one(i * unroll + u, u)
        return carry

    lax.fori_loop(0, (count + unroll - 1) // unroll, group, 0)


def forward_kernel(
    dims, base_ref, count_ref, source_ref, block_ref, seed_ref, field_ref, keep_ref, send_ref,
    tab_ref, rows_ref, sum_a, sum_b,
):
    events, comps, eblocks, nodes, tiles, blocks, group = dims
    fill_table(tab_ref, nodes)
    sum_a[...] = jnp.zeros_like(sum_a)
    sum_b[...] = jnp.zeros_like(sum_b)
    for v in range(events):
        for c in range(comps):
            rows_ref[pl.ds(v * eblocks * ROW + c, eblocks, stride=ROW), :] = field_ref[
                v, c
            ].astype(jnp.float32)
    for v in range(events):
        count = count_ref[v]

        def one(t, u, v=v, count=count):
            at = v * tiles + t
            src = pl.multiple_of(source_ref[at] * ROW + v * eblocks * ROW, ROW)
            block = jnp.where(t < count, block_ref[at], blocks)
            shape = pl.multiple_of(seed_ref[at] * nodes, nodes)
            x = rows_ref[pl.ds(src, ROW), :].astype(jnp.bfloat16)
            y = jnp.dot(x, tab_ref[pl.ds(shape, nodes), :], preferred_element_type=jnp.float32)
            y = y.astype(jnp.bfloat16).astype(jnp.float32)
            total = sum_a if u % 2 == 0 else sum_b
            to = pl.ds(pl.multiple_of(block * ROW, ROW), ROW)
            total[to, :] = total[to, :] + y

        tile_loop(count, UNROLL, one)
    chunks = keep_ref.shape[0]
    for half, out_ref in enumerate((keep_ref, send_ref)):

        def put(j, carry, half=half, out_ref=out_ref):
            first = base_ref[half * chunks + j] * ROW
            for c in range(comps):
                at = pl.ds(first + c, group, stride=ROW)
                out_ref[j, pl.ds(c * group, group), :] = sum_a[at, :] + sum_b[at, :]
            return carry

        lax.fori_loop(0, chunks, put, 0)


def backward_kernel(
    dims, base_ref, count_ref, source_ref, block_ref, seed_ref, mine_ref, other_ref, out_ref,
    tab_ref, rows_ref, sum_ref,
):
    events, comps, eblocks, nodes, tiles, blocks, group = dims
    fill_table(tab_ref, nodes)
    sum_ref[...] = jnp.zeros_like(sum_ref)
    chunks = mine_ref.shape[0]
    for half, in_ref in enumerate((mine_ref, other_ref)):

        def take(j, carry, half=half, in_ref=in_ref):
            first = base_ref[half * chunks + j] * ROW
            values = in_ref[j].astype(jnp.float32)
            for c in range(comps):
                rows_ref[pl.ds(first + c, group, stride=ROW), :] = values[
                    c * group : (c + 1) * group
                ]
            return carry

        lax.fori_loop(0, chunks, take, 0)
    for v in range(events):
        count = count_ref[v]

        def one(t, u, v=v, count=count):
            at = v * tiles + t
            src = jnp.where(t < count, source_ref[at] + v * eblocks, events * eblocks)
            seed = seed_ref[at]
            shape = pl.multiple_of(seed * nodes, nodes)
            x = rows_ref[pl.ds(pl.multiple_of(block_ref[at] * ROW, ROW), ROW), :]
            y = jnp.dot(
                x.astype(jnp.bfloat16),
                tab_ref[pl.ds(shape, nodes), :],
                preferred_element_type=jnp.float32,
            )
            to = pl.ds(pl.multiple_of(src * ROW, ROW), ROW)
            sum_ref[to, :] = sum_ref[to, :] + y

        tile_loop(count, UNROLL, one)
    for v in range(events):
        for c in range(comps):
            out_ref[v, c] = sum_ref[pl.ds(v * eblocks * ROW + c, eblocks, stride=ROW), :]


def smem():
    return pl.BlockSpec(memory_space=pltpu.SMEM)


def vmem():
    return pl.BlockSpec(memory_space=pltpu.VMEM)


def body(
    kernels, tile_owner, tile_source, tile_target, tile_seed, tile_count, prev_gradient,
    prev_step, precond,
):
    events, comps, eblocks, nodes = kernels.shape
    tiles = tile_source.shape[1]
    parts = lax.axis_size("mesh")
    evs = lax.axis_size("ev")
    group = precond.shape[2]
    subs = group * evs
    blocks = parts * subs
    bits = parts.bit_length() - 1
    me = lax.axis_index("mesh")
    ev = lax.axis_index("ev")
    dims = (events, comps, eblocks, nodes, tiles, blocks, group)
    half = parts // 2

    def relation(odd, j):
        r = j << 1
        if bits < 3:
            return jnp.full_like(odd, r)
        a, b = (r >> 1) & 1, (r >> 2) & 1
        swapped = (r & ~6) | (a << 2) | (b << 1)
        return jnp.where(odd == 1, swapped, r)

    def bit_of(odd, step):
        if bits < 3 or step not in (1, 2):
            return 1 << step
        return (1 << (3 - step)) if odd else (1 << step)

    def swap(x, step):
        pairs = [(i, i ^ bit_of(i & 1, step)) for i in range(parts)]
        return lax.ppermute(x, "mesh", pairs)

    ev_slots = [jnp.remainder(ev + k, evs) for k in range(evs)]

    def slot_bases(device, odd):
        return [
            (device ^ relation(odd, j)) * subs + ev_slots[k] * group
            for j in range(half)
            for k in range(evs)
        ]

    odd = me & 1
    mine = slot_bases(me, odd)
    other = slot_bases(me ^ 1, 1 - odd)
    bases = jnp.stack(mine + other).astype(jnp.int32)

    block_ids = (tile_owner.reshape(events, tiles) * subs + tile_target).reshape(events * tiles)
    source_ids = tile_source.reshape(events * tiles)
    seed_ids = tile_seed.reshape(events * tiles)
    turned = seed_ids - 2 * (seed_ids % OFFSETS) + (OFFSETS - 1)
    counts = tile_count.reshape(events)
    chunks = half * evs
    chunk_rows = comps * group

    keep, send = pl.pallas_call(
        functools.partial(forward_kernel, dims),
        out_shape=[jax.ShapeDtypeStruct((chunks, chunk_rows, nodes), jnp.float32)] * 2,
        in_specs=[smem()] * 5 + [vmem()],
        out_specs=[vmem()] * 2,
        scratch_shapes=[
            pltpu.VMEM((SHAPES * nodes, nodes), jnp.bfloat16),
            pltpu.VMEM((events * eblocks * ROW, nodes), jnp.float32),
            pltpu.VMEM(((blocks + 1) * ROW, nodes), jnp.float32),
            pltpu.VMEM(((blocks + 1) * ROW, nodes), jnp.float32),
        ],
        name="forward",
    )(bases, counts, source_ids, block_ids, seed_ids, kernels)

    got = swap(send, 0)
    held = keep + got
    slots = half
    for step in range(1, bits):
        view = held.reshape(slots // 2, 2, evs, chunk_rows, nodes)
        got = swap(view[:, 1], step)
        held = (view[:, 0] + got).reshape(slots // 2 * evs, chunk_rows, nodes)
        slots //= 2
    held = held.reshape(evs, chunk_rows, nodes)
    total = held[0]
    for k in range(1, evs):
        total = total + lax.ppermute(held[k], "ev", [(i, (i + k) % evs) for i in range(evs)])
    gradient = total.reshape(comps, 1, group, nodes)

    change = gradient - prev_gradient
    weighted = precond * change
    local = jnp.stack(
        [
            jnp.sum(prev_step * change),
            jnp.sum(prev_step * gradient),
            jnp.sum(weighted * gradient),
            jnp.sum(weighted * change),
        ]
    )
    spread = jnp.broadcast_to(jnp.pad(local, (0, nodes - 4))[None, :], (parts * evs, nodes))
    sums = jnp.sum(lax.all_to_all(spread, ("ev", "mesh"), 0, 0, tiled=True), axis=0)
    curvature, slope, cross_term, self_term = sums[0], sums[1], sums[2], sums[3]
    alpha = slope / curvature
    scaled = precond * (gradient - alpha * change)
    beta = (cross_term - alpha * self_term) / curvature
    inversion_direction = -(scaled + (alpha - beta) * prev_step)
    rounded = inversion_direction.astype(jnp.bfloat16).reshape(chunk_rows, nodes)

    pieces = [rounded] + [
        lax.ppermute(rounded, "ev", [(i, (i - k) % evs) for i in range(evs)])
        for k in range(1, evs)
    ]
    gathered = jnp.stack(pieces)[None]
    for step in reversed(range(1, bits)):
        gathered = jnp.stack([gathered, swap(gathered, step)], axis=1)
        gathered = gathered.reshape((-1,) + gathered.shape[2:])
    gathered = gathered.reshape(chunks, chunk_rows, nodes)
    partner = swap(gathered, 0)

    event_direction = pl.pallas_call(
        functools.partial(backward_kernel, dims),
        out_shape=jax.ShapeDtypeStruct((events, comps, eblocks, nodes), jnp.float32),
        in_specs=[smem()] * 5 + [vmem()] * 2,
        out_specs=vmem(),
        scratch_shapes=[
            pltpu.VMEM((SHAPES * nodes, nodes), jnp.bfloat16),
            pltpu.VMEM(((blocks + 1) * ROW, nodes), jnp.float32),
            pltpu.VMEM(((events * eblocks + 1) * ROW, nodes), jnp.float32),
        ],
        name="backward",
    )(bases, counts, source_ids, block_ids, turned, gathered, partner)
    return inversion_direction, event_direction


def solution(mesh):
    in_specs = (
        P("ev", None, "mesh", None),
        P("ev", "mesh", None),
        P("ev", "mesh"),
        P("ev", "mesh"),
        P("ev", "mesh"),
        P("ev", "mesh"),
        P(None, "mesh", "ev", None),
        P(None, "mesh", "ev", None),
        P(None, "mesh", "ev", None),
    )
    out_specs = (P(None, "mesh", "ev", None), P("ev", None, "mesh", None))
    return jax.shard_map(body, mesh=mesh, in_specs=in_specs, out_specs=out_specs, check_vma=False)
```

time: 327 us -> 126 us (0.39)
  blocking collectives: 94.1 us -> 10.9 us
  local copies, waits for them, and re-layouts: 81.9 us -> 5.36 us
  matrix products: 60.5 us -> 0 us
  Pallas kernels: 0 us -> 51.5 us
  waiting for transfers between devices: 59.2 us -> 30 us
  between operations: 17.4 us -> 4.09 us
  starting transfers between devices: 7.42 us -> 16.7 us
    dot_general x8 -> x0, matrix products: 60.3 us -> none  [the longest x2 24.1 us: backward_block(): jnp.einsum('tcm,tnm->tcn', block_dirs, tile_mats, preferred_element_type=...]
    pallas_call x0 -> x2, Pallas kernels: none -> 51.5 us  [the longest x1 26.1 us: body(): pl.pallas_call(functools.partial(forward_kernel, dims), out_shape=[jax.Sh...]
    all_to_all x2 -> x0, waiting for transfers between devices: 39.1 us -> none  [the longest x1 37.8 us: body(): lax.all_to_all(requested.reshape(partitions, event_local * capacity, comp...]
    psum x1 -> x0, blocking collectives: 39 us -> none  [body(): lax.psum((jnp.sum(prev_step * change), jnp.sum(prev_step * gradient), jnp...]
    gather x6 -> x0, local copies, waits for them, and re-layouts: 34.1 us -> none  [the longest x2 13.6 us: body(): contribution[fill_from]]
    all_to_all x1, blocking collectives: 43 us -> 10.9 us  [body(): lax.all_to_all(spread, ('ev', 'mesh'), 0, 0, tiled=True)]
    ppermute x0 -> x12, waiting for transfers between devices: none -> 30 us  [the longest x6 23.1 us: swap(): return lax.ppermute(x, 'mesh', pairs)]
    reduce_scatter x1 -> x0, waiting for transfers between devices: 20.1 us -> none  [body(): owned = lax.psum_scatter(partial_sum, 'ev', scatter_dimension=0, tiled=True)]
  transfers between devices with their start and end apart: 3 -> 12, of which waited for: 3 -> 10; matrix products, arithmetic and copies ran while one was open for 1% -> 1% of each run, Pallas kernels for 0% -> 0%
where the time goes in v1:
time: 126 us; the launch traced here: 125 us
  Pallas kernels  51.5 us (41%)
  waiting for transfers between devices  30 us (24%)
  starting transfers between devices  16.7 us (13%)
  blocking collectives  10.9 us (9%)
  other arithmetic  6.1 us (5%)
  local copies, waits for them, and re-layouts  5.36 us (4%)
  between operations  4.09 us (3%)
    pallas_call x1, Pallas kernels, body(): pl.pallas_call(functools.partial(forward_kernel, dims), out_shape=[jax.Sh...  26.1 us
    pallas_call x1, Pallas kernels, body(): pl.pallas_call(functools.partial(backward_kernel, dims), out_shape=jax.Sh...  25.4 us
    ppermute x6, waiting for transfers between devices, swap(): return lax.ppermute(x, 'mesh', pairs)  23.1 us
    all_to_all x1, blocking collectives, body(): lax.all_to_all(spread, ('ev', 'mesh'), 0, 0, tiled=True)  10.9 us
    ppermute x3, starting transfers between devices, body(): lax.ppermute(held[k], 'ev', [(i, (i + k) % evs) for i in range(evs)])  7.97 us
    ppermute x6, starting transfers between devices, swap(): return lax.ppermute(x, 'mesh', pairs)  4.81 us
    ppermute x3, waiting for transfers between devices, body(): lax.ppermute(held[k], 'ev', [(i, (i + k) % evs) for i in range(evs)])  4.57 us
    unnamed x17, local copies, waits for them, and re-layouts  3.92 us
  transfers between devices with their start and end apart: 12, of which 10 were waited for; matrix products, arithmetic and copies ran while one was open for 1% of the time, Pallas kernels for 0%

profile of v1, /device:TPU:0, one launch (start us, length us, event | category | flops | bytes accessed | tf_op | source)
XLA Modules:
  0.0 124.7 jit_solution(4067975776300393011)
XLA Ops:
  0.7 0.7 fusion.14
  1.4 0.6 copy.23
  2.0 1.3 %copy.22 = s32[1,4,2,128]{3,1,2,0:T(4,128)} copy(s32[1,4,2,128]{3,2,1,0:T(2,128)} %bitcast.128) | data formatting | bytes 8192
  3.3 1.3 %copy.24 = s32[1,4,2,128]{3,1,2,0:T(4,128)} copy(s32[1,4,2,128]{3,2,1,0:T(2,128)} %bitcast.129) | data formatting | bytes 8192
  4.6 0.7 stack.170.base_ref
  5.3 26.1 %forward.1 = (f32[16,96,128]{2,1,0:T(8,128)}, f32[16,96,128]{2,1,0:T(8,128)}) custom-call(s32[32]{0:T(128)} %stack.170.base_ref, s32[2]{0:T(128)} %bitcast.130, s32[1024]{0:T(1024)} %bitcast.121, s32[1024]{0:T(1024)} %bitcast.119, s32[1024]{0:T(1024)} %bitcast.123, bf16[2,12,256,128]{3,2,1,0:T(8,128)(2,1)} %field_ref.1), custom_call_target="tpu_custom_call" | custom-call | tf_op jit(solution)/shard_map/forward/pallas_call | solution.py:196
  31.4 0.0 copy-start.2
  31.4 0.0 copy-start.3
  31.4 0.0 copy-start.5
  31.4 0.1 collective-permute-start
  31.5 2.5 %collective-permute-done = f32[16,96,128]{2,1,0:T(8,128)S(1)} collective-permute-done((f32[16,96,128]{2,1,0:T(8,128)}, f32[16,96,128]{2,1,0:T(8,128)S(1)}, u32[]{:S(2)}, u32[]{:S(2)}) %collective-permute-start) | collective-permute-done | bytes 786464 | tf_op jit(solution)/shard_map/ppermute | solution.py:172
  33.9 1.2 add.196
  35.2 0.0 copy-start.6
  35.2 1.2 collective-permute-start.1
  36.4 6.7 %collective-permute-done.1 = f32[2,4,96,128]{3,2,1,0:T(8,128)S(1)} collective-permute-done((f32[2,4,96,128]{3,2,1,0:T(8,128)S(1)}, f32[2,4,96,128]{3,2,1,0:T(8,128)S(1)}, u32[]{:S(2)}, u32[]{:S(2)}) %collective-permute-start.1) | collective-permute-done | bytes 393248 | tf_op jit(solution)/shard_map/ppermute | solution.py:172
  43.1 0.1 fusion.1
  43.1 2.3 %collective-permute-start.2 = (f32[1,4,96,128]{3,2,1,0:T(8,128)S(1)}, f32[1,4,96,128]{3,2,1,0:T(8,128)S(1)}, u32[]{:S(2)}, u32[]{:S(2)}) collective-permute-start(f32[1,4,96,128]{3,2,1,0:T(8,128)S(1)} %slice_bitcast_fusion.2), channel_id=1, source_target_pairs={{0,4},{1,3},{2,6},{3,1},{4,0},{5,7},{6,2},{7,5},{8,12},{9,11},{10,... | collective-permute-start | bytes 589832 | tf_op jit(solution)/shard_map/ppermute | solution.py:172
  45.4 3.6 %collective-permute-done.2 = f32[1,4,96,128]{3,2,1,0:T(8,128)S(1)} collective-permute-done((f32[1,4,96,128]{3,2,1,0:T(8,128)S(1)}, f32[1,4,96,128]{3,2,1,0:T(8,128)S(1)}, u32[]{:S(2)}, u32[]{:S(2)}) %collective-permute-start.2) | collective-permute-done | bytes 196640 | tf_op jit(solution)/shard_map/ppermute | solution.py:172
  49.1 3.2 %collective-permute-start.3 = (f32[96,128]{1,0:T(8,128)S(1)}, f32[96,128]{1,0:T(8,128)S(1)}, u32[]{:S(2)}, u32[]{:S(2)}) collective-permute-start(f32[96,128]{1,0:T(8,128)S(1)} %get-tuple-element.16), channel_id=1, source_target_pairs={{0,8},{8,16},{16,24},{24,0},{1,9},{9,17},{17,25},{25,1},{2,10},{10... | collective-permute-start | bytes 147464 | tf_op jit(solution)/shard_map/ppermute | solution.py:221
  52.3 4.3 %collective-permute-start.5 = (f32[96,128]{1,0:T(8,128)S(1)}, f32[96,128]{1,0:T(8,128)S(1)}, u32[]{:S(2)}, u32[]{:S(2)}) collective-permute-start(f32[96,128]{1,0:T(8,128)S(1)} %get-tuple-element.17), channel_id=1, source_target_pairs={{0,24},{8,0},{16,8},{24,16},{1,25},{9,1},{17,9},{25,17},{2,26},{10... | collective-permute-start | bytes 147464 | tf_op jit(solution)/shard_map/ppermute | solution.py:221
  56.6 0.5 collective-permute-start.4
  57.1 2.1 %collective-permute-done.3 = f32[96,128]{1,0:T(8,128)S(1)} collective-permute-done((f32[96,128]{1,0:T(8,128)S(1)}, f32[96,128]{1,0:T(8,128)S(1)}, u32[]{:S(2)}, u32[]{:S(2)}) %collective-permute-start.3) | collective-permute-done | bytes 49184 | tf_op jit(solution)/shard_map/ppermute | solution.py:221
  59.2 0.0 collective-permute-done.5
  59.2 2.5 %collective-permute-done.4 = f32[96,128]{1,0:T(8,128)S(1)} collective-permute-done((f32[96,128]{1,0:T(8,128)S(1)}, f32[96,128]{1,0:T(8,128)S(1)}, u32[]{:S(2)}, u32[]{:S(2)}) %collective-permute-start.4) | collective-permute-done | bytes 49184 | tf_op jit(solution)/shard_map/ppermute | solution.py:221
  61.7 0.0 copy-done.2
  61.7 0.0 copy-done.3
  61.7 0.0 copy-done.5
  61.7 0.7 multiply_reduce_fusion.1
  62.4 2.6 %select_maximum_fusion = f32[128]{0:T(128)S(1)} fusion(f32[1]{0:T(128)} %bitcast.48, f32[1]{0:T(128)} %bitcast.47, f32[1]{0:T(128)} %bitcast.46, f32[1]{0:T(128)} %bitcast.45), kind=kLoop, calls=%fused_computation.37 | loop fusion | flops 1024 | bytes 528 | tf_op jit(solution)/shard_map/stack | solution.py:226
  65.0 10.9 %all_to_all.6 = f32[32,1,128]{2,1,0:T(1,128)S(1)} all-to-all(f32[32,1,128]{2,1,0:T(1,128)S(1)} %broadcast_in_dim.4), channel_id=1, replica_groups=mesh['ev'=4,'mesh'=8] {'ev','mesh'}, dimensions={0} | all-to-all | bytes 32768 | tf_op jit(solution)/shard_map/all_to_all | solution.py:235
  76.0 0.7 fusion.16
  79.9 0.0 copy-start.4
  79.9 0.6 collective-permute-start.8
  80.6 0.6 collective-permute-start.7
  81.1 2.7 %collective-permute-start.6 = (bf16[96,128]{1,0:T(8,128)(2,1)S(1)}, bf16[96,128]{1,0:T(8,128)(2,1)S(1)}, u32[]{:S(2)}, u32[]{:S(2)}) collective-permute-start(bf16[96,128]{1,0:T(8,128)(2,1)S(1)} %convert_bitcast_fusion), channel_id=1, source_target_pairs={{0,24},{8,0},{16,8},{24,16},{1,25},{9,1},{17,9},{25,17},{2,26},{10... | collective-permute-start | bytes 73736 | tf_op jit(solution)/shard_map/ppermute | solution.py:244
  83.8 1.8 %collective-permute-done.8 = bf16[96,128]{1,0:T(8,128)(2,1)S(1)} collective-permute-done((bf16[96,128]{1,0:T(8,128)(2,1)S(1)}, bf16[96,128]{1,0:T(8,128)(2,1)S(1)}, u32[]{:S(2)}, u32[]{:S(2)}) %collective-permute-start.8) | collective-permute-done | bytes 24608 | tf_op jit(solution)/shard_map/ppermute | solution.py:244
  85.6 0.0 collective-permute-done.7
  85.6 0.6 collective-permute-done.6
  86.2 0.6 collective-permute-start.9
  86.8 4.1 %collective-permute-done.9 = bf16[1,4,96,128]{3,2,1,0:T(8,128)(2,1)S(1)} collective-permute-done((bf16[1,4,96,128]{3,2,1,0:T(8,128)(2,1)S(1)}, bf16[1,4,96,128]{3,2,1,0:T(8,128)(2,1)S(1)}, u32[]{:S(2)}, u32[]{:S(2)}) %collective-permute-start.9) | collective-permute-done | bytes 98336 | tf_op jit(solution)/shard_map/ppermute | solution.py:172
  90.9 0.6 collective-permute-start.10
  91.5 5.1 %collective-permute-done.10 = bf16[2,4,96,128]{3,2,1,0:T(8,128)(2,1)S(1)} collective-permute-done((bf16[2,4,96,128]{3,2,1,0:T(8,128)(2,1)S(1)}, bf16[2,4,96,128]{3,2,1,0:T(8,128)(2,1)S(1)}, u32[]{:S(2)}, u32[]{:S(2)}) %collective-permute-start.10) | collective-permute-done | bytes 196640 | tf_op jit(solution)/shard_map/ppermute | solution.py:172
  96.7 0.0 copy-start
  96.7 0.1 collective-permute-start.11
  96.8 0.0 copy-done.6
  96.8 0.6 fusion.13.seed_ref
  97.4 1.1 collective-permute-done.11.other_ref
  98.5 0.0 copy-done
  98.5 0.0 copy-start.1
  98.5 0.7 copy-done.1
  99.3 25.4 %backward.1 = f32[2,12,256,128]{3,2,1,0:T(8,128)} custom-call(s32[32]{0:T(128)} %stack.170.base_ref, s32[2]{0:T(128)} %bitcast.131, s32[1024]{0:T(1024)} %bitcast.122, s32[1024]{0:T(1024)} %bitcast.120, s32[1024]{0:T(1024)} %fusion.13.seed_ref, bf16[16,96,128]{2,1,0:T(8,128)(2,1)} %bitcast.115, bf16[16,96,128]{2,1,0:T(8,128)(2,1)} %copy-done.1), custom_call_target="tpu_custom_call" | custom-call | tf_op jit(solution)/shard_map/backward/pallas_call | solution.py:254
  124.7 0.0 copy-done.4
  (11 shorter events, 0.2 us)
Async XLA Ops:
  31.4 30.3 %copy-start.2 = (f32[12,1,8,128]{3,2,1,0:T(8,128)S(1)}, f32[12,1,8,128]{3,2,1,0:T(8,128)}, u32[]{:S(2)}) copy-start(f32[12,1,8,128]{3,2,1,0:T(8,128)} %param.16) | copy-start | bytes 147460
  31.4 30.3 %copy-start.3 = (f32[12,1,8,128]{3,2,1,0:T(8,128)S(1)}, f32[12,1,8,128]{3,2,1,0:T(8,128)}, u32[]{:S(2)}) copy-start(f32[12,1,8,128]{3,2,1,0:T(8,128)} %param.17) | copy-start | bytes 147460
  31.4 30.3 %copy-start.5 = (f32[12,1,8,128]{3,2,1,0:T(8,128)S(1)}, f32[12,1,8,128]{3,2,1,0:T(8,128)}, u32[]{:S(2)}) copy-start(f32[12,1,8,128]{3,2,1,0:T(8,128)} %param.15) | copy-start | bytes 147460
  31.4 2.6 %collective-permute-start = (f32[16,96,128]{2,1,0:T(8,128)}, f32[16,96,128]{2,1,0:T(8,128)S(1)}, u32[]{:S(2)}, u32[]{:S(2)}) collective-permute-start(f32[16,96,128]{2,1,0:T(8,128)} %get-tuple-element.5), channel_id=1, source_target_pairs={{0,1},{1,0},{2,3},{3,2},{4,5},{5,4},{6,7},{7,6},{8,9},{9,8},{10,11... | collective-permute-start | bytes 2359304 | tf_op jit(solution)/shard_map/ppermute | solution.py:172
  35.2 61.6 %copy-start.6 = (s32[1,4,2,128]{3,1,2,0:T(4,128)S(1)}, s32[1,4,2,128]{3,1,2,0:T(4,128)}, u32[]{:S(2)}) copy-start(s32[1,4,2,128]{3,1,2,0:T(4,128)} %copy.24) | copy-start | bytes 12292
  35.2 7.8 %collective-permute-start.1 = (f32[2,4,96,128]{3,2,1,0:T(8,128)S(1)}, f32[2,4,96,128]{3,2,1,0:T(8,128)S(1)}, u32[]{:S(2)}, u32[]{:S(2)}) collective-permute-start(f32[2,4,96,128]{3,2,1,0:T(8,128)S(1)} %slice_bitcast_fusion), channel_id=1, source_target_pairs={{0,2},{1,5},{2,0},{3,7},{4,6},{5,1},{6,4},{7,3},{8,10},{9,13},{10,... | collective-permute-start | bytes 1179656 | tf_op jit(solution)/shard_map/ppermute | solution.py:172
  43.1 5.9 %collective-permute-start.2 = (f32[1,4,96,128]{3,2,1,0:T(8,128)S(1)}, f32[1,4,96,128]{3,2,1,0:T(8,128)S(1)}, u32[]{:S(2)}, u32[]{:S(2)}) collective-permute-start(f32[1,4,96,128]{3,2,1,0:T(8,128)S(1)} %slice_bitcast_fusion.2), channel_id=1, source_target_pairs={{0,4},{1,3},{2,6},{3,1},{4,0},{5,7},{6,2},{7,5},{8,12},{9,11},{10,... | collective-permute-start | bytes 589832 | tf_op jit(solution)/shard_map/ppermute | solution.py:172
  49.1 10.0 %collective-permute-start.3 = (f32[96,128]{1,0:T(8,128)S(1)}, f32[96,128]{1,0:T(8,128)S(1)}, u32[]{:S(2)}, u32[]{:S(2)}) collective-permute-start(f32[96,128]{1,0:T(8,128)S(1)} %get-tuple-element.16), channel_id=1, source_target_pairs={{0,8},{8,16},{16,24},{24,0},{1,9},{9,17},{17,25},{25,1},{2,10},{10... | collective-permute-start | bytes 147464 | tf_op jit(solution)/shard_map/ppermute | solution.py:221
  52.3 6.9 %collective-permute-start.5 = (f32[96,128]{1,0:T(8,128)S(1)}, f32[96,128]{1,0:T(8,128)S(1)}, u32[]{:S(2)}, u32[]{:S(2)}) collective-permute-start(f32[96,128]{1,0:T(8,128)S(1)} %get-tuple-element.17), channel_id=1, source_target_pairs={{0,24},{8,0},{16,8},{24,16},{1,25},{9,1},{17,9},{25,17},{2,26},{10... | collective-permute-start | bytes 147464 | tf_op jit(solution)/shard_map/ppermute | solution.py:221
  56.6 5.1 %collective-permute-start.4 = (f32[96,128]{1,0:T(8,128)S(1)}, f32[96,128]{1,0:T(8,128)S(1)}, u32[]{:S(2)}, u32[]{:S(2)}) collective-permute-start(f32[96,128]{1,0:T(8,128)S(1)} %get-tuple-element.18), channel_id=1, source_target_pairs={{0,16},{8,24},{16,0},{24,8},{1,17},{9,25},{17,1},{25,9},{2,18},{10... | collective-permute-start | bytes 147464 | tf_op jit(solution)/shard_map/ppermute | solution.py:221
  79.9 44.8 %copy-start.4 = (f32[12,1,8,128]{3,2,1,0:T(8,128)}, f32[12,1,8,128]{3,2,1,0:T(8,128)S(1)}, u32[]{:S(2)}) copy-start(f32[12,1,8,128]{3,2,1,0:T(8,128)S(1)} %get-tuple-element.11) | copy-start | bytes 147460
  79.9 5.7 %collective-permute-start.8 = (bf16[96,128]{1,0:T(8,128)(2,1)S(1)}, bf16[96,128]{1,0:T(8,128)(2,1)S(1)}, u32[]{:S(2)}, u32[]{:S(2)}) collective-permute-start(bf16[96,128]{1,0:T(8,128)(2,1)S(1)} %convert_bitcast_fusion), channel_id=1, source_target_pairs={{0,8},{8,16},{16,24},{24,0},{1,9},{9,17},{17,25},{25,1},{2,10},{10... | collective-permute-start | bytes 73736 | tf_op jit(solution)/shard_map/ppermute | solution.py:244
  80.6 5.1 %collective-permute-start.7 = (bf16[96,128]{1,0:T(8,128)(2,1)S(1)}, bf16[96,128]{1,0:T(8,128)(2,1)S(1)}, u32[]{:S(2)}, u32[]{:S(2)}) collective-permute-start(bf16[96,128]{1,0:T(8,128)(2,1)S(1)} %convert_bitcast_fusion), channel_id=1, source_target_pairs={{0,16},{8,24},{16,0},{24,8},{1,17},{9,25},{17,1},{25,9},{2,18},{10... | collective-permute-start | bytes 73736 | tf_op jit(solution)/shard_map/ppermute | solution.py:244
  81.1 5.1 %collective-permute-start.6 = (bf16[96,128]{1,0:T(8,128)(2,1)S(1)}, bf16[96,128]{1,0:T(8,128)(2,1)S(1)}, u32[]{:S(2)}, u32[]{:S(2)}) collective-permute-start(bf16[96,128]{1,0:T(8,128)(2,1)S(1)} %convert_bitcast_fusion), channel_id=1, source_target_pairs={{0,24},{8,0},{16,8},{24,16},{1,25},{9,1},{17,9},{25,17},{2,26},{10... | collective-permute-start | bytes 73736 | tf_op jit(solution)/shard_map/ppermute | solution.py:244
  86.2 4.7 %collective-permute-start.9 = (bf16[1,4,96,128]{3,2,1,0:T(8,128)(2,1)S(1)}, bf16[1,4,96,128]{3,2,1,0:T(8,128)(2,1)S(1)}, u32[]{:S(2)}, u32[]{:S(2)}) collective-permute-start(bf16[1,4,96,128]{3,2,1,0:T(8,128)(2,1)S(1)} %get-tuple-element.20), channel_id=1, source_target_pairs={{0,4},{1,3},{2,6},{3,1},{4,0},{5,7},{6,2},{7,5},{8,12},{9,11},{10,... | collective-permute-start | bytes 294920 | tf_op jit(solution)/shard_map/ppermute | solution.py:172
  90.9 5.7 %collective-permute-start.10 = (bf16[2,4,96,128]{3,2,1,0:T(8,128)(2,1)S(1)}, bf16[2,4,96,128]{3,2,1,0:T(8,128)(2,1)S(1)}, u32[]{:S(2)}, u32[]{:S(2)}) collective-permute-start(bf16[2,4,96,128]{3,2,1,0:T(8,128)(2,1)S(1)} %get-tuple-element.15), channel_id=1, source_target_pairs={{0,2},{1,5},{2,0},{3,7},{4,6},{5,1},{6,4},{7,3},{8,10},{9,13},{10,... | collective-permute-start | bytes 589832 | tf_op jit(solution)/shard_map/ppermute | solution.py:172
  96.7 1.8 %copy-start = (bf16[2,2,4,96,128]{4,3,2,1,0:T(8,128)(2,1)}, bf16[2,2,4,96,128]{4,3,2,1,0:T(8,128)(2,1)S(1)}, u32[]{:S(2)}) copy-start(bf16[2,2,4,96,128]{4,3,2,1,0:T(8,128)(2,1)S(1)} %pad_maximum_fusion) | copy-start | bytes 1179652
  96.7 1.8 %collective-permute-start.11 = (bf16[16,96,128]{2,1,0:T(8,128)(2,1)S(1)}, bf16[16,96,128]{2,1,0:T(8,128)(2,1)S(1)}, u32[]{:S(2)}, u32[]{:S(2)}) collective-permute-start(bf16[16,96,128]{2,1,0:T(8,128)(2,1)S(1)} %bitcast.114), channel_id=1, source_target_pairs={{0,1},{1,0},{2,3},{3,2},{4,5},{5,4},{6,7},{7,6},{8,9},{9,8},{10,11... | collective-permute-start | bytes 1179656 | tf_op jit(solution)/shard_map/ppermute | solution.py:172
  98.5 0.7 copy-start.1

commit v2 on v1

v2 whole, which is shorter than its diff:
```python
import functools

import jax
import jax.numpy as jnp
import numpy as np
from jax import lax
from jax.experimental import pallas as pl
from jax.experimental.pallas import tpu as pltpu
from jax.sharding import PartitionSpec as P

OFFSETS = 7
SPREADS = 3
WEIGHTS = 4
SHAPES = OFFSETS * SPREADS * WEIGHTS
ROW = 16
LANES = 128
BAND = 16
BODY = 64


def fill_table(tab_ref, nodes):
    row = lax.broadcasted_iota(jnp.int32, (8, nodes), 0)
    lane = lax.broadcasted_iota(jnp.int32, (8, nodes), 1)
    signed = jnp.where(lane < nodes // 2, lane, lane - nodes)

    def one(k, carry):
        offset = k % OFFSETS - OFFSETS // 2
        spread = 0.55 + 0.1 * (k // OFFSETS).astype(jnp.float32)
        wrapped = row - signed - offset
        distance = wrapped.astype(jnp.float32)
        base = jnp.exp(-distance * distance / (2.0 * spread * spread))
        bells = []
        for i in range(0, nodes, 8):
            bell = base if i == 0 else pltpu.roll(base, i, 1)
            if i < 2 * BAND or i >= nodes - 2 * BAND:
                near = jnp.abs(row + i - lane) < nodes // 2
                bell = jnp.where(near, bell, 0.0)
            bells.append(bell)
        for w in range(WEIGHTS):
            weight = np.float32(0.1) + np.float32(0.1) * np.float32(w)
            at = pl.multiple_of((w * OFFSETS * SPREADS + k) * nodes, nodes)
            for i in range(0, len(bells), 2):
                pair = jnp.concatenate([weight * bells[i], weight * bells[i + 1]], axis=0)
                tab_ref[pl.ds(at + i * 8, 16), :] = pair.astype(jnp.bfloat16)
        return carry

    lax.fori_loop(0, OFFSETS * SPREADS, one, 0)


def tile_loop(count, load, add):
    def group(i, carry):
        results = []
        for u in range(0, BODY, 2):
            x0, g0 = load(i * BODY + u)
            x1, g1 = load(i * BODY + u + 1)
            y = jnp.dot(
                jnp.concatenate([x0, x1], axis=0),
                jnp.concatenate([g0, g1], axis=1),
                preferred_element_type=jnp.float32,
            )
            results += [y[:ROW, :LANES], y[ROW:, LANES:]]
        for u in range(BODY):
            add(i * BODY + u, results[u])
        return carry

    lax.fori_loop(0, (count + BODY - 1) // BODY, group, 0)


def slot_of(dims, owner, target):
    half, subs = dims["half"], dims["subs"]
    r = lax.axis_index("mesh") ^ owner
    return ((r & 1) * half + (r >> 1)) * subs + target


def forward_kernel(
    dims, count_ref, owner_ref, target_ref, source_ref, seed_ref, field_ref,
    sum_ref, tab_out, tab_ref, raw_ref, rows_ref, sems,
):
    events, comps, eblocks, nodes = dims["field"]
    blocks = dims["blocks"]
    fetch = pltpu.make_async_copy(field_ref, raw_ref, sems.at[0])
    fetch.start()
    fill_table(tab_ref, nodes)
    hand_on = pltpu.make_async_copy(tab_ref, tab_out, sems.at[1])
    sum_ref[...] = jnp.zeros_like(sum_ref)
    fetch.wait()
    for v in range(events):
        for c in range(comps):
            rows_ref[pl.ds(v * eblocks * ROW + c, eblocks, stride=ROW), :] = raw_ref[
                v, c
            ].astype(jnp.float32)
    hand_on.start()
    for v in range(events):
        count = count_ref[v, 0]

        def load(t, v=v):
            src = pl.multiple_of(source_ref[v, t] * ROW + v * eblocks * ROW, ROW)
            shape = pl.multiple_of(seed_ref[v, t] * nodes, nodes)
            return rows_ref[pl.ds(src, ROW), :].astype(jnp.bfloat16), tab_ref[pl.ds(shape, nodes), :]

        def add(t, y, v=v, count=count):
            slot = slot_of(dims, owner_ref[v, 0, t], target_ref[v, t])
            at = pl.ds(pl.multiple_of(jnp.where(t < count, slot, blocks) * comps, 4), comps)
            y = y.astype(jnp.bfloat16).astype(jnp.float32)
            sum_ref[at, :] = sum_ref[at, :] + y[:comps]

        tile_loop(count, load, add)
    hand_on.wait()


def backward_kernel(
    dims, count_ref, owner_ref, target_ref, source_ref, seed_ref, tab_in, *refs,
):
    events, comps, eblocks, nodes = dims["field"]
    half, subs = dims["half"], dims["subs"]
    mine_refs, (other_ref, out_ref, tab_ref, rows_ref, sum_ref, tile_ref, sems) = (
        refs[:half], refs[half:],
    )
    fetch = pltpu.make_async_copy(tab_in, tab_ref, sems.at[0])
    fetch.start()
    sum_ref[...] = jnp.zeros_like(sum_ref)
    part = subs * comps
    for j in range(half):
        rows_ref[pl.ds(j * part, part), :] = mine_refs[j][...].astype(jnp.float32)
        rows_ref[pl.ds((half + j) * part, part), :] = other_ref[j].astype(jnp.float32)
    fetch.wait()
    sends = []
    for v in range(events):
        count = count_ref[v, 0]

        def load(t, v=v):
            slot = slot_of(dims, owner_ref[v, 0, t], target_ref[v, t])
            seed = seed_ref[v, t]
            turned = seed - 2 * lax.rem(seed, OFFSETS) + (OFFSETS - 1)
            shape = pl.multiple_of(turned * nodes, nodes)
            at = pl.ds(pl.multiple_of(slot * comps, 4), ROW)
            return rows_ref[at, :].astype(jnp.bfloat16), tab_ref[pl.ds(shape, nodes), :]

        def add(t, y, v=v, count=count):
            src = jnp.where(t < count, source_ref[v, t] + v * eblocks, events * eblocks)
            at = pl.ds(pl.multiple_of(src * ROW, ROW), ROW)
            sum_ref[at, :] = sum_ref[at, :] + y

        tile_loop(count, load, add)
        for c in range(comps):
            tile_ref[v, c] = sum_ref[pl.ds(v * eblocks * ROW + c, eblocks, stride=ROW), :]
        send = pltpu.make_async_copy(tile_ref.at[v], out_ref.at[v], sems.at[1 + v])
        send.start()
        sends.append(send)
    for send in sends:
        send.wait()


def pack_kernel(comps, group, *refs):
    ins, (out_ref, wide_ref) = refs[:-2], refs[-2:]
    rows = comps * group
    for n, ref in enumerate(ins):
        for c in range(comps):
            wide_ref[pl.ds(c, group, stride=ROW), :] = ref[c, 0]
        for s in range(group):
            out_ref[n, pl.ds(s * comps, comps), :] = wide_ref[pl.ds(s * ROW, comps), :]


def terms(a_ref, b_ref, hist_ref, k, rows, evs):
    group = lax.axis_index("ev") ^ k
    at = pl.ds(pl.multiple_of(group * rows, 8), rows)
    gradient = a_ref[at, :] + b_ref[at, :]
    prev_gradient, prev_step, precond = hist_ref[k, 0], hist_ref[k, 1], hist_ref[k, 2]
    return at, gradient, gradient - prev_gradient, prev_step, precond


def sums_kernel(rows, evs, a_ref, b_ref, hist_ref, out_ref):
    total = [jnp.zeros((8, LANES), jnp.float32) for _ in range(4)]
    for k in range(evs):
        _, gradient, change, prev_step, precond = terms(a_ref, b_ref, hist_ref, k, rows, evs)
        weighted = precond * change
        parts = (prev_step * change, prev_step * gradient, weighted * gradient, weighted * change)
        for n, part in enumerate(parts):
            total[n] = total[n] + jnp.sum(part.reshape(rows // 8, 8, LANES), axis=0)
    for n in range(4):
        out_ref[pl.ds(n, 1), :] = jnp.sum(total[n], axis=0, keepdims=True)
    out_ref[pl.ds(4, 4), :] = jnp.zeros((4, LANES), jnp.float32)


def direction_kernel(rows, evs, comps, group, a_ref, b_ref, hist_ref, *refs):
    sum_refs, (inv_ref, round_ref, wide_ref) = refs[:-3], refs[-3:]
    level = [ref[...] for ref in sum_refs]
    while len(level) > 1:
        level = [level[i] + level[i + 1] for i in range(0, len(level), 2)]
    sums = jnp.sum(level[0], axis=1, keepdims=True)
    curvature, slope, cross_term, self_term = (sums[n : n + 1] for n in range(4))
    alpha = slope / curvature
    beta = (cross_term - alpha * self_term) / curvature
    bend = alpha - beta
    for k in range(evs):
        at, gradient, change, prev_step, precond = terms(a_ref, b_ref, hist_ref, k, rows, evs)
        scaled = precond * (gradient - alpha * change)
        direction = -(scaled + bend * prev_step)
        round_ref[at, :] = direction.astype(jnp.bfloat16)
        if k == 0:
            for s in range(group):
                wide_ref[pl.ds(s * ROW, comps), :] = direction[s * comps : (s + 1) * comps]
            for c in range(comps):
                inv_ref[c, 0] = wide_ref[pl.ds(c, group, stride=ROW), :]


def in_smem():
    return pl.BlockSpec(memory_space=pltpu.SMEM)


def in_vmem():
    return pl.BlockSpec(memory_space=pltpu.VMEM)


def in_place():
    return pl.BlockSpec(memory_space=pl.ANY)


def limit(mib):
    return pltpu.CompilerParams(vmem_limit_bytes=mib << 20)


def f32(*shape):
    return jax.ShapeDtypeStruct(shape, jnp.float32)


def bf16(*shape):
    return jax.ShapeDtypeStruct(shape, jnp.bfloat16)


def body(
    kernels, tile_owner, tile_source, tile_target, tile_seed, tile_count, prev_gradient,
    prev_step, precond,
):
    events, comps, eblocks, nodes = kernels.shape
    parts = lax.axis_size("mesh")
    evs = lax.axis_size("ev")
    group = precond.shape[2]
    subs = group * evs
    blocks = parts * subs
    half = parts // 2
    rows = comps * group
    part_rows = comps * subs
    dims = dict(field=kernels.shape, half=half, subs=subs, blocks=blocks)

    def swap(x, axis, k):
        size = parts if axis == "mesh" else evs
        return lax.ppermute(x, axis, [(i, i ^ k) for i in range(size)])

    owners = jnp.transpose(tile_owner, (0, 2, 1))
    lists = (tile_count, owners, tile_target, tile_source, tile_seed)
    table = bf16(SHAPES * nodes, nodes)

    packed = pl.pallas_call(
        functools.partial(pack_kernel, comps, group),
        out_shape=f32(3, rows, nodes),
        in_specs=[in_vmem()] * 3,
        out_specs=in_vmem(),
        scratch_shapes=[pltpu.VMEM((group * ROW, nodes), jnp.float32)],
        compiler_params=limit(2),
        name="pack",
    )(prev_gradient, prev_step, precond)

    sums, tab = pl.pallas_call(
        functools.partial(forward_kernel, dims),
        out_shape=[f32(blocks * comps + ROW, nodes), table],
        in_specs=[in_smem()] * 5 + [in_place()],
        out_specs=[in_vmem(), in_place()],
        scratch_shapes=[
            pltpu.VMEM(table.shape, jnp.bfloat16),
            pltpu.VMEM(kernels.shape, jnp.bfloat16),
            pltpu.VMEM((events * eblocks * ROW, nodes), jnp.float32),
            pltpu.SemaphoreType.DMA((2,)),
        ],
        compiler_params=limit(20),
        name="forward",
    )(*lists, kernels)

    hist = packed[None]
    for bit in range(evs.bit_length() - 1):
        hist = jnp.concatenate([hist, swap(hist, "ev", 1 << bit)], axis=0)

    keep = sums[: half * part_rows].reshape(half, part_rows, nodes)
    send = sums[half * part_rows : 2 * half * part_rows].reshape(half, part_rows, nodes)
    got = swap(send, "mesh", 1)
    held = [keep[j] + got[j] for j in range(half)]
    arrived = [swap(held[j], "mesh", 2 * j) for j in range(1, half)]
    total = held[0]
    for piece in arrived:
        total = total + piece
    bits = evs.bit_length() - 1
    for bit in range(bits - 1):
        total = total + swap(total, "ev", 1 << bit)
    across = swap(total, "ev", 1 << (bits - 1))

    local = pl.pallas_call(
        functools.partial(sums_kernel, rows, evs),
        out_shape=f32(8, nodes),
        in_specs=[in_vmem()] * 3,
        out_specs=in_vmem(),
        compiler_params=limit(4),
        name="sums",
    )(total, across, hist)
    local = local + swap(local, "mesh", 1)
    spread = [local] + [swap(local, "mesh", 2 * j) for j in range(1, half)]
    inversion_direction, rounded = pl.pallas_call(
        functools.partial(direction_kernel, rows, evs, comps, group),
        out_shape=[f32(*precond.shape), bf16(part_rows, nodes)],
        in_specs=[in_vmem()] * (3 + half),
        out_specs=[in_vmem()] * 2,
        scratch_shapes=[pltpu.VMEM((group * ROW, nodes), jnp.float32)],
        compiler_params=limit(4),
        name="direction",
    )(total, across, hist, *spread)

    mine = [rounded] + [swap(rounded, "mesh", 2 * j) for j in range(1, half)]
    other = swap(jnp.stack(mine), "mesh", 1)

    event_direction = pl.pallas_call(
        functools.partial(backward_kernel, dims),
        out_shape=f32(*kernels.shape),
        in_specs=[in_smem()] * 5 + [in_place()] + [in_vmem()] * (half + 1),
        out_specs=in_place(),
        scratch_shapes=[
            pltpu.VMEM(table.shape, jnp.bfloat16),
            pltpu.VMEM((blocks * comps + ROW, nodes), jnp.float32),
            pltpu.VMEM(((events * eblocks + 1) * ROW, nodes), jnp.float32),
            pltpu.VMEM(kernels.shape, jnp.float32),
            pltpu.SemaphoreType.DMA((1 + events,)),
        ],
        compiler_params=limit(24),
        name="backward",
    )(*lists, tab, *mine, other)
    return inversion_direction, event_direction


def solution(mesh):
    in_specs = (
        P("ev", None, "mesh", None),
        P("ev", "mesh", None),
        P("ev", "mesh"),
        P("ev", "mesh"),
        P("ev", "mesh"),
        P("ev", "mesh"),
        P(None, "mesh", "ev", None),
        P(None, "mesh", "ev", None),
        P(None, "mesh", "ev", None),
    )
    out_specs = (P(None, "mesh", "ev", None), P("ev", None, "mesh", None))
    return jax.shard_map(body, mesh=mesh, in_specs=in_specs, out_specs=out_specs, check_vma=False)
```

time: 126 us -> 95.5 us (0.76); the launches traced: 125 us -> 95.9 us
  Pallas kernels: 51.5 us -> 34.4 us
  blocking collectives: 10.9 us -> 0 us
  waiting for transfers between devices: 30 us -> 37.4 us
  other arithmetic: 6.1 us -> 0.28 us
  between operations: 4.09 us -> 0.79 us
  starting transfers between devices: 16.7 us -> 18.1 us
    pallas_call x2 -> x5, Pallas kernels: 51.5 us -> 34.4 us  [the longest x1 17.4 us: body(): pl.pallas_call(functools.partial(backward_kernel, dims), out_shape=f32(*k...]
    all_to_all x1 -> x0, blocking collectives: 10.9 us -> none  [body(): lax.all_to_all(spread, ('ev', 'mesh'), 0, 0, tiled=True)]
    ppermute x12 -> x16, waiting for transfers between devices: 30 us -> 37.4 us  [swap(): return lax.ppermute(x, axis, [(i, i ^ k) for i in range(size)])]
    another operation x6 -> x1, other arithmetic: 2.79 us -> 0.05 us  [body(): other = swap(jnp.stack(mine), 'mesh', 1)]
    add x3 -> x4, other arithmetic: 1.88 us -> 0.17 us  [the longest x1 0.07 us: body(): held = [keep[j] + got[j] for j in range(half)]]
    ppermute x12 -> x16, starting transfers between devices: 16.7 us -> 18.1 us  [swap(): return lax.ppermute(x, axis, [(i, i ^ k) for i in range(size)])]
    unnamed x17 -> x25, local copies, waits for them, and re-layouts: 3.92 us -> 4.93 us
  transfers between devices with their start and end apart: 12 -> 16, of which waited for: 10 -> 14; matrix products, arithmetic and copies ran while one was open for 1% -> 0% of each run, Pallas kernels for 0% -> 0%
where the time goes in v2:
time: 95.5 us; the launch traced here: 95.9 us
  waiting for transfers between devices  37.4 us (39%)
  Pallas kernels  34.4 us (36%)
  starting transfers between devices  18.1 us (19%)
  local copies, waits for them, and re-layouts  4.98 us (5%)
    ppermute x16, waiting for transfers between devices, swap(): return lax.ppermute(x, axis, [(i, i ^ k) for i in range(size)])  37.4 us
    ppermute x16, starting transfers between devices, swap(): return lax.ppermute(x, axis, [(i, i ^ k) for i in range(size)])  18.1 us
    pallas_call x1, Pallas kernels, body(): pl.pallas_call(functools.partial(backward_kernel, dims), out_shape=f32(*k...  17.4 us
    pallas_call x1, Pallas kernels, body(): pl.pallas_call(functools.partial(forward_kernel, dims), out_shape=[f32(bl...  16 us
    unnamed x25, local copies, waits for them, and re-layouts  4.93 us
  transfers between devices with their start and end apart: 16, of which 14 were waited for; matrix products, arithmetic and copies ran while one was open for 0% of the time, Pallas kernels for 0%

profile of v2, /device:TPU:0, one launch (start us, length us, event | category | flops | bytes accessed | tf_op | source)
XLA Modules:
  0.0 95.9 jit_solution(13307097162713870219)
XLA Ops:
  0.6 0.7 copy.11.count_ref
  1.4 0.0 copy-start
  1.4 1.4 %copy-done = bf16[2,12,256,128]{3,2,1,0:T(8,128)(2,1)S(1)} copy-done((bf16[2,12,256,128]{3,2,1,0:T(8,128)(2,1)S(1)}, bf16[2,12,256,128]{3,2,1,0:T(8,128)(2,1)}, u32[]{:S(2)}) %copy-start) | copy-done | bytes 1572888
  2.8 0.0 copy-start.4
  2.8 0.7 copy-done.4
  3.5 0.0 copy-start.6
  3.5 0.7 copy-done.6
  4.2 0.0 copy-start.8
  4.2 0.7 copy-done.8
  4.8 0.0 copy-start.10
  4.8 0.7 copy-done.10
  5.5 0.0 copy-start.1
  5.5 16.0 %forward.1 = (f32[3088,128]{1,0:T(8,128)S(1)}, bf16[10752,128]{1,0:T(8,128)(2,1)S(1)}) custom-call(s32[2,1]{1,0:T(2,128)S(1)} %copy.11.count_ref, s32[2,1,512]{2,1,0:T(1,128)S(1)} %bitcast.36, s32[2,512]{1,0:T(2,128)S(1)} %copy-done.6, s32[2,512]{1,0:T(2,128)S(1)} %copy-done.8, s32[2,512]{1,0:T(2,128)S(1)} %copy-done.10, bf16[2,12,256,128]{3,2,1,0:T(8,128)(2,1)S(1)} %copy-done), custom_call_target="tpu_custom_call" | custom-call | tf_op jit(solution)/shard_map/forward/pallas_call | solution.py:264
  21.5 0.1 slice.37
  21.6 0.1 collective-permute-start
  21.7 0.0 copy-done.1
  21.7 0.0 copy-done.2
  21.7 0.0 copy-done.3
  21.7 0.1 pack.1
  21.8 1.6 %collective-permute-start.6 = (f32[1,3,96,128]{3,2,1,0:T(8,128)S(1)}, f32[1,3,96,128]{3,2,1,0:T(8,128)S(1)}, u32[]{:S(2)}, u32[]{:S(2)}) collective-permute-start(f32[1,3,96,128]{3,2,1,0:T(8,128)S(1)} %bitcast.29), channel_id=1, source_target_pairs={{0,8},{8,0},{16,24},{24,16},{1,9},{9,1},{17,25},{25,17},{2,10},{10... | collective-permute-start | bytes 442376 | tf_op jit(solution)/shard_map/ppermute | solution.py:248
  23.4 0.5 collective-permute-done
  23.9 0.1 fusion.2
  24.0 1.9 %collective-permute-start.1 = (f32[384,128]{1,0:T(8,128)S(1)}, f32[384,128]{1,0:T(8,128)S(1)}, u32[]{:S(2)}, u32[]{:S(2)}) collective-permute-start(f32[384,128]{1,0:T(8,128)S(1)} %get-tuple-element.10), channel_id=1, source_target_pairs={{0,2},{1,3},{2,0},{3,1},{4,6},{5,7},{6,4},{7,5},{8,10},{9,11},{10,... | collective-permute-start | bytes 589832 | tf_op jit(solution)/shard_map/ppermute | solution.py:248
  25.9 2.2 %collective-permute-start.3 = (f32[384,128]{1,0:T(8,128)S(1)}, f32[384,128]{1,0:T(8,128)S(1)}, u32[]{:S(2)}, u32[]{:S(2)}) collective-permute-start(f32[384,128]{1,0:T(8,128)S(1)} %get-tuple-element.11), channel_id=1, source_target_pairs={{0,6},{1,7},{2,4},{3,5},{4,2},{5,3},{6,0},{7,1},{8,14},{9,15},{10,... | collective-permute-start | bytes 589832 | tf_op jit(solution)/shard_map/ppermute | solution.py:248
  28.1 0.5 collective-permute-start.2
  28.6 0.0 collective-permute-done.6
  28.6 2.8 %collective-permute-start.7 = (f32[2,3,96,128]{3,2,1,0:T(8,128)S(1)}, f32[2,3,96,128]{3,2,1,0:T(8,128)S(1)}, u32[]{:S(2)}, u32[]{:S(2)}) collective-permute-start(f32[2,3,96,128]{3,2,1,0:T(8,128)S(1)} %pad_maximum_fusion.2), channel_id=1, source_target_pairs={{0,16},{8,24},{16,0},{24,8},{1,17},{9,25},{17,1},{25,9},{2,18},{10... | collective-permute-start | bytes 884744 | tf_op jit(solution)/shard_map/ppermute | solution.py:248
  31.4 0.3 collective-permute-done.1
  31.7 5.8 %collective-permute-done.3 = f32[384,128]{1,0:T(8,128)S(1)} collective-permute-done((f32[384,128]{1,0:T(8,128)S(1)}, f32[384,128]{1,0:T(8,128)S(1)}, u32[]{:S(2)}, u32[]{:S(2)}) %collective-permute-start.3) | collective-permute-done | bytes 196640 | tf_op jit(solution)/shard_map/ppermute | solution.py:248
  37.5 1.4 %collective-permute-done.2 = f32[384,128]{1,0:T(8,128)S(1)} collective-permute-done((f32[384,128]{1,0:T(8,128)S(1)}, f32[384,128]{1,0:T(8,128)S(1)}, u32[]{:S(2)}, u32[]{:S(2)}) %collective-permute-start.2) | collective-permute-done | bytes 196640 | tf_op jit(solution)/shard_map/ppermute | solution.py:248
  38.9 0.1 fusion.6
  39.0 0.1 collective-permute-start.4
  39.1 9.5 %collective-permute-done.4 = f32[384,128]{1,0:T(8,128)S(1)} collective-permute-done((f32[384,128]{1,0:T(8,128)S(1)}, f32[384,128]{1,0:T(8,128)S(1)}, u32[]{:S(2)}, u32[]{:S(2)}) %collective-permute-start.4) | collective-permute-done | bytes 196640 | tf_op jit(solution)/shard_map/ppermute | solution.py:248
  48.6 1.7 %collective-permute-start.5 = (f32[384,128]{1,0:T(8,128)S(1)}, f32[384,128]{1,0:T(8,128)S(1)}, u32[]{:S(2)}, u32[]{:S(2)}) collective-permute-start(f32[384,128]{1,0:T(8,128)S(1)} %add.34.a_ref), channel_id=1, source_target_pairs={{0,16},{8,24},{16,0},{24,8},{1,17},{9,25},{17,1},{25,9},{2,18},{10... | collective-permute-start | bytes 589832 | tf_op jit(solution)/shard_map/ppermute | solution.py:248
  50.3 0.0 collective-permute-done.7
  50.4 0.0 copy-start.5
  50.4 0.0 copy-start.7
  50.4 0.0 copy-start.9
  50.4 0.0 copy-start.11
  50.4 10.2 %collective-permute-done.5.b_ref = f32[384,128]{1,0:T(8,128)S(1)} collective-permute-done((f32[384,128]{1,0:T(8,128)S(1)}, f32[384,128]{1,0:T(8,128)S(1)}, u32[]{:S(2)}, u32[]{:S(2)}) %collective-permute-start.5) | collective-permute-done | bytes 196640 | tf_op jit(solution)/shard_map/ppermute | solution.py:248
  60.6 0.1 sums.1
  60.7 0.1 collective-permute-start.8
  60.8 1.2 %collective-permute-done.8 = f32[8,128]{1,0:T(8,128)S(1)} collective-permute-done((f32[8,128]{1,0:T(8,128)S(1)}, f32[8,128]{1,0:T(8,128)S(1)}, u32[]{:S(2)}, u32[]{:S(2)}) %collective-permute-start.8) | collective-permute-done | bytes 4128 | tf_op jit(solution)/shard_map/ppermute | solution.py:248
  62.0 3.1 %collective-permute-start.11 = (f32[8,128]{1,0:T(8,128)S(1)}, f32[8,128]{1,0:T(8,128)S(1)}, u32[]{:S(2)}, u32[]{:S(2)}) collective-permute-start(f32[8,128]{1,0:T(8,128)S(1)} %add.35.refs_0_), channel_id=1, source_target_pairs={{0,6},{1,7},{2,4},{3,5},{4,2},{5,3},{6,0},{7,1},{8,14},{9,15},{10,... | collective-permute-start | bytes 12296 | tf_op jit(solution)/shard_map/ppermute | solution.py:248
  65.0 0.3 collective-permute-start.10
  65.4 0.2 collective-permute-start.9
  65.6 1.0 %collective-permute-done.11.refs_3_ = f32[8,128]{1,0:T(8,128)S(1)} collective-permute-done((f32[8,128]{1,0:T(8,128)S(1)}, f32[8,128]{1,0:T(8,128)S(1)}, u32[]{:S(2)}, u32[]{:S(2)}) %collective-permute-start.11) | collective-permute-done | bytes 4128 | tf_op jit(solution)/shard_map/ppermute | solution.py:248
  66.6 2.0 %collective-permute-done.10.refs_2_ = f32[8,128]{1,0:T(8,128)S(1)} collective-permute-done((f32[8,128]{1,0:T(8,128)S(1)}, f32[8,128]{1,0:T(8,128)S(1)}, u32[]{:S(2)}, u32[]{:S(2)}) %collective-permute-start.10) | collective-permute-done | bytes 4128 | tf_op jit(solution)/shard_map/ppermute | solution.py:248
  68.6 0.3 collective-permute-done.9.refs_1_
  69.0 0.8 direction.1
  69.8 1.3 %collective-permute-start.14 = (bf16[384,128]{1,0:T(8,128)(2,1)S(1)}, bf16[384,128]{1,0:T(8,128)(2,1)S(1)}, u32[]{:S(2)}, u32[]{:S(2)}) collective-permute-start(bf16[384,128]{1,0:T(8,128)(2,1)S(1)} %get-tuple-element.9.refs_0_), channel_id=1, source_target_pairs={{0,6},{1,7},{2,4},{3,5},{4,2},{5,3},{6,0},{7,1},{8,14},{9,15},{10,... | collective-permute-start | bytes 294920 | tf_op jit(solution)/shard_map/ppermute | solution.py:248
  71.1 0.4 collective-permute-start.13
  71.5 1.8 %collective-permute-start.12 = (bf16[384,128]{1,0:T(8,128)(2,1)S(1)}, bf16[384,128]{1,0:T(8,128)(2,1)S(1)}, u32[]{:S(2)}, u32[]{:S(2)}) collective-permute-start(bf16[384,128]{1,0:T(8,128)(2,1)S(1)} %get-tuple-element.9.refs_0_), channel_id=1, source_target_pairs={{0,2},{1,3},{2,0},{3,1},{4,6},{5,7},{6,4},{7,5},{8,10},{9,11},{10,... | collective-permute-start | bytes 294920 | tf_op jit(solution)/shard_map/ppermute | solution.py:248
  73.3 2.1 %collective-permute-done.14.refs_3_ = bf16[384,128]{1,0:T(8,128)(2,1)S(1)} collective-permute-done((bf16[384,128]{1,0:T(8,128)(2,1)S(1)}, bf16[384,128]{1,0:T(8,128)(2,1)S(1)}, u32[]{:S(2)}, u32[]{:S(2)}) %collective-permute-start.14) | collective-permute-done | bytes 98336 | tf_op jit(solution)/shard_map/ppermute | solution.py:248
  75.3 1.0 %collective-permute-done.13.refs_2_ = bf16[384,128]{1,0:T(8,128)(2,1)S(1)} collective-permute-done((bf16[384,128]{1,0:T(8,128)(2,1)S(1)}, bf16[384,128]{1,0:T(8,128)(2,1)S(1)}, u32[]{:S(2)}, u32[]{:S(2)}) %collective-permute-start.13) | collective-permute-done | bytes 98336 | tf_op jit(solution)/shard_map/ppermute | solution.py:248
  76.3 0.3 collective-permute-done.12.refs_1_
  76.6 0.1 pad_maximum_fusion.1
  76.7 0.1 collective-permute-start.15
  76.8 1.7 %collective-permute-done.15.refs_4_ = bf16[4,384,128]{2,1,0:T(8,128)(2,1)S(1)} collective-permute-done((bf16[4,384,128]{2,1,0:T(8,128)(2,1)S(1)}, bf16[4,384,128]{2,1,0:T(8,128)(2,1)S(1)}, u32[]{:S(2)}, u32[]{:S(2)}) %collective-permute-start.15) | collective-permute-done | bytes 393248 | tf_op jit(solution)/shard_map/ppermute | solution.py:248
  78.5 0.0 copy-done.5
  78.5 0.0 copy-done.7
  78.5 0.0 copy-done.9
  78.5 0.0 copy-done.11
  78.5 17.4 %backward.1 = f32[2,12,256,128]{3,2,1,0:T(8,128)} custom-call(s32[2,1]{1,0:T(2,128)S(1)} %copy.11.count_ref, s32[2,1,512]{2,1,0:T(1,128)S(1)} %bitcast.37, s32[2,512]{1,0:T(2,128)S(1)} %copy-done.7, s32[2,512]{1,0:T(2,128)S(1)} %copy-done.9, s32[2,512]{1,0:T(2,128)S(1)} %copy-done.11, bf16[10752,128]{1,0:T(8,128)(2,1)S(1)} %get-tuple-element.8.tab_in, ...), custom_call_target="tpu_custom_call" | custom-call | tf_op jit(solution)/shard_map/backward/pallas_call | solution.py:319
  (6 shorter events, 0.1 us)
Async XLA Ops:
  1.4 1.4 %copy-start = (bf16[2,12,256,128]{3,2,1,0:T(8,128)(2,1)S(1)}, bf16[2,12,256,128]{3,2,1,0:T(8,128)(2,1)}, u32[]{:S(2)}) copy-start(bf16[2,12,256,128]{3,2,1,0:T(8,128)(2,1)} %field_ref.1) | copy-start | bytes 4718596
  2.8 0.7 copy-start.4
  3.5 0.7 copy-start.6
  4.2 0.7 copy-start.8
  4.8 0.7 copy-start.10
  5.5 16.1 %copy-start.1 = (f32[12,1,8,128]{3,2,1,0:T(8,128)S(1)}, f32[12,1,8,128]{3,2,1,0:T(8,128)}, u32[]{:S(2)}) copy-start(f32[12,1,8,128]{3,2,1,0:T(8,128)} %refs_0_.1) | copy-start | bytes 147460
  5.5 16.2 %copy-start.2 = (f32[12,1,8,128]{3,2,1,0:T(8,128)S(1)}, f32[12,1,8,128]{3,2,1,0:T(8,128)}, u32[]{:S(2)}) copy-start(f32[12,1,8,128]{3,2,1,0:T(8,128)} %refs_1_.1) | copy-start | bytes 147460
  5.5 16.2 %copy-start.3 = (f32[12,1,8,128]{3,2,1,0:T(8,128)S(1)}, f32[12,1,8,128]{3,2,1,0:T(8,128)}, u32[]{:S(2)}) copy-start(f32[12,1,8,128]{3,2,1,0:T(8,128)} %refs_2_.1) | copy-start | bytes 147460
  21.6 2.4 %collective-permute-start = (f32[4,384,128]{2,1,0:T(8,128)S(1)}, f32[4,384,128]{2,1,0:T(8,128)S(1)}, u32[]{:S(2)}, u32[]{:S(2)}) collective-permute-start(f32[4,384,128]{2,1,0:T(8,128)S(1)} %bitcast.38), channel_id=1, source_target_pairs={{0,1},{1,0},{2,3},{3,2},{4,5},{5,4},{6,7},{7,6},{8,9},{9,8},{10,11... | collective-permute-start | bytes 2359304 | tf_op jit(solution)/shard_map/ppermute | solution.py:248
  21.8 6.8 %collective-permute-start.6 = (f32[1,3,96,128]{3,2,1,0:T(8,128)S(1)}, f32[1,3,96,128]{3,2,1,0:T(8,128)S(1)}, u32[]{:S(2)}, u32[]{:S(2)}) collective-permute-start(f32[1,3,96,128]{3,2,1,0:T(8,128)S(1)} %bitcast.29), channel_id=1, source_target_pairs={{0,8},{8,0},{16,24},{24,16},{1,9},{9,1},{17,25},{25,17},{2,10},{10... | collective-permute-start | bytes 442376 | tf_op jit(solution)/shard_map/ppermute | solution.py:248
  24.0 7.7 %collective-permute-start.1 = (f32[384,128]{1,0:T(8,128)S(1)}, f32[384,128]{1,0:T(8,128)S(1)}, u32[]{:S(2)}, u32[]{:S(2)}) collective-permute-start(f32[384,128]{1,0:T(8,128)S(1)} %get-tuple-element.10), channel_id=1, source_target_pairs={{0,2},{1,3},{2,0},{3,1},{4,6},{5,7},{6,4},{7,5},{8,10},{9,11},{10,... | collective-permute-start | bytes 589832 | tf_op jit(solution)/shard_map/ppermute | solution.py:248
  25.9 11.6 %collective-permute-start.3 = (f32[384,128]{1,0:T(8,128)S(1)}, f32[384,128]{1,0:T(8,128)S(1)}, u32[]{:S(2)}, u32[]{:S(2)}) collective-permute-start(f32[384,128]{1,0:T(8,128)S(1)} %get-tuple-element.11), channel_id=1, source_target_pairs={{0,6},{1,7},{2,4},{3,5},{4,2},{5,3},{6,0},{7,1},{8,14},{9,15},{10,... | collective-permute-start | bytes 589832 | tf_op jit(solution)/shard_map/ppermute | solution.py:248
  28.1 10.9 %collective-permute-start.2 = (f32[384,128]{1,0:T(8,128)S(1)}, f32[384,128]{1,0:T(8,128)S(1)}, u32[]{:S(2)}, u32[]{:S(2)}) collective-permute-start(f32[384,128]{1,0:T(8,128)S(1)} %get-tuple-element.12), channel_id=1, source_target_pairs={{0,4},{1,5},{2,6},{3,7},{4,0},{5,1},{6,2},{7,3},{8,12},{9,13},{10,... | collective-permute-start | bytes 589832 | tf_op jit(solution)/shard_map/ppermute | solution.py:248
  28.6 21.7 %collective-permute-start.7 = (f32[2,3,96,128]{3,2,1,0:T(8,128)S(1)}, f32[2,3,96,128]{3,2,1,0:T(8,128)S(1)}, u32[]{:S(2)}, u32[]{:S(2)}) collective-permute-start(f32[2,3,96,128]{3,2,1,0:T(8,128)S(1)} %pad_maximum_fusion.2), channel_id=1, source_target_pairs={{0,16},{8,24},{16,0},{24,8},{1,17},{9,25},{17,1},{25,9},{2,18},{10... | collective-permute-start | bytes 884744 | tf_op jit(solution)/shard_map/ppermute | solution.py:248
  39.0 9.6 %collective-permute-start.4 = (f32[384,128]{1,0:T(8,128)S(1)}, f32[384,128]{1,0:T(8,128)S(1)}, u32[]{:S(2)}, u32[]{:S(2)}) collective-permute-start(f32[384,128]{1,0:T(8,128)S(1)} %fusion.6), channel_id=1, source_target_pairs={{0,8},{8,0},{16,24},{24,16},{1,9},{9,1},{17,25},{25,17},{2,10},{10... | collective-permute-start | bytes 589832 | tf_op jit(solution)/shard_map/ppermute | solution.py:248
  48.6 12.0 %collective-permute-start.5 = (f32[384,128]{1,0:T(8,128)S(1)}, f32[384,128]{1,0:T(8,128)S(1)}, u32[]{:S(2)}, u32[]{:S(2)}) collective-permute-start(f32[384,128]{1,0:T(8,128)S(1)} %add.34.a_ref), channel_id=1, source_target_pairs={{0,16},{8,24},{16,0},{24,8},{1,17},{9,25},{17,1},{25,9},{2,18},{10... | collective-permute-start | bytes 589832 | tf_op jit(solution)/shard_map/ppermute | solution.py:248
  50.4 28.1 %copy-start.5 = (s32[2,512,1]{1,2,0:T(1,128)S(1)}, s32[2,512,1]{1,2,0:T(1,128)}, u32[]{:S(2)}) copy-start(s32[2,512,1]{1,2,0:T(1,128)} %param.10) | copy-start | bytes 12292
  50.4 28.1 %copy-start.7 = (s32[2,512]{1,0:T(2,128)S(1)}, s32[2,512]{1,0:T(2,128)}, u32[]{:S(2)}) copy-start(s32[2,512]{1,0:T(2,128)} %target_ref.3) | copy-start | bytes 12292
  50.4 28.1 %copy-start.9 = (s32[2,512]{1,0:T(2,128)S(1)}, s32[2,512]{1,0:T(2,128)}, u32[]{:S(2)}) copy-start(s32[2,512]{1,0:T(2,128)} %source_ref.3) | copy-start | bytes 12292
  50.4 28.1 %copy-start.11 = (s32[2,512]{1,0:T(2,128)S(1)}, s32[2,512]{1,0:T(2,128)}, u32[]{:S(2)}) copy-start(s32[2,512]{1,0:T(2,128)} %seed_ref.3) | copy-start | bytes 12292
  60.7 1.2 %collective-permute-start.8 = (f32[8,128]{1,0:T(8,128)S(1)}, f32[8,128]{1,0:T(8,128)S(1)}, u32[]{:S(2)}, u32[]{:S(2)}) collective-permute-start(f32[8,128]{1,0:T(8,128)S(1)} %sums.1), channel_id=1, source_target_pairs={{0,1},{1,0},{2,3},{3,2},{4,5},{5,4},{6,7},{7,6},{8,9},{9,8},{10,11... | collective-permute-start | bytes 12296 | tf_op jit(solution)/shard_map/ppermute | solution.py:248
  62.0 4.6 %collective-permute-start.11 = (f32[8,128]{1,0:T(8,128)S(1)}, f32[8,128]{1,0:T(8,128)S(1)}, u32[]{:S(2)}, u32[]{:S(2)}) collective-permute-start(f32[8,128]{1,0:T(8,128)S(1)} %add.35.refs_0_), channel_id=1, source_target_pairs={{0,6},{1,7},{2,4},{3,5},{4,2},{5,3},{6,0},{7,1},{8,14},{9,15},{10,... | collective-permute-start | bytes 12296 | tf_op jit(solution)/shard_map/ppermute | solution.py:248
  65.0 3.6 %collective-permute-start.10 = (f32[8,128]{1,0:T(8,128)S(1)}, f32[8,128]{1,0:T(8,128)S(1)}, u32[]{:S(2)}, u32[]{:S(2)}) collective-permute-start(f32[8,128]{1,0:T(8,128)S(1)} %add.35.refs_0_), channel_id=1, source_target_pairs={{0,4},{1,5},{2,6},{3,7},{4,0},{5,1},{6,2},{7,3},{8,12},{9,13},{10,... | collective-permute-start | bytes 12296 | tf_op jit(solution)/shard_map/ppermute | solution.py:248
  65.4 3.6 %collective-permute-start.9 = (f32[8,128]{1,0:T(8,128)S(1)}, f32[8,128]{1,0:T(8,128)S(1)}, u32[]{:S(2)}, u32[]{:S(2)}) collective-permute-start(f32[8,128]{1,0:T(8,128)S(1)} %add.35.refs_0_), channel_id=1, source_target_pairs={{0,2},{1,3},{2,0},{3,1},{4,6},{5,7},{6,4},{7,5},{8,10},{9,11},{10,... | collective-permute-start | bytes 12296 | tf_op jit(solution)/shard_map/ppermute | solution.py:248
  69.8 5.6 %collective-permute-start.14 = (bf16[384,128]{1,0:T(8,128)(2,1)S(1)}, bf16[384,128]{1,0:T(8,128)(2,1)S(1)}, u32[]{:S(2)}, u32[]{:S(2)}) collective-permute-start(bf16[384,128]{1,0:T(8,128)(2,1)S(1)} %get-tuple-element.9.refs_0_), channel_id=1, source_target_pairs={{0,6},{1,7},{2,4},{3,5},{4,2},{5,3},{6,0},{7,1},{8,14},{9,15},{10,... | collective-permute-start | bytes 294920 | tf_op jit(solution)/shard_map/ppermute | solution.py:248
  71.1 5.2 %collective-permute-start.13 = (bf16[384,128]{1,0:T(8,128)(2,1)S(1)}, bf16[384,128]{1,0:T(8,128)(2,1)S(1)}, u32[]{:S(2)}, u32[]{:S(2)}) collective-permute-start(bf16[384,128]{1,0:T(8,128)(2,1)S(1)} %get-tuple-element.9.refs_0_), channel_id=1, source_target_pairs={{0,4},{1,5},{2,6},{3,7},{4,0},{5,1},{6,2},{7,3},{8,12},{9,13},{10,... | collective-permute-start | bytes 294920 | tf_op jit(solution)/shard_map/ppermute | solution.py:248
  71.5 5.2 %collective-permute-start.12 = (bf16[384,128]{1,0:T(8,128)(2,1)S(1)}, bf16[384,128]{1,0:T(8,128)(2,1)S(1)}, u32[]{:S(2)}, u32[]{:S(2)}) collective-permute-start(bf16[384,128]{1,0:T(8,128)(2,1)S(1)} %get-tuple-element.9.refs_0_), channel_id=1, source_target_pairs={{0,2},{1,3},{2,0},{3,1},{4,6},{5,7},{6,4},{7,5},{8,10},{9,11},{10,... | collective-permute-start | bytes 294920 | tf_op jit(solution)/shard_map/ppermute | solution.py:248
  76.7 1.8 %collective-permute-start.15 = (bf16[4,384,128]{2,1,0:T(8,128)(2,1)S(1)}, bf16[4,384,128]{2,1,0:T(8,128)(2,1)S(1)}, u32[]{:S(2)}, u32[]{:S(2)}) collective-permute-start(bf16[4,384,128]{2,1,0:T(8,128)(2,1)S(1)} %pad_maximum_fusion.1), channel_id=1, source_target_pairs={{0,1},{1,0},{2,3},{3,2},{4,5},{5,4},{6,7},{7,6},{8,9},{9,8},{10,11... | collective-permute-start | bytes 1179656 | tf_op jit(solution)/shard_map/ppermute | solution.py:248

commit v3 on v2

v3 whole, which is shorter than its diff:
```python
import functools

import jax
import jax.numpy as jnp
import numpy as np
from jax import lax
from jax.experimental import pallas as pl
from jax.experimental.pallas import tpu as pltpu
from jax.sharding import PartitionSpec as P

OFFSETS = 7
SPREADS = 3
WEIGHTS = 4
SHAPES = OFFSETS * SPREADS * WEIGHTS
ROW = 16
PITCH = 13
LANES = 128
BAND = 16
CODES = 4


def fill_table(tab_ref, nodes):
    row = lax.broadcasted_iota(jnp.int32, (8, nodes), 0)
    lane = lax.broadcasted_iota(jnp.int32, (8, nodes), 1)
    signed = jnp.where(lane < nodes // 2, lane, lane - nodes)

    def one(k, carry):
        spread = 0.55 + 0.1 * k.astype(jnp.float32)
        for o in range(OFFSETS):
            distance = (row - signed - (o - OFFSETS // 2)).astype(jnp.float32)
            base = jnp.exp(-distance * distance / (2.0 * spread * spread))
            bells = []
            for i in range(0, nodes, 8):
                bell = base if i == 0 else pltpu.roll(base, i, 1)
                if i < 2 * BAND or i >= nodes - 2 * BAND:
                    near = jnp.abs(row + i - lane) < nodes // 2
                    bell = jnp.where(near, bell, 0.0)
                bells.append(bell)
            for w in range(WEIGHTS):
                weight = np.float32(0.1) + np.float32(0.1) * np.float32(w)
                first = (k + w * SPREADS) * (OFFSETS * nodes) + o * nodes
                for i in range(0, len(bells), 2):
                    pair = jnp.concatenate([weight * bells[i], weight * bells[i + 1]], axis=0)
                    at = pl.ds(pl.multiple_of(first + i * 8, ROW), ROW)
                    tab_ref[at, :] = pair.astype(jnp.bfloat16)
        return carry

    lax.fori_loop(0, SPREADS, one, 0)


def fill_codes(dims, counts, owner_ref, target_ref, source_ref, seed_ref, codes_ref):
    events, comps, eblocks, nodes = dims["field"]
    half, subs, blocks = dims["half"], dims["subs"], dims["blocks"]
    groups = dims["tiles"] // LANES
    lists = events * groups
    me = lax.axis_index("mesh")
    lane = lax.broadcasted_iota(jnp.int32, (1, LANES), 1)
    for v in range(events):
        for g in range(groups):
            at = pl.ds(g * LANES, LANES)
            live = lane + g * LANES < counts[v]
            r = owner_ref[v, :, at] ^ me
            slot = ((r & 1) * half + (r >> 1)) * subs + target_ref[pl.ds(v, 1), at]
            source = source_ref[pl.ds(v, 1), at] + v * eblocks
            seed = seed_ref[pl.ds(v, 1), at]
            turned = 2 * OFFSETS * ((seed * 9363) >> 16) - seed + (OFFSETS - 1)
            codes = (
                jnp.where(live, source, events * eblocks) * PITCH,
                jnp.where(live, slot, blocks) * comps,
                seed * nodes,
                turned * nodes,
            )
            for n, code in enumerate(codes):
                codes_ref[pl.ds(n * lists + v * groups + g, 1), :] = code


def tile_loop(v, count, groups, load, add):
    def group(i, carry):
        results = []
        for u in range(0, LANES, 2):
            x0, g0 = load(v * groups + i, u)
            x1, g1 = load(v * groups + i, u + 1)
            y = jnp.dot(
                jnp.concatenate([x0, x1], axis=0),
                jnp.concatenate([g0, g1], axis=1),
                preferred_element_type=jnp.float32,
            )
            results += [y[:ROW, :LANES], y[ROW:, LANES:]]
        for u in range(LANES):
            add(v * groups + i, u, results[u])
        return carry

    lax.fori_loop(0, (count + LANES - 1) // LANES, group, 0)


def forward_kernel(
    dims, count_hbm, owner_hbm, target_hbm, source_hbm, seed_hbm, field_hbm, order_ref,
    sum_ref, tab_ref, codes_ref,
    raw_ref, rows_ref, owner_ref, target_ref, source_ref, seed_ref, count_ref, code_ref, sems,
):
    events, comps, eblocks, nodes = dims["field"]
    groups = dims["tiles"] // LANES
    lists = events * groups
    pairs = (
        (count_hbm, count_ref), (owner_hbm, owner_ref), (target_hbm, target_ref),
        (source_hbm, source_ref), (seed_hbm, seed_ref), (field_hbm, raw_ref),
    )
    fetches = [pltpu.make_async_copy(a, b, sems.at[n]) for n, (a, b) in enumerate(pairs)]
    for fetch in fetches:
        fetch.start()
    sum_ref[...] = jnp.zeros_like(sum_ref)
    for fetch in fetches[:-1]:
        fetch.wait()
    counts = [count_ref[0, v] for v in range(events)]
    fill_codes(dims, counts, owner_ref, target_ref, source_ref, seed_ref, codes_ref)
    fill_table(tab_ref, nodes)
    to_smem = pltpu.make_async_copy(codes_ref, code_ref, sems.at[len(pairs)])
    to_smem.start()
    fetches[-1].wait()
    for v in range(events):
        for c in range(comps):
            rows_ref[pl.ds(v * eblocks * PITCH + c, eblocks, stride=PITCH), :] = raw_ref[
                v, c
            ].astype(jnp.float32)
    to_smem.wait()

    def load(i, u):
        shape = pl.multiple_of(code_ref[2 * lists + i, u], nodes)
        x = rows_ref[pl.ds(code_ref[i, u], ROW), :]
        return x.astype(jnp.bfloat16), tab_ref[pl.ds(shape, nodes), :]

    def add(i, u, y):
        at = pl.ds(pl.multiple_of(code_ref[lists + i, u], 4), comps)
        y = y.astype(jnp.bfloat16).astype(jnp.float32)
        sum_ref[at, :] = sum_ref[at, :] + y[:comps]

    for v in range(events):
        tile_loop(v, counts[v], groups, load, add)


def backward_kernel(dims, count_ref, codes_in, tab_ref, *refs):
    events, comps, eblocks, nodes = dims["field"]
    half, subs = dims["half"], dims["subs"]
    groups = dims["tiles"] // LANES
    lists = events * groups
    mine_refs, (other_ref, out_ref, rows_ref, sum_ref, tile_ref, code_ref, sems) = (
        refs[:half], refs[half:],
    )
    to_smem = pltpu.make_async_copy(codes_in, code_ref, sems.at[0])
    to_smem.start()
    sum_ref[...] = jnp.zeros_like(sum_ref)
    part = subs * comps
    for j in range(half):
        rows_ref[pl.ds(j * part, part), :] = mine_refs[j][...].astype(jnp.float32)
        rows_ref[pl.ds((half + j) * part, part), :] = other_ref[j].astype(jnp.float32)
    to_smem.wait()

    def load(i, u):
        shape = pl.multiple_of(code_ref[3 * lists + i, u], nodes)
        x = rows_ref[pl.ds(pl.multiple_of(code_ref[lists + i, u], 4), ROW), :]
        return x.astype(jnp.bfloat16), tab_ref[pl.ds(shape, nodes), :]

    def add(i, u, y):
        at = pl.ds(code_ref[i, u], comps)
        sum_ref[at, :] = sum_ref[at, :] + y[:comps]

    sends = []
    for v in range(events):
        tile_loop(v, count_ref[0, v], groups, load, add)
        for c in range(comps):
            tile_ref[v, c] = sum_ref[pl.ds(v * eblocks * PITCH + c, eblocks, stride=PITCH), :]
        send = pltpu.make_async_copy(tile_ref.at[v], out_ref.at[v], sems.at[1 + v])
        send.start()
        sends.append(send)
    for send in sends:
        send.wait()


def pack_kernel(comps, group, *refs):
    ins, (out_ref, wide_ref) = refs[:-2], refs[-2:]
    rows = comps * group
    for n, ref in enumerate(ins):
        for c in range(comps):
            wide_ref[pl.ds(c, group, stride=PITCH), :] = ref[c, 0]
        for s in range(group):
            out_ref[n, pl.ds(s * comps, comps), :] = wide_ref[pl.ds(s * PITCH, comps), :]


def terms(a_ref, b_ref, hist_ref, k, rows, evs):
    group = lax.axis_index("ev") ^ k
    at = pl.ds(pl.multiple_of(group * rows, 8), rows)
    gradient = a_ref[at, :] + b_ref[at, :]
    prev_gradient, prev_step, precond = hist_ref[k, 0], hist_ref[k, 1], hist_ref[k, 2]
    return at, gradient, gradient - prev_gradient, prev_step, precond


def sums_kernel(rows, evs, a_ref, b_ref, hist_ref, out_ref):
    total = [jnp.zeros((8, LANES), jnp.float32) for _ in range(4)]
    for k in range(evs):
        _, gradient, change, prev_step, precond = terms(a_ref, b_ref, hist_ref, k, rows, evs)
        weighted = precond * change
        parts = (prev_step * change, prev_step * gradient, weighted * gradient, weighted * change)
        for n, part in enumerate(parts):
            total[n] = total[n] + jnp.sum(part.reshape(rows // 8, 8, LANES), axis=0)
    for n in range(4):
        out_ref[pl.ds(n, 1), :] = jnp.sum(total[n], axis=0, keepdims=True)
    out_ref[pl.ds(4, 4), :] = jnp.zeros((4, LANES), jnp.float32)


def direction_kernel(rows, evs, comps, group, a_ref, b_ref, hist_ref, *refs):
    sum_refs, (inv_ref, round_ref, wide_ref) = refs[:-3], refs[-3:]
    level = [ref[...] for ref in sum_refs]
    while len(level) > 1:
        level = [level[i] + level[i + 1] for i in range(0, len(level), 2)]
    sums = jnp.sum(level[0], axis=1, keepdims=True)
    curvature, slope, cross_term, self_term = (sums[n : n + 1] for n in range(4))
    alpha = slope / curvature
    beta = (cross_term - alpha * self_term) / curvature
    bend = alpha - beta
    for k in range(evs):
        at, gradient, change, prev_step, precond = terms(a_ref, b_ref, hist_ref, k, rows, evs)
        scaled = precond * (gradient - alpha * change)
        direction = -(scaled + bend * prev_step)
        round_ref[at, :] = direction.astype(jnp.bfloat16)
        if k == 0:
            for s in range(group):
                wide_ref[pl.ds(s * PITCH, comps), :] = direction[s * comps : (s + 1) * comps]
            for c in range(comps):
                inv_ref[c, 0] = wide_ref[pl.ds(c, group, stride=PITCH), :]


def in_smem():
    return pl.BlockSpec(memory_space=pltpu.SMEM)


def in_vmem():
    return pl.BlockSpec(memory_space=pltpu.VMEM)


def in_hbm():
    return pl.BlockSpec(memory_space=pltpu.HBM)


def limit(mib):
    return pltpu.CompilerParams(vmem_limit_bytes=mib << 20)


def f32(*shape):
    return jax.ShapeDtypeStruct(shape, jnp.float32)


def bf16(*shape):
    return jax.ShapeDtypeStruct(shape, jnp.bfloat16)


def body(
    kernels, tile_owner, tile_source, tile_target, tile_seed, tile_count, prev_gradient,
    prev_step, precond,
):
    events, comps, eblocks, nodes = kernels.shape
    parts = lax.axis_size("mesh")
    evs = lax.axis_size("ev")
    group = precond.shape[2]
    subs = group * evs
    blocks = parts * subs
    half = parts // 2
    rows = comps * group
    part_rows = comps * subs
    tiles = tile_source.shape[1]
    dims = dict(field=kernels.shape, half=half, subs=subs, blocks=blocks, tiles=tiles)

    def swap(x, axis, k):
        size = parts if axis == "mesh" else evs
        return lax.ppermute(x, axis, [(i, i ^ k) for i in range(size)])

    owners = jnp.transpose(tile_owner, (0, 2, 1))
    counts = jnp.transpose(tile_count)
    table = bf16(SHAPES * nodes, nodes)
    code_rows = (CODES * events * tiles // LANES, LANES)
    codes_shape = jax.ShapeDtypeStruct(code_rows, jnp.int32)

    packed = pl.pallas_call(
        functools.partial(pack_kernel, comps, group),
        out_shape=f32(3, rows, nodes),
        in_specs=[in_vmem()] * 3,
        out_specs=in_vmem(),
        scratch_shapes=[pltpu.VMEM((group * PITCH, nodes), jnp.float32)],
        compiler_params=limit(2),
        name="pack",
    )(prev_gradient, prev_step, precond)
    hist = jnp.stack([packed] + [swap(packed, "ev", k) for k in range(1, evs)])

    sums, tab, codes = pl.pallas_call(
        functools.partial(forward_kernel, dims),
        out_shape=[f32(blocks * comps + ROW, nodes), table, codes_shape],
        in_specs=[in_hbm()] * 6 + [in_vmem()],
        out_specs=[in_vmem()] * 3,
        scratch_shapes=[
            pltpu.VMEM(kernels.shape, jnp.bfloat16),
            pltpu.VMEM((events * eblocks * PITCH + ROW, nodes), jnp.float32),
            pltpu.VMEM(owners.shape, jnp.int32),
            pltpu.VMEM(tile_target.shape, jnp.int32),
            pltpu.VMEM(tile_source.shape, jnp.int32),
            pltpu.VMEM(tile_seed.shape, jnp.int32),
            pltpu.SMEM(counts.shape, jnp.int32),
            pltpu.SMEM(code_rows, jnp.int32),
            pltpu.SemaphoreType.DMA((7,)),
        ],
        compiler_params=limit(20),
        cost_estimate=pl.CostEstimate(
            flops=2 * events * tiles * ROW * nodes * nodes * 64,
            bytes_accessed=16 << 20,
            transcendentals=0,
        ),
        name="forward",
    )(counts, owners, tile_target, tile_source, tile_seed, kernels, packed)

    keep = sums[: half * part_rows].reshape(half, part_rows, nodes)
    send = sums[half * part_rows : 2 * half * part_rows].reshape(half, part_rows, nodes)
    got = swap(send, "mesh", 1)
    held = [keep[j] + got[j] for j in range(half)]
    arrived = [swap(held[j], "mesh", 2 * j) for j in range(1, half)]
    total = held[0]
    for piece in arrived:
        total = total + piece
    bits = evs.bit_length() - 1
    for bit in range(bits - 1):
        total = total + swap(total, "ev", 1 << bit)
    across = swap(total, "ev", 1 << (bits - 1))

    local = pl.pallas_call(
        functools.partial(sums_kernel, rows, evs),
        out_shape=f32(8, nodes),
        in_specs=[in_vmem()] * 3,
        out_specs=in_vmem(),
        compiler_params=limit(4),
        name="sums",
    )(total, across, hist)
    local = local + swap(local, "mesh", 1)
    spread = [local] + [swap(local, "mesh", 2 * j) for j in range(1, half)]
    inversion_direction, rounded = pl.pallas_call(
        functools.partial(direction_kernel, rows, evs, comps, group),
        out_shape=[f32(*precond.shape), bf16(part_rows, nodes)],
        in_specs=[in_vmem()] * (3 + half),
        out_specs=[in_vmem()] * 2,
        scratch_shapes=[pltpu.VMEM((group * PITCH, nodes), jnp.float32)],
        compiler_params=limit(4),
        name="direction",
    )(total, across, hist, *spread)

    mine = [rounded] + [swap(rounded, "mesh", 2 * j) for j in range(1, half)]
    other = swap(jnp.stack(mine), "mesh", 1)

    event_direction = pl.pallas_call(
        functools.partial(backward_kernel, dims),
        out_shape=f32(*kernels.shape),
        in_specs=[in_smem()] + [in_vmem()] * (half + 3),
        out_specs=in_hbm(),
        scratch_shapes=[
            pltpu.VMEM((blocks * comps + ROW, nodes), jnp.float32),
            pltpu.VMEM((events * eblocks * PITCH + ROW, nodes), jnp.float32),
            pltpu.VMEM(kernels.shape, jnp.float32),
            pltpu.SMEM(code_rows, jnp.int32),
            pltpu.SemaphoreType.DMA((1 + events,)),
        ],
        compiler_params=limit(24),
        name="backward",
    )(counts, codes, tab, *mine, other)
    return inversion_direction, event_direction


def solution(mesh):
    in_specs = (
        P("ev", None, "mesh", None),
        P("ev", "mesh", None),
        P("ev", "mesh"),
        P("ev", "mesh"),
        P("ev", "mesh"),
        P("ev", "mesh"),
        P(None, "mesh", "ev", None),
        P(None, "mesh", "ev", None),
        P(None, "mesh", "ev", None),
    )
    out_specs = (P(None, "mesh", "ev", None), P("ev", None, "mesh", None))
    return jax.shard_map(body, mesh=mesh, in_specs=in_specs, out_specs=out_specs, check_vma=False)
```

time: 95.5 us -> 86.1 us (0.902); the launches traced: 95.9 us -> 85.3 us
  Pallas kernels: 34.4 us -> 16.9 us
  starting transfers between devices: 18.1 us -> 26.8 us
  waiting for transfers between devices: 37.4 us -> 33.4 us
  local copies, waits for them, and re-layouts: 4.98 us -> 7.25 us
    pallas_call x1, Pallas kernels: 17.4 us -> 8.04 us  [body(): pl.pallas_call(functools.partial(backward_kernel, dims), out_shape=f32(*k...]
    ppermute x16 -> x17, starting transfers between devices: 18.1 us -> 26.8 us  [swap(): return lax.ppermute(x, axis, [(i, i ^ k) for i in range(size)])]
    pallas_call x1, Pallas kernels: 16 us -> 7.93 us  [body(): pl.pallas_call(functools.partial(forward_kernel, dims), out_shape=[f32(bl...]
    ppermute x16 -> x17, waiting for transfers between devices: 37.4 us -> 33.4 us  [swap(): return lax.ppermute(x, axis, [(i, i ^ k) for i in range(size)])]
    unnamed x25 -> x20, local copies, waits for them, and re-layouts: 4.93 us -> 7.2 us
  transfers between devices with their start and end apart: 16 -> 17, of which waited for: 14 -> 15; matrix products, arithmetic and copies ran while one was open for 0% -> 0% of each run, Pallas kernels for 0% -> 0%
where the time goes in v3:
time: 86.1 us; the launch traced here: 85.3 us
  waiting for transfers between devices  33.4 us (39%)
  starting transfers between devices  26.8 us (31%)
  Pallas kernels  16.9 us (20%)
  local copies, waits for them, and re-layouts  7.25 us (8%)
    ppermute x17, waiting for transfers between devices, swap(): return lax.ppermute(x, axis, [(i, i ^ k) for i in range(size)])  33.4 us
    ppermute x17, starting transfers between devices, swap(): return lax.ppermute(x, axis, [(i, i ^ k) for i in range(size)])  26.8 us
    pallas_call x1, Pallas kernels, body(): pl.pallas_call(functools.partial(backward_kernel, dims), out_shape=f32(*k...  8.04 us
    pallas_call x1, Pallas kernels, body(): pl.pallas_call(functools.partial(forward_kernel, dims), out_shape=[f32(bl...  7.93 us
    unnamed x20, local copies, waits for them, and re-layouts  7.2 us
  transfers between devices with their start and end apart: 17, of which 15 were waited for; matrix products, arithmetic and copies ran while one was open for 0% of the time, Pallas kernels for 0%

profile of v3, /device:TPU:0, one launch (start us, length us, event | category | flops | bytes accessed | tf_op | source)
XLA Modules:
  0.0 85.3 jit_solution(11697407547725589677)
XLA Ops:
  0.6 0.0 copy-start
  0.6 0.8 copy-done
  1.4 0.0 copy-start.1
  1.4 0.8 copy-done.1
  2.2 0.0 copy-start.2
  2.2 0.8 copy-done.2
  3.1 0.0 copy-start.3
  3.1 0.6 copy-done.3
  3.7 0.0 copy-start.5
  3.7 1.4 %copy-done.5 = bf16[2,12,256,128]{3,2,1,0:T(8,128)(2,1)S(1)} copy-done((bf16[2,12,256,128]{3,2,1,0:T(8,128)(2,1)S(1)}, bf16[2,12,256,128]{3,2,1,0:T(8,128)(2,1)}, u32[]{:S(2)}) %copy-start.5) | copy-done | bytes 1572888
  5.1 0.0 copy-start.6
  5.1 0.7 copy-done.6
  5.8 0.0 copy-start.7
  5.8 0.7 copy-done.7
  6.5 0.0 copy-start.8
  6.5 0.7 copy-done.8
  7.2 0.0 copy-start.9
  7.2 0.7 copy-done.9
  7.9 7.9 %forward.1 = (f32[3088,128]{1,0:T(8,128)S(1)}, bf16[10752,128]{1,0:T(8,128)(2,1)S(1)}, s32[32,128]{1,0:T(8,128)S(1)}) custom-call(s32[1,2]{1,0:T(1,128)S(1)} %bitcast.38, s32[2,1,512]{2,1,0:T(1,128)S(1)} %bitcast.40, s32[2,512]{1,0:T(2,128)S(1)} %copy-done.7, s32[2,512]{1,0:T(2,128)S(1)} %copy-done.8, s32[2,512]{1,0:T(2,128)S(1)} %copy-done.9, ...), custom_call_target="tpu_custom_call" | custom-call | flops 34359738368 | bytes 16777216 | tf_op jit(solution)/shard_map/forward/pallas_call | solution.py:293
  15.8 0.1 slice.37
  15.9 0.6 collective-permute-start
  16.4 1.9 %collective-permute-done = f32[4,384,128]{2,1,0:T(8,128)S(1)} collective-permute-done((f32[4,384,128]{2,1,0:T(8,128)S(1)}, f32[4,384,128]{2,1,0:T(8,128)S(1)}, u32[]{:S(2)}, u32[]{:S(2)}) %collective-permute-start) | collective-permute-done | bytes 786464 | tf_op jit(solution)/shard_map/ppermute | solution.py:274
  18.4 0.1 fusion.2
  18.4 4.5 %collective-permute-start.1 = (f32[384,128]{1,0:T(8,128)S(1)}, f32[384,128]{1,0:T(8,128)S(1)}, u32[]{:S(2)}, u32[]{:S(2)}) collective-permute-start(f32[384,128]{1,0:T(8,128)S(1)} %get-tuple-element.12), channel_id=1, source_target_pairs={{0,2},{1,3},{2,0},{3,1},{4,6},{5,7},{6,4},{7,5},{8,10},{9,11},{10,... | collective-permute-start | bytes 589832 | tf_op jit(solution)/shard_map/ppermute | solution.py:274
  23.0 0.6 collective-permute-start.3
  23.5 0.9 %collective-permute-start.2 = (f32[384,128]{1,0:T(8,128)S(1)}, f32[384,128]{1,0:T(8,128)S(1)}, u32[]{:S(2)}, u32[]{:S(2)}) collective-permute-start(f32[384,128]{1,0:T(8,128)S(1)} %get-tuple-element.14), channel_id=1, source_target_pairs={{0,4},{1,5},{2,6},{3,7},{4,0},{5,1},{6,2},{7,3},{8,12},{9,13},{10,... | collective-permute-start | bytes 589832 | tf_op jit(solution)/shard_map/ppermute | solution.py:274
  24.5 4.2 %collective-permute-done.1 = f32[384,128]{1,0:T(8,128)S(1)} collective-permute-done((f32[384,128]{1,0:T(8,128)S(1)}, f32[384,128]{1,0:T(8,128)S(1)}, u32[]{:S(2)}, u32[]{:S(2)}) %collective-permute-start.1) | collective-permute-done | bytes 196640 | tf_op jit(solution)/shard_map/ppermute | solution.py:274
  28.7 4.1 %collective-permute-done.3 = f32[384,128]{1,0:T(8,128)S(1)} collective-permute-done((f32[384,128]{1,0:T(8,128)S(1)}, f32[384,128]{1,0:T(8,128)S(1)}, u32[]{:S(2)}, u32[]{:S(2)}) %collective-permute-start.3) | collective-permute-done | bytes 196640 | tf_op jit(solution)/shard_map/ppermute | solution.py:274
  32.8 1.4 %collective-permute-done.2 = f32[384,128]{1,0:T(8,128)S(1)} collective-permute-done((f32[384,128]{1,0:T(8,128)S(1)}, f32[384,128]{1,0:T(8,128)S(1)}, u32[]{:S(2)}, u32[]{:S(2)}) %collective-permute-start.2) | collective-permute-done | bytes 196640 | tf_op jit(solution)/shard_map/ppermute | solution.py:274
  34.1 0.1 fusion.6
  34.2 2.4 %collective-permute-start.4 = (f32[384,128]{1,0:T(8,128)S(1)}, f32[384,128]{1,0:T(8,128)S(1)}, u32[]{:S(2)}, u32[]{:S(2)}) collective-permute-start(f32[384,128]{1,0:T(8,128)S(1)} %fusion.6), channel_id=1, source_target_pairs={{0,8},{8,0},{16,24},{24,16},{1,9},{9,1},{17,25},{25,17},{2,10},{10... | collective-permute-start | bytes 589832 | tf_op jit(solution)/shard_map/ppermute | solution.py:274
  36.7 2.0 %collective-permute-start.8 = (f32[3,96,128]{2,1,0:T(8,128)S(1)}, f32[3,96,128]{2,1,0:T(8,128)S(1)}, u32[]{:S(2)}, u32[]{:S(2)}) collective-permute-start(f32[3,96,128]{2,1,0:T(8,128)S(1)} %pack.1.order_ref), channel_id=1, source_target_pairs={{0,24},{8,16},{16,8},{24,0},{1,25},{9,17},{17,9},{25,1},{2,26},{10... | collective-permute-start | bytes 442376 | tf_op jit(solution)/shard_map/ppermute | solution.py:274
  38.6 0.5 collective-permute-start.7
  39.1 1.9 %collective-permute-start.6 = (f32[3,96,128]{2,1,0:T(8,128)S(1)}, f32[3,96,128]{2,1,0:T(8,128)S(1)}, u32[]{:S(2)}, u32[]{:S(2)}) collective-permute-start(f32[3,96,128]{2,1,0:T(8,128)S(1)} %pack.1.order_ref), channel_id=1, source_target_pairs={{0,8},{8,0},{16,24},{24,16},{1,9},{9,1},{17,25},{25,17},{2,10},{10... | collective-permute-start | bytes 442376 | tf_op jit(solution)/shard_map/ppermute | solution.py:274
  41.0 0.9 %collective-permute-done.4 = f32[384,128]{1,0:T(8,128)S(1)} collective-permute-done((f32[384,128]{1,0:T(8,128)S(1)}, f32[384,128]{1,0:T(8,128)S(1)}, u32[]{:S(2)}, u32[]{:S(2)}) %collective-permute-start.4) | collective-permute-done | bytes 196640 | tf_op jit(solution)/shard_map/ppermute | solution.py:274
  42.0 6.2 %collective-permute-start.5 = (f32[384,128]{1,0:T(8,128)S(1)}, f32[384,128]{1,0:T(8,128)S(1)}, u32[]{:S(2)}, u32[]{:S(2)}) collective-permute-start(f32[384,128]{1,0:T(8,128)S(1)} %add.34.a_ref), channel_id=1, source_target_pairs={{0,16},{8,24},{16,0},{24,8},{1,17},{9,25},{17,1},{25,9},{2,18},{10... | collective-permute-start | bytes 589832 | tf_op jit(solution)/shard_map/ppermute | solution.py:274
  48.2 0.0 collective-permute-done.8
  48.2 9.1 %collective-permute-done.7 = f32[3,96,128]{2,1,0:T(8,128)S(1)} collective-permute-done((f32[3,96,128]{2,1,0:T(8,128)S(1)}, f32[3,96,128]{2,1,0:T(8,128)S(1)}, u32[]{:S(2)}, u32[]{:S(2)}) %collective-permute-start.7) | collective-permute-done | bytes 147488 | tf_op jit(solution)/shard_map/ppermute | solution.py:274
  57.3 0.0 collective-permute-done.6
  57.4 0.0 copy-start.4
  57.4 2.7 %collective-permute-done.5.b_ref = f32[384,128]{1,0:T(8,128)S(1)} collective-permute-done((f32[384,128]{1,0:T(8,128)S(1)}, f32[384,128]{1,0:T(8,128)S(1)}, u32[]{:S(2)}, u32[]{:S(2)}) %collective-permute-start.5) | collective-permute-done | bytes 196640 | tf_op jit(solution)/shard_map/ppermute | solution.py:274
  60.1 0.1 sums.1
  60.2 0.1 collective-permute-start.9
  60.3 1.2 %collective-permute-done.9 = f32[8,128]{1,0:T(8,128)S(1)} collective-permute-done((f32[8,128]{1,0:T(8,128)S(1)}, f32[8,128]{1,0:T(8,128)S(1)}, u32[]{:S(2)}, u32[]{:S(2)}) %collective-permute-start.9) | collective-permute-done | bytes 4128 | tf_op jit(solution)/shard_map/ppermute | solution.py:274
  61.5 1.4 %collective-permute-start.12 = (f32[8,128]{1,0:T(8,128)S(1)}, f32[8,128]{1,0:T(8,128)S(1)}, u32[]{:S(2)}, u32[]{:S(2)}) collective-permute-start(f32[8,128]{1,0:T(8,128)S(1)} %add.35.refs_0_), channel_id=1, source_target_pairs={{0,6},{1,7},{2,4},{3,5},{4,2},{5,3},{6,0},{7,1},{8,14},{9,15},{10,... | collective-permute-start | bytes 12296 | tf_op jit(solution)/shard_map/ppermute | solution.py:274
  62.8 0.0 collective-permute-start.11
  62.8 2.1 %collective-permute-start.10 = (f32[8,128]{1,0:T(8,128)S(1)}, f32[8,128]{1,0:T(8,128)S(1)}, u32[]{:S(2)}, u32[]{:S(2)}) collective-permute-start(f32[8,128]{1,0:T(8,128)S(1)} %add.35.refs_0_), channel_id=1, source_target_pairs={{0,2},{1,3},{2,0},{3,1},{4,6},{5,7},{6,4},{7,5},{8,10},{9,11},{10,... | collective-permute-start | bytes 12296 | tf_op jit(solution)/shard_map/ppermute | solution.py:274
  65.0 1.0 %collective-permute-done.12.refs_3_ = f32[8,128]{1,0:T(8,128)S(1)} collective-permute-done((f32[8,128]{1,0:T(8,128)S(1)}, f32[8,128]{1,0:T(8,128)S(1)}, u32[]{:S(2)}, u32[]{:S(2)}) %collective-permute-start.12) | collective-permute-done | bytes 4128 | tf_op jit(solution)/shard_map/ppermute | solution.py:274
  66.0 0.5 collective-permute-done.11.refs_2_
  66.4 0.1 collective-permute-done.10.refs_1_
  66.5 0.8 direction.1
  67.3 1.7 %collective-permute-start.15 = (bf16[384,128]{1,0:T(8,128)(2,1)S(1)}, bf16[384,128]{1,0:T(8,128)(2,1)S(1)}, u32[]{:S(2)}, u32[]{:S(2)}) collective-permute-start(bf16[384,128]{1,0:T(8,128)(2,1)S(1)} %get-tuple-element.11.refs_0_), channel_id=1, source_target_pairs={{0,6},{1,7},{2,4},{3,5},{4,2},{5,3},{6,0},{7,1},{8,14},{9,15},{10,... | collective-permute-start | bytes 294920 | tf_op jit(solution)/shard_map/ppermute | solution.py:274
  69.1 1.7 %collective-permute-start.14 = (bf16[384,128]{1,0:T(8,128)(2,1)S(1)}, bf16[384,128]{1,0:T(8,128)(2,1)S(1)}, u32[]{:S(2)}, u32[]{:S(2)}) collective-permute-start(bf16[384,128]{1,0:T(8,128)(2,1)S(1)} %get-tuple-element.11.refs_0_), channel_id=1, source_target_pairs={{0,4},{1,5},{2,6},{3,7},{4,0},{5,1},{6,2},{7,3},{8,12},{9,13},{10,... | collective-permute-start | bytes 294920 | tf_op jit(solution)/shard_map/ppermute | solution.py:274
  70.8 0.0 collective-permute-start.13
  70.8 2.7 %collective-permute-done.15.refs_3_ = bf16[384,128]{1,0:T(8,128)(2,1)S(1)} collective-permute-done((bf16[384,128]{1,0:T(8,128)(2,1)S(1)}, bf16[384,128]{1,0:T(8,128)(2,1)S(1)}, u32[]{:S(2)}, u32[]{:S(2)}) %collective-permute-start.15) | collective-permute-done | bytes 98336 | tf_op jit(solution)/shard_map/ppermute | solution.py:274
  73.5 0.8 collective-permute-done.14.refs_2_
  74.3 1.1 %collective-permute-done.13.refs_1_ = bf16[384,128]{1,0:T(8,128)(2,1)S(1)} collective-permute-done((bf16[384,128]{1,0:T(8,128)(2,1)S(1)}, bf16[384,128]{1,0:T(8,128)(2,1)S(1)}, u32[]{:S(2)}, u32[]{:S(2)}) %collective-permute-start.13) | collective-permute-done | bytes 98336 | tf_op jit(solution)/shard_map/ppermute | solution.py:274
  75.4 0.1 pad_maximum_fusion.1
  75.5 0.1 collective-permute-start.16
  75.6 1.7 %collective-permute-done.16.refs_4_ = bf16[4,384,128]{2,1,0:T(8,128)(2,1)S(1)} collective-permute-done((bf16[4,384,128]{2,1,0:T(8,128)(2,1)S(1)}, bf16[4,384,128]{2,1,0:T(8,128)(2,1)S(1)}, u32[]{:S(2)}, u32[]{:S(2)}) %collective-permute-start.16) | collective-permute-done | bytes 393248 | tf_op jit(solution)/shard_map/ppermute | solution.py:274
  77.3 0.0 copy-done.4
  77.3 8.0 %backward.1 = f32[2,12,256,128]{3,2,1,0:T(8,128)} custom-call(s32[1,2]{1,0:T(1,128)S(1)} %bitcast.39, s32[32,128]{1,0:T(8,128)S(1)} %get-tuple-element.9.codes_in, bf16[10752,128]{1,0:T(8,128)(2,1)S(1)} %get-tuple-element.10.tab_ref, bf16[384,128]{1,0:T(8,128)(2,1)S(1)} %get-tuple-element.11.refs_0_, bf16[384,128]{1,0:T(8,128)(2,1)S(1)} %collective-permute-done.13.refs_1_, ...), custom_call_target="tpu_custom_call" | custom-call | tf_op jit(solution)/shard_map/backward/pallas_call | solution.py:354
  (4 shorter events, 0.1 us)
Async XLA Ops:
  0.6 0.8 copy-start
  1.4 0.8 copy-start.1
  2.2 0.8 copy-start.2
  3.1 0.7 copy-start.3
  3.7 1.4 %copy-start.5 = (bf16[2,12,256,128]{3,2,1,0:T(8,128)(2,1)S(1)}, bf16[2,12,256,128]{3,2,1,0:T(8,128)(2,1)}, u32[]{:S(2)}) copy-start(bf16[2,12,256,128]{3,2,1,0:T(8,128)(2,1)} %field_hbm.1) | copy-start | bytes 4718596
  5.1 0.7 copy-start.6
  5.8 0.7 copy-start.7
  6.5 0.7 copy-start.8
  7.2 0.7 copy-start.9
  15.9 2.5 %collective-permute-start = (f32[4,384,128]{2,1,0:T(8,128)S(1)}, f32[4,384,128]{2,1,0:T(8,128)S(1)}, u32[]{:S(2)}, u32[]{:S(2)}) collective-permute-start(f32[4,384,128]{2,1,0:T(8,128)S(1)} %bitcast.41), channel_id=1, source_target_pairs={{0,1},{1,0},{2,3},{3,2},{4,5},{5,4},{6,7},{7,6},{8,9},{9,8},{10,11... | collective-permute-start | bytes 2359304 | tf_op jit(solution)/shard_map/ppermute | solution.py:274
  18.4 10.3 %collective-permute-start.1 = (f32[384,128]{1,0:T(8,128)S(1)}, f32[384,128]{1,0:T(8,128)S(1)}, u32[]{:S(2)}, u32[]{:S(2)}) collective-permute-start(f32[384,128]{1,0:T(8,128)S(1)} %get-tuple-element.12), channel_id=1, source_target_pairs={{0,2},{1,3},{2,0},{3,1},{4,6},{5,7},{6,4},{7,5},{8,10},{9,11},{10,... | collective-permute-start | bytes 589832 | tf_op jit(solution)/shard_map/ppermute | solution.py:274
  23.0 9.8 %collective-permute-start.3 = (f32[384,128]{1,0:T(8,128)S(1)}, f32[384,128]{1,0:T(8,128)S(1)}, u32[]{:S(2)}, u32[]{:S(2)}) collective-permute-start(f32[384,128]{1,0:T(8,128)S(1)} %get-tuple-element.13), channel_id=1, source_target_pairs={{0,6},{1,7},{2,4},{3,5},{4,2},{5,3},{6,0},{7,1},{8,14},{9,15},{10,... | collective-permute-start | bytes 589832 | tf_op jit(solution)/shard_map/ppermute | solution.py:274
  23.5 10.6 %collective-permute-start.2 = (f32[384,128]{1,0:T(8,128)S(1)}, f32[384,128]{1,0:T(8,128)S(1)}, u32[]{:S(2)}, u32[]{:S(2)}) collective-permute-start(f32[384,128]{1,0:T(8,128)S(1)} %get-tuple-element.14), channel_id=1, source_target_pairs={{0,4},{1,5},{2,6},{3,7},{4,0},{5,1},{6,2},{7,3},{8,12},{9,13},{10,... | collective-permute-start | bytes 589832 | tf_op jit(solution)/shard_map/ppermute | solution.py:274
  34.2 7.7 %collective-permute-start.4 = (f32[384,128]{1,0:T(8,128)S(1)}, f32[384,128]{1,0:T(8,128)S(1)}, u32[]{:S(2)}, u32[]{:S(2)}) collective-permute-start(f32[384,128]{1,0:T(8,128)S(1)} %fusion.6), channel_id=1, source_target_pairs={{0,8},{8,0},{16,24},{24,16},{1,9},{9,1},{17,25},{25,17},{2,10},{10... | collective-permute-start | bytes 589832 | tf_op jit(solution)/shard_map/ppermute | solution.py:274
  36.7 11.5 %collective-permute-start.8 = (f32[3,96,128]{2,1,0:T(8,128)S(1)}, f32[3,96,128]{2,1,0:T(8,128)S(1)}, u32[]{:S(2)}, u32[]{:S(2)}) collective-permute-start(f32[3,96,128]{2,1,0:T(8,128)S(1)} %pack.1.order_ref), channel_id=1, source_target_pairs={{0,24},{8,16},{16,8},{24,0},{1,25},{9,17},{17,9},{25,1},{2,26},{10... | collective-permute-start | bytes 442376 | tf_op jit(solution)/shard_map/ppermute | solution.py:274
  38.6 18.7 %collective-permute-start.7 = (f32[3,96,128]{2,1,0:T(8,128)S(1)}, f32[3,96,128]{2,1,0:T(8,128)S(1)}, u32[]{:S(2)}, u32[]{:S(2)}) collective-permute-start(f32[3,96,128]{2,1,0:T(8,128)S(1)} %pack.1.order_ref), channel_id=1, source_target_pairs={{0,16},{8,24},{16,0},{24,8},{1,17},{9,25},{17,1},{25,9},{2,18},{10... | collective-permute-start | bytes 442376 | tf_op jit(solution)/shard_map/ppermute | solution.py:274
  39.1 18.2 %collective-permute-start.6 = (f32[3,96,128]{2,1,0:T(8,128)S(1)}, f32[3,96,128]{2,1,0:T(8,128)S(1)}, u32[]{:S(2)}, u32[]{:S(2)}) collective-permute-start(f32[3,96,128]{2,1,0:T(8,128)S(1)} %pack.1.order_ref), channel_id=1, source_target_pairs={{0,8},{8,0},{16,24},{24,16},{1,9},{9,1},{17,25},{25,17},{2,10},{10... | collective-permute-start | bytes 442376 | tf_op jit(solution)/shard_map/ppermute | solution.py:274
  42.0 18.2 %collective-permute-start.5 = (f32[384,128]{1,0:T(8,128)S(1)}, f32[384,128]{1,0:T(8,128)S(1)}, u32[]{:S(2)}, u32[]{:S(2)}) collective-permute-start(f32[384,128]{1,0:T(8,128)S(1)} %add.34.a_ref), channel_id=1, source_target_pairs={{0,16},{8,24},{16,0},{24,8},{1,17},{9,25},{17,1},{25,9},{2,18},{10... | collective-permute-start | bytes 589832 | tf_op jit(solution)/shard_map/ppermute | solution.py:274
  57.4 19.9 %copy-start.4 = (s32[2,1]{0,1:T(1,128)S(1)}, s32[2,1]{0,1:T(1,128)}, u32[]{:S(2)}) copy-start(s32[2,1]{0,1:T(1,128)} %param.14) | copy-start | bytes 28
  60.2 1.2 %collective-permute-start.9 = (f32[8,128]{1,0:T(8,128)S(1)}, f32[8,128]{1,0:T(8,128)S(1)}, u32[]{:S(2)}, u32[]{:S(2)}) collective-permute-start(f32[8,128]{1,0:T(8,128)S(1)} %sums.1), channel_id=1, source_target_pairs={{0,1},{1,0},{2,3},{3,2},{4,5},{5,4},{6,7},{7,6},{8,9},{9,8},{10,11... | collective-permute-start | bytes 12296 | tf_op jit(solution)/shard_map/ppermute | solution.py:274
  61.5 4.5 %collective-permute-start.12 = (f32[8,128]{1,0:T(8,128)S(1)}, f32[8,128]{1,0:T(8,128)S(1)}, u32[]{:S(2)}, u32[]{:S(2)}) collective-permute-start(f32[8,128]{1,0:T(8,128)S(1)} %add.35.refs_0_), channel_id=1, source_target_pairs={{0,6},{1,7},{2,4},{3,5},{4,2},{5,3},{6,0},{7,1},{8,14},{9,15},{10,... | collective-permute-start | bytes 12296 | tf_op jit(solution)/shard_map/ppermute | solution.py:274
  62.8 3.6 %collective-permute-start.11 = (f32[8,128]{1,0:T(8,128)S(1)}, f32[8,128]{1,0:T(8,128)S(1)}, u32[]{:S(2)}, u32[]{:S(2)}) collective-permute-start(f32[8,128]{1,0:T(8,128)S(1)} %add.35.refs_0_), channel_id=1, source_target_pairs={{0,4},{1,5},{2,6},{3,7},{4,0},{5,1},{6,2},{7,3},{8,12},{9,13},{10,... | collective-permute-start | bytes 12296 | tf_op jit(solution)/shard_map/ppermute | solution.py:274
  62.8 3.7 %collective-permute-start.10 = (f32[8,128]{1,0:T(8,128)S(1)}, f32[8,128]{1,0:T(8,128)S(1)}, u32[]{:S(2)}, u32[]{:S(2)}) collective-permute-start(f32[8,128]{1,0:T(8,128)S(1)} %add.35.refs_0_), channel_id=1, source_target_pairs={{0,2},{1,3},{2,0},{3,1},{4,6},{5,7},{6,4},{7,5},{8,10},{9,11},{10,... | collective-permute-start | bytes 12296 | tf_op jit(solution)/shard_map/ppermute | solution.py:274
  67.3 6.2 %collective-permute-start.15 = (bf16[384,128]{1,0:T(8,128)(2,1)S(1)}, bf16[384,128]{1,0:T(8,128)(2,1)S(1)}, u32[]{:S(2)}, u32[]{:S(2)}) collective-permute-start(bf16[384,128]{1,0:T(8,128)(2,1)S(1)} %get-tuple-element.11.refs_0_), channel_id=1, source_target_pairs={{0,6},{1,7},{2,4},{3,5},{4,2},{5,3},{6,0},{7,1},{8,14},{9,15},{10,... | collective-permute-start | bytes 294920 | tf_op jit(solution)/shard_map/ppermute | solution.py:274
  69.1 5.2 %collective-permute-start.14 = (bf16[384,128]{1,0:T(8,128)(2,1)S(1)}, bf16[384,128]{1,0:T(8,128)(2,1)S(1)}, u32[]{:S(2)}, u32[]{:S(2)}) collective-permute-start(bf16[384,128]{1,0:T(8,128)(2,1)S(1)} %get-tuple-element.11.refs_0_), channel_id=1, source_target_pairs={{0,4},{1,5},{2,6},{3,7},{4,0},{5,1},{6,2},{7,3},{8,12},{9,13},{10,... | collective-permute-start | bytes 294920 | tf_op jit(solution)/shard_map/ppermute | solution.py:274
  70.8 4.6 %collective-permute-start.13 = (bf16[384,128]{1,0:T(8,128)(2,1)S(1)}, bf16[384,128]{1,0:T(8,128)(2,1)S(1)}, u32[]{:S(2)}, u32[]{:S(2)}) collective-permute-start(bf16[384,128]{1,0:T(8,128)(2,1)S(1)} %get-tuple-element.11.refs_0_), channel_id=1, source_target_pairs={{0,2},{1,3},{2,0},{3,1},{4,6},{5,7},{6,4},{7,5},{8,10},{9,11},{10,... | collective-permute-start | bytes 294920 | tf_op jit(solution)/shard_map/ppermute | solution.py:274
  75.5 1.8 %collective-permute-start.16 = (bf16[4,384,128]{2,1,0:T(8,128)(2,1)S(1)}, bf16[4,384,128]{2,1,0:T(8,128)(2,1)S(1)}, u32[]{:S(2)}, u32[]{:S(2)}) collective-permute-start(bf16[4,384,128]{2,1,0:T(8,128)(2,1)S(1)} %pad_maximum_fusion.1), channel_id=1, source_target_pairs={{0,1},{1,0},{2,3},{3,2},{4,5},{5,4},{6,7},{7,6},{8,9},{9,8},{10,11... | collective-permute-start | bytes 1179656 | tf_op jit(solution)/shard_map/ppermute | solution.py:274

commit v4 on v3

--- a/solution.py
+++ b/solution.py
@@ -7,6 +7,7 @@
 from jax.experimental import pallas as pl
 from jax.experimental.pallas import tpu as pltpu
 from jax.sharding import PartitionSpec as P
+
 
 OFFSETS = 7
 SPREADS = 3
@@ -19,7 +20,7 @@
 CODES = 4
 
 
-def fill_table(tab_ref, nodes):
+def table_kernel(nodes, tab_ref):
     row = lax.broadcasted_iota(jnp.int32, (8, nodes), 0)
     lane = lax.broadcasted_iota(jnp.int32, (8, nodes), 1)
     signed = jnp.where(lane < nodes // 2, lane, lane - nodes)
@@ -94,32 +95,20 @@
 
 
 def forward_kernel(
-    dims, count_hbm, owner_hbm, target_hbm, source_hbm, seed_hbm, field_hbm, order_ref,
-    sum_ref, tab_ref, codes_ref,
-    raw_ref, rows_ref, owner_ref, target_ref, source_ref, seed_ref, count_ref, code_ref, sems,
+    dims, count_ref, owner_ref, target_ref, source_ref, seed_ref, field_ref, tab_ref,
+    sum_ref, codes_ref, rows_ref, code_ref, sems,
 ):
     events, comps, eblocks, nodes = dims["field"]
     groups = dims["tiles"] // LANES
     lists = events * groups
-    pairs = (
-        (count_hbm, count_ref), (owner_hbm, owner_ref), (target_hbm, target_ref),
-        (source_hbm, source_ref), (seed_hbm, seed_ref), (field_hbm, raw_ref),
-    )
-    fetches = [pltpu.make_async_copy(a, b, sems.at[n]) for n, (a, b) in enumerate(pairs)]
-    for fetch in fetches:
-        fetch.start()
-    sum_ref[...] = jnp.zeros_like(sum_ref)
-    for fetch in fetches[:-1]:
-        fetch.wait()
     counts = [count_ref[0, v] for v in range(events)]
     fill_codes(dims, counts, owner_ref, target_ref, source_ref, seed_ref, codes_ref)
-    fill_table(tab_ref, nodes)
-    to_smem = pltpu.make_async_copy(codes_ref, code_ref, sems.at[len(pairs)])
+    sum_ref[...] = jnp.zeros_like(sum_ref)
+    to_smem = pltpu.make_async_copy(codes_ref, code_ref, sems.at[0])
     to_smem.start()
-    fetches[-1].wait()
     for v in range(events):
         for c in range(comps):
-            rows_ref[pl.ds(v * eblocks * PITCH + c, eblocks, stride=PITCH), :] = raw_ref[
+            rows_ref[pl.ds(v * eblocks * PITCH + c, eblocks, stride=PITCH), :] = field_ref[
                 v, c
             ].astype(jnp.float32)
     to_smem.wait()
@@ -178,7 +167,6 @@
 
 def pack_kernel(comps, group, *refs):
     ins, (out_ref, wide_ref) = refs[:-2], refs[-2:]
-    rows = comps * group
     for n, ref in enumerate(ins):
         for c in range(comps):
             wide_ref[pl.ds(c, group, stride=PITCH), :] = ref[c, 0]
@@ -186,7 +174,11 @@
             out_ref[n, pl.ds(s * comps, comps), :] = wide_ref[pl.ds(s * PITCH, comps), :]
 
 
-def terms(a_ref, b_ref, hist_ref, k, rows, evs):
+def fold_kernel(a_ref, b_ref, out_ref):
+    out_ref[...] = a_ref[...] + b_ref[...]
+
+
+def terms(a_ref, b_ref, hist_ref, k, rows):
     group = lax.axis_index("ev") ^ k
     at = pl.ds(pl.multiple_of(group * rows, 8), rows)
     gradient = a_ref[at, :] + b_ref[at, :]
@@ -197,7 +189,7 @@
 def sums_kernel(rows, evs, a_ref, b_ref, hist_ref, out_ref):
     total = [jnp.zeros((8, LANES), jnp.float32) for _ in range(4)]
     for k in range(evs):
-        _, gradient, change, prev_step, precond = terms(a_ref, b_ref, hist_ref, k, rows, evs)
+        _, gradient, change, prev_step, precond = terms(a_ref, b_ref, hist_ref, k, rows)
         weighted = precond * change
         parts = (prev_step * change, prev_step * gradient, weighted * gradient, weighted * change)
         for n, part in enumerate(parts):
@@ -218,7 +210,7 @@
     beta = (cross_term - alpha * self_term) / curvature
     bend = alpha - beta
     for k in range(evs):
-        at, gradient, change, prev_step, precond = terms(a_ref, b_ref, hist_ref, k, rows, evs)
+        at, gradient, change, prev_step, precond = terms(a_ref, b_ref, hist_ref, k, rows)
         scaled = precond * (gradient - alpha * change)
         direction = -(scaled + bend * prev_step)
         round_ref[at, :] = direction.astype(jnp.bfloat16)
@@ -288,23 +280,28 @@
         compiler_params=limit(2),
         name="pack",
     )(prev_gradient, prev_step, precond)
-    hist = jnp.stack([packed] + [swap(packed, "ev", k) for k in range(1, evs)])
-
-    sums, tab, codes = pl.pallas_call(
+    hist = [packed]
+    for k in range(1, evs):
+        hist.append(swap(packed, "ev", k))
+    hist = jnp.stack(hist)
+
+    tab = pl.pallas_call(
+        functools.partial(table_kernel, nodes),
+        out_shape=table,
+        out_specs=in_vmem(),
+        compiler_params=limit(1),
+        cost_estimate=pl.CostEstimate(flops=1 << 28, bytes_accessed=4 << 20, transcendentals=0),
+        name="table",
+    )()
+    sums, codes = pl.pallas_call(
         functools.partial(forward_kernel, dims),
-        out_shape=[f32(blocks * comps + ROW, nodes), table, codes_shape],
-        in_specs=[in_hbm()] * 6 + [in_vmem()],
-        out_specs=[in_vmem()] * 3,
+        out_shape=[f32(blocks * comps + ROW, nodes), codes_shape],
+        in_specs=[in_smem()] + [in_vmem()] * 6,
+        out_specs=[in_vmem()] * 2,
         scratch_shapes=[
-            pltpu.VMEM(kernels.shape, jnp.bfloat16),
             pltpu.VMEM((events * eblocks * PITCH + ROW, nodes), jnp.float32),
-            pltpu.VMEM(owners.shape, jnp.int32),
-            pltpu.VMEM(tile_target.shape, jnp.int32),
-            pltpu.VMEM(tile_source.shape, jnp.int32),
-            pltpu.VMEM(tile_seed.shape, jnp.int32),
-            pltpu.SMEM(counts.shape, jnp.int32),
             pltpu.SMEM(code_rows, jnp.int32),
-            pltpu.SemaphoreType.DMA((7,)),
+            pltpu.SemaphoreType.DMA((1,)),
         ],
         compiler_params=limit(20),
         cost_estimate=pl.CostEstimate(
@@ -313,14 +310,23 @@
             transcendentals=0,
         ),
         name="forward",
-    )(counts, owners, tile_target, tile_source, tile_seed, kernels, packed)
+    )(counts, owners, tile_target, tile_source, tile_seed, kernels, tab)
 
     keep = sums[: half * part_rows].reshape(half, part_rows, nodes)
     send = sums[half * part_rows : 2 * half * part_rows].reshape(half, part_rows, nodes)
     got = swap(send, "mesh", 1)
-    held = [keep[j] + got[j] for j in range(half)]
-    arrived = [swap(held[j], "mesh", 2 * j) for j in range(1, half)]
-    total = held[0]
+    held = [None] + [keep[j] + got[j] for j in range(1, half)]
+    arrived = []
+    for j in range(1, half):
+        arrived.append(swap(held[j], "mesh", 2 * j))
+    total = pl.pallas_call(
+        fold_kernel,
+        out_shape=f32(part_rows, nodes),
+        in_specs=[in_vmem()] * 2,
+        out_specs=in_vmem(),
+        compiler_params=limit(2),
+        name="fold",
+    )(keep[0], got[0])
     for piece in arrived:
         total = total + piece
     bits = evs.bit_length() - 1
@@ -382,4 +388,5 @@
         P(None, "mesh", "ev", None),
     )
     out_specs = (P(None, "mesh", "ev", None), P("ev", None, "mesh", None))
+
     return jax.shard_map(body, mesh=mesh, in_specs=in_specs, out_specs=out_specs, check_vma=False)

time: 86.1 us -> 79.3 us (0.921)
  local copies, waits for them, and re-layouts: 7.25 us -> 0.31 us
  starting transfers between devices: 26.8 us -> 21.9 us
  Pallas kernels: 16.9 us -> 19.8 us
  waiting for transfers between devices: 33.4 us -> 36.1 us
    unnamed x20 -> x18, local copies, waits for them, and re-layouts: 7.2 us -> 0.24 us
    ppermute x17, starting transfers between devices: 26.8 us -> 21.9 us  [swap(): return lax.ppermute(x, axis, [(i, i ^ k) for i in range(size)])]
    ppermute x17, waiting for transfers between devices: 33.4 us -> 36.1 us  [swap(): return lax.ppermute(x, axis, [(i, i ^ k) for i in range(size)])]
    pallas_call x1, Pallas kernels: 8.04 us -> 9.46 us  [body(): pl.pallas_call(functools.partial(backward_kernel, dims), out_shape=f32(*k...]
    pallas_call x0 -> x2, Pallas kernels: none -> 1.19 us  [the longest x1 1.17 us: body(): pl.pallas_call(functools.partial(table_kernel, nodes), out_shape=table, o...]
where the time goes in v4:
time: 79.3 us; the launch traced here: 79.2 us
  waiting for transfers between devices  36.1 us (46%)
  starting transfers between devices  21.9 us (28%)
  Pallas kernels  19.8 us (25%)
  between operations  0.83 us (1%)
    ppermute x17, waiting for transfers between devices, swap(): return lax.ppermute(x, axis, [(i, i ^ k) for i in range(size)])  36.1 us
    ppermute x17, starting transfers between devices, swap(): return lax.ppermute(x, axis, [(i, i ^ k) for i in range(size)])  21.9 us
    pallas_call x1, Pallas kernels, body(): pl.pallas_call(functools.partial(backward_kernel, dims), out_shape=f32(*k...  9.46 us
    pallas_call x1, Pallas kernels, body(): pl.pallas_call(functools.partial(forward_kernel, dims), out_shape=[f32(bl...  8.21 us
  transfers between devices with their start and end apart: 17, of which 15 were waited for; matrix products, arithmetic and copies ran while one was open for 0% of the time, Pallas kernels for 0%

profile of v4, /device:TPU:0, one launch (start us, length us, event | category | flops | bytes accessed | tf_op | source)
XLA Modules:
  0.0 79.2 jit_solution(2514006986413921025)
XLA Ops:
  0.6 0.0 copy-start.3
  0.6 0.0 copy-start.8
  0.7 0.0 copy-start.6
  0.7 0.0 copy-start.7
  0.7 0.0 copy-start.5
  0.7 0.0 copy-start.4
  0.7 1.2 %table.1.tab_ref = bf16[10752,128]{1,0:T(8,128)(2,1)S(1)} custom-call(), custom_call_target="tpu_custom_call" | custom-call | flops 268435456 | bytes 4194304 | tf_op jit(solution)/shard_map/table/pallas_call | solution.py:288
  1.9 0.0 copy-done.3
  1.9 0.0 copy-done.8
  1.9 0.0 copy-done.6
  1.9 0.0 copy-done.7
  1.9 0.0 copy-done.5
  1.9 0.2 copy-done.4
  2.1 8.2 %forward.1 = (f32[3088,128]{1,0:T(8,128)S(1)}, s32[32,128]{1,0:T(8,128)S(1)}) custom-call(s32[1,2]{1,0:T(1,128)S(1)} %bitcast.30, s32[2,1,512]{2,1,0:T(1,128)S(1)} %bitcast.32, s32[2,512]{1,0:T(2,128)S(1)} %copy-done.6, s32[2,512]{1,0:T(2,128)S(1)} %copy-done.7, s32[2,512]{1,0:T(2,128)S(1)} %copy-done.8, bf16[2,12,256,128]{3,2,1,0:T(8,128)(2,1)S(1)} %copy-done.4, ...), custom_call_target="tpu_custom_call" | custom-call | flops 34359738368 | bytes 16777216 | tf_op jit(solution)/shard_map/forward/pallas_call | solution.py:296
  10.3 0.1 slice.37
  10.4 0.0 copy-start
  10.4 0.0 copy-start.1
  10.4 0.0 copy-start.2
  10.4 0.1 collective-permute-start
  10.5 2.3 %collective-permute-done = f32[4,384,128]{2,1,0:T(8,128)S(1)} collective-permute-done((f32[4,384,128]{2,1,0:T(8,128)S(1)}, f32[4,384,128]{2,1,0:T(8,128)S(1)}, u32[]{:S(2)}, u32[]{:S(2)}) %collective-permute-start) | collective-permute-done | bytes 786464 | tf_op jit(solution)/shard_map/ppermute | solution.py:266
  12.8 0.1 fusion.2
  12.9 1.7 %collective-permute-start.1 = (f32[384,128]{1,0:T(8,128)S(1)}, f32[384,128]{1,0:T(8,128)S(1)}, u32[]{:S(2)}, u32[]{:S(2)}) collective-permute-start(f32[384,128]{1,0:T(8,128)S(1)} %get-tuple-element.10), channel_id=1, source_target_pairs={{0,2},{1,3},{2,0},{3,1},{4,6},{5,7},{6,4},{7,5},{8,10},{9,11},{10,... | collective-permute-start | bytes 589832 | tf_op jit(solution)/shard_map/ppermute | solution.py:266
  14.6 2.1 %collective-permute-start.3 = (f32[384,128]{1,0:T(8,128)S(1)}, f32[384,128]{1,0:T(8,128)S(1)}, u32[]{:S(2)}, u32[]{:S(2)}) collective-permute-start(f32[384,128]{1,0:T(8,128)S(1)} %get-tuple-element.11), channel_id=1, source_target_pairs={{0,6},{1,7},{2,4},{3,5},{4,2},{5,3},{6,0},{7,1},{8,14},{9,15},{10,... | collective-permute-start | bytes 589832 | tf_op jit(solution)/shard_map/ppermute | solution.py:266
  16.6 0.5 collective-permute-start.2
  17.2 3.6 %collective-permute-done.1 = f32[384,128]{1,0:T(8,128)S(1)} collective-permute-done((f32[384,128]{1,0:T(8,128)S(1)}, f32[384,128]{1,0:T(8,128)S(1)}, u32[]{:S(2)}, u32[]{:S(2)}) %collective-permute-start.1) | collective-permute-done | bytes 196640 | tf_op jit(solution)/shard_map/ppermute | solution.py:266
  20.7 5.6 %collective-permute-done.3 = f32[384,128]{1,0:T(8,128)S(1)} collective-permute-done((f32[384,128]{1,0:T(8,128)S(1)}, f32[384,128]{1,0:T(8,128)S(1)}, u32[]{:S(2)}, u32[]{:S(2)}) %collective-permute-start.3) | collective-permute-done | bytes 196640 | tf_op jit(solution)/shard_map/ppermute | solution.py:266
  26.3 1.4 %collective-permute-done.2 = f32[384,128]{1,0:T(8,128)S(1)} collective-permute-done((f32[384,128]{1,0:T(8,128)S(1)}, f32[384,128]{1,0:T(8,128)S(1)}, u32[]{:S(2)}, u32[]{:S(2)}) %collective-permute-start.2) | collective-permute-done | bytes 196640 | tf_op jit(solution)/shard_map/ppermute | solution.py:266
  27.7 0.1 add_add_fusion
  27.8 2.0 %collective-permute-start.4 = (f32[384,128]{1,0:T(8,128)S(1)}, f32[384,128]{1,0:T(8,128)S(1)}, u32[]{:S(2)}, u32[]{:S(2)}) collective-permute-start(f32[384,128]{1,0:T(8,128)S(1)} %add_add_fusion), channel_id=1, source_target_pairs={{0,8},{8,0},{16,24},{24,16},{1,9},{9,1},{17,25},{25,17},{2,10},{10... | collective-permute-start | bytes 589832 | tf_op jit(solution)/shard_map/ppermute | solution.py:266
  29.8 0.0 copy-done
  29.8 0.0 copy-done.1
  29.8 0.0 copy-done.2
  29.8 2.7 %collective-permute-start.8 = (f32[3,96,128]{2,1,0:T(8,128)S(1)}, f32[3,96,128]{2,1,0:T(8,128)S(1)}, u32[]{:S(2)}, u32[]{:S(2)}) collective-permute-start(f32[3,96,128]{2,1,0:T(8,128)S(1)} %pack.1), channel_id=1, source_target_pairs={{0,24},{8,16},{16,8},{24,0},{1,25},{9,17},{17,9},{25,1},{2,26},{10... | collective-permute-start | bytes 442376 | tf_op jit(solution)/shard_map/ppermute | solution.py:266
  32.5 0.0 collective-permute-start.7
  32.5 1.8 %collective-permute-start.6 = (f32[3,96,128]{2,1,0:T(8,128)S(1)}, f32[3,96,128]{2,1,0:T(8,128)S(1)}, u32[]{:S(2)}, u32[]{:S(2)}) collective-permute-start(f32[3,96,128]{2,1,0:T(8,128)S(1)} %pack.1), channel_id=1, source_target_pairs={{0,8},{8,0},{16,24},{24,16},{1,9},{9,1},{17,25},{25,17},{2,10},{10... | collective-permute-start | bytes 442376 | tf_op jit(solution)/shard_map/ppermute | solution.py:266
  34.3 2.8 %collective-permute-done.4 = f32[384,128]{1,0:T(8,128)S(1)} collective-permute-done((f32[384,128]{1,0:T(8,128)S(1)}, f32[384,128]{1,0:T(8,128)S(1)}, u32[]{:S(2)}, u32[]{:S(2)}) %collective-permute-start.4) | collective-permute-done | bytes 196640 | tf_op jit(solution)/shard_map/ppermute | solution.py:266
  37.1 4.0 %collective-permute-start.5 = (f32[384,128]{1,0:T(8,128)S(1)}, f32[384,128]{1,0:T(8,128)S(1)}, u32[]{:S(2)}, u32[]{:S(2)}) collective-permute-start(f32[384,128]{1,0:T(8,128)S(1)} %add.30.a_ref), channel_id=1, source_target_pairs={{0,16},{8,24},{16,0},{24,8},{1,17},{9,25},{17,1},{25,9},{2,18},{10... | collective-permute-start | bytes 589832 | tf_op jit(solution)/shard_map/ppermute | solution.py:266
  41.1 0.2 collective-permute-done.8
  41.3 8.6 %collective-permute-done.7 = f32[3,96,128]{2,1,0:T(8,128)S(1)} collective-permute-done((f32[3,96,128]{2,1,0:T(8,128)S(1)}, f32[3,96,128]{2,1,0:T(8,128)S(1)}, u32[]{:S(2)}, u32[]{:S(2)}) %collective-permute-start.7) | collective-permute-done | bytes 147488 | tf_op jit(solution)/shard_map/ppermute | solution.py:266
  49.9 0.0 collective-permute-done.6
  49.9 2.6 %collective-permute-done.5.b_ref = f32[384,128]{1,0:T(8,128)S(1)} collective-permute-done((f32[384,128]{1,0:T(8,128)S(1)}, f32[384,128]{1,0:T(8,128)S(1)}, u32[]{:S(2)}, u32[]{:S(2)}) %collective-permute-start.5) | collective-permute-done | bytes 196640 | tf_op jit(solution)/shard_map/ppermute | solution.py:266
  52.5 0.1 sums.1
  52.6 0.1 collective-permute-start.9
  52.7 1.2 %collective-permute-done.9 = f32[8,128]{1,0:T(8,128)S(1)} collective-permute-done((f32[8,128]{1,0:T(8,128)S(1)}, f32[8,128]{1,0:T(8,128)S(1)}, u32[]{:S(2)}, u32[]{:S(2)}) %collective-permute-start.9) | collective-permute-done | bytes 4128 | tf_op jit(solution)/shard_map/ppermute | solution.py:266
  53.9 2.0 %collective-permute-start.12 = (f32[8,128]{1,0:T(8,128)S(1)}, f32[8,128]{1,0:T(8,128)S(1)}, u32[]{:S(2)}, u32[]{:S(2)}) collective-permute-start(f32[8,128]{1,0:T(8,128)S(1)} %add.31.refs_0_), channel_id=1, source_target_pairs={{0,6},{1,7},{2,4},{3,5},{4,2},{5,3},{6,0},{7,1},{8,14},{9,15},{10,... | collective-permute-start | bytes 12296 | tf_op jit(solution)/shard_map/ppermute | solution.py:266
  55.9 1.0 %collective-permute-start.11 = (f32[8,128]{1,0:T(8,128)S(1)}, f32[8,128]{1,0:T(8,128)S(1)}, u32[]{:S(2)}, u32[]{:S(2)}) collective-permute-start(f32[8,128]{1,0:T(8,128)S(1)} %add.31.refs_0_), channel_id=1, source_target_pairs={{0,4},{1,5},{2,6},{3,7},{4,0},{5,1},{6,2},{7,3},{8,12},{9,13},{10,... | collective-permute-start | bytes 12296 | tf_op jit(solution)/shard_map/ppermute | solution.py:266
  56.9 0.4 collective-permute-start.10
  57.3 1.0 %collective-permute-done.12.refs_3_ = f32[8,128]{1,0:T(8,128)S(1)} collective-permute-done((f32[8,128]{1,0:T(8,128)S(1)}, f32[8,128]{1,0:T(8,128)S(1)}, u32[]{:S(2)}, u32[]{:S(2)}) %collective-permute-start.12) | collective-permute-done | bytes 4128 | tf_op jit(solution)/shard_map/ppermute | solution.py:266
  58.4 1.1 %collective-permute-done.11.refs_2_ = f32[8,128]{1,0:T(8,128)S(1)} collective-permute-done((f32[8,128]{1,0:T(8,128)S(1)}, f32[8,128]{1,0:T(8,128)S(1)}, u32[]{:S(2)}, u32[]{:S(2)}) %collective-permute-start.11) | collective-permute-done | bytes 4128 | tf_op jit(solution)/shard_map/ppermute | solution.py:266
  59.5 1.0 %collective-permute-done.10.refs_1_ = f32[8,128]{1,0:T(8,128)S(1)} collective-permute-done((f32[8,128]{1,0:T(8,128)S(1)}, f32[8,128]{1,0:T(8,128)S(1)}, u32[]{:S(2)}, u32[]{:S(2)}) %collective-permute-start.10) | collective-permute-done | bytes 4128 | tf_op jit(solution)/shard_map/ppermute | solution.py:266
  60.5 0.8 direction.1
  61.3 1.1 %collective-permute-start.15 = (bf16[384,128]{1,0:T(8,128)(2,1)S(1)}, bf16[384,128]{1,0:T(8,128)(2,1)S(1)}, u32[]{:S(2)}, u32[]{:S(2)}) collective-permute-start(bf16[384,128]{1,0:T(8,128)(2,1)S(1)} %get-tuple-element.9.refs_0_), channel_id=1, source_target_pairs={{0,6},{1,7},{2,4},{3,5},{4,2},{5,3},{6,0},{7,1},{8,14},{9,15},{10,... | collective-permute-start | bytes 294920 | tf_op jit(solution)/shard_map/ppermute | solution.py:266
  62.3 0.8 %collective-permute-start.14 = (bf16[384,128]{1,0:T(8,128)(2,1)S(1)}, bf16[384,128]{1,0:T(8,128)(2,1)S(1)}, u32[]{:S(2)}, u32[]{:S(2)}) collective-permute-start(bf16[384,128]{1,0:T(8,128)(2,1)S(1)} %get-tuple-element.9.refs_0_), channel_id=1, source_target_pairs={{0,4},{1,5},{2,6},{3,7},{4,0},{5,1},{6,2},{7,3},{8,12},{9,13},{10,... | collective-permute-start | bytes 294920 | tf_op jit(solution)/shard_map/ppermute | solution.py:266
  63.2 1.6 %collective-permute-start.13 = (bf16[384,128]{1,0:T(8,128)(2,1)S(1)}, bf16[384,128]{1,0:T(8,128)(2,1)S(1)}, u32[]{:S(2)}, u32[]{:S(2)}) collective-permute-start(bf16[384,128]{1,0:T(8,128)(2,1)S(1)} %get-tuple-element.9.refs_0_), channel_id=1, source_target_pairs={{0,2},{1,3},{2,0},{3,1},{4,6},{5,7},{6,4},{7,5},{8,10},{9,11},{10,... | collective-permute-start | bytes 294920 | tf_op jit(solution)/shard_map/ppermute | solution.py:266
  64.8 2.1 %collective-permute-done.15.refs_3_ = bf16[384,128]{1,0:T(8,128)(2,1)S(1)} collective-permute-done((bf16[384,128]{1,0:T(8,128)(2,1)S(1)}, bf16[384,128]{1,0:T(8,128)(2,1)S(1)}, u32[]{:S(2)}, u32[]{:S(2)}) %collective-permute-start.15) | collective-permute-done | bytes 98336 | tf_op jit(solution)/shard_map/ppermute | solution.py:266
  66.9 1.0 %collective-permute-done.14.refs_2_ = bf16[384,128]{1,0:T(8,128)(2,1)S(1)} collective-permute-done((bf16[384,128]{1,0:T(8,128)(2,1)S(1)}, bf16[384,128]{1,0:T(8,128)(2,1)S(1)}, u32[]{:S(2)}, u32[]{:S(2)}) %collective-permute-start.14) | collective-permute-done | bytes 98336 | tf_op jit(solution)/shard_map/ppermute | solution.py:266
  67.8 0.0 collective-permute-done.13.refs_1_
  67.9 0.1 pad_maximum_fusion.1
  67.9 0.1 collective-permute-start.16
  68.0 1.7 %collective-permute-done.16.refs_4_ = bf16[4,384,128]{2,1,0:T(8,128)(2,1)S(1)} collective-permute-done((bf16[4,384,128]{2,1,0:T(8,128)(2,1)S(1)}, bf16[4,384,128]{2,1,0:T(8,128)(2,1)S(1)}, u32[]{:S(2)}, u32[]{:S(2)}) %collective-permute-start.16) | collective-permute-done | bytes 393248 | tf_op jit(solution)/shard_map/ppermute | solution.py:266
  69.7 9.5 %backward.1 = f32[2,12,256,128]{3,2,1,0:T(8,128)} custom-call(s32[1,2]{1,0:T(1,128)S(1)} %bitcast.31, s32[32,128]{1,0:T(8,128)S(1)} %get-tuple-element.8.codes_in, bf16[10752,128]{1,0:T(8,128)(2,1)S(1)} %table.1.tab_ref, bf16[384,128]{1,0:T(8,128)(2,1)S(1)} %get-tuple-element.9.refs_0_, bf16[384,128]{1,0:T(8,128)(2,1)S(1)} %collective-permute-done.13.refs_1_, ...), custom_call_target="tpu_custom_call" | custom-call | tf_op jit(solution)/shard_map/backward/pallas_call | solution.py:360
  (6 shorter events, 0.2 us)
Async XLA Ops:
  0.6 1.2 %copy-start.3 = (s32[2,1]{0,1:T(1,128)S(1)}, s32[2,1]{0,1:T(1,128)}, u32[]{:S(2)}) copy-start(s32[2,1]{0,1:T(1,128)} %param.14) | copy-start | bytes 28
  0.6 1.2 %copy-start.8 = (s32[2,512]{1,0:T(2,128)S(1)}, s32[2,512]{1,0:T(2,128)}, u32[]{:S(2)}) copy-start(s32[2,512]{1,0:T(2,128)} %seed_ref.1) | copy-start | bytes 12292
  0.7 1.2 %copy-start.6 = (s32[2,512]{1,0:T(2,128)S(1)}, s32[2,512]{1,0:T(2,128)}, u32[]{:S(2)}) copy-start(s32[2,512]{1,0:T(2,128)} %target_ref.1) | copy-start | bytes 12292
  0.7 1.2 %copy-start.7 = (s32[2,512]{1,0:T(2,128)S(1)}, s32[2,512]{1,0:T(2,128)}, u32[]{:S(2)}) copy-start(s32[2,512]{1,0:T(2,128)} %source_ref.1) | copy-start | bytes 12292
  0.7 1.2 %copy-start.5 = (s32[2,512,1]{1,2,0:T(1,128)S(1)}, s32[2,512,1]{1,2,0:T(1,128)}, u32[]{:S(2)}) copy-start(s32[2,512,1]{1,2,0:T(1,128)} %param.10) | copy-start | bytes 12292
  0.7 1.4 %copy-start.4 = (bf16[2,12,256,128]{3,2,1,0:T(8,128)(2,1)S(1)}, bf16[2,12,256,128]{3,2,1,0:T(8,128)(2,1)}, u32[]{:S(2)}) copy-start(bf16[2,12,256,128]{3,2,1,0:T(8,128)(2,1)} %field_ref.1) | copy-start | bytes 4718596
  10.4 19.4 %copy-start = (f32[12,1,8,128]{3,2,1,0:T(8,128)S(1)}, f32[12,1,8,128]{3,2,1,0:T(8,128)}, u32[]{:S(2)}) copy-start(f32[12,1,8,128]{3,2,1,0:T(8,128)} %refs_0_.1) | copy-start | bytes 147460
  10.4 19.4 %copy-start.1 = (f32[12,1,8,128]{3,2,1,0:T(8,128)S(1)}, f32[12,1,8,128]{3,2,1,0:T(8,128)}, u32[]{:S(2)}) copy-start(f32[12,1,8,128]{3,2,1,0:T(8,128)} %refs_1_.1) | copy-start | bytes 147460
  10.4 19.4 %copy-start.2 = (f32[12,1,8,128]{3,2,1,0:T(8,128)S(1)}, f32[12,1,8,128]{3,2,1,0:T(8,128)}, u32[]{:S(2)}) copy-start(f32[12,1,8,128]{3,2,1,0:T(8,128)} %refs_2_.1) | copy-start | bytes 147460
  10.4 2.4 %collective-permute-start = (f32[4,384,128]{2,1,0:T(8,128)S(1)}, f32[4,384,128]{2,1,0:T(8,128)S(1)}, u32[]{:S(2)}, u32[]{:S(2)}) collective-permute-start(f32[4,384,128]{2,1,0:T(8,128)S(1)} %bitcast.33), channel_id=1, source_target_pairs={{0,1},{1,0},{2,3},{3,2},{4,5},{5,4},{6,7},{7,6},{8,9},{9,8},{10,11... | collective-permute-start | bytes 2359304 | tf_op jit(solution)/shard_map/ppermute | solution.py:266
  12.9 7.8 %collective-permute-start.1 = (f32[384,128]{1,0:T(8,128)S(1)}, f32[384,128]{1,0:T(8,128)S(1)}, u32[]{:S(2)}, u32[]{:S(2)}) collective-permute-start(f32[384,128]{1,0:T(8,128)S(1)} %get-tuple-element.10), channel_id=1, source_target_pairs={{0,2},{1,3},{2,0},{3,1},{4,6},{5,7},{6,4},{7,5},{8,10},{9,11},{10,... | collective-permute-start | bytes 589832 | tf_op jit(solution)/shard_map/ppermute | solution.py:266
  14.6 11.7 %collective-permute-start.3 = (f32[384,128]{1,0:T(8,128)S(1)}, f32[384,128]{1,0:T(8,128)S(1)}, u32[]{:S(2)}, u32[]{:S(2)}) collective-permute-start(f32[384,128]{1,0:T(8,128)S(1)} %get-tuple-element.11), channel_id=1, source_target_pairs={{0,6},{1,7},{2,4},{3,5},{4,2},{5,3},{6,0},{7,1},{8,14},{9,15},{10,... | collective-permute-start | bytes 589832 | tf_op jit(solution)/shard_map/ppermute | solution.py:266
  16.6 11.1 %collective-permute-start.2 = (f32[384,128]{1,0:T(8,128)S(1)}, f32[384,128]{1,0:T(8,128)S(1)}, u32[]{:S(2)}, u32[]{:S(2)}) collective-permute-start(f32[384,128]{1,0:T(8,128)S(1)} %get-tuple-element.12), channel_id=1, source_target_pairs={{0,4},{1,5},{2,6},{3,7},{4,0},{5,1},{6,2},{7,3},{8,12},{9,13},{10,... | collective-permute-start | bytes 589832 | tf_op jit(solution)/shard_map/ppermute | solution.py:266
  27.8 9.3 %collective-permute-start.4 = (f32[384,128]{1,0:T(8,128)S(1)}, f32[384,128]{1,0:T(8,128)S(1)}, u32[]{:S(2)}, u32[]{:S(2)}) collective-permute-start(f32[384,128]{1,0:T(8,128)S(1)} %add_add_fusion), channel_id=1, source_target_pairs={{0,8},{8,0},{16,24},{24,16},{1,9},{9,1},{17,25},{25,17},{2,10},{10... | collective-permute-start | bytes 589832 | tf_op jit(solution)/shard_map/ppermute | solution.py:266
  29.8 11.5 %collective-permute-start.8 = (f32[3,96,128]{2,1,0:T(8,128)S(1)}, f32[3,96,128]{2,1,0:T(8,128)S(1)}, u32[]{:S(2)}, u32[]{:S(2)}) collective-permute-start(f32[3,96,128]{2,1,0:T(8,128)S(1)} %pack.1), channel_id=1, source_target_pairs={{0,24},{8,16},{16,8},{24,0},{1,25},{9,17},{17,9},{25,1},{2,26},{10... | collective-permute-start | bytes 442376 | tf_op jit(solution)/shard_map/ppermute | solution.py:266
  32.5 17.4 %collective-permute-start.7 = (f32[3,96,128]{2,1,0:T(8,128)S(1)}, f32[3,96,128]{2,1,0:T(8,128)S(1)}, u32[]{:S(2)}, u32[]{:S(2)}) collective-permute-start(f32[3,96,128]{2,1,0:T(8,128)S(1)} %pack.1), channel_id=1, source_target_pairs={{0,16},{8,24},{16,0},{24,8},{1,17},{9,25},{17,1},{25,9},{2,18},{10... | collective-permute-start | bytes 442376 | tf_op jit(solution)/shard_map/ppermute | solution.py:266
  32.5 17.4 %collective-permute-start.6 = (f32[3,96,128]{2,1,0:T(8,128)S(1)}, f32[3,96,128]{2,1,0:T(8,128)S(1)}, u32[]{:S(2)}, u32[]{:S(2)}) collective-permute-start(f32[3,96,128]{2,1,0:T(8,128)S(1)} %pack.1), channel_id=1, source_target_pairs={{0,8},{8,0},{16,24},{24,16},{1,9},{9,1},{17,25},{25,17},{2,10},{10... | collective-permute-start | bytes 442376 | tf_op jit(solution)/shard_map/ppermute | solution.py:266
  37.1 15.4 %collective-permute-start.5 = (f32[384,128]{1,0:T(8,128)S(1)}, f32[384,128]{1,0:T(8,128)S(1)}, u32[]{:S(2)}, u32[]{:S(2)}) collective-permute-start(f32[384,128]{1,0:T(8,128)S(1)} %add.30.a_ref), channel_id=1, source_target_pairs={{0,16},{8,24},{16,0},{24,8},{1,17},{9,25},{17,1},{25,9},{2,18},{10... | collective-permute-start | bytes 589832 | tf_op jit(solution)/shard_map/ppermute | solution.py:266
  52.6 1.2 %collective-permute-start.9 = (f32[8,128]{1,0:T(8,128)S(1)}, f32[8,128]{1,0:T(8,128)S(1)}, u32[]{:S(2)}, u32[]{:S(2)}) collective-permute-start(f32[8,128]{1,0:T(8,128)S(1)} %sums.1), channel_id=1, source_target_pairs={{0,1},{1,0},{2,3},{3,2},{4,5},{5,4},{6,7},{7,6},{8,9},{9,8},{10,11... | collective-permute-start | bytes 12296 | tf_op jit(solution)/shard_map/ppermute | solution.py:266
  53.9 4.5 %collective-permute-start.12 = (f32[8,128]{1,0:T(8,128)S(1)}, f32[8,128]{1,0:T(8,128)S(1)}, u32[]{:S(2)}, u32[]{:S(2)}) collective-permute-start(f32[8,128]{1,0:T(8,128)S(1)} %add.31.refs_0_), channel_id=1, source_target_pairs={{0,6},{1,7},{2,4},{3,5},{4,2},{5,3},{6,0},{7,1},{8,14},{9,15},{10,... | collective-permute-start | bytes 12296 | tf_op jit(solution)/shard_map/ppermute | solution.py:266
  55.9 3.6 %collective-permute-start.11 = (f32[8,128]{1,0:T(8,128)S(1)}, f32[8,128]{1,0:T(8,128)S(1)}, u32[]{:S(2)}, u32[]{:S(2)}) collective-permute-start(f32[8,128]{1,0:T(8,128)S(1)} %add.31.refs_0_), channel_id=1, source_target_pairs={{0,4},{1,5},{2,6},{3,7},{4,0},{5,1},{6,2},{7,3},{8,12},{9,13},{10,... | collective-permute-start | bytes 12296 | tf_op jit(solution)/shard_map/ppermute | solution.py:266
  56.9 3.6 %collective-permute-start.10 = (f32[8,128]{1,0:T(8,128)S(1)}, f32[8,128]{1,0:T(8,128)S(1)}, u32[]{:S(2)}, u32[]{:S(2)}) collective-permute-start(f32[8,128]{1,0:T(8,128)S(1)} %add.31.refs_0_), channel_id=1, source_target_pairs={{0,2},{1,3},{2,0},{3,1},{4,6},{5,7},{6,4},{7,5},{8,10},{9,11},{10,... | collective-permute-start | bytes 12296 | tf_op jit(solution)/shard_map/ppermute | solution.py:266
  61.3 5.6 %collective-permute-start.15 = (bf16[384,128]{1,0:T(8,128)(2,1)S(1)}, bf16[384,128]{1,0:T(8,128)(2,1)S(1)}, u32[]{:S(2)}, u32[]{:S(2)}) collective-permute-start(bf16[384,128]{1,0:T(8,128)(2,1)S(1)} %get-tuple-element.9.refs_0_), channel_id=1, source_target_pairs={{0,6},{1,7},{2,4},{3,5},{4,2},{5,3},{6,0},{7,1},{8,14},{9,15},{10,... | collective-permute-start | bytes 294920 | tf_op jit(solution)/shard_map/ppermute | solution.py:266
  62.3 5.5 %collective-permute-start.14 = (bf16[384,128]{1,0:T(8,128)(2,1)S(1)}, bf16[384,128]{1,0:T(8,128)(2,1)S(1)}, u32[]{:S(2)}, u32[]{:S(2)}) collective-permute-start(bf16[384,128]{1,0:T(8,128)(2,1)S(1)} %get-tuple-element.9.refs_0_), channel_id=1, source_target_pairs={{0,4},{1,5},{2,6},{3,7},{4,0},{5,1},{6,2},{7,3},{8,12},{9,13},{10,... | collective-permute-start | bytes 294920 | tf_op jit(solution)/shard_map/ppermute | solution.py:266
  63.2 4.7 %collective-permute-start.13 = (bf16[384,128]{1,0:T(8,128)(2,1)S(1)}, bf16[384,128]{1,0:T(8,128)(2,1)S(1)}, u32[]{:S(2)}, u32[]{:S(2)}) collective-permute-start(bf16[384,128]{1,0:T(8,128)(2,1)S(1)} %get-tuple-element.9.refs_0_), channel_id=1, source_target_pairs={{0,2},{1,3},{2,0},{3,1},{4,6},{5,7},{6,4},{7,5},{8,10},{9,11},{10,... | collective-permute-start | bytes 294920 | tf_op jit(solution)/shard_map/ppermute | solution.py:266
  67.9 1.8 %collective-permute-start.16 = (bf16[4,384,128]{2,1,0:T(8,128)(2,1)S(1)}, bf16[4,384,128]{2,1,0:T(8,128)(2,1)S(1)}, u32[]{:S(2)}, u32[]{:S(2)}) collective-permute-start(bf16[4,384,128]{2,1,0:T(8,128)(2,1)S(1)} %pad_maximum_fusion.1), channel_id=1, source_target_pairs={{0,1},{1,0},{2,3},{3,2},{4,5},{5,4},{6,7},{7,6},{8,9},{9,8},{10,11... | collective-permute-start | bytes 1179656 | tf_op jit(solution)/shard_map/ppermute | solution.py:266

commit v5 on v4

--- a/solution.py
+++ b/solution.py
@@ -172,10 +172,6 @@
             wide_ref[pl.ds(c, group, stride=PITCH), :] = ref[c, 0]
         for s in range(group):
             out_ref[n, pl.ds(s * comps, comps), :] = wide_ref[pl.ds(s * PITCH, comps), :]
-
-
-def fold_kernel(a_ref, b_ref, out_ref):
-    out_ref[...] = a_ref[...] + b_ref[...]
 
 
 def terms(a_ref, b_ref, hist_ref, k, rows):
@@ -319,14 +315,7 @@
     arrived = []
     for j in range(1, half):
         arrived.append(swap(held[j], "mesh", 2 * j))
-    total = pl.pallas_call(
-        fold_kernel,
-        out_shape=f32(part_rows, nodes),
-        in_specs=[in_vmem()] * 2,
-        out_specs=in_vmem(),
-        compiler_params=limit(2),
-        name="fold",
-    )(keep[0], got[0])
+    total = keep[0] + got[0]
     for piece in arrived:
         total = total + piece
     bits = evs.bit_length() - 1

time: 79.3 us -> 79.3 us (level)
  no operation moved by 1% of the time
where the time goes in v5:
time: 79.3 us; the launch traced here: 79.2 us
  waiting for transfers between devices  36.1 us (46%)
  starting transfers between devices  21.9 us (28%)
  Pallas kernels  19.8 us (25%)
  between operations  0.82 us (1%)
    ppermute x17, waiting for transfers between devices, swap(): return lax.ppermute(x, axis, [(i, i ^ k) for i in range(size)])  36.1 us
    ppermute x17, starting transfers between devices, swap(): return lax.ppermute(x, axis, [(i, i ^ k) for i in range(size)])  21.9 us
    pallas_call x1, Pallas kernels, body(): pl.pallas_call(functools.partial(backward_kernel, dims), out_shape=f32(*k...  9.46 us
    pallas_call x1, Pallas kernels, body(): pl.pallas_call(functools.partial(forward_kernel, dims), out_shape=[f32(bl...  8.21 us
  transfers between devices with their start and end apart: 17, of which 15 were waited for; matrix products, arithmetic and copies ran while one was open for 0% of the time, Pallas kernels for 0%

profile of v5, /device:TPU:0, one launch (start us, length us, event | category | flops | bytes accessed | tf_op | source)
XLA Modules:
  0.0 79.2 jit_solution(1123009983529708925)
XLA Ops:
  0.6 0.0 copy-start.3
  0.6 0.0 copy-start.8
  0.7 0.0 copy-start.6
  0.7 0.0 copy-start.7
  0.7 0.0 copy-start.5
  0.7 0.0 copy-start.4
  0.7 1.2 %table.1.tab_ref = bf16[10752,128]{1,0:T(8,128)(2,1)S(1)} custom-call(), custom_call_target="tpu_custom_call" | custom-call | flops 268435456 | bytes 4194304 | tf_op jit(solution)/shard_map/table/pallas_call | solution.py:284
  1.9 0.0 copy-done.3
  1.9 0.0 copy-done.8
  1.9 0.0 copy-done.6
  1.9 0.0 copy-done.7
  1.9 0.0 copy-done.5
  1.9 0.2 copy-done.4
  2.1 8.2 %forward.1 = (f32[3088,128]{1,0:T(8,128)S(1)}, s32[32,128]{1,0:T(8,128)S(1)}) custom-call(s32[1,2]{1,0:T(1,128)S(1)} %bitcast.38, s32[2,1,512]{2,1,0:T(1,128)S(1)} %bitcast.40, s32[2,512]{1,0:T(2,128)S(1)} %copy-done.6, s32[2,512]{1,0:T(2,128)S(1)} %copy-done.7, s32[2,512]{1,0:T(2,128)S(1)} %copy-done.8, bf16[2,12,256,128]{3,2,1,0:T(8,128)(2,1)S(1)} %copy-done.4, ...), custom_call_target="tpu_custom_call" | custom-call | flops 34359738368 | bytes 16777216 | tf_op jit(solution)/shard_map/forward/pallas_call | solution.py:292
  10.3 0.1 slice.37
  10.4 0.0 copy-start
  10.4 0.0 copy-start.1
  10.4 0.0 copy-start.2
  10.4 0.1 collective-permute-start
  10.5 2.3 %collective-permute-done = f32[4,384,128]{2,1,0:T(8,128)S(1)} collective-permute-done((f32[4,384,128]{2,1,0:T(8,128)S(1)}, f32[4,384,128]{2,1,0:T(8,128)S(1)}, u32[]{:S(2)}, u32[]{:S(2)}) %collective-permute-start) | collective-permute-done | bytes 786464 | tf_op jit(solution)/shard_map/ppermute | solution.py:262
  12.8 0.1 fusion.2
  12.9 1.7 %collective-permute-start.1 = (f32[384,128]{1,0:T(8,128)S(1)}, f32[384,128]{1,0:T(8,128)S(1)}, u32[]{:S(2)}, u32[]{:S(2)}) collective-permute-start(f32[384,128]{1,0:T(8,128)S(1)} %get-tuple-element.10), channel_id=1, source_target_pairs={{0,2},{1,3},{2,0},{3,1},{4,6},{5,7},{6,4},{7,5},{8,10},{9,11},{10,... | collective-permute-start | bytes 589832 | tf_op jit(solution)/shard_map/ppermute | solution.py:262
  14.5 2.1 %collective-permute-start.3 = (f32[384,128]{1,0:T(8,128)S(1)}, f32[384,128]{1,0:T(8,128)S(1)}, u32[]{:S(2)}, u32[]{:S(2)}) collective-permute-start(f32[384,128]{1,0:T(8,128)S(1)} %get-tuple-element.11), channel_id=1, source_target_pairs={{0,6},{1,7},{2,4},{3,5},{4,2},{5,3},{6,0},{7,1},{8,14},{9,15},{10,... | collective-permute-start | bytes 589832 | tf_op jit(solution)/shard_map/ppermute | solution.py:262
  16.6 0.5 collective-permute-start.2
  17.1 3.6 %collective-permute-done.1 = f32[384,128]{1,0:T(8,128)S(1)} collective-permute-done((f32[384,128]{1,0:T(8,128)S(1)}, f32[384,128]{1,0:T(8,128)S(1)}, u32[]{:S(2)}, u32[]{:S(2)}) %collective-permute-start.1) | collective-permute-done | bytes 196640 | tf_op jit(solution)/shard_map/ppermute | solution.py:262
  20.7 5.6 %collective-permute-done.3 = f32[384,128]{1,0:T(8,128)S(1)} collective-permute-done((f32[384,128]{1,0:T(8,128)S(1)}, f32[384,128]{1,0:T(8,128)S(1)}, u32[]{:S(2)}, u32[]{:S(2)}) %collective-permute-start.3) | collective-permute-done | bytes 196640 | tf_op jit(solution)/shard_map/ppermute | solution.py:262
  26.3 1.4 %collective-permute-done.2 = f32[384,128]{1,0:T(8,128)S(1)} collective-permute-done((f32[384,128]{1,0:T(8,128)S(1)}, f32[384,128]{1,0:T(8,128)S(1)}, u32[]{:S(2)}, u32[]{:S(2)}) %collective-permute-start.2) | collective-permute-done | bytes 196640 | tf_op jit(solution)/shard_map/ppermute | solution.py:262
  27.7 0.1 fusion.6
  27.8 2.0 %collective-permute-start.4 = (f32[384,128]{1,0:T(8,128)S(1)}, f32[384,128]{1,0:T(8,128)S(1)}, u32[]{:S(2)}, u32[]{:S(2)}) collective-permute-start(f32[384,128]{1,0:T(8,128)S(1)} %fusion.6), channel_id=1, source_target_pairs={{0,8},{8,0},{16,24},{24,16},{1,9},{9,1},{17,25},{25,17},{2,10},{10... | collective-permute-start | bytes 589832 | tf_op jit(solution)/shard_map/ppermute | solution.py:262
  29.8 0.0 copy-done
  29.8 0.0 copy-done.1
  29.8 0.0 copy-done.2
  29.8 2.7 %collective-permute-start.8 = (f32[3,96,128]{2,1,0:T(8,128)S(1)}, f32[3,96,128]{2,1,0:T(8,128)S(1)}, u32[]{:S(2)}, u32[]{:S(2)}) collective-permute-start(f32[3,96,128]{2,1,0:T(8,128)S(1)} %pack.1), channel_id=1, source_target_pairs={{0,24},{8,16},{16,8},{24,0},{1,25},{9,17},{17,9},{25,1},{2,26},{10... | collective-permute-start | bytes 442376 | tf_op jit(solution)/shard_map/ppermute | solution.py:262
  32.5 0.0 collective-permute-start.7
  32.5 1.8 %collective-permute-start.6 = (f32[3,96,128]{2,1,0:T(8,128)S(1)}, f32[3,96,128]{2,1,0:T(8,128)S(1)}, u32[]{:S(2)}, u32[]{:S(2)}) collective-permute-start(f32[3,96,128]{2,1,0:T(8,128)S(1)} %pack.1), channel_id=1, source_target_pairs={{0,8},{8,0},{16,24},{24,16},{1,9},{9,1},{17,25},{25,17},{2,10},{10... | collective-permute-start | bytes 442376 | tf_op jit(solution)/shard_map/ppermute | solution.py:262
  34.3 2.8 %collective-permute-done.4 = f32[384,128]{1,0:T(8,128)S(1)} collective-permute-done((f32[384,128]{1,0:T(8,128)S(1)}, f32[384,128]{1,0:T(8,128)S(1)}, u32[]{:S(2)}, u32[]{:S(2)}) %collective-permute-start.4) | collective-permute-done | bytes 196640 | tf_op jit(solution)/shard_map/ppermute | solution.py:262
  37.1 4.0 %collective-permute-start.5 = (f32[384,128]{1,0:T(8,128)S(1)}, f32[384,128]{1,0:T(8,128)S(1)}, u32[]{:S(2)}, u32[]{:S(2)}) collective-permute-start(f32[384,128]{1,0:T(8,128)S(1)} %add.34.a_ref), channel_id=1, source_target_pairs={{0,16},{8,24},{16,0},{24,8},{1,17},{9,25},{17,1},{25,9},{2,18},{10... | collective-permute-start | bytes 589832 | tf_op jit(solution)/shard_map/ppermute | solution.py:262
  41.1 0.2 collective-permute-done.8
  41.3 8.6 %collective-permute-done.7 = f32[3,96,128]{2,1,0:T(8,128)S(1)} collective-permute-done((f32[3,96,128]{2,1,0:T(8,128)S(1)}, f32[3,96,128]{2,1,0:T(8,128)S(1)}, u32[]{:S(2)}, u32[]{:S(2)}) %collective-permute-start.7) | collective-permute-done | bytes 147488 | tf_op jit(solution)/shard_map/ppermute | solution.py:262
  49.9 0.0 collective-permute-done.6
  49.9 2.6 %collective-permute-done.5.b_ref = f32[384,128]{1,0:T(8,128)S(1)} collective-permute-done((f32[384,128]{1,0:T(8,128)S(1)}, f32[384,128]{1,0:T(8,128)S(1)}, u32[]{:S(2)}, u32[]{:S(2)}) %collective-permute-start.5) | collective-permute-done | bytes 196640 | tf_op jit(solution)/shard_map/ppermute | solution.py:262
  52.5 0.1 sums.1
  52.6 0.1 collective-permute-start.9
  52.7 1.2 %collective-permute-done.9 = f32[8,128]{1,0:T(8,128)S(1)} collective-permute-done((f32[8,128]{1,0:T(8,128)S(1)}, f32[8,128]{1,0:T(8,128)S(1)}, u32[]{:S(2)}, u32[]{:S(2)}) %collective-permute-start.9) | collective-permute-done | bytes 4128 | tf_op jit(solution)/shard_map/ppermute | solution.py:262
  53.8 2.0 %collective-permute-start.12 = (f32[8,128]{1,0:T(8,128)S(1)}, f32[8,128]{1,0:T(8,128)S(1)}, u32[]{:S(2)}, u32[]{:S(2)}) collective-permute-start(f32[8,128]{1,0:T(8,128)S(1)} %add.35.refs_0_), channel_id=1, source_target_pairs={{0,6},{1,7},{2,4},{3,5},{4,2},{5,3},{6,0},{7,1},{8,14},{9,15},{10,... | collective-permute-start | bytes 12296 | tf_op jit(solution)/shard_map/ppermute | solution.py:262
  55.9 1.0 %collective-permute-start.11 = (f32[8,128]{1,0:T(8,128)S(1)}, f32[8,128]{1,0:T(8,128)S(1)}, u32[]{:S(2)}, u32[]{:S(2)}) collective-permute-start(f32[8,128]{1,0:T(8,128)S(1)} %add.35.refs_0_), channel_id=1, source_target_pairs={{0,4},{1,5},{2,6},{3,7},{4,0},{5,1},{6,2},{7,3},{8,12},{9,13},{10,... | collective-permute-start | bytes 12296 | tf_op jit(solution)/shard_map/ppermute | solution.py:262
  56.9 0.4 collective-permute-start.10
  57.3 1.0 %collective-permute-done.12.refs_3_ = f32[8,128]{1,0:T(8,128)S(1)} collective-permute-done((f32[8,128]{1,0:T(8,128)S(1)}, f32[8,128]{1,0:T(8,128)S(1)}, u32[]{:S(2)}, u32[]{:S(2)}) %collective-permute-start.12) | collective-permute-done | bytes 4128 | tf_op jit(solution)/shard_map/ppermute | solution.py:262
  58.4 1.1 %collective-permute-done.11.refs_2_ = f32[8,128]{1,0:T(8,128)S(1)} collective-permute-done((f32[8,128]{1,0:T(8,128)S(1)}, f32[8,128]{1,0:T(8,128)S(1)}, u32[]{:S(2)}, u32[]{:S(2)}) %collective-permute-start.11) | collective-permute-done | bytes 4128 | tf_op jit(solution)/shard_map/ppermute | solution.py:262
  59.5 1.0 %collective-permute-done.10.refs_1_ = f32[8,128]{1,0:T(8,128)S(1)} collective-permute-done((f32[8,128]{1,0:T(8,128)S(1)}, f32[8,128]{1,0:T(8,128)S(1)}, u32[]{:S(2)}, u32[]{:S(2)}) %collective-permute-start.10) | collective-permute-done | bytes 4128 | tf_op jit(solution)/shard_map/ppermute | solution.py:262
  60.5 0.8 direction.1
  61.3 1.1 %collective-permute-start.15 = (bf16[384,128]{1,0:T(8,128)(2,1)S(1)}, bf16[384,128]{1,0:T(8,128)(2,1)S(1)}, u32[]{:S(2)}, u32[]{:S(2)}) collective-permute-start(bf16[384,128]{1,0:T(8,128)(2,1)S(1)} %get-tuple-element.9.refs_0_), channel_id=1, source_target_pairs={{0,6},{1,7},{2,4},{3,5},{4,2},{5,3},{6,0},{7,1},{8,14},{9,15},{10,... | collective-permute-start | bytes 294920 | tf_op jit(solution)/shard_map/ppermute | solution.py:262
  62.3 0.8 %collective-permute-start.14 = (bf16[384,128]{1,0:T(8,128)(2,1)S(1)}, bf16[384,128]{1,0:T(8,128)(2,1)S(1)}, u32[]{:S(2)}, u32[]{:S(2)}) collective-permute-start(bf16[384,128]{1,0:T(8,128)(2,1)S(1)} %get-tuple-element.9.refs_0_), channel_id=1, source_target_pairs={{0,4},{1,5},{2,6},{3,7},{4,0},{5,1},{6,2},{7,3},{8,12},{9,13},{10,... | collective-permute-start | bytes 294920 | tf_op jit(solution)/shard_map/ppermute | solution.py:262
  63.2 1.6 %collective-permute-start.13 = (bf16[384,128]{1,0:T(8,128)(2,1)S(1)}, bf16[384,128]{1,0:T(8,128)(2,1)S(1)}, u32[]{:S(2)}, u32[]{:S(2)}) collective-permute-start(bf16[384,128]{1,0:T(8,128)(2,1)S(1)} %get-tuple-element.9.refs_0_), channel_id=1, source_target_pairs={{0,2},{1,3},{2,0},{3,1},{4,6},{5,7},{6,4},{7,5},{8,10},{9,11},{10,... | collective-permute-start | bytes 294920 | tf_op jit(solution)/shard_map/ppermute | solution.py:262
  64.8 2.1 %collective-permute-done.15.refs_3_ = bf16[384,128]{1,0:T(8,128)(2,1)S(1)} collective-permute-done((bf16[384,128]{1,0:T(8,128)(2,1)S(1)}, bf16[384,128]{1,0:T(8,128)(2,1)S(1)}, u32[]{:S(2)}, u32[]{:S(2)}) %collective-permute-start.15) | collective-permute-done | bytes 98336 | tf_op jit(solution)/shard_map/ppermute | solution.py:262
  66.9 1.0 %collective-permute-done.14.refs_2_ = bf16[384,128]{1,0:T(8,128)(2,1)S(1)} collective-permute-done((bf16[384,128]{1,0:T(8,128)(2,1)S(1)}, bf16[384,128]{1,0:T(8,128)(2,1)S(1)}, u32[]{:S(2)}, u32[]{:S(2)}) %collective-permute-start.14) | collective-permute-done | bytes 98336 | tf_op jit(solution)/shard_map/ppermute | solution.py:262
  67.8 0.0 collective-permute-done.13.refs_1_
  67.8 0.1 pad_maximum_fusion.1
  67.9 0.1 collective-permute-start.16
  68.0 1.7 %collective-permute-done.16.refs_4_ = bf16[4,384,128]{2,1,0:T(8,128)(2,1)S(1)} collective-permute-done((bf16[4,384,128]{2,1,0:T(8,128)(2,1)S(1)}, bf16[4,384,128]{2,1,0:T(8,128)(2,1)S(1)}, u32[]{:S(2)}, u32[]{:S(2)}) %collective-permute-start.16) | collective-permute-done | bytes 393248 | tf_op jit(solution)/shard_map/ppermute | solution.py:262
  69.7 9.5 %backward.1 = f32[2,12,256,128]{3,2,1,0:T(8,128)} custom-call(s32[1,2]{1,0:T(1,128)S(1)} %bitcast.39, s32[32,128]{1,0:T(8,128)S(1)} %get-tuple-element.8.codes_in, bf16[10752,128]{1,0:T(8,128)(2,1)S(1)} %table.1.tab_ref, bf16[384,128]{1,0:T(8,128)(2,1)S(1)} %get-tuple-element.9.refs_0_, bf16[384,128]{1,0:T(8,128)(2,1)S(1)} %collective-permute-done.13.refs_1_, ...), custom_call_target="tpu_custom_call" | custom-call | tf_op jit(solution)/shard_map/backward/pallas_call | solution.py:349
  (4 shorter events, 0.1 us)
Async XLA Ops:
  0.6 1.2 %copy-start.3 = (s32[2,1]{0,1:T(1,128)S(1)}, s32[2,1]{0,1:T(1,128)}, u32[]{:S(2)}) copy-start(s32[2,1]{0,1:T(1,128)} %param.14) | copy-start | bytes 28
  0.6 1.2 %copy-start.8 = (s32[2,512]{1,0:T(2,128)S(1)}, s32[2,512]{1,0:T(2,128)}, u32[]{:S(2)}) copy-start(s32[2,512]{1,0:T(2,128)} %seed_ref.1) | copy-start | bytes 12292
  0.7 1.2 %copy-start.6 = (s32[2,512]{1,0:T(2,128)S(1)}, s32[2,512]{1,0:T(2,128)}, u32[]{:S(2)}) copy-start(s32[2,512]{1,0:T(2,128)} %target_ref.1) | copy-start | bytes 12292
  0.7 1.2 %copy-start.7 = (s32[2,512]{1,0:T(2,128)S(1)}, s32[2,512]{1,0:T(2,128)}, u32[]{:S(2)}) copy-start(s32[2,512]{1,0:T(2,128)} %source_ref.1) | copy-start | bytes 12292
  0.7 1.2 %copy-start.5 = (s32[2,512,1]{1,2,0:T(1,128)S(1)}, s32[2,512,1]{1,2,0:T(1,128)}, u32[]{:S(2)}) copy-start(s32[2,512,1]{1,2,0:T(1,128)} %param.10) | copy-start | bytes 12292
  0.7 1.4 %copy-start.4 = (bf16[2,12,256,128]{3,2,1,0:T(8,128)(2,1)S(1)}, bf16[2,12,256,128]{3,2,1,0:T(8,128)(2,1)}, u32[]{:S(2)}) copy-start(bf16[2,12,256,128]{3,2,1,0:T(8,128)(2,1)} %field_ref.1) | copy-start | bytes 4718596
  10.4 19.4 %copy-start = (f32[12,1,8,128]{3,2,1,0:T(8,128)S(1)}, f32[12,1,8,128]{3,2,1,0:T(8,128)}, u32[]{:S(2)}) copy-start(f32[12,1,8,128]{3,2,1,0:T(8,128)} %refs_0_.1) | copy-start | bytes 147460
  10.4 19.4 %copy-start.1 = (f32[12,1,8,128]{3,2,1,0:T(8,128)S(1)}, f32[12,1,8,128]{3,2,1,0:T(8,128)}, u32[]{:S(2)}) copy-start(f32[12,1,8,128]{3,2,1,0:T(8,128)} %refs_1_.1) | copy-start | bytes 147460
  10.4 19.4 %copy-start.2 = (f32[12,1,8,128]{3,2,1,0:T(8,128)S(1)}, f32[12,1,8,128]{3,2,1,0:T(8,128)}, u32[]{:S(2)}) copy-start(f32[12,1,8,128]{3,2,1,0:T(8,128)} %refs_2_.1) | copy-start | bytes 147460
  10.4 2.4 %collective-permute-start = (f32[4,384,128]{2,1,0:T(8,128)S(1)}, f32[4,384,128]{2,1,0:T(8,128)S(1)}, u32[]{:S(2)}, u32[]{:S(2)}) collective-permute-start(f32[4,384,128]{2,1,0:T(8,128)S(1)} %bitcast.41), channel_id=1, source_target_pairs={{0,1},{1,0},{2,3},{3,2},{4,5},{5,4},{6,7},{7,6},{8,9},{9,8},{10,11... | collective-permute-start | bytes 2359304 | tf_op jit(solution)/shard_map/ppermute | solution.py:262
  12.9 7.8 %collective-permute-start.1 = (f32[384,128]{1,0:T(8,128)S(1)}, f32[384,128]{1,0:T(8,128)S(1)}, u32[]{:S(2)}, u32[]{:S(2)}) collective-permute-start(f32[384,128]{1,0:T(8,128)S(1)} %get-tuple-element.10), channel_id=1, source_target_pairs={{0,2},{1,3},{2,0},{3,1},{4,6},{5,7},{6,4},{7,5},{8,10},{9,11},{10,... | collective-permute-start | bytes 589832 | tf_op jit(solution)/shard_map/ppermute | solution.py:262
  14.5 11.7 %collective-permute-start.3 = (f32[384,128]{1,0:T(8,128)S(1)}, f32[384,128]{1,0:T(8,128)S(1)}, u32[]{:S(2)}, u32[]{:S(2)}) collective-permute-start(f32[384,128]{1,0:T(8,128)S(1)} %get-tuple-element.11), channel_id=1, source_target_pairs={{0,6},{1,7},{2,4},{3,5},{4,2},{5,3},{6,0},{7,1},{8,14},{9,15},{10,... | collective-permute-start | bytes 589832 | tf_op jit(solution)/shard_map/ppermute | solution.py:262
  16.6 11.1 %collective-permute-start.2 = (f32[384,128]{1,0:T(8,128)S(1)}, f32[384,128]{1,0:T(8,128)S(1)}, u32[]{:S(2)}, u32[]{:S(2)}) collective-permute-start(f32[384,128]{1,0:T(8,128)S(1)} %get-tuple-element.12), channel_id=1, source_target_pairs={{0,4},{1,5},{2,6},{3,7},{4,0},{5,1},{6,2},{7,3},{8,12},{9,13},{10,... | collective-permute-start | bytes 589832 | tf_op jit(solution)/shard_map/ppermute | solution.py:262
  27.8 9.3 %collective-permute-start.4 = (f32[384,128]{1,0:T(8,128)S(1)}, f32[384,128]{1,0:T(8,128)S(1)}, u32[]{:S(2)}, u32[]{:S(2)}) collective-permute-start(f32[384,128]{1,0:T(8,128)S(1)} %fusion.6), channel_id=1, source_target_pairs={{0,8},{8,0},{16,24},{24,16},{1,9},{9,1},{17,25},{25,17},{2,10},{10... | collective-permute-start | bytes 589832 | tf_op jit(solution)/shard_map/ppermute | solution.py:262
  29.8 11.5 %collective-permute-start.8 = (f32[3,96,128]{2,1,0:T(8,128)S(1)}, f32[3,96,128]{2,1,0:T(8,128)S(1)}, u32[]{:S(2)}, u32[]{:S(2)}) collective-permute-start(f32[3,96,128]{2,1,0:T(8,128)S(1)} %pack.1), channel_id=1, source_target_pairs={{0,24},{8,16},{16,8},{24,0},{1,25},{9,17},{17,9},{25,1},{2,26},{10... | collective-permute-start | bytes 442376 | tf_op jit(solution)/shard_map/ppermute | solution.py:262
  32.5 17.4 %collective-permute-start.7 = (f32[3,96,128]{2,1,0:T(8,128)S(1)}, f32[3,96,128]{2,1,0:T(8,128)S(1)}, u32[]{:S(2)}, u32[]{:S(2)}) collective-permute-start(f32[3,96,128]{2,1,0:T(8,128)S(1)} %pack.1), channel_id=1, source_target_pairs={{0,16},{8,24},{16,0},{24,8},{1,17},{9,25},{17,1},{25,9},{2,18},{10... | collective-permute-start | bytes 442376 | tf_op jit(solution)/shard_map/ppermute | solution.py:262
  32.5 17.4 %collective-permute-start.6 = (f32[3,96,128]{2,1,0:T(8,128)S(1)}, f32[3,96,128]{2,1,0:T(8,128)S(1)}, u32[]{:S(2)}, u32[]{:S(2)}) collective-permute-start(f32[3,96,128]{2,1,0:T(8,128)S(1)} %pack.1), channel_id=1, source_target_pairs={{0,8},{8,0},{16,24},{24,16},{1,9},{9,1},{17,25},{25,17},{2,10},{10... | collective-permute-start | bytes 442376 | tf_op jit(solution)/shard_map/ppermute | solution.py:262
  37.1 15.4 %collective-permute-start.5 = (f32[384,128]{1,0:T(8,128)S(1)}, f32[384,128]{1,0:T(8,128)S(1)}, u32[]{:S(2)}, u32[]{:S(2)}) collective-permute-start(f32[384,128]{1,0:T(8,128)S(1)} %add.34.a_ref), channel_id=1, source_target_pairs={{0,16},{8,24},{16,0},{24,8},{1,17},{9,25},{17,1},{25,9},{2,18},{10... | collective-permute-start | bytes 589832 | tf_op jit(solution)/shard_map/ppermute | solution.py:262
  52.6 1.2 %collective-permute-start.9 = (f32[8,128]{1,0:T(8,128)S(1)}, f32[8,128]{1,0:T(8,128)S(1)}, u32[]{:S(2)}, u32[]{:S(2)}) collective-permute-start(f32[8,128]{1,0:T(8,128)S(1)} %sums.1), channel_id=1, source_target_pairs={{0,1},{1,0},{2,3},{3,2},{4,5},{5,4},{6,7},{7,6},{8,9},{9,8},{10,11... | collective-permute-start | bytes 12296 | tf_op jit(solution)/shard_map/ppermute | solution.py:262
  53.8 4.5 %collective-permute-start.12 = (f32[8,128]{1,0:T(8,128)S(1)}, f32[8,128]{1,0:T(8,128)S(1)}, u32[]{:S(2)}, u32[]{:S(2)}) collective-permute-start(f32[8,128]{1,0:T(8,128)S(1)} %add.35.refs_0_), channel_id=1, source_target_pairs={{0,6},{1,7},{2,4},{3,5},{4,2},{5,3},{6,0},{7,1},{8,14},{9,15},{10,... | collective-permute-start | bytes 12296 | tf_op jit(solution)/shard_map/ppermute | solution.py:262
  55.9 3.6 %collective-permute-start.11 = (f32[8,128]{1,0:T(8,128)S(1)}, f32[8,128]{1,0:T(8,128)S(1)}, u32[]{:S(2)}, u32[]{:S(2)}) collective-permute-start(f32[8,128]{1,0:T(8,128)S(1)} %add.35.refs_0_), channel_id=1, source_target_pairs={{0,4},{1,5},{2,6},{3,7},{4,0},{5,1},{6,2},{7,3},{8,12},{9,13},{10,... | collective-permute-start | bytes 12296 | tf_op jit(solution)/shard_map/ppermute | solution.py:262
  56.9 3.6 %collective-permute-start.10 = (f32[8,128]{1,0:T(8,128)S(1)}, f32[8,128]{1,0:T(8,128)S(1)}, u32[]{:S(2)}, u32[]{:S(2)}) collective-permute-start(f32[8,128]{1,0:T(8,128)S(1)} %add.35.refs_0_), channel_id=1, source_target_pairs={{0,2},{1,3},{2,0},{3,1},{4,6},{5,7},{6,4},{7,5},{8,10},{9,11},{10,... | collective-permute-start | bytes 12296 | tf_op jit(solution)/shard_map/ppermute | solution.py:262
  61.3 5.6 %collective-permute-start.15 = (bf16[384,128]{1,0:T(8,128)(2,1)S(1)}, bf16[384,128]{1,0:T(8,128)(2,1)S(1)}, u32[]{:S(2)}, u32[]{:S(2)}) collective-permute-start(bf16[384,128]{1,0:T(8,128)(2,1)S(1)} %get-tuple-element.9.refs_0_), channel_id=1, source_target_pairs={{0,6},{1,7},{2,4},{3,5},{4,2},{5,3},{6,0},{7,1},{8,14},{9,15},{10,... | collective-permute-start | bytes 294920 | tf_op jit(solution)/shard_map/ppermute | solution.py:262
  62.3 5.5 %collective-permute-start.14 = (bf16[384,128]{1,0:T(8,128)(2,1)S(1)}, bf16[384,128]{1,0:T(8,128)(2,1)S(1)}, u32[]{:S(2)}, u32[]{:S(2)}) collective-permute-start(bf16[384,128]{1,0:T(8,128)(2,1)S(1)} %get-tuple-element.9.refs_0_), channel_id=1, source_target_pairs={{0,4},{1,5},{2,6},{3,7},{4,0},{5,1},{6,2},{7,3},{8,12},{9,13},{10,... | collective-permute-start | bytes 294920 | tf_op jit(solution)/shard_map/ppermute | solution.py:262
  63.2 4.7 %collective-permute-start.13 = (bf16[384,128]{1,0:T(8,128)(2,1)S(1)}, bf16[384,128]{1,0:T(8,128)(2,1)S(1)}, u32[]{:S(2)}, u32[]{:S(2)}) collective-permute-start(bf16[384,128]{1,0:T(8,128)(2,1)S(1)} %get-tuple-element.9.refs_0_), channel_id=1, source_target_pairs={{0,2},{1,3},{2,0},{3,1},{4,6},{5,7},{6,4},{7,5},{8,10},{9,11},{10,... | collective-permute-start | bytes 294920 | tf_op jit(solution)/shard_map/ppermute | solution.py:262
  67.9 1.8 %collective-permute-start.16 = (bf16[4,384,128]{2,1,0:T(8,128)(2,1)S(1)}, bf16[4,384,128]{2,1,0:T(8,128)(2,1)S(1)}, u32[]{:S(2)}, u32[]{:S(2)}) collective-permute-start(bf16[4,384,128]{2,1,0:T(8,128)(2,1)S(1)} %pad_maximum_fusion.1), channel_id=1, source_target_pairs={{0,1},{1,0},{2,3},{3,2},{4,5},{5,4},{6,7},{7,6},{8,9},{9,8},{10,11... | collective-permute-start | bytes 1179656 | tf_op jit(solution)/shard_map/ppermute | solution.py:262

commit v6 on v4

--- a/solution.py
+++ b/solution.py
@@ -199,8 +199,8 @@
     out_ref[pl.ds(4, 4), :] = jnp.zeros((4, LANES), jnp.float32)
 
 
-def direction_kernel(rows, evs, comps, group, a_ref, b_ref, hist_ref, *refs):
-    sum_refs, (inv_ref, round_ref, wide_ref) = refs[:-3], refs[-3:]
+def direction_kernel(rows, evs, a_ref, b_ref, hist_ref, *refs):
+    sum_refs, (inv_ref, round_ref) = refs[:-2], refs[-2:]
     level = [ref[...] for ref in sum_refs]
     while len(level) > 1:
         level = [level[i] + level[i + 1] for i in range(0, len(level), 2)]
@@ -215,10 +215,14 @@
         direction = -(scaled + bend * prev_step)
         round_ref[at, :] = direction.astype(jnp.bfloat16)
         if k == 0:
-            for s in range(group):
-                wide_ref[pl.ds(s * PITCH, comps), :] = direction[s * comps : (s + 1) * comps]
-            for c in range(comps):
-                inv_ref[c, 0] = wide_ref[pl.ds(c, group, stride=PITCH), :]
+            inv_ref[...] = direction
+
+
+def unpack_kernel(comps, group, in_ref, out_ref, wide_ref):
+    for s in range(group):
+        wide_ref[pl.ds(s * PITCH, comps), :] = in_ref[pl.ds(s * comps, comps), :]
+    for c in range(comps):
+        out_ref[c, 0] = wide_ref[pl.ds(c, group, stride=PITCH), :]
 
 
 def in_smem():
@@ -280,10 +284,9 @@
         compiler_params=limit(2),
         name="pack",
     )(prev_gradient, prev_step, precond)
-    hist = [packed]
-    for k in range(1, evs):
-        hist.append(swap(packed, "ev", k))
-    hist = jnp.stack(hist)
+    hist = packed[None]
+    for bit in range(evs.bit_length() - 1):
+        hist = jnp.concatenate([hist, swap(hist, "ev", 1 << bit)], axis=0)
 
     tab = pl.pallas_call(
         functools.partial(table_kernel, nodes),
@@ -344,17 +347,27 @@
     )(total, across, hist)
     local = local + swap(local, "mesh", 1)
     spread = [local] + [swap(local, "mesh", 2 * j) for j in range(1, half)]
-    inversion_direction, rounded = pl.pallas_call(
-        functools.partial(direction_kernel, rows, evs, comps, group),
-        out_shape=[f32(*precond.shape), bf16(part_rows, nodes)],
+    inverse, rounded = pl.pallas_call(
+        functools.partial(direction_kernel, rows, evs),
+        out_shape=[f32(rows, nodes), bf16(part_rows, nodes)],
         in_specs=[in_vmem()] * (3 + half),
         out_specs=[in_vmem()] * 2,
-        scratch_shapes=[pltpu.VMEM((group * PITCH, nodes), jnp.float32)],
         compiler_params=limit(4),
         name="direction",
     )(total, across, hist, *spread)
-
-    mine = [rounded] + [swap(rounded, "mesh", 2 * j) for j in range(1, half)]
+    inversion_direction = pl.pallas_call(
+        functools.partial(unpack_kernel, comps, group),
+        out_shape=f32(*precond.shape),
+        in_specs=[in_vmem()],
+        out_specs=in_vmem(),
+        scratch_shapes=[pltpu.VMEM((group * PITCH, nodes), jnp.float32)],
+        compiler_params=limit(2),
+        name="unpack",
+    )(inverse)
+
+    mine = [rounded]
+    for j in range(1, half):
+        mine.append(swap(rounded, "mesh", 2 * j))
     other = swap(jnp.stack(mine), "mesh", 1)
 
     event_direction = pl.pallas_call(

time: 79.3 us -> 75.1 us (0.947)
  starting transfers between devices: 21.9 us -> 18 us
  waiting for transfers between devices: 36.1 us -> 34.9 us
    ppermute x17 -> x16, starting transfers between devices: 21.9 us -> 18 us  [swap(): return lax.ppermute(x, axis, [(i, i ^ k) for i in range(size)])]
    ppermute x17 -> x16, waiting for transfers between devices: 36.1 us -> 34.9 us  [swap(): return lax.ppermute(x, axis, [(i, i ^ k) for i in range(size)])]
  transfers between devices with their start and end apart: 17 -> 16, of which waited for: 15 -> 13; matrix products, arithmetic and copies ran while one was open for 0% -> 0% of each run, Pallas kernels for 0% -> 1%
where the time goes in v6:
time: 75.1 us; the launch traced here: 74.9 us
  waiting for transfers between devices  34.9 us (46%)
  Pallas kernels  19.8 us (26%)
  starting transfers between devices  18 us (24%)
  local copies, waits for them, and re-layouts  0.98 us (1%)
  between operations  0.84 us (1%)
    ppermute x16, waiting for transfers between devices, swap(): return lax.ppermute(x, axis, [(i, i ^ k) for i in range(size)])  34.9 us
    ppermute x16, starting transfers between devices, swap(): return lax.ppermute(x, axis, [(i, i ^ k) for i in range(size)])  18 us
    pallas_call x1, Pallas kernels, body(): pl.pallas_call(functools.partial(backward_kernel, dims), out_shape=f32(*k...  9.45 us
    pallas_call x1, Pallas kernels, body(): pl.pallas_call(functools.partial(forward_kernel, dims), out_shape=[f32(bl...  8.21 us
  transfers between devices with their start and end apart: 16, of which 13 were waited for; matrix products, arithmetic and copies ran while one was open for 0% of the time, Pallas kernels for 1%

profile of v6, /device:TPU:0, one launch (start us, length us, event | category | flops | bytes accessed | tf_op | source)
XLA Modules:
  0.0 74.9 jit_solution(7435231339023062449)
XLA Ops:
  0.6 0.0 copy-start.3
  0.6 0.0 copy-start.8
  0.7 0.0 copy-start.6
  0.7 0.0 copy-start.7
  0.7 0.0 copy-start.5
  0.7 0.0 copy-start.4
  0.7 1.2 %table.1.tab_ref = bf16[10752,128]{1,0:T(8,128)(2,1)S(1)} custom-call(), custom_call_target="tpu_custom_call" | custom-call | flops 268435456 | bytes 4194304 | tf_op jit(solution)/shard_map/table/pallas_call | solution.py:291
  1.9 0.0 copy-done.3
  1.9 0.0 copy-done.8
  1.9 0.0 copy-done.6
  1.9 0.0 copy-done.7
  1.9 0.0 copy-done.5
  1.9 0.2 copy-done.4
  2.1 8.2 %forward.1 = (f32[3088,128]{1,0:T(8,128)S(1)}, s32[32,128]{1,0:T(8,128)S(1)}) custom-call(s32[1,2]{1,0:T(1,128)S(1)} %bitcast.29, s32[2,1,512]{2,1,0:T(1,128)S(1)} %bitcast.31, s32[2,512]{1,0:T(2,128)S(1)} %copy-done.6, s32[2,512]{1,0:T(2,128)S(1)} %copy-done.7, s32[2,512]{1,0:T(2,128)S(1)} %copy-done.8, bf16[2,12,256,128]{3,2,1,0:T(8,128)(2,1)S(1)} %copy-done.4, ...), custom_call_target="tpu_custom_call" | custom-call | flops 34359738368 | bytes 16777216 | tf_op jit(solution)/shard_map/forward/pallas_call | solution.py:299
  10.3 0.0 copy-start
  10.4 0.0 copy-start.1
  10.4 0.0 copy-start.2
  10.4 0.1 slice.37
  10.4 0.1 collective-permute-start
  10.5 0.6 copy-done
  11.1 0.0 copy-done.1
  11.2 0.0 copy-done.2
  11.2 1.7 %collective-permute-start.6 = (f32[1,3,96,128]{3,2,1,0:T(8,128)S(1)}, f32[1,3,96,128]{3,2,1,0:T(8,128)S(1)}, u32[]{:S(2)}, u32[]{:S(2)}) collective-permute-start(f32[1,3,96,128]{3,2,1,0:T(8,128)S(1)} %bitcast.22), channel_id=1, source_target_pairs={{0,8},{8,0},{16,24},{24,16},{1,9},{9,1},{17,25},{25,17},{2,10},{10... | collective-permute-start | bytes 442376 | tf_op jit(solution)/shard_map/ppermute | solution.py:270
  12.9 4.7 %collective-permute-done.6 = f32[1,3,96,128]{3,2,1,0:T(8,128)S(1)} collective-permute-done((f32[1,3,96,128]{3,2,1,0:T(8,128)S(1)}, f32[1,3,96,128]{3,2,1,0:T(8,128)S(1)}, u32[]{:S(2)}, u32[]{:S(2)}) %collective-permute-start.6) | collective-permute-done | bytes 147488 | tf_op jit(solution)/shard_map/ppermute | solution.py:270
  17.6 3.6 %collective-permute-start.7 = (f32[2,3,96,128]{3,2,1,0:T(8,128)S(1)}, f32[2,3,96,128]{3,2,1,0:T(8,128)S(1)}, u32[]{:S(2)}, u32[]{:S(2)}) collective-permute-start(f32[2,3,96,128]{3,2,1,0:T(8,128)S(1)} %pad_maximum_fusion.2), channel_id=1, source_target_pairs={{0,16},{8,24},{16,0},{24,8},{1,17},{9,25},{17,1},{25,9},{2,18},{10... | collective-permute-start | bytes 884744 | tf_op jit(solution)/shard_map/ppermute | solution.py:270
  21.2 0.0 collective-permute-done
  21.2 0.1 fusion.2
  21.3 1.5 %collective-permute-start.1 = (f32[384,128]{1,0:T(8,128)S(1)}, f32[384,128]{1,0:T(8,128)S(1)}, u32[]{:S(2)}, u32[]{:S(2)}) collective-permute-start(f32[384,128]{1,0:T(8,128)S(1)} %get-tuple-element.10), channel_id=1, source_target_pairs={{0,2},{1,3},{2,0},{3,1},{4,6},{5,7},{6,4},{7,5},{8,10},{9,11},{10,... | collective-permute-start | bytes 589832 | tf_op jit(solution)/shard_map/ppermute | solution.py:270
  22.8 1.6 %collective-permute-start.3 = (f32[384,128]{1,0:T(8,128)S(1)}, f32[384,128]{1,0:T(8,128)S(1)}, u32[]{:S(2)}, u32[]{:S(2)}) collective-permute-start(f32[384,128]{1,0:T(8,128)S(1)} %get-tuple-element.11), channel_id=1, source_target_pairs={{0,6},{1,7},{2,4},{3,5},{4,2},{5,3},{6,0},{7,1},{8,14},{9,15},{10,... | collective-permute-start | bytes 589832 | tf_op jit(solution)/shard_map/ppermute | solution.py:270
  24.4 0.5 collective-permute-start.2
  24.9 4.2 %collective-permute-done.1 = f32[384,128]{1,0:T(8,128)S(1)} collective-permute-done((f32[384,128]{1,0:T(8,128)S(1)}, f32[384,128]{1,0:T(8,128)S(1)}, u32[]{:S(2)}, u32[]{:S(2)}) %collective-permute-start.1) | collective-permute-done | bytes 196640 | tf_op jit(solution)/shard_map/ppermute | solution.py:270
  29.1 2.9 %collective-permute-done.3 = f32[384,128]{1,0:T(8,128)S(1)} collective-permute-done((f32[384,128]{1,0:T(8,128)S(1)}, f32[384,128]{1,0:T(8,128)S(1)}, u32[]{:S(2)}, u32[]{:S(2)}) %collective-permute-start.3) | collective-permute-done | bytes 196640 | tf_op jit(solution)/shard_map/ppermute | solution.py:270
  32.1 1.5 %collective-permute-done.2 = f32[384,128]{1,0:T(8,128)S(1)} collective-permute-done((f32[384,128]{1,0:T(8,128)S(1)}, f32[384,128]{1,0:T(8,128)S(1)}, u32[]{:S(2)}, u32[]{:S(2)}) %collective-permute-start.2) | collective-permute-done | bytes 196640 | tf_op jit(solution)/shard_map/ppermute | solution.py:270
  33.5 0.1 add_add_fusion
  33.6 1.3 %collective-permute-start.4 = (f32[384,128]{1,0:T(8,128)S(1)}, f32[384,128]{1,0:T(8,128)S(1)}, u32[]{:S(2)}, u32[]{:S(2)}) collective-permute-start(f32[384,128]{1,0:T(8,128)S(1)} %add_add_fusion), channel_id=1, source_target_pairs={{0,8},{8,0},{16,24},{24,16},{1,9},{9,1},{17,25},{25,17},{2,10},{10... | collective-permute-start | bytes 589832 | tf_op jit(solution)/shard_map/ppermute | solution.py:270
  34.9 4.4 %collective-permute-done.4 = f32[384,128]{1,0:T(8,128)S(1)} collective-permute-done((f32[384,128]{1,0:T(8,128)S(1)}, f32[384,128]{1,0:T(8,128)S(1)}, u32[]{:S(2)}, u32[]{:S(2)}) %collective-permute-start.4) | collective-permute-done | bytes 196640 | tf_op jit(solution)/shard_map/ppermute | solution.py:270
  39.4 0.6 collective-permute-start.5
  40.0 0.0 collective-permute-done.7
  40.0 0.1 pad_maximum_fusion.hist_ref
  40.0 8.4 %collective-permute-done.5.b_ref = f32[384,128]{1,0:T(8,128)S(1)} collective-permute-done((f32[384,128]{1,0:T(8,128)S(1)}, f32[384,128]{1,0:T(8,128)S(1)}, u32[]{:S(2)}, u32[]{:S(2)}) %collective-permute-start.5) | collective-permute-done | bytes 196640 | tf_op jit(solution)/shard_map/ppermute | solution.py:270
  48.5 0.1 sums.1
  48.6 0.1 collective-permute-start.8
  48.7 1.2 %collective-permute-done.8 = f32[8,128]{1,0:T(8,128)S(1)} collective-permute-done((f32[8,128]{1,0:T(8,128)S(1)}, f32[8,128]{1,0:T(8,128)S(1)}, u32[]{:S(2)}, u32[]{:S(2)}) %collective-permute-start.8) | collective-permute-done | bytes 4128 | tf_op jit(solution)/shard_map/ppermute | solution.py:270
  49.8 2.7 %collective-permute-start.11 = (f32[8,128]{1,0:T(8,128)S(1)}, f32[8,128]{1,0:T(8,128)S(1)}, u32[]{:S(2)}, u32[]{:S(2)}) collective-permute-start(f32[8,128]{1,0:T(8,128)S(1)} %add.31.refs_0_), channel_id=1, source_target_pairs={{0,6},{1,7},{2,4},{3,5},{4,2},{5,3},{6,0},{7,1},{8,14},{9,15},{10,... | collective-permute-start | bytes 12296 | tf_op jit(solution)/shard_map/ppermute | solution.py:270
  52.6 0.6 collective-permute-start.10
  53.1 0.2 collective-permute-start.9
  53.3 1.0 %collective-permute-done.11.refs_3_ = f32[8,128]{1,0:T(8,128)S(1)} collective-permute-done((f32[8,128]{1,0:T(8,128)S(1)}, f32[8,128]{1,0:T(8,128)S(1)}, u32[]{:S(2)}, u32[]{:S(2)}) %collective-permute-start.11) | collective-permute-done | bytes 4128 | tf_op jit(solution)/shard_map/ppermute | solution.py:270
  54.3 1.8 %collective-permute-done.10.refs_2_ = f32[8,128]{1,0:T(8,128)S(1)} collective-permute-done((f32[8,128]{1,0:T(8,128)S(1)}, f32[8,128]{1,0:T(8,128)S(1)}, u32[]{:S(2)}, u32[]{:S(2)}) %collective-permute-start.10) | collective-permute-done | bytes 4128 | tf_op jit(solution)/shard_map/ppermute | solution.py:270
  56.2 0.6 collective-permute-done.9.refs_1_
  56.7 0.2 direction.1
  56.9 1.0 %collective-permute-start.14 = (bf16[384,128]{1,0:T(8,128)(2,1)S(1)}, bf16[384,128]{1,0:T(8,128)(2,1)S(1)}, u32[]{:S(2)}, u32[]{:S(2)}) collective-permute-start(bf16[384,128]{1,0:T(8,128)(2,1)S(1)} %get-tuple-element.9.refs_0_), channel_id=1, source_target_pairs={{0,6},{1,7},{2,4},{3,5},{4,2},{5,3},{6,0},{7,1},{8,14},{9,15},{10,... | collective-permute-start | bytes 294920 | tf_op jit(solution)/shard_map/ppermute | solution.py:270
  57.9 0.8 %collective-permute-start.13 = (bf16[384,128]{1,0:T(8,128)(2,1)S(1)}, bf16[384,128]{1,0:T(8,128)(2,1)S(1)}, u32[]{:S(2)}, u32[]{:S(2)}) collective-permute-start(bf16[384,128]{1,0:T(8,128)(2,1)S(1)} %get-tuple-element.9.refs_0_), channel_id=1, source_target_pairs={{0,4},{1,5},{2,6},{3,7},{4,0},{5,1},{6,2},{7,3},{8,12},{9,13},{10,... | collective-permute-start | bytes 294920 | tf_op jit(solution)/shard_map/ppermute | solution.py:270
  58.6 1.8 %collective-permute-start.12 = (bf16[384,128]{1,0:T(8,128)(2,1)S(1)}, bf16[384,128]{1,0:T(8,128)(2,1)S(1)}, u32[]{:S(2)}, u32[]{:S(2)}) collective-permute-start(bf16[384,128]{1,0:T(8,128)(2,1)S(1)} %get-tuple-element.9.refs_0_), channel_id=1, source_target_pairs={{0,2},{1,3},{2,0},{3,1},{4,6},{5,7},{6,4},{7,5},{8,10},{9,11},{10,... | collective-permute-start | bytes 294920 | tf_op jit(solution)/shard_map/ppermute | solution.py:270
  60.5 2.1 %collective-permute-done.14.refs_3_ = bf16[384,128]{1,0:T(8,128)(2,1)S(1)} collective-permute-done((bf16[384,128]{1,0:T(8,128)(2,1)S(1)}, bf16[384,128]{1,0:T(8,128)(2,1)S(1)}, u32[]{:S(2)}, u32[]{:S(2)}) %collective-permute-start.14) | collective-permute-done | bytes 98336 | tf_op jit(solution)/shard_map/ppermute | solution.py:270
  62.6 0.9 %collective-permute-done.13.refs_2_ = bf16[384,128]{1,0:T(8,128)(2,1)S(1)} collective-permute-done((bf16[384,128]{1,0:T(8,128)(2,1)S(1)}, bf16[384,128]{1,0:T(8,128)(2,1)S(1)}, u32[]{:S(2)}, u32[]{:S(2)}) %collective-permute-start.13) | collective-permute-done | bytes 98336 | tf_op jit(solution)/shard_map/ppermute | solution.py:270
  63.5 0.0 collective-permute-done.12.refs_1_
  63.6 0.1 pad_maximum_fusion.1
  63.6 0.1 collective-permute-start.15
  63.7 0.6 unpack.1
  64.4 1.1 %collective-permute-done.15.refs_4_ = bf16[4,384,128]{2,1,0:T(8,128)(2,1)S(1)} collective-permute-done((bf16[4,384,128]{2,1,0:T(8,128)(2,1)S(1)}, bf16[4,384,128]{2,1,0:T(8,128)(2,1)S(1)}, u32[]{:S(2)}, u32[]{:S(2)}) %collective-permute-start.15) | collective-permute-done | bytes 393248 | tf_op jit(solution)/shard_map/ppermute | solution.py:270
  65.4 9.5 %backward.1 = f32[2,12,256,128]{3,2,1,0:T(8,128)} custom-call(s32[1,2]{1,0:T(1,128)S(1)} %bitcast.30, s32[32,128]{1,0:T(8,128)S(1)} %get-tuple-element.8.codes_in, bf16[10752,128]{1,0:T(8,128)(2,1)S(1)} %table.1.tab_ref, bf16[384,128]{1,0:T(8,128)(2,1)S(1)} %get-tuple-element.9.refs_0_, bf16[384,128]{1,0:T(8,128)(2,1)S(1)} %collective-permute-done.12.refs_1_, ...), custom_call_target="tpu_custom_call" | custom-call | tf_op jit(solution)/shard_map/backward/pallas_call | solution.py:373
  (6 shorter events, 0.1 us)
Async XLA Ops:
  0.6 1.2 %copy-start.3 = (s32[2,1]{0,1:T(1,128)S(1)}, s32[2,1]{0,1:T(1,128)}, u32[]{:S(2)}) copy-start(s32[2,1]{0,1:T(1,128)} %param.14) | copy-start | bytes 28
  0.6 1.2 %copy-start.8 = (s32[2,512]{1,0:T(2,128)S(1)}, s32[2,512]{1,0:T(2,128)}, u32[]{:S(2)}) copy-start(s32[2,512]{1,0:T(2,128)} %seed_ref.1) | copy-start | bytes 12292
  0.7 1.2 %copy-start.6 = (s32[2,512]{1,0:T(2,128)S(1)}, s32[2,512]{1,0:T(2,128)}, u32[]{:S(2)}) copy-start(s32[2,512]{1,0:T(2,128)} %target_ref.1) | copy-start | bytes 12292
  0.7 1.2 %copy-start.7 = (s32[2,512]{1,0:T(2,128)S(1)}, s32[2,512]{1,0:T(2,128)}, u32[]{:S(2)}) copy-start(s32[2,512]{1,0:T(2,128)} %source_ref.1) | copy-start | bytes 12292
  0.7 1.2 %copy-start.5 = (s32[2,512,1]{1,2,0:T(1,128)S(1)}, s32[2,512,1]{1,2,0:T(1,128)}, u32[]{:S(2)}) copy-start(s32[2,512,1]{1,2,0:T(1,128)} %param.10) | copy-start | bytes 12292
  0.7 1.4 %copy-start.4 = (bf16[2,12,256,128]{3,2,1,0:T(8,128)(2,1)S(1)}, bf16[2,12,256,128]{3,2,1,0:T(8,128)(2,1)}, u32[]{:S(2)}) copy-start(bf16[2,12,256,128]{3,2,1,0:T(8,128)(2,1)} %field_ref.1) | copy-start | bytes 4718596
  10.3 0.8 %copy-start = (f32[12,1,8,128]{3,2,1,0:T(8,128)S(1)}, f32[12,1,8,128]{3,2,1,0:T(8,128)}, u32[]{:S(2)}) copy-start(f32[12,1,8,128]{3,2,1,0:T(8,128)} %refs_0_.1) | copy-start | bytes 147460
  10.4 0.8 %copy-start.1 = (f32[12,1,8,128]{3,2,1,0:T(8,128)S(1)}, f32[12,1,8,128]{3,2,1,0:T(8,128)}, u32[]{:S(2)}) copy-start(f32[12,1,8,128]{3,2,1,0:T(8,128)} %refs_1_.1) | copy-start | bytes 147460
  10.4 0.8 %copy-start.2 = (f32[12,1,8,128]{3,2,1,0:T(8,128)S(1)}, f32[12,1,8,128]{3,2,1,0:T(8,128)}, u32[]{:S(2)}) copy-start(f32[12,1,8,128]{3,2,1,0:T(8,128)} %refs_2_.1) | copy-start | bytes 147460
  10.4 10.8 %collective-permute-start = (f32[4,384,128]{2,1,0:T(8,128)S(1)}, f32[4,384,128]{2,1,0:T(8,128)S(1)}, u32[]{:S(2)}, u32[]{:S(2)}) collective-permute-start(f32[4,384,128]{2,1,0:T(8,128)S(1)} %bitcast.32), channel_id=1, source_target_pairs={{0,1},{1,0},{2,3},{3,2},{4,5},{5,4},{6,7},{7,6},{8,9},{9,8},{10,11... | collective-permute-start | bytes 2359304 | tf_op jit(solution)/shard_map/ppermute | solution.py:270
  11.2 6.4 %collective-permute-start.6 = (f32[1,3,96,128]{3,2,1,0:T(8,128)S(1)}, f32[1,3,96,128]{3,2,1,0:T(8,128)S(1)}, u32[]{:S(2)}, u32[]{:S(2)}) collective-permute-start(f32[1,3,96,128]{3,2,1,0:T(8,128)S(1)} %bitcast.22), channel_id=1, source_target_pairs={{0,8},{8,0},{16,24},{24,16},{1,9},{9,1},{17,25},{25,17},{2,10},{10... | collective-permute-start | bytes 442376 | tf_op jit(solution)/shard_map/ppermute | solution.py:270
  17.6 22.3 %collective-permute-start.7 = (f32[2,3,96,128]{3,2,1,0:T(8,128)S(1)}, f32[2,3,96,128]{3,2,1,0:T(8,128)S(1)}, u32[]{:S(2)}, u32[]{:S(2)}) collective-permute-start(f32[2,3,96,128]{3,2,1,0:T(8,128)S(1)} %pad_maximum_fusion.2), channel_id=1, source_target_pairs={{0,16},{8,24},{16,0},{24,8},{1,17},{9,25},{17,1},{25,9},{2,18},{10... | collective-permute-start | bytes 884744 | tf_op jit(solution)/shard_map/ppermute | solution.py:270
  21.3 7.8 %collective-permute-start.1 = (f32[384,128]{1,0:T(8,128)S(1)}, f32[384,128]{1,0:T(8,128)S(1)}, u32[]{:S(2)}, u32[]{:S(2)}) collective-permute-start(f32[384,128]{1,0:T(8,128)S(1)} %get-tuple-element.10), channel_id=1, source_target_pairs={{0,2},{1,3},{2,0},{3,1},{4,6},{5,7},{6,4},{7,5},{8,10},{9,11},{10,... | collective-permute-start | bytes 589832 | tf_op jit(solution)/shard_map/ppermute | solution.py:270
  22.8 9.3 %collective-permute-start.3 = (f32[384,128]{1,0:T(8,128)S(1)}, f32[384,128]{1,0:T(8,128)S(1)}, u32[]{:S(2)}, u32[]{:S(2)}) collective-permute-start(f32[384,128]{1,0:T(8,128)S(1)} %get-tuple-element.11), channel_id=1, source_target_pairs={{0,6},{1,7},{2,4},{3,5},{4,2},{5,3},{6,0},{7,1},{8,14},{9,15},{10,... | collective-permute-start | bytes 589832 | tf_op jit(solution)/shard_map/ppermute | solution.py:270
  24.4 9.1 %collective-permute-start.2 = (f32[384,128]{1,0:T(8,128)S(1)}, f32[384,128]{1,0:T(8,128)S(1)}, u32[]{:S(2)}, u32[]{:S(2)}) collective-permute-start(f32[384,128]{1,0:T(8,128)S(1)} %get-tuple-element.12), channel_id=1, source_target_pairs={{0,4},{1,5},{2,6},{3,7},{4,0},{5,1},{6,2},{7,3},{8,12},{9,13},{10,... | collective-permute-start | bytes 589832 | tf_op jit(solution)/shard_map/ppermute | solution.py:270
  33.6 5.7 %collective-permute-start.4 = (f32[384,128]{1,0:T(8,128)S(1)}, f32[384,128]{1,0:T(8,128)S(1)}, u32[]{:S(2)}, u32[]{:S(2)}) collective-permute-start(f32[384,128]{1,0:T(8,128)S(1)} %add_add_fusion), channel_id=1, source_target_pairs={{0,8},{8,0},{16,24},{24,16},{1,9},{9,1},{17,25},{25,17},{2,10},{10... | collective-permute-start | bytes 589832 | tf_op jit(solution)/shard_map/ppermute | solution.py:270
  39.4 9.1 %collective-permute-start.5 = (f32[384,128]{1,0:T(8,128)S(1)}, f32[384,128]{1,0:T(8,128)S(1)}, u32[]{:S(2)}, u32[]{:S(2)}) collective-permute-start(f32[384,128]{1,0:T(8,128)S(1)} %add.30.a_ref), channel_id=1, source_target_pairs={{0,16},{8,24},{16,0},{24,8},{1,17},{9,25},{17,1},{25,9},{2,18},{10... | collective-permute-start | bytes 589832 | tf_op jit(solution)/shard_map/ppermute | solution.py:270
  48.6 1.2 %collective-permute-start.8 = (f32[8,128]{1,0:T(8,128)S(1)}, f32[8,128]{1,0:T(8,128)S(1)}, u32[]{:S(2)}, u32[]{:S(2)}) collective-permute-start(f32[8,128]{1,0:T(8,128)S(1)} %sums.1), channel_id=1, source_target_pairs={{0,1},{1,0},{2,3},{3,2},{4,5},{5,4},{6,7},{7,6},{8,9},{9,8},{10,11... | collective-permute-start | bytes 12296 | tf_op jit(solution)/shard_map/ppermute | solution.py:270
  49.8 4.5 %collective-permute-start.11 = (f32[8,128]{1,0:T(8,128)S(1)}, f32[8,128]{1,0:T(8,128)S(1)}, u32[]{:S(2)}, u32[]{:S(2)}) collective-permute-start(f32[8,128]{1,0:T(8,128)S(1)} %add.31.refs_0_), channel_id=1, source_target_pairs={{0,6},{1,7},{2,4},{3,5},{4,2},{5,3},{6,0},{7,1},{8,14},{9,15},{10,... | collective-permute-start | bytes 12296 | tf_op jit(solution)/shard_map/ppermute | solution.py:270
  52.6 3.6 %collective-permute-start.10 = (f32[8,128]{1,0:T(8,128)S(1)}, f32[8,128]{1,0:T(8,128)S(1)}, u32[]{:S(2)}, u32[]{:S(2)}) collective-permute-start(f32[8,128]{1,0:T(8,128)S(1)} %add.31.refs_0_), channel_id=1, source_target_pairs={{0,4},{1,5},{2,6},{3,7},{4,0},{5,1},{6,2},{7,3},{8,12},{9,13},{10,... | collective-permute-start | bytes 12296 | tf_op jit(solution)/shard_map/ppermute | solution.py:270
  53.1 3.6 %collective-permute-start.9 = (f32[8,128]{1,0:T(8,128)S(1)}, f32[8,128]{1,0:T(8,128)S(1)}, u32[]{:S(2)}, u32[]{:S(2)}) collective-permute-start(f32[8,128]{1,0:T(8,128)S(1)} %add.31.refs_0_), channel_id=1, source_target_pairs={{0,2},{1,3},{2,0},{3,1},{4,6},{5,7},{6,4},{7,5},{8,10},{9,11},{10,... | collective-permute-start | bytes 12296 | tf_op jit(solution)/shard_map/ppermute | solution.py:270
  56.9 5.7 %collective-permute-start.14 = (bf16[384,128]{1,0:T(8,128)(2,1)S(1)}, bf16[384,128]{1,0:T(8,128)(2,1)S(1)}, u32[]{:S(2)}, u32[]{:S(2)}) collective-permute-start(bf16[384,128]{1,0:T(8,128)(2,1)S(1)} %get-tuple-element.9.refs_0_), channel_id=1, source_target_pairs={{0,6},{1,7},{2,4},{3,5},{4,2},{5,3},{6,0},{7,1},{8,14},{9,15},{10,... | collective-permute-start | bytes 294920 | tf_op jit(solution)/shard_map/ppermute | solution.py:270
  57.9 5.7 %collective-permute-start.13 = (bf16[384,128]{1,0:T(8,128)(2,1)S(1)}, bf16[384,128]{1,0:T(8,128)(2,1)S(1)}, u32[]{:S(2)}, u32[]{:S(2)}) collective-permute-start(bf16[384,128]{1,0:T(8,128)(2,1)S(1)} %get-tuple-element.9.refs_0_), channel_id=1, source_target_pairs={{0,4},{1,5},{2,6},{3,7},{4,0},{5,1},{6,2},{7,3},{8,12},{9,13},{10,... | collective-permute-start | bytes 294920 | tf_op jit(solution)/shard_map/ppermute | solution.py:270
  58.6 5.0 %collective-permute-start.12 = (bf16[384,128]{1,0:T(8,128)(2,1)S(1)}, bf16[384,128]{1,0:T(8,128)(2,1)S(1)}, u32[]{:S(2)}, u32[]{:S(2)}) collective-permute-start(bf16[384,128]{1,0:T(8,128)(2,1)S(1)} %get-tuple-element.9.refs_0_), channel_id=1, source_target_pairs={{0,2},{1,3},{2,0},{3,1},{4,6},{5,7},{6,4},{7,5},{8,10},{9,11},{10,... | collective-permute-start | bytes 294920 | tf_op jit(solution)/shard_map/ppermute | solution.py:270
  63.6 1.8 %collective-permute-start.15 = (bf16[4,384,128]{2,1,0:T(8,128)(2,1)S(1)}, bf16[4,384,128]{2,1,0:T(8,128)(2,1)S(1)}, u32[]{:S(2)}, u32[]{:S(2)}) collective-permute-start(bf16[4,384,128]{2,1,0:T(8,128)(2,1)S(1)} %pad_maximum_fusion.1), channel_id=1, source_target_pairs={{0,1},{1,0},{2,3},{3,2},{4,5},{5,4},{6,7},{7,6},{8,9},{9,8},{10,11... | collective-permute-start | bytes 1179656 | tf_op jit(solution)/shard_map/ppermute | solution.py:270

commit v7 on v6

--- a/solution.py
+++ b/solution.py
@@ -178,18 +178,31 @@
     out_ref[...] = a_ref[...] + b_ref[...]
 
 
-def terms(a_ref, b_ref, hist_ref, k, rows):
-    group = lax.axis_index("ev") ^ k
-    at = pl.ds(pl.multiple_of(group * rows, 8), rows)
-    gradient = a_ref[at, :] + b_ref[at, :]
+def merge_kernel(*refs):
+    ins, (stay_ref, go_ref) = refs[:-2], refs[-2:]
+    rows = stay_ref.shape[0]
+    odd = lax.axis_index("ev") & 1
+    for out_ref, part in ((stay_ref, odd), (go_ref, 1 - odd)):
+        at = pl.ds(pl.multiple_of(part * rows, 8), rows)
+        total = ins[0][at, :]
+        for ref in ins[1:]:
+            total = total + ref[at, :]
+        out_ref[...] = total
+
+
+def terms(gradient, hist_ref, k):
     prev_gradient, prev_step, precond = hist_ref[k, 0], hist_ref[k, 1], hist_ref[k, 2]
-    return at, gradient, gradient - prev_gradient, prev_step, precond
-
-
-def sums_kernel(rows, evs, a_ref, b_ref, hist_ref, out_ref):
+    return gradient - prev_gradient, prev_step, precond
+
+
+def sums_kernel(rows, evs, a_ref, b_ref, hist_ref, grad_ref, out_ref):
+    ev = lax.axis_index("ev")
+    grad_ref[...] = a_ref[...] + b_ref[...]
     total = [jnp.zeros((8, LANES), jnp.float32) for _ in range(4)]
-    for k in range(evs):
-        _, gradient, change, prev_step, precond = terms(a_ref, b_ref, hist_ref, k, rows)
+    for i in range(evs // 2):
+        k = ((ev & 1) * (evs // 2) + i) ^ ev
+        gradient = grad_ref[pl.ds(i * rows, rows), :]
+        change, prev_step, precond = terms(gradient, hist_ref, k)
         weighted = precond * change
         parts = (prev_step * change, prev_step * gradient, weighted * gradient, weighted * change)
         for n, part in enumerate(parts):
@@ -199,8 +212,9 @@
     out_ref[pl.ds(4, 4), :] = jnp.zeros((4, LANES), jnp.float32)
 
 
-def direction_kernel(rows, evs, a_ref, b_ref, hist_ref, *refs):
-    sum_refs, (inv_ref, round_ref) = refs[:-2], refs[-2:]
+def direction_kernel(rows, evs, mine_ref, other_ref, hist_ref, *refs):
+    sum_refs, (inv_ref, round_ref, grad_ref) = refs[:-3], refs[-3:]
+    ev = lax.axis_index("ev")
     level = [ref[...] for ref in sum_refs]
     while len(level) > 1:
         level = [level[i] + level[i + 1] for i in range(0, len(level), 2)]
@@ -209,8 +223,13 @@
     alpha = slope / curvature
     beta = (cross_term - alpha * self_term) / curvature
     bend = alpha - beta
+    half_rows = mine_ref.shape[0]
+    for ref, part in ((mine_ref, ev & 1), (other_ref, 1 - (ev & 1))):
+        grad_ref[pl.ds(pl.multiple_of(part * half_rows, 8), half_rows), :] = ref[...]
     for k in range(evs):
-        at, gradient, change, prev_step, precond = terms(a_ref, b_ref, hist_ref, k, rows)
+        at = pl.ds(pl.multiple_of((ev ^ k) * rows, ROW), rows)
+        gradient = grad_ref[at, :]
+        change, prev_step, precond = terms(gradient, hist_ref, k)
         scaled = precond * (gradient - alpha * change)
         direction = -(scaled + bend * prev_step)
         round_ref[at, :] = direction.astype(jnp.bfloat16)
@@ -330,21 +349,30 @@
         compiler_params=limit(2),
         name="fold",
     )(keep[0], got[0])
-    for piece in arrived:
-        total = total + piece
-    bits = evs.bit_length() - 1
-    for bit in range(bits - 1):
-        total = total + swap(total, "ev", 1 << bit)
-    across = swap(total, "ev", 1 << (bits - 1))
-
-    local = pl.pallas_call(
+    half_rows = part_rows // 2
+    stay, go = pl.pallas_call(
+        merge_kernel,
+        out_shape=[f32(half_rows, nodes)] * 2,
+        in_specs=[in_vmem()] * half,
+        out_specs=[in_vmem()] * 2,
+        compiler_params=limit(4),
+        name="merge",
+    )(total, *arrived)
+    total, across = stay, swap(go, "ev", 1)
+    for bit in range(1, evs.bit_length() - 1):
+        total = total + across
+        across = swap(total, "ev", 1 << bit)
+
+    gradient, local = pl.pallas_call(
         functools.partial(sums_kernel, rows, evs),
-        out_shape=f32(8, nodes),
+        out_shape=[f32(half_rows, nodes), f32(8, nodes)],
         in_specs=[in_vmem()] * 3,
-        out_specs=in_vmem(),
+        out_specs=[in_vmem()] * 2,
         compiler_params=limit(4),
         name="sums",
     )(total, across, hist)
+    local = local + swap(local, "ev", 1)
+    gradient_other = swap(gradient, "ev", 1)
     local = local + swap(local, "mesh", 1)
     spread = [local] + [swap(local, "mesh", 2 * j) for j in range(1, half)]
     inverse, rounded = pl.pallas_call(
@@ -352,9 +380,10 @@
         out_shape=[f32(rows, nodes), bf16(part_rows, nodes)],
         in_specs=[in_vmem()] * (3 + half),
         out_specs=[in_vmem()] * 2,
+        scratch_shapes=[pltpu.VMEM((part_rows, nodes), jnp.float32)],
         compiler_params=limit(4),
         name="direction",
-    )(total, across, hist, *spread)
+    )(gradient, gradient_other, hist, *spread)
     inversion_direction = pl.pallas_call(
         functools.partial(unpack_kernel, comps, group),
         out_shape=f32(*precond.shape),

time: 75.1 us -> 75 us (level)
  starting transfers between devices: 18 us -> 19 us
  waiting for transfers between devices: 34.9 us -> 34 us
    ppermute x16 -> x18, starting transfers between devices: 18 us -> 19 us  [swap(): return lax.ppermute(x, axis, [(i, i ^ k) for i in range(size)])]
    ppermute x16 -> x18, waiting for transfers between devices: 34.9 us -> 34 us  [swap(): return lax.ppermute(x, axis, [(i, i ^ k) for i in range(size)])]
  transfers between devices with their start and end apart: 16 -> 18, of which waited for: 13 -> 14; matrix products, arithmetic and copies ran while one was open for 0% -> 0% of each run, Pallas kernels for 1% -> 1%
where the time goes in v7:
time: 75 us; the launch traced here: 74.8 us
  waiting for transfers between devices  34 us (45%)
  Pallas kernels  19.8 us (26%)
  starting transfers between devices  19 us (25%)
  local copies, waits for them, and re-layouts  0.98 us (1%)
  between operations  0.85 us (1%)
    ppermute x18, waiting for transfers between devices, swap(): return lax.ppermute(x, axis, [(i, i ^ k) for i in range(size)])  34 us
    ppermute x18, starting transfers between devices, swap(): return lax.ppermute(x, axis, [(i, i ^ k) for i in range(size)])  19 us
    pallas_call x1, Pallas kernels, body(): pl.pallas_call(functools.partial(backward_kernel, dims), out_shape=f32(*k...  9.46 us
    pallas_call x1, Pallas kernels, body(): pl.pallas_call(functools.partial(forward_kernel, dims), out_shape=[f32(bl...  8.21 us
  transfers between devices with their start and end apart: 18, of which 14 were waited for; matrix products, arithmetic and copies ran while one was open for 0% of the time, Pallas kernels for 1%

profile of v7, /device:TPU:0, one launch (start us, length us, event | category | flops | bytes accessed | tf_op | source)
XLA Modules:
  0.0 74.8 jit_solution(11296844561271430396)
XLA Ops:
  0.6 0.0 copy-start.3
  0.6 0.0 copy-start.8
  0.7 0.0 copy-start.6
  0.7 0.0 copy-start.7
  0.7 0.0 copy-start.5
  0.7 0.0 copy-start.4
  0.7 1.2 %table.1.tab_ref = bf16[10752,128]{1,0:T(8,128)(2,1)S(1)} custom-call(), custom_call_target="tpu_custom_call" | custom-call | flops 268435456 | bytes 4194304 | tf_op jit(solution)/shard_map/table/pallas_call | solution.py:310
  1.9 0.0 copy-done.3
  1.9 0.0 copy-done.8
  1.9 0.0 copy-done.6
  1.9 0.0 copy-done.7
  1.9 0.0 copy-done.5
  1.9 0.2 copy-done.4
  2.1 8.2 %forward.1 = (f32[3088,128]{1,0:T(8,128)S(1)}, s32[32,128]{1,0:T(8,128)S(1)}) custom-call(s32[1,2]{1,0:T(1,128)S(1)} %bitcast.29, s32[2,1,512]{2,1,0:T(1,128)S(1)} %bitcast.31, s32[2,512]{1,0:T(2,128)S(1)} %copy-done.6, s32[2,512]{1,0:T(2,128)S(1)} %copy-done.7, s32[2,512]{1,0:T(2,128)S(1)} %copy-done.8, bf16[2,12,256,128]{3,2,1,0:T(8,128)(2,1)S(1)} %copy-done.4, ...), custom_call_target="tpu_custom_call" | custom-call | flops 34359738368 | bytes 16777216 | tf_op jit(solution)/shard_map/forward/pallas_call | solution.py:318
  10.3 0.0 copy-start
  10.4 0.0 copy-start.1
  10.4 0.0 copy-start.2
  10.4 0.1 slice.37
  10.4 0.1 collective-permute-start
  10.5 0.6 copy-done
  11.1 0.0 copy-done.1
  11.2 0.0 copy-done.2
  11.2 1.7 %collective-permute-start.6 = (f32[1,3,96,128]{3,2,1,0:T(8,128)S(1)}, f32[1,3,96,128]{3,2,1,0:T(8,128)S(1)}, u32[]{:S(2)}, u32[]{:S(2)}) collective-permute-start(f32[1,3,96,128]{3,2,1,0:T(8,128)S(1)} %bitcast.22), channel_id=1, source_target_pairs={{0,8},{8,0},{16,24},{24,16},{1,9},{9,1},{17,25},{25,17},{2,10},{10... | collective-permute-start | bytes 442376 | tf_op jit(solution)/shard_map/ppermute | solution.py:289
  12.9 4.7 %collective-permute-done.6 = f32[1,3,96,128]{3,2,1,0:T(8,128)S(1)} collective-permute-done((f32[1,3,96,128]{3,2,1,0:T(8,128)S(1)}, f32[1,3,96,128]{3,2,1,0:T(8,128)S(1)}, u32[]{:S(2)}, u32[]{:S(2)}) %collective-permute-start.6) | collective-permute-done | bytes 147488 | tf_op jit(solution)/shard_map/ppermute | solution.py:289
  17.6 3.6 %collective-permute-start.7 = (f32[2,3,96,128]{3,2,1,0:T(8,128)S(1)}, f32[2,3,96,128]{3,2,1,0:T(8,128)S(1)}, u32[]{:S(2)}, u32[]{:S(2)}) collective-permute-start(f32[2,3,96,128]{3,2,1,0:T(8,128)S(1)} %pad_maximum_fusion.2), channel_id=1, source_target_pairs={{0,16},{8,24},{16,0},{24,8},{1,17},{9,25},{17,1},{25,9},{2,18},{10... | collective-permute-start | bytes 884744 | tf_op jit(solution)/shard_map/ppermute | solution.py:289
  21.2 0.0 collective-permute-done
  21.2 0.1 fusion
  21.3 1.6 %collective-permute-start.3 = (f32[384,128]{1,0:T(8,128)S(1)}, f32[384,128]{1,0:T(8,128)S(1)}, u32[]{:S(2)}, u32[]{:S(2)}) collective-permute-start(f32[384,128]{1,0:T(8,128)S(1)} %get-tuple-element.18), channel_id=1, source_target_pairs={{0,6},{1,7},{2,4},{3,5},{4,2},{5,3},{6,0},{7,1},{8,14},{9,15},{10,... | collective-permute-start | bytes 589832 | tf_op jit(solution)/shard_map/ppermute | solution.py:289
  23.0 1.3 %collective-permute-start.2 = (f32[384,128]{1,0:T(8,128)S(1)}, f32[384,128]{1,0:T(8,128)S(1)}, u32[]{:S(2)}, u32[]{:S(2)}) collective-permute-start(f32[384,128]{1,0:T(8,128)S(1)} %get-tuple-element.19), channel_id=1, source_target_pairs={{0,4},{1,5},{2,6},{3,7},{4,0},{5,1},{6,2},{7,3},{8,12},{9,13},{10,... | collective-permute-start | bytes 589832 | tf_op jit(solution)/shard_map/ppermute | solution.py:289
  24.2 0.6 collective-permute-start.1
  24.9 5.2 %collective-permute-done.3.refs_3_ = f32[384,128]{1,0:T(8,128)S(1)} collective-permute-done((f32[384,128]{1,0:T(8,128)S(1)}, f32[384,128]{1,0:T(8,128)S(1)}, u32[]{:S(2)}, u32[]{:S(2)}) %collective-permute-start.3) | collective-permute-done | bytes 196640 | tf_op jit(solution)/shard_map/ppermute | solution.py:289
  30.1 2.7 %collective-permute-done.2.refs_2_ = f32[384,128]{1,0:T(8,128)S(1)} collective-permute-done((f32[384,128]{1,0:T(8,128)S(1)}, f32[384,128]{1,0:T(8,128)S(1)}, u32[]{:S(2)}, u32[]{:S(2)}) %collective-permute-start.2) | collective-permute-done | bytes 196640 | tf_op jit(solution)/shard_map/ppermute | solution.py:289
  32.8 0.0 collective-permute-done.1.refs_1_
  32.9 0.5 collective-permute-start.4
  33.4 4.2 %collective-permute-done.4 = f32[192,128]{1,0:T(8,128)S(1)} collective-permute-done((f32[192,128]{1,0:T(8,128)S(1)}, f32[192,128]{1,0:T(8,128)S(1)}, u32[]{:S(2)}, u32[]{:S(2)}) %collective-permute-start.4) | collective-permute-done | bytes 98336 | tf_op jit(solution)/shard_map/ppermute | solution.py:289
  37.7 0.4 collective-permute-start.5
  38.1 0.0 collective-permute-done.7
  38.1 6.0 %collective-permute-done.5.b_ref = f32[192,128]{1,0:T(8,128)S(1)} collective-permute-done((f32[192,128]{1,0:T(8,128)S(1)}, f32[192,128]{1,0:T(8,128)S(1)}, u32[]{:S(2)}, u32[]{:S(2)}) %collective-permute-start.5) | collective-permute-done | bytes 98336 | tf_op jit(solution)/shard_map/ppermute | solution.py:289
  44.1 0.1 sums.1
  44.2 0.1 collective-permute-start.8
  44.3 2.0 %collective-permute-start.9 = (f32[8,128]{1,0:T(8,128)S(1)}, f32[8,128]{1,0:T(8,128)S(1)}, u32[]{:S(2)}, u32[]{:S(2)}) collective-permute-start(f32[8,128]{1,0:T(8,128)S(1)} %get-tuple-element.14), channel_id=1, source_target_pairs={{0,8},{8,0},{16,24},{24,16},{1,9},{9,1},{17,25},{25,17},{2,10},{10... | collective-permute-start | bytes 12296 | tf_op jit(solution)/shard_map/ppermute | solution.py:289
  46.3 2.6 %collective-permute-done.9 = f32[8,128]{1,0:T(8,128)S(1)} collective-permute-done((f32[8,128]{1,0:T(8,128)S(1)}, f32[8,128]{1,0:T(8,128)S(1)}, u32[]{:S(2)}, u32[]{:S(2)}) %collective-permute-start.9) | collective-permute-done | bytes 4128 | tf_op jit(solution)/shard_map/ppermute | solution.py:289
  48.9 0.0 collective-permute-start.10
  48.9 1.2 %collective-permute-done.10 = f32[8,128]{1,0:T(8,128)S(1)} collective-permute-done((f32[8,128]{1,0:T(8,128)S(1)}, f32[8,128]{1,0:T(8,128)S(1)}, u32[]{:S(2)}, u32[]{:S(2)}) %collective-permute-start.10) | collective-permute-done | bytes 4128 | tf_op jit(solution)/shard_map/ppermute | solution.py:289
  50.1 1.2 %collective-permute-start.13 = (f32[8,128]{1,0:T(8,128)S(1)}, f32[8,128]{1,0:T(8,128)S(1)}, u32[]{:S(2)}, u32[]{:S(2)}) collective-permute-start(f32[8,128]{1,0:T(8,128)S(1)} %add.23.refs_0_), channel_id=1, source_target_pairs={{0,6},{1,7},{2,4},{3,5},{4,2},{5,3},{6,0},{7,1},{8,14},{9,15},{10,... | collective-permute-start | bytes 12296 | tf_op jit(solution)/shard_map/ppermute | solution.py:289
  51.3 0.5 collective-permute-start.12
  51.8 1.7 %collective-permute-start.11 = (f32[8,128]{1,0:T(8,128)S(1)}, f32[8,128]{1,0:T(8,128)S(1)}, u32[]{:S(2)}, u32[]{:S(2)}) collective-permute-start(f32[8,128]{1,0:T(8,128)S(1)} %add.23.refs_0_), channel_id=1, source_target_pairs={{0,2},{1,3},{2,0},{3,1},{4,6},{5,7},{6,4},{7,5},{8,10},{9,11},{10,... | collective-permute-start | bytes 12296 | tf_op jit(solution)/shard_map/ppermute | solution.py:289
  53.6 1.0 %collective-permute-done.13.refs_3_ = f32[8,128]{1,0:T(8,128)S(1)} collective-permute-done((f32[8,128]{1,0:T(8,128)S(1)}, f32[8,128]{1,0:T(8,128)S(1)}, u32[]{:S(2)}, u32[]{:S(2)}) %collective-permute-start.13) | collective-permute-done | bytes 4128 | tf_op jit(solution)/shard_map/ppermute | solution.py:289
  54.6 0.3 collective-permute-done.12.refs_2_
  54.9 0.5 collective-permute-done.11.refs_1_
  55.4 0.0 collective-permute-done.8.other_ref
  55.4 0.2 direction.1
  55.6 2.0 %collective-permute-start.16 = (bf16[384,128]{1,0:T(8,128)(2,1)S(1)}, bf16[384,128]{1,0:T(8,128)(2,1)S(1)}, u32[]{:S(2)}, u32[]{:S(2)}) collective-permute-start(bf16[384,128]{1,0:T(8,128)(2,1)S(1)} %get-tuple-element.17.refs_0_), channel_id=1, source_target_pairs={{0,6},{1,7},{2,4},{3,5},{4,2},{5,3},{6,0},{7,1},{8,14},{9,15},{10,... | collective-permute-start | bytes 294920 | tf_op jit(solution)/shard_map/ppermute | solution.py:289
  57.7 1.2 %collective-permute-start.15 = (bf16[384,128]{1,0:T(8,128)(2,1)S(1)}, bf16[384,128]{1,0:T(8,128)(2,1)S(1)}, u32[]{:S(2)}, u32[]{:S(2)}) collective-permute-start(bf16[384,128]{1,0:T(8,128)(2,1)S(1)} %get-tuple-element.17.refs_0_), channel_id=1, source_target_pairs={{0,4},{1,5},{2,6},{3,7},{4,0},{5,1},{6,2},{7,3},{8,12},{9,13},{10,... | collective-permute-start | bytes 294920 | tf_op jit(solution)/shard_map/ppermute | solution.py:289
  58.9 0.3 collective-permute-start.14
  59.2 2.7 %collective-permute-done.16.refs_3_ = bf16[384,128]{1,0:T(8,128)(2,1)S(1)} collective-permute-done((bf16[384,128]{1,0:T(8,128)(2,1)S(1)}, bf16[384,128]{1,0:T(8,128)(2,1)S(1)}, u32[]{:S(2)}, u32[]{:S(2)}) %collective-permute-start.16) | collective-permute-done | bytes 98336 | tf_op jit(solution)/shard_map/ppermute | solution.py:289
  61.9 0.9 %collective-permute-done.15.refs_2_ = bf16[384,128]{1,0:T(8,128)(2,1)S(1)} collective-permute-done((bf16[384,128]{1,0:T(8,128)(2,1)S(1)}, bf16[384,128]{1,0:T(8,128)(2,1)S(1)}, u32[]{:S(2)}, u32[]{:S(2)}) %collective-permute-start.15) | collective-permute-done | bytes 98336 | tf_op jit(solution)/shard_map/ppermute | solution.py:289
  62.8 0.7 collective-permute-done.14.refs_1_
  63.5 0.1 pad_maximum_fusion.1
  63.6 0.1 collective-permute-start.17
  63.7 0.6 unpack.1
  64.3 1.1 %collective-permute-done.17.refs_4_ = bf16[4,384,128]{2,1,0:T(8,128)(2,1)S(1)} collective-permute-done((bf16[4,384,128]{2,1,0:T(8,128)(2,1)S(1)}, bf16[4,384,128]{2,1,0:T(8,128)(2,1)S(1)}, u32[]{:S(2)}, u32[]{:S(2)}) %collective-permute-start.17) | collective-permute-done | bytes 393248 | tf_op jit(solution)/shard_map/ppermute | solution.py:289
  65.4 9.5 %backward.1 = f32[2,12,256,128]{3,2,1,0:T(8,128)} custom-call(s32[1,2]{1,0:T(1,128)S(1)} %bitcast.30, s32[32,128]{1,0:T(8,128)S(1)} %get-tuple-element.16.codes_in, bf16[10752,128]{1,0:T(8,128)(2,1)S(1)} %table.1.tab_ref, bf16[384,128]{1,0:T(8,128)(2,1)S(1)} %get-tuple-element.17.refs_0_, bf16[384,128]{1,0:T(8,128)(2,1)S(1)} %collective-permute-done.14.refs_1_, ...), custom_call_target="tpu_custom_call" | custom-call | tf_op jit(solution)/shard_map/backward/pallas_call | solution.py:402
  (9 shorter events, 0.2 us)
Async XLA Ops:
  0.6 1.2 %copy-start.3 = (s32[2,1]{0,1:T(1,128)S(1)}, s32[2,1]{0,1:T(1,128)}, u32[]{:S(2)}) copy-start(s32[2,1]{0,1:T(1,128)} %param.14) | copy-start | bytes 28
  0.6 1.2 %copy-start.8 = (s32[2,512]{1,0:T(2,128)S(1)}, s32[2,512]{1,0:T(2,128)}, u32[]{:S(2)}) copy-start(s32[2,512]{1,0:T(2,128)} %seed_ref.1) | copy-start | bytes 12292
  0.7 1.2 %copy-start.6 = (s32[2,512]{1,0:T(2,128)S(1)}, s32[2,512]{1,0:T(2,128)}, u32[]{:S(2)}) copy-start(s32[2,512]{1,0:T(2,128)} %target_ref.1) | copy-start | bytes 12292
  0.7 1.2 %copy-start.7 = (s32[2,512]{1,0:T(2,128)S(1)}, s32[2,512]{1,0:T(2,128)}, u32[]{:S(2)}) copy-start(s32[2,512]{1,0:T(2,128)} %source_ref.1) | copy-start | bytes 12292
  0.7 1.2 %copy-start.5 = (s32[2,512,1]{1,2,0:T(1,128)S(1)}, s32[2,512,1]{1,2,0:T(1,128)}, u32[]{:S(2)}) copy-start(s32[2,512,1]{1,2,0:T(1,128)} %param.10) | copy-start | bytes 12292
  0.7 1.4 %copy-start.4 = (bf16[2,12,256,128]{3,2,1,0:T(8,128)(2,1)S(1)}, bf16[2,12,256,128]{3,2,1,0:T(8,128)(2,1)}, u32[]{:S(2)}) copy-start(bf16[2,12,256,128]{3,2,1,0:T(8,128)(2,1)} %field_ref.1) | copy-start | bytes 4718596
  10.3 0.8 %copy-start = (f32[12,1,8,128]{3,2,1,0:T(8,128)S(1)}, f32[12,1,8,128]{3,2,1,0:T(8,128)}, u32[]{:S(2)}) copy-start(f32[12,1,8,128]{3,2,1,0:T(8,128)} %refs_0_.1) | copy-start | bytes 147460
  10.4 0.8 %copy-start.1 = (f32[12,1,8,128]{3,2,1,0:T(8,128)S(1)}, f32[12,1,8,128]{3,2,1,0:T(8,128)}, u32[]{:S(2)}) copy-start(f32[12,1,8,128]{3,2,1,0:T(8,128)} %refs_1_.1) | copy-start | bytes 147460
  10.4 0.8 %copy-start.2 = (f32[12,1,8,128]{3,2,1,0:T(8,128)S(1)}, f32[12,1,8,128]{3,2,1,0:T(8,128)}, u32[]{:S(2)}) copy-start(f32[12,1,8,128]{3,2,1,0:T(8,128)} %refs_2_.1) | copy-start | bytes 147460
  10.4 10.8 %collective-permute-start = (f32[4,384,128]{2,1,0:T(8,128)S(1)}, f32[4,384,128]{2,1,0:T(8,128)S(1)}, u32[]{:S(2)}, u32[]{:S(2)}) collective-permute-start(f32[4,384,128]{2,1,0:T(8,128)S(1)} %bitcast.32), channel_id=1, source_target_pairs={{0,1},{1,0},{2,3},{3,2},{4,5},{5,4},{6,7},{7,6},{8,9},{9,8},{10,11... | collective-permute-start | bytes 2359304 | tf_op jit(solution)/shard_map/ppermute | solution.py:289
  11.2 6.4 %collective-permute-start.6 = (f32[1,3,96,128]{3,2,1,0:T(8,128)S(1)}, f32[1,3,96,128]{3,2,1,0:T(8,128)S(1)}, u32[]{:S(2)}, u32[]{:S(2)}) collective-permute-start(f32[1,3,96,128]{3,2,1,0:T(8,128)S(1)} %bitcast.22), channel_id=1, source_target_pairs={{0,8},{8,0},{16,24},{24,16},{1,9},{9,1},{17,25},{25,17},{2,10},{10... | collective-permute-start | bytes 442376 | tf_op jit(solution)/shard_map/ppermute | solution.py:289
  17.6 20.4 %collective-permute-start.7 = (f32[2,3,96,128]{3,2,1,0:T(8,128)S(1)}, f32[2,3,96,128]{3,2,1,0:T(8,128)S(1)}, u32[]{:S(2)}, u32[]{:S(2)}) collective-permute-start(f32[2,3,96,128]{3,2,1,0:T(8,128)S(1)} %pad_maximum_fusion.2), channel_id=1, source_target_pairs={{0,16},{8,24},{16,0},{24,8},{1,17},{9,25},{17,1},{25,9},{2,18},{10... | collective-permute-start | bytes 884744 | tf_op jit(solution)/shard_map/ppermute | solution.py:289
  21.3 8.8 %collective-permute-start.3 = (f32[384,128]{1,0:T(8,128)S(1)}, f32[384,128]{1,0:T(8,128)S(1)}, u32[]{:S(2)}, u32[]{:S(2)}) collective-permute-start(f32[384,128]{1,0:T(8,128)S(1)} %get-tuple-element.18), channel_id=1, source_target_pairs={{0,6},{1,7},{2,4},{3,5},{4,2},{5,3},{6,0},{7,1},{8,14},{9,15},{10,... | collective-permute-start | bytes 589832 | tf_op jit(solution)/shard_map/ppermute | solution.py:289
  23.0 9.9 %collective-permute-start.2 = (f32[384,128]{1,0:T(8,128)S(1)}, f32[384,128]{1,0:T(8,128)S(1)}, u32[]{:S(2)}, u32[]{:S(2)}) collective-permute-start(f32[384,128]{1,0:T(8,128)S(1)} %get-tuple-element.19), channel_id=1, source_target_pairs={{0,4},{1,5},{2,6},{3,7},{4,0},{5,1},{6,2},{7,3},{8,12},{9,13},{10,... | collective-permute-start | bytes 589832 | tf_op jit(solution)/shard_map/ppermute | solution.py:289
  24.2 8.6 %collective-permute-start.1 = (f32[384,128]{1,0:T(8,128)S(1)}, f32[384,128]{1,0:T(8,128)S(1)}, u32[]{:S(2)}, u32[]{:S(2)}) collective-permute-start(f32[384,128]{1,0:T(8,128)S(1)} %get-tuple-element.20), channel_id=1, source_target_pairs={{0,2},{1,3},{2,0},{3,1},{4,6},{5,7},{6,4},{7,5},{8,10},{9,11},{10,... | collective-permute-start | bytes 589832 | tf_op jit(solution)/shard_map/ppermute | solution.py:289
  32.9 4.8 %collective-permute-start.4 = (f32[192,128]{1,0:T(8,128)S(1)}, f32[192,128]{1,0:T(8,128)S(1)}, u32[]{:S(2)}, u32[]{:S(2)}) collective-permute-start(f32[192,128]{1,0:T(8,128)S(1)} %get-tuple-element.12), channel_id=1, source_target_pairs={{0,8},{8,0},{16,24},{24,16},{1,9},{9,1},{17,25},{25,17},{2,10},{10... | collective-permute-start | bytes 294920 | tf_op jit(solution)/shard_map/ppermute | solution.py:289
  37.7 6.4 %collective-permute-start.5 = (f32[192,128]{1,0:T(8,128)S(1)}, f32[192,128]{1,0:T(8,128)S(1)}, u32[]{:S(2)}, u32[]{:S(2)}) collective-permute-start(f32[192,128]{1,0:T(8,128)S(1)} %add.21.a_ref), channel_id=1, source_target_pairs={{0,16},{8,24},{16,0},{24,8},{1,17},{9,25},{17,1},{25,9},{2,18},{10... | collective-permute-start | bytes 294920 | tf_op jit(solution)/shard_map/ppermute | solution.py:289
  44.2 11.3 %collective-permute-start.8 = (f32[192,128]{1,0:T(8,128)S(1)}, f32[192,128]{1,0:T(8,128)S(1)}, u32[]{:S(2)}, u32[]{:S(2)}) collective-permute-start(f32[192,128]{1,0:T(8,128)S(1)} %get-tuple-element.13.mine_ref), channel_id=1, source_target_pairs={{0,8},{8,0},{16,24},{24,16},{1,9},{9,1},{17,25},{25,17},{2,10},{10... | collective-permute-start | bytes 294920 | tf_op jit(solution)/shard_map/ppermute | solution.py:289
  44.3 4.6 %collective-permute-start.9 = (f32[8,128]{1,0:T(8,128)S(1)}, f32[8,128]{1,0:T(8,128)S(1)}, u32[]{:S(2)}, u32[]{:S(2)}) collective-permute-start(f32[8,128]{1,0:T(8,128)S(1)} %get-tuple-element.14), channel_id=1, source_target_pairs={{0,8},{8,0},{16,24},{24,16},{1,9},{9,1},{17,25},{25,17},{2,10},{10... | collective-permute-start | bytes 12296 | tf_op jit(solution)/shard_map/ppermute | solution.py:289
  48.9 1.2 %collective-permute-start.10 = (f32[8,128]{1,0:T(8,128)S(1)}, f32[8,128]{1,0:T(8,128)S(1)}, u32[]{:S(2)}, u32[]{:S(2)}) collective-permute-start(f32[8,128]{1,0:T(8,128)S(1)} %add.22), channel_id=1, source_target_pairs={{0,1},{1,0},{2,3},{3,2},{4,5},{5,4},{6,7},{7,6},{8,9},{9,8},{10,11... | collective-permute-start | bytes 12296 | tf_op jit(solution)/shard_map/ppermute | solution.py:289
  50.1 4.5 %collective-permute-start.13 = (f32[8,128]{1,0:T(8,128)S(1)}, f32[8,128]{1,0:T(8,128)S(1)}, u32[]{:S(2)}, u32[]{:S(2)}) collective-permute-start(f32[8,128]{1,0:T(8,128)S(1)} %add.23.refs_0_), channel_id=1, source_target_pairs={{0,6},{1,7},{2,4},{3,5},{4,2},{5,3},{6,0},{7,1},{8,14},{9,15},{10,... | collective-permute-start | bytes 12296 | tf_op jit(solution)/shard_map/ppermute | solution.py:289
  51.3 3.6 %collective-permute-start.12 = (f32[8,128]{1,0:T(8,128)S(1)}, f32[8,128]{1,0:T(8,128)S(1)}, u32[]{:S(2)}, u32[]{:S(2)}) collective-permute-start(f32[8,128]{1,0:T(8,128)S(1)} %add.23.refs_0_), channel_id=1, source_target_pairs={{0,4},{1,5},{2,6},{3,7},{4,0},{5,1},{6,2},{7,3},{8,12},{9,13},{10,... | collective-permute-start | bytes 12296 | tf_op jit(solution)/shard_map/ppermute | solution.py:289
  51.8 3.6 %collective-permute-start.11 = (f32[8,128]{1,0:T(8,128)S(1)}, f32[8,128]{1,0:T(8,128)S(1)}, u32[]{:S(2)}, u32[]{:S(2)}) collective-permute-start(f32[8,128]{1,0:T(8,128)S(1)} %add.23.refs_0_), channel_id=1, source_target_pairs={{0,2},{1,3},{2,0},{3,1},{4,6},{5,7},{6,4},{7,5},{8,10},{9,11},{10,... | collective-permute-start | bytes 12296 | tf_op jit(solution)/shard_map/ppermute | solution.py:289
  55.6 6.3 %collective-permute-start.16 = (bf16[384,128]{1,0:T(8,128)(2,1)S(1)}, bf16[384,128]{1,0:T(8,128)(2,1)S(1)}, u32[]{:S(2)}, u32[]{:S(2)}) collective-permute-start(bf16[384,128]{1,0:T(8,128)(2,1)S(1)} %get-tuple-element.17.refs_0_), channel_id=1, source_target_pairs={{0,6},{1,7},{2,4},{3,5},{4,2},{5,3},{6,0},{7,1},{8,14},{9,15},{10,... | collective-permute-start | bytes 294920 | tf_op jit(solution)/shard_map/ppermute | solution.py:289
  57.7 5.1 %collective-permute-start.15 = (bf16[384,128]{1,0:T(8,128)(2,1)S(1)}, bf16[384,128]{1,0:T(8,128)(2,1)S(1)}, u32[]{:S(2)}, u32[]{:S(2)}) collective-permute-start(bf16[384,128]{1,0:T(8,128)(2,1)S(1)} %get-tuple-element.17.refs_0_), channel_id=1, source_target_pairs={{0,4},{1,5},{2,6},{3,7},{4,0},{5,1},{6,2},{7,3},{8,12},{9,13},{10,... | collective-permute-start | bytes 294920 | tf_op jit(solution)/shard_map/ppermute | solution.py:289
  58.9 4.6 %collective-permute-start.14 = (bf16[384,128]{1,0:T(8,128)(2,1)S(1)}, bf16[384,128]{1,0:T(8,128)(2,1)S(1)}, u32[]{:S(2)}, u32[]{:S(2)}) collective-permute-start(bf16[384,128]{1,0:T(8,128)(2,1)S(1)} %get-tuple-element.17.refs_0_), channel_id=1, source_target_pairs={{0,2},{1,3},{2,0},{3,1},{4,6},{5,7},{6,4},{7,5},{8,10},{9,11},{10,... | collective-permute-start | bytes 294920 | tf_op jit(solution)/shard_map/ppermute | solution.py:289
  63.6 1.8 %collective-permute-start.17 = (bf16[4,384,128]{2,1,0:T(8,128)(2,1)S(1)}, bf16[4,384,128]{2,1,0:T(8,128)(2,1)S(1)}, u32[]{:S(2)}, u32[]{:S(2)}) collective-permute-start(bf16[4,384,128]{2,1,0:T(8,128)(2,1)S(1)} %pad_maximum_fusion.1), channel_id=1, source_target_pairs={{0,1},{1,0},{2,3},{3,2},{4,5},{5,4},{6,7},{7,6},{8,9},{9,8},{10,11... | collective-permute-start | bytes 1179656 | tf_op jit(solution)/shard_map/ppermute | solution.py:289

commit v8 on v7

--- a/solution.py
+++ b/solution.py
@@ -1,4 +1,5 @@
 import functools
+import math
 
 import jax
 import jax.numpy as jnp
@@ -18,6 +19,7 @@
 LANES = 128
 BAND = 16
 CODES = 4
+BODY = 2
 
 
 def table_kernel(nodes, tab_ref):
@@ -76,22 +78,27 @@
 
 
 def tile_loop(v, count, groups, load, add):
+    body = math.gcd(BODY, groups)
+
     def group(i, carry):
+        first = v * groups + i * body
+        places = [(first + p, u) for p in range(body) for u in range(LANES)]
         results = []
-        for u in range(0, LANES, 2):
-            x0, g0 = load(v * groups + i, u)
-            x1, g1 = load(v * groups + i, u + 1)
+        for n in range(0, len(places), 2):
+            x0, g0 = load(*places[n])
+            x1, g1 = load(*places[n + 1])
             y = jnp.dot(
                 jnp.concatenate([x0, x1], axis=0),
                 jnp.concatenate([g0, g1], axis=1),
                 preferred_element_type=jnp.float32,
             )
             results += [y[:ROW, :LANES], y[ROW:, LANES:]]
-        for u in range(LANES):
-            add(v * groups + i, u, results[u])
+        for place, y in zip(places, results):
+            add(*place, y)
         return carry
 
-    lax.fori_loop(0, (count + LANES - 1) // LANES, group, 0)
+    size = body * LANES
+    lax.fori_loop(0, (count + size - 1) // size, group, 0)
 
 
 def forward_kernel(

time: 75 us -> 73.9 us (0.985)
  starting transfers between devices: 19 us -> 22.5 us
  waiting for transfers between devices: 34 us -> 30.9 us
  Pallas kernels: 19.8 us -> 18.8 us
    ppermute x18, starting transfers between devices: 19 us -> 22.5 us  [swap(): return lax.ppermute(x, axis, [(i, i ^ k) for i in range(size)])]
    ppermute x18, waiting for transfers between devices: 34 us -> 30.9 us  [swap(): return lax.ppermute(x, axis, [(i, i ^ k) for i in range(size)])]
where the time goes in v8:
time: 73.9 us; the launch traced here: 73.5 us
  waiting for transfers between devices  30.9 us (42%)
  starting transfers between devices  22.5 us (30%)
  Pallas kernels  18.8 us (25%)
  between operations  0.83 us (1%)
    ppermute x18, waiting for transfers between devices, swap(): return lax.ppermute(x, axis, [(i, i ^ k) for i in range(size)])  30.9 us
    ppermute x18, starting transfers between devices, swap(): return lax.ppermute(x, axis, [(i, i ^ k) for i in range(size)])  22.5 us
    pallas_call x1, Pallas kernels, body(): pl.pallas_call(functools.partial(backward_kernel, dims), out_shape=f32(*k...  8.95 us
    pallas_call x1, Pallas kernels, body(): pl.pallas_call(functools.partial(forward_kernel, dims), out_shape=[f32(bl...  7.72 us
  transfers between devices with their start and end apart: 18, of which 14 were waited for; matrix products, arithmetic and copies ran while one was open for 0% of the time, Pallas kernels for 1%

profile of v8, /device:TPU:0, one launch (start us, length us, event | category | flops | bytes accessed | tf_op | source)
XLA Modules:
  0.0 73.5 jit_solution(16809797297754018063)
XLA Ops:
  0.6 0.0 copy-start.3
  0.6 0.0 copy-start.8
  0.7 0.0 copy-start.6
  0.7 0.0 copy-start.7
  0.7 0.0 copy-start.5
  0.7 0.0 copy-start.4
  0.7 1.2 %table.1.tab_ref = bf16[10752,128]{1,0:T(8,128)(2,1)S(1)} custom-call(), custom_call_target="tpu_custom_call" | custom-call | flops 268435456 | bytes 4194304 | tf_op jit(solution)/shard_map/table/pallas_call | solution.py:317
  1.9 0.0 copy-done.3
  1.9 0.0 copy-done.8
  1.9 0.0 copy-done.6
  1.9 0.0 copy-done.7
  1.9 0.0 copy-done.5
  1.9 0.2 copy-done.4
  2.1 7.7 %forward.1 = (f32[3088,128]{1,0:T(8,128)S(1)}, s32[32,128]{1,0:T(8,128)S(1)}) custom-call(s32[1,2]{1,0:T(1,128)S(1)} %bitcast.29, s32[2,1,512]{2,1,0:T(1,128)S(1)} %bitcast.31, s32[2,512]{1,0:T(2,128)S(1)} %copy-done.6, s32[2,512]{1,0:T(2,128)S(1)} %copy-done.7, s32[2,512]{1,0:T(2,128)S(1)} %copy-done.8, bf16[2,12,256,128]{3,2,1,0:T(8,128)(2,1)S(1)} %copy-done.4, ...), custom_call_target="tpu_custom_call" | custom-call | flops 34359738368 | bytes 16777216 | tf_op jit(solution)/shard_map/forward/pallas_call | solution.py:325
  9.9 0.0 copy-start
  9.9 0.0 copy-start.1
  9.9 0.0 copy-start.2
  9.9 0.1 slice.37
  9.9 1.1 %collective-permute-start = (f32[4,384,128]{2,1,0:T(8,128)S(1)}, f32[4,384,128]{2,1,0:T(8,128)S(1)}, u32[]{:S(2)}, u32[]{:S(2)}) collective-permute-start(f32[4,384,128]{2,1,0:T(8,128)S(1)} %bitcast.32), channel_id=1, source_target_pairs={{0,1},{1,0},{2,3},{3,2},{4,5},{5,4},{6,7},{7,6},{8,9},{9,8},{10,11... | collective-permute-start | bytes 2359304 | tf_op jit(solution)/shard_map/ppermute | solution.py:296
  11.0 0.0 copy-done
  11.0 0.0 copy-done.1
  11.0 0.0 copy-done.2
  11.1 3.3 %collective-permute-start.6 = (f32[1,3,96,128]{3,2,1,0:T(8,128)S(1)}, f32[1,3,96,128]{3,2,1,0:T(8,128)S(1)}, u32[]{:S(2)}, u32[]{:S(2)}) collective-permute-start(f32[1,3,96,128]{3,2,1,0:T(8,128)S(1)} %bitcast.22), channel_id=1, source_target_pairs={{0,8},{8,0},{16,24},{24,16},{1,9},{9,1},{17,25},{25,17},{2,10},{10... | collective-permute-start | bytes 442376 | tf_op jit(solution)/shard_map/ppermute | solution.py:296
  14.4 3.8 %collective-permute-done.6 = f32[1,3,96,128]{3,2,1,0:T(8,128)S(1)} collective-permute-done((f32[1,3,96,128]{3,2,1,0:T(8,128)S(1)}, f32[1,3,96,128]{3,2,1,0:T(8,128)S(1)}, u32[]{:S(2)}, u32[]{:S(2)}) %collective-permute-start.6) | collective-permute-done | bytes 147488 | tf_op jit(solution)/shard_map/ppermute | solution.py:296
  18.2 2.8 %collective-permute-start.7 = (f32[2,3,96,128]{3,2,1,0:T(8,128)S(1)}, f32[2,3,96,128]{3,2,1,0:T(8,128)S(1)}, u32[]{:S(2)}, u32[]{:S(2)}) collective-permute-start(f32[2,3,96,128]{3,2,1,0:T(8,128)S(1)} %pad_maximum_fusion.2), channel_id=1, source_target_pairs={{0,16},{8,24},{16,0},{24,8},{1,17},{9,25},{17,1},{25,9},{2,18},{10... | collective-permute-start | bytes 884744 | tf_op jit(solution)/shard_map/ppermute | solution.py:296
  21.1 0.0 collective-permute-done
  21.1 0.1 fusion
  21.2 2.5 %collective-permute-start.3 = (f32[384,128]{1,0:T(8,128)S(1)}, f32[384,128]{1,0:T(8,128)S(1)}, u32[]{:S(2)}, u32[]{:S(2)}) collective-permute-start(f32[384,128]{1,0:T(8,128)S(1)} %get-tuple-element.18), channel_id=1, source_target_pairs={{0,6},{1,7},{2,4},{3,5},{4,2},{5,3},{6,0},{7,1},{8,14},{9,15},{10,... | collective-permute-start | bytes 589832 | tf_op jit(solution)/shard_map/ppermute | solution.py:296
  23.7 0.4 collective-permute-start.2
  24.1 0.6 collective-permute-start.1
  24.8 5.0 %collective-permute-done.3.refs_3_ = f32[384,128]{1,0:T(8,128)S(1)} collective-permute-done((f32[384,128]{1,0:T(8,128)S(1)}, f32[384,128]{1,0:T(8,128)S(1)}, u32[]{:S(2)}, u32[]{:S(2)}) %collective-permute-start.3) | collective-permute-done | bytes 196640 | tf_op jit(solution)/shard_map/ppermute | solution.py:296
  29.8 2.1 %collective-permute-done.2.refs_2_ = f32[384,128]{1,0:T(8,128)S(1)} collective-permute-done((f32[384,128]{1,0:T(8,128)S(1)}, f32[384,128]{1,0:T(8,128)S(1)}, u32[]{:S(2)}, u32[]{:S(2)}) %collective-permute-start.2) | collective-permute-done | bytes 196640 | tf_op jit(solution)/shard_map/ppermute | solution.py:296
  31.9 0.0 collective-permute-done.1.refs_1_
  31.9 1.7 %collective-permute-start.4 = (f32[192,128]{1,0:T(8,128)S(1)}, f32[192,128]{1,0:T(8,128)S(1)}, u32[]{:S(2)}, u32[]{:S(2)}) collective-permute-start(f32[192,128]{1,0:T(8,128)S(1)} %get-tuple-element.12), channel_id=1, source_target_pairs={{0,8},{8,0},{16,24},{24,16},{1,9},{9,1},{17,25},{25,17},{2,10},{10... | collective-permute-start | bytes 294920 | tf_op jit(solution)/shard_map/ppermute | solution.py:296
  33.6 3.0 %collective-permute-done.4 = f32[192,128]{1,0:T(8,128)S(1)} collective-permute-done((f32[192,128]{1,0:T(8,128)S(1)}, f32[192,128]{1,0:T(8,128)S(1)}, u32[]{:S(2)}, u32[]{:S(2)}) %collective-permute-start.4) | collective-permute-done | bytes 98336 | tf_op jit(solution)/shard_map/ppermute | solution.py:296
  36.6 0.8 %collective-permute-start.5 = (f32[192,128]{1,0:T(8,128)S(1)}, f32[192,128]{1,0:T(8,128)S(1)}, u32[]{:S(2)}, u32[]{:S(2)}) collective-permute-start(f32[192,128]{1,0:T(8,128)S(1)} %add.21.a_ref), channel_id=1, source_target_pairs={{0,16},{8,24},{16,0},{24,8},{1,17},{9,25},{17,1},{25,9},{2,18},{10... | collective-permute-start | bytes 294920 | tf_op jit(solution)/shard_map/ppermute | solution.py:296
  37.4 0.0 collective-permute-done.7
  37.4 4.9 %collective-permute-done.5.b_ref = f32[192,128]{1,0:T(8,128)S(1)} collective-permute-done((f32[192,128]{1,0:T(8,128)S(1)}, f32[192,128]{1,0:T(8,128)S(1)}, u32[]{:S(2)}, u32[]{:S(2)}) %collective-permute-start.5) | collective-permute-done | bytes 98336 | tf_op jit(solution)/shard_map/ppermute | solution.py:296
  42.3 0.1 sums.1
  42.3 1.7 %collective-permute-start.8 = (f32[192,128]{1,0:T(8,128)S(1)}, f32[192,128]{1,0:T(8,128)S(1)}, u32[]{:S(2)}, u32[]{:S(2)}) collective-permute-start(f32[192,128]{1,0:T(8,128)S(1)} %get-tuple-element.13.mine_ref), channel_id=1, source_target_pairs={{0,8},{8,0},{16,24},{24,16},{1,9},{9,1},{17,25},{25,17},{2,10},{10... | collective-permute-start | bytes 294920 | tf_op jit(solution)/shard_map/ppermute | solution.py:296
  44.0 0.4 collective-permute-start.9
  44.4 3.2 %collective-permute-done.9 = f32[8,128]{1,0:T(8,128)S(1)} collective-permute-done((f32[8,128]{1,0:T(8,128)S(1)}, f32[8,128]{1,0:T(8,128)S(1)}, u32[]{:S(2)}, u32[]{:S(2)}) %collective-permute-start.9) | collective-permute-done | bytes 4128 | tf_op jit(solution)/shard_map/ppermute | solution.py:296
  47.6 0.0 collective-permute-start.10
  47.6 1.2 %collective-permute-done.10 = f32[8,128]{1,0:T(8,128)S(1)} collective-permute-done((f32[8,128]{1,0:T(8,128)S(1)}, f32[8,128]{1,0:T(8,128)S(1)}, u32[]{:S(2)}, u32[]{:S(2)}) %collective-permute-start.10) | collective-permute-done | bytes 4128 | tf_op jit(solution)/shard_map/ppermute | solution.py:296
  48.8 2.9 %collective-permute-start.13 = (f32[8,128]{1,0:T(8,128)S(1)}, f32[8,128]{1,0:T(8,128)S(1)}, u32[]{:S(2)}, u32[]{:S(2)}) collective-permute-start(f32[8,128]{1,0:T(8,128)S(1)} %add.23.refs_0_), channel_id=1, source_target_pairs={{0,6},{1,7},{2,4},{3,5},{4,2},{5,3},{6,0},{7,1},{8,14},{9,15},{10,... | collective-permute-start | bytes 12296 | tf_op jit(solution)/shard_map/ppermute | solution.py:296
  51.7 0.3 collective-permute-start.12
  52.0 0.3 collective-permute-start.11
  52.3 1.0 %collective-permute-done.13.refs_3_ = f32[8,128]{1,0:T(8,128)S(1)} collective-permute-done((f32[8,128]{1,0:T(8,128)S(1)}, f32[8,128]{1,0:T(8,128)S(1)}, u32[]{:S(2)}, u32[]{:S(2)}) %collective-permute-start.13) | collective-permute-done | bytes 4128 | tf_op jit(solution)/shard_map/ppermute | solution.py:296
  53.3 2.0 %collective-permute-done.12.refs_2_ = f32[8,128]{1,0:T(8,128)S(1)} collective-permute-done((f32[8,128]{1,0:T(8,128)S(1)}, f32[8,128]{1,0:T(8,128)S(1)}, u32[]{:S(2)}, u32[]{:S(2)}) %collective-permute-start.12) | collective-permute-done | bytes 4128 | tf_op jit(solution)/shard_map/ppermute | solution.py:296
  55.3 0.3 collective-permute-done.11.refs_1_
  55.6 0.0 collective-permute-done.8.other_ref
  55.6 0.2 direction.1
  55.8 1.2 %collective-permute-start.16 = (bf16[384,128]{1,0:T(8,128)(2,1)S(1)}, bf16[384,128]{1,0:T(8,128)(2,1)S(1)}, u32[]{:S(2)}, u32[]{:S(2)}) collective-permute-start(bf16[384,128]{1,0:T(8,128)(2,1)S(1)} %get-tuple-element.17.refs_0_), channel_id=1, source_target_pairs={{0,6},{1,7},{2,4},{3,5},{4,2},{5,3},{6,0},{7,1},{8,14},{9,15},{10,... | collective-permute-start | bytes 294920 | tf_op jit(solution)/shard_map/ppermute | solution.py:296
  57.0 0.6 collective-permute-start.15
  57.7 1.7 %collective-permute-start.14 = (bf16[384,128]{1,0:T(8,128)(2,1)S(1)}, bf16[384,128]{1,0:T(8,128)(2,1)S(1)}, u32[]{:S(2)}, u32[]{:S(2)}) collective-permute-start(bf16[384,128]{1,0:T(8,128)(2,1)S(1)} %get-tuple-element.17.refs_0_), channel_id=1, source_target_pairs={{0,2},{1,3},{2,0},{3,1},{4,6},{5,7},{6,4},{7,5},{8,10},{9,11},{10,... | collective-permute-start | bytes 294920 | tf_op jit(solution)/shard_map/ppermute | solution.py:296
  59.3 2.1 %collective-permute-done.16.refs_3_ = bf16[384,128]{1,0:T(8,128)(2,1)S(1)} collective-permute-done((bf16[384,128]{1,0:T(8,128)(2,1)S(1)}, bf16[384,128]{1,0:T(8,128)(2,1)S(1)}, u32[]{:S(2)}, u32[]{:S(2)}) %collective-permute-start.16) | collective-permute-done | bytes 98336 | tf_op jit(solution)/shard_map/ppermute | solution.py:296
  61.4 1.0 %collective-permute-done.15.refs_2_ = bf16[384,128]{1,0:T(8,128)(2,1)S(1)} collective-permute-done((bf16[384,128]{1,0:T(8,128)(2,1)S(1)}, bf16[384,128]{1,0:T(8,128)(2,1)S(1)}, u32[]{:S(2)}, u32[]{:S(2)}) %collective-permute-start.15) | collective-permute-done | bytes 98336 | tf_op jit(solution)/shard_map/ppermute | solution.py:296
  62.4 0.3 collective-permute-done.14.refs_1_
  62.7 0.1 pad_maximum_fusion.1
  62.8 0.1 collective-permute-start.17
  62.9 0.6 unpack.1
  63.5 1.1 %collective-permute-done.17.refs_4_ = bf16[4,384,128]{2,1,0:T(8,128)(2,1)S(1)} collective-permute-done((bf16[4,384,128]{2,1,0:T(8,128)(2,1)S(1)}, bf16[4,384,128]{2,1,0:T(8,128)(2,1)S(1)}, u32[]{:S(2)}, u32[]{:S(2)}) %collective-permute-start.17) | collective-permute-done | bytes 393248 | tf_op jit(solution)/shard_map/ppermute | solution.py:296
  64.6 9.0 %backward.1 = f32[2,12,256,128]{3,2,1,0:T(8,128)} custom-call(s32[1,2]{1,0:T(1,128)S(1)} %bitcast.30, s32[32,128]{1,0:T(8,128)S(1)} %get-tuple-element.16.codes_in, bf16[10752,128]{1,0:T(8,128)(2,1)S(1)} %table.1.tab_ref, bf16[384,128]{1,0:T(8,128)(2,1)S(1)} %get-tuple-element.17.refs_0_, bf16[384,128]{1,0:T(8,128)(2,1)S(1)} %collective-permute-done.14.refs_1_, ...), custom_call_target="tpu_custom_call" | custom-call | tf_op jit(solution)/shard_map/backward/pallas_call | solution.py:409
  (9 shorter events, 0.2 us)
Async XLA Ops:
  0.6 1.2 %copy-start.3 = (s32[2,1]{0,1:T(1,128)S(1)}, s32[2,1]{0,1:T(1,128)}, u32[]{:S(2)}) copy-start(s32[2,1]{0,1:T(1,128)} %param.14) | copy-start | bytes 28
  0.6 1.2 %copy-start.8 = (s32[2,512]{1,0:T(2,128)S(1)}, s32[2,512]{1,0:T(2,128)}, u32[]{:S(2)}) copy-start(s32[2,512]{1,0:T(2,128)} %seed_ref.1) | copy-start | bytes 12292
  0.7 1.2 %copy-start.6 = (s32[2,512]{1,0:T(2,128)S(1)}, s32[2,512]{1,0:T(2,128)}, u32[]{:S(2)}) copy-start(s32[2,512]{1,0:T(2,128)} %target_ref.1) | copy-start | bytes 12292
  0.7 1.2 %copy-start.7 = (s32[2,512]{1,0:T(2,128)S(1)}, s32[2,512]{1,0:T(2,128)}, u32[]{:S(2)}) copy-start(s32[2,512]{1,0:T(2,128)} %source_ref.1) | copy-start | bytes 12292
  0.7 1.2 %copy-start.5 = (s32[2,512,1]{1,2,0:T(1,128)S(1)}, s32[2,512,1]{1,2,0:T(1,128)}, u32[]{:S(2)}) copy-start(s32[2,512,1]{1,2,0:T(1,128)} %param.10) | copy-start | bytes 12292
  0.7 1.4 %copy-start.4 = (bf16[2,12,256,128]{3,2,1,0:T(8,128)(2,1)S(1)}, bf16[2,12,256,128]{3,2,1,0:T(8,128)(2,1)}, u32[]{:S(2)}) copy-start(bf16[2,12,256,128]{3,2,1,0:T(8,128)(2,1)} %field_ref.1) | copy-start | bytes 4718596
  9.9 1.2 %copy-start = (f32[12,1,8,128]{3,2,1,0:T(8,128)S(1)}, f32[12,1,8,128]{3,2,1,0:T(8,128)}, u32[]{:S(2)}) copy-start(f32[12,1,8,128]{3,2,1,0:T(8,128)} %refs_0_.1) | copy-start | bytes 147460
  9.9 1.2 %copy-start.1 = (f32[12,1,8,128]{3,2,1,0:T(8,128)S(1)}, f32[12,1,8,128]{3,2,1,0:T(8,128)}, u32[]{:S(2)}) copy-start(f32[12,1,8,128]{3,2,1,0:T(8,128)} %refs_1_.1) | copy-start | bytes 147460
  9.9 1.2 %copy-start.2 = (f32[12,1,8,128]{3,2,1,0:T(8,128)S(1)}, f32[12,1,8,128]{3,2,1,0:T(8,128)}, u32[]{:S(2)}) copy-start(f32[12,1,8,128]{3,2,1,0:T(8,128)} %refs_2_.1) | copy-start | bytes 147460
  9.9 11.1 %collective-permute-start = (f32[4,384,128]{2,1,0:T(8,128)S(1)}, f32[4,384,128]{2,1,0:T(8,128)S(1)}, u32[]{:S(2)}, u32[]{:S(2)}) collective-permute-start(f32[4,384,128]{2,1,0:T(8,128)S(1)} %bitcast.32), channel_id=1, source_target_pairs={{0,1},{1,0},{2,3},{3,2},{4,5},{5,4},{6,7},{7,6},{8,9},{9,8},{10,11... | collective-permute-start | bytes 2359304 | tf_op jit(solution)/shard_map/ppermute | solution.py:296
  11.1 7.1 %collective-permute-start.6 = (f32[1,3,96,128]{3,2,1,0:T(8,128)S(1)}, f32[1,3,96,128]{3,2,1,0:T(8,128)S(1)}, u32[]{:S(2)}, u32[]{:S(2)}) collective-permute-start(f32[1,3,96,128]{3,2,1,0:T(8,128)S(1)} %bitcast.22), channel_id=1, source_target_pairs={{0,8},{8,0},{16,24},{24,16},{1,9},{9,1},{17,25},{25,17},{2,10},{10... | collective-permute-start | bytes 442376 | tf_op jit(solution)/shard_map/ppermute | solution.py:296
  18.2 19.1 %collective-permute-start.7 = (f32[2,3,96,128]{3,2,1,0:T(8,128)S(1)}, f32[2,3,96,128]{3,2,1,0:T(8,128)S(1)}, u32[]{:S(2)}, u32[]{:S(2)}) collective-permute-start(f32[2,3,96,128]{3,2,1,0:T(8,128)S(1)} %pad_maximum_fusion.2), channel_id=1, source_target_pairs={{0,16},{8,24},{16,0},{24,8},{1,17},{9,25},{17,1},{25,9},{2,18},{10... | collective-permute-start | bytes 884744 | tf_op jit(solution)/shard_map/ppermute | solution.py:296
  21.2 8.6 %collective-permute-start.3 = (f32[384,128]{1,0:T(8,128)S(1)}, f32[384,128]{1,0:T(8,128)S(1)}, u32[]{:S(2)}, u32[]{:S(2)}) collective-permute-start(f32[384,128]{1,0:T(8,128)S(1)} %get-tuple-element.18), channel_id=1, source_target_pairs={{0,6},{1,7},{2,4},{3,5},{4,2},{5,3},{6,0},{7,1},{8,14},{9,15},{10,... | collective-permute-start | bytes 589832 | tf_op jit(solution)/shard_map/ppermute | solution.py:296
  23.7 8.2 %collective-permute-start.2 = (f32[384,128]{1,0:T(8,128)S(1)}, f32[384,128]{1,0:T(8,128)S(1)}, u32[]{:S(2)}, u32[]{:S(2)}) collective-permute-start(f32[384,128]{1,0:T(8,128)S(1)} %get-tuple-element.19), channel_id=1, source_target_pairs={{0,4},{1,5},{2,6},{3,7},{4,0},{5,1},{6,2},{7,3},{8,12},{9,13},{10,... | collective-permute-start | bytes 589832 | tf_op jit(solution)/shard_map/ppermute | solution.py:296
  24.1 7.8 %collective-permute-start.1 = (f32[384,128]{1,0:T(8,128)S(1)}, f32[384,128]{1,0:T(8,128)S(1)}, u32[]{:S(2)}, u32[]{:S(2)}) collective-permute-start(f32[384,128]{1,0:T(8,128)S(1)} %get-tuple-element.20), channel_id=1, source_target_pairs={{0,2},{1,3},{2,0},{3,1},{4,6},{5,7},{6,4},{7,5},{8,10},{9,11},{10,... | collective-permute-start | bytes 589832 | tf_op jit(solution)/shard_map/ppermute | solution.py:296
  31.9 4.7 %collective-permute-start.4 = (f32[192,128]{1,0:T(8,128)S(1)}, f32[192,128]{1,0:T(8,128)S(1)}, u32[]{:S(2)}, u32[]{:S(2)}) collective-permute-start(f32[192,128]{1,0:T(8,128)S(1)} %get-tuple-element.12), channel_id=1, source_target_pairs={{0,8},{8,0},{16,24},{24,16},{1,9},{9,1},{17,25},{25,17},{2,10},{10... | collective-permute-start | bytes 294920 | tf_op jit(solution)/shard_map/ppermute | solution.py:296
  36.6 5.7 %collective-permute-start.5 = (f32[192,128]{1,0:T(8,128)S(1)}, f32[192,128]{1,0:T(8,128)S(1)}, u32[]{:S(2)}, u32[]{:S(2)}) collective-permute-start(f32[192,128]{1,0:T(8,128)S(1)} %add.21.a_ref), channel_id=1, source_target_pairs={{0,16},{8,24},{16,0},{24,8},{1,17},{9,25},{17,1},{25,9},{2,18},{10... | collective-permute-start | bytes 294920 | tf_op jit(solution)/shard_map/ppermute | solution.py:296
  42.3 13.3 %collective-permute-start.8 = (f32[192,128]{1,0:T(8,128)S(1)}, f32[192,128]{1,0:T(8,128)S(1)}, u32[]{:S(2)}, u32[]{:S(2)}) collective-permute-start(f32[192,128]{1,0:T(8,128)S(1)} %get-tuple-element.13.mine_ref), channel_id=1, source_target_pairs={{0,8},{8,0},{16,24},{24,16},{1,9},{9,1},{17,25},{25,17},{2,10},{10... | collective-permute-start | bytes 294920 | tf_op jit(solution)/shard_map/ppermute | solution.py:296
  44.0 3.6 %collective-permute-start.9 = (f32[8,128]{1,0:T(8,128)S(1)}, f32[8,128]{1,0:T(8,128)S(1)}, u32[]{:S(2)}, u32[]{:S(2)}) collective-permute-start(f32[8,128]{1,0:T(8,128)S(1)} %get-tuple-element.14), channel_id=1, source_target_pairs={{0,8},{8,0},{16,24},{24,16},{1,9},{9,1},{17,25},{25,17},{2,10},{10... | collective-permute-start | bytes 12296 | tf_op jit(solution)/shard_map/ppermute | solution.py:296
  47.6 1.2 %collective-permute-start.10 = (f32[8,128]{1,0:T(8,128)S(1)}, f32[8,128]{1,0:T(8,128)S(1)}, u32[]{:S(2)}, u32[]{:S(2)}) collective-permute-start(f32[8,128]{1,0:T(8,128)S(1)} %add.22), channel_id=1, source_target_pairs={{0,1},{1,0},{2,3},{3,2},{4,5},{5,4},{6,7},{7,6},{8,9},{9,8},{10,11... | collective-permute-start | bytes 12296 | tf_op jit(solution)/shard_map/ppermute | solution.py:296
  48.8 4.5 %collective-permute-start.13 = (f32[8,128]{1,0:T(8,128)S(1)}, f32[8,128]{1,0:T(8,128)S(1)}, u32[]{:S(2)}, u32[]{:S(2)}) collective-permute-start(f32[8,128]{1,0:T(8,128)S(1)} %add.23.refs_0_), channel_id=1, source_target_pairs={{0,6},{1,7},{2,4},{3,5},{4,2},{5,3},{6,0},{7,1},{8,14},{9,15},{10,... | collective-permute-start | bytes 12296 | tf_op jit(solution)/shard_map/ppermute | solution.py:296
  51.7 3.6 %collective-permute-start.12 = (f32[8,128]{1,0:T(8,128)S(1)}, f32[8,128]{1,0:T(8,128)S(1)}, u32[]{:S(2)}, u32[]{:S(2)}) collective-permute-start(f32[8,128]{1,0:T(8,128)S(1)} %add.23.refs_0_), channel_id=1, source_target_pairs={{0,4},{1,5},{2,6},{3,7},{4,0},{5,1},{6,2},{7,3},{8,12},{9,13},{10,... | collective-permute-start | bytes 12296 | tf_op jit(solution)/shard_map/ppermute | solution.py:296
  52.0 3.6 %collective-permute-start.11 = (f32[8,128]{1,0:T(8,128)S(1)}, f32[8,128]{1,0:T(8,128)S(1)}, u32[]{:S(2)}, u32[]{:S(2)}) collective-permute-start(f32[8,128]{1,0:T(8,128)S(1)} %add.23.refs_0_), channel_id=1, source_target_pairs={{0,2},{1,3},{2,0},{3,1},{4,6},{5,7},{6,4},{7,5},{8,10},{9,11},{10,... | collective-permute-start | bytes 12296 | tf_op jit(solution)/shard_map/ppermute | solution.py:296
  55.8 5.7 %collective-permute-start.16 = (bf16[384,128]{1,0:T(8,128)(2,1)S(1)}, bf16[384,128]{1,0:T(8,128)(2,1)S(1)}, u32[]{:S(2)}, u32[]{:S(2)}) collective-permute-start(bf16[384,128]{1,0:T(8,128)(2,1)S(1)} %get-tuple-element.17.refs_0_), channel_id=1, source_target_pairs={{0,6},{1,7},{2,4},{3,5},{4,2},{5,3},{6,0},{7,1},{8,14},{9,15},{10,... | collective-permute-start | bytes 294920 | tf_op jit(solution)/shard_map/ppermute | solution.py:296
  57.0 5.4 %collective-permute-start.15 = (bf16[384,128]{1,0:T(8,128)(2,1)S(1)}, bf16[384,128]{1,0:T(8,128)(2,1)S(1)}, u32[]{:S(2)}, u32[]{:S(2)}) collective-permute-start(bf16[384,128]{1,0:T(8,128)(2,1)S(1)} %get-tuple-element.17.refs_0_), channel_id=1, source_target_pairs={{0,4},{1,5},{2,6},{3,7},{4,0},{5,1},{6,2},{7,3},{8,12},{9,13},{10,... | collective-permute-start | bytes 294920 | tf_op jit(solution)/shard_map/ppermute | solution.py:296
  57.7 5.1 %collective-permute-start.14 = (bf16[384,128]{1,0:T(8,128)(2,1)S(1)}, bf16[384,128]{1,0:T(8,128)(2,1)S(1)}, u32[]{:S(2)}, u32[]{:S(2)}) collective-permute-start(bf16[384,128]{1,0:T(8,128)(2,1)S(1)} %get-tuple-element.17.refs_0_), channel_id=1, source_target_pairs={{0,2},{1,3},{2,0},{3,1},{4,6},{5,7},{6,4},{7,5},{8,10},{9,11},{10,... | collective-permute-start | bytes 294920 | tf_op jit(solution)/shard_map/ppermute | solution.py:296
  62.8 1.8 %collective-permute-start.17 = (bf16[4,384,128]{2,1,0:T(8,128)(2,1)S(1)}, bf16[4,384,128]{2,1,0:T(8,128)(2,1)S(1)}, u32[]{:S(2)}, u32[]{:S(2)}) collective-permute-start(bf16[4,384,128]{2,1,0:T(8,128)(2,1)S(1)} %pad_maximum_fusion.1), channel_id=1, source_target_pairs={{0,1},{1,0},{2,3},{3,2},{4,5},{5,4},{6,7},{7,6},{8,9},{9,8},{10,11... | collective-permute-start | bytes 1179656 | tf_op jit(solution)/shard_map/ppermute | solution.py:296

commit v9 on v8

--- a/solution.py
+++ b/solution.py
@@ -165,9 +165,10 @@
         tile_loop(v, count_ref[0, v], groups, load, add)
         for c in range(comps):
             tile_ref[v, c] = sum_ref[pl.ds(v * eblocks * PITCH + c, eblocks, stride=PITCH), :]
-        send = pltpu.make_async_copy(tile_ref.at[v], out_ref.at[v], sems.at[1 + v])
-        send.start()
-        sends.append(send)
+            sem = sems.at[1 + v * comps + c]
+            send = pltpu.make_async_copy(tile_ref.at[v, c], out_ref.at[v, c], sem)
+            send.start()
+            sends.append(send)
     for send in sends:
         send.wait()
 
@@ -378,9 +379,12 @@
         compiler_params=limit(4),
         name="sums",
     )(total, across, hist)
-    local = local + swap(local, "ev", 1)
+    across_both = [(i, i ^ (parts + 1)) for i in range(evs * parts)]
+    by_ev = swap(local, "ev", 1)
+    by_both = lax.ppermute(local, ("ev", "mesh"), across_both)
+    by_core = swap(local, "mesh", 1)
     gradient_other = swap(gradient, "ev", 1)
-    local = local + swap(local, "mesh", 1)
+    local = (local + by_core) + (by_ev + by_both)
     spread = [local] + [swap(local, "mesh", 2 * j) for j in range(1, half)]
     inverse, rounded = pl.pallas_call(
         functools.partial(direction_kernel, rows, evs),
@@ -416,7 +420,7 @@
             pltpu.VMEM((events * eblocks * PITCH + ROW, nodes), jnp.float32),
             pltpu.VMEM(kernels.shape, jnp.float32),
             pltpu.SMEM(code_rows, jnp.int32),
-            pltpu.SemaphoreType.DMA((1 + events,)),
+            pltpu.SemaphoreType.DMA((1 + events * comps,)),
         ],
         compiler_params=limit(24),
         name="backward",

time: 73.9 us -> 71.9 us (0.973)
  waiting for transfers between devices: 30.9 us -> 27.1 us
  starting transfers between devices: 22.5 us -> 24.1 us
    ppermute x18, waiting for transfers between devices: 30.9 us -> 27.1 us  [swap(): return lax.ppermute(x, axis, [(i, i ^ k) for i in range(size)])]
    ppermute x18, starting transfers between devices: 22.5 us -> 23.5 us  [swap(): return lax.ppermute(x, axis, [(i, i ^ k) for i in range(size)])]
  transfers between devices with their start and end apart: 18 -> 19, of which waited for: 14 -> 12; matrix products, arithmetic and copies ran while one was open for 0% -> 0% of each run, Pallas kernels for 1% -> 1%
where the time goes in v9:
time: 71.9 us; the launch traced here: 71.5 us
  waiting for transfers between devices  27.1 us (38%)
  starting transfers between devices  24.1 us (34%)
  Pallas kernels  18.9 us (26%)
  between operations  0.84 us (1%)
    ppermute x18, waiting for transfers between devices, swap(): return lax.ppermute(x, axis, [(i, i ^ k) for i in range(size)])  27.1 us
    ppermute x18, starting transfers between devices, swap(): return lax.ppermute(x, axis, [(i, i ^ k) for i in range(size)])  23.5 us
    pallas_call x1, Pallas kernels, body(): pl.pallas_call(functools.partial(backward_kernel, dims), out_shape=f32(*k...  9.04 us
    pallas_call x1, Pallas kernels, body(): pl.pallas_call(functools.partial(forward_kernel, dims), out_shape=[f32(bl...  7.72 us
  transfers between devices with their start and end apart: 19, of which 12 were waited for; matrix products, arithmetic and copies ran while one was open for 0% of the time, Pallas kernels for 1%

profile of v9, /device:TPU:0, one launch (start us, length us, event | category | flops | bytes accessed | tf_op | source)
XLA Modules:
  0.0 71.5 jit_solution(288874886359366253)
XLA Ops:
  0.6 0.0 copy-start.3
  0.6 0.0 copy-start.8
  0.7 0.0 copy-start.6
  0.7 0.0 copy-start.7
  0.7 0.0 copy-start.5
  0.7 0.0 copy-start.4
  0.7 1.2 %table.1.tab_ref = bf16[10752,128]{1,0:T(8,128)(2,1)S(1)} custom-call(), custom_call_target="tpu_custom_call" | custom-call | flops 268435456 | bytes 4194304 | tf_op jit(solution)/shard_map/table/pallas_call | solution.py:318
  1.9 0.0 copy-done.3
  1.9 0.0 copy-done.8
  1.9 0.0 copy-done.6
  1.9 0.0 copy-done.7
  1.9 0.0 copy-done.5
  1.9 0.2 copy-done.4
  2.1 7.7 %forward.1 = (f32[3088,128]{1,0:T(8,128)S(1)}, s32[32,128]{1,0:T(8,128)S(1)}) custom-call(s32[1,2]{1,0:T(1,128)S(1)} %bitcast.29, s32[2,1,512]{2,1,0:T(1,128)S(1)} %bitcast.31, s32[2,512]{1,0:T(2,128)S(1)} %copy-done.6, s32[2,512]{1,0:T(2,128)S(1)} %copy-done.7, s32[2,512]{1,0:T(2,128)S(1)} %copy-done.8, bf16[2,12,256,128]{3,2,1,0:T(8,128)(2,1)S(1)} %copy-done.4, ...), custom_call_target="tpu_custom_call" | custom-call | flops 34359738368 | bytes 16777216 | tf_op jit(solution)/shard_map/forward/pallas_call | solution.py:326
  9.9 0.0 copy-start
  9.9 0.0 copy-start.1
  9.9 0.0 copy-start.2
  9.9 0.1 slice.37
  9.9 1.1 %collective-permute-start = (f32[4,384,128]{2,1,0:T(8,128)S(1)}, f32[4,384,128]{2,1,0:T(8,128)S(1)}, u32[]{:S(2)}, u32[]{:S(2)}) collective-permute-start(f32[4,384,128]{2,1,0:T(8,128)S(1)} %bitcast.32), channel_id=1, source_target_pairs={{0,1},{1,0},{2,3},{3,2},{4,5},{5,4},{6,7},{7,6},{8,9},{9,8},{10,11... | collective-permute-start | bytes 2359304 | tf_op jit(solution)/shard_map/ppermute | solution.py:297
  11.0 0.0 copy-done
  11.0 0.0 copy-done.1
  11.1 3.3 %collective-permute-start.6 = (f32[1,3,96,128]{3,2,1,0:T(8,128)S(1)}, f32[1,3,96,128]{3,2,1,0:T(8,128)S(1)}, u32[]{:S(2)}, u32[]{:S(2)}) collective-permute-start(f32[1,3,96,128]{3,2,1,0:T(8,128)S(1)} %bitcast.22), channel_id=1, source_target_pairs={{0,8},{8,0},{16,24},{24,16},{1,9},{9,1},{17,25},{25,17},{2,10},{10... | collective-permute-start | bytes 442376 | tf_op jit(solution)/shard_map/ppermute | solution.py:297
  14.4 3.8 %collective-permute-done.6 = f32[1,3,96,128]{3,2,1,0:T(8,128)S(1)} collective-permute-done((f32[1,3,96,128]{3,2,1,0:T(8,128)S(1)}, f32[1,3,96,128]{3,2,1,0:T(8,128)S(1)}, u32[]{:S(2)}, u32[]{:S(2)}) %collective-permute-start.6) | collective-permute-done | bytes 147488 | tf_op jit(solution)/shard_map/ppermute | solution.py:297
  18.2 2.8 %collective-permute-start.7 = (f32[2,3,96,128]{3,2,1,0:T(8,128)S(1)}, f32[2,3,96,128]{3,2,1,0:T(8,128)S(1)}, u32[]{:S(2)}, u32[]{:S(2)}) collective-permute-start(f32[2,3,96,128]{3,2,1,0:T(8,128)S(1)} %pad_maximum_fusion.2), channel_id=1, source_target_pairs={{0,16},{8,24},{16,0},{24,8},{1,17},{9,25},{17,1},{25,9},{2,18},{10... | collective-permute-start | bytes 884744 | tf_op jit(solution)/shard_map/ppermute | solution.py:297
  21.1 0.0 collective-permute-done
  21.1 0.1 fusion
  21.2 2.5 %collective-permute-start.3 = (f32[384,128]{1,0:T(8,128)S(1)}, f32[384,128]{1,0:T(8,128)S(1)}, u32[]{:S(2)}, u32[]{:S(2)}) collective-permute-start(f32[384,128]{1,0:T(8,128)S(1)} %get-tuple-element.18), channel_id=1, source_target_pairs={{0,6},{1,7},{2,4},{3,5},{4,2},{5,3},{6,0},{7,1},{8,14},{9,15},{10,... | collective-permute-start | bytes 589832 | tf_op jit(solution)/shard_map/ppermute | solution.py:297
  23.7 0.4 collective-permute-start.2
  24.1 0.6 collective-permute-start.1
  24.8 5.0 %collective-permute-done.3.refs_3_ = f32[384,128]{1,0:T(8,128)S(1)} collective-permute-done((f32[384,128]{1,0:T(8,128)S(1)}, f32[384,128]{1,0:T(8,128)S(1)}, u32[]{:S(2)}, u32[]{:S(2)}) %collective-permute-start.3) | collective-permute-done | bytes 196640 | tf_op jit(solution)/shard_map/ppermute | solution.py:297
  29.8 2.1 %collective-permute-done.2.refs_2_ = f32[384,128]{1,0:T(8,128)S(1)} collective-permute-done((f32[384,128]{1,0:T(8,128)S(1)}, f32[384,128]{1,0:T(8,128)S(1)}, u32[]{:S(2)}, u32[]{:S(2)}) %collective-permute-start.2) | collective-permute-done | bytes 196640 | tf_op jit(solution)/shard_map/ppermute | solution.py:297
  31.9 0.0 collective-permute-done.1.refs_1_
  31.9 1.7 %collective-permute-start.4 = (f32[192,128]{1,0:T(8,128)S(1)}, f32[192,128]{1,0:T(8,128)S(1)}, u32[]{:S(2)}, u32[]{:S(2)}) collective-permute-start(f32[192,128]{1,0:T(8,128)S(1)} %get-tuple-element.12), channel_id=1, source_target_pairs={{0,8},{8,0},{16,24},{24,16},{1,9},{9,1},{17,25},{25,17},{2,10},{10... | collective-permute-start | bytes 294920 | tf_op jit(solution)/shard_map/ppermute | solution.py:297
  33.6 3.0 %collective-permute-done.4 = f32[192,128]{1,0:T(8,128)S(1)} collective-permute-done((f32[192,128]{1,0:T(8,128)S(1)}, f32[192,128]{1,0:T(8,128)S(1)}, u32[]{:S(2)}, u32[]{:S(2)}) %collective-permute-start.4) | collective-permute-done | bytes 98336 | tf_op jit(solution)/shard_map/ppermute | solution.py:297
  36.6 0.8 %collective-permute-start.5 = (f32[192,128]{1,0:T(8,128)S(1)}, f32[192,128]{1,0:T(8,128)S(1)}, u32[]{:S(2)}, u32[]{:S(2)}) collective-permute-start(f32[192,128]{1,0:T(8,128)S(1)} %add.24.a_ref), channel_id=1, source_target_pairs={{0,16},{8,24},{16,0},{24,8},{1,17},{9,25},{17,1},{25,9},{2,18},{10... | collective-permute-start | bytes 294920 | tf_op jit(solution)/shard_map/ppermute | solution.py:297
  37.4 0.0 collective-permute-done.7
  37.4 4.9 %collective-permute-done.5.b_ref = f32[192,128]{1,0:T(8,128)S(1)} collective-permute-done((f32[192,128]{1,0:T(8,128)S(1)}, f32[192,128]{1,0:T(8,128)S(1)}, u32[]{:S(2)}, u32[]{:S(2)}) %collective-permute-start.5) | collective-permute-done | bytes 98336 | tf_op jit(solution)/shard_map/ppermute | solution.py:297
  42.3 0.1 sums.1
  42.3 0.6 collective-permute-start.11
  42.9 1.2 %collective-permute-start.10 = (f32[8,128]{1,0:T(8,128)S(1)}, f32[8,128]{1,0:T(8,128)S(1)}, u32[]{:S(2)}, u32[]{:S(2)}) collective-permute-start(f32[8,128]{1,0:T(8,128)S(1)} %get-tuple-element.14), channel_id=1, source_target_pairs={{0,8},{8,0},{16,24},{24,16},{1,9},{9,1},{17,25},{25,17},{2,10},{10... | collective-permute-start | bytes 12296 | tf_op jit(solution)/shard_map/ppermute | solution.py:297
  44.1 0.2 collective-permute-start.9
  44.3 1.6 %collective-permute-start.8 = (f32[192,128]{1,0:T(8,128)S(1)}, f32[192,128]{1,0:T(8,128)S(1)}, u32[]{:S(2)}, u32[]{:S(2)}) collective-permute-start(f32[192,128]{1,0:T(8,128)S(1)} %get-tuple-element.13.mine_ref), channel_id=1, source_target_pairs={{0,8},{8,0},{16,24},{24,16},{1,9},{9,1},{17,25},{25,17},{2,10},{10... | collective-permute-start | bytes 294920 | tf_op jit(solution)/shard_map/ppermute | solution.py:297
  45.9 0.0 collective-permute-done.11
  45.9 0.7 collective-permute-done.10
  46.5 0.0 collective-permute-done.9
  46.5 3.1 %collective-permute-start.14 = (f32[8,128]{1,0:T(8,128)S(1)}, f32[8,128]{1,0:T(8,128)S(1)}, u32[]{:S(2)}, u32[]{:S(2)}) collective-permute-start(f32[8,128]{1,0:T(8,128)S(1)} %add_add_fusion.refs_0_), channel_id=1, source_target_pairs={{0,6},{1,7},{2,4},{3,5},{4,2},{5,3},{6,0},{7,1},{8,14},{9,15},{10,... | collective-permute-start | bytes 12296 | tf_op jit(solution)/shard_map/ppermute | solution.py:297
  49.6 0.0 collective-permute-start.13
  49.6 0.6 collective-permute-start.12
  50.3 0.9 %collective-permute-done.14.refs_3_ = f32[8,128]{1,0:T(8,128)S(1)} collective-permute-done((f32[8,128]{1,0:T(8,128)S(1)}, f32[8,128]{1,0:T(8,128)S(1)}, u32[]{:S(2)}, u32[]{:S(2)}) %collective-permute-start.14) | collective-permute-done | bytes 4128 | tf_op jit(solution)/shard_map/ppermute | solution.py:297
  51.2 2.0 %collective-permute-done.13.refs_2_ = f32[8,128]{1,0:T(8,128)S(1)} collective-permute-done((f32[8,128]{1,0:T(8,128)S(1)}, f32[8,128]{1,0:T(8,128)S(1)}, u32[]{:S(2)}, u32[]{:S(2)}) %collective-permute-start.13) | collective-permute-done | bytes 4128 | tf_op jit(solution)/shard_map/ppermute | solution.py:297
  53.2 0.0 collective-permute-done.12.refs_1_
  53.2 0.0 collective-permute-done.8.other_ref
  53.2 0.2 direction.1
  53.4 1.5 %collective-permute-start.17 = (bf16[384,128]{1,0:T(8,128)(2,1)S(1)}, bf16[384,128]{1,0:T(8,128)(2,1)S(1)}, u32[]{:S(2)}, u32[]{:S(2)}) collective-permute-start(bf16[384,128]{1,0:T(8,128)(2,1)S(1)} %get-tuple-element.17.refs_0_), channel_id=1, source_target_pairs={{0,6},{1,7},{2,4},{3,5},{4,2},{5,3},{6,0},{7,1},{8,14},{9,15},{10,... | collective-permute-start | bytes 294920 | tf_op jit(solution)/shard_map/ppermute | solution.py:297
  54.9 0.6 collective-permute-start.16
  55.6 1.4 %collective-permute-start.15 = (bf16[384,128]{1,0:T(8,128)(2,1)S(1)}, bf16[384,128]{1,0:T(8,128)(2,1)S(1)}, u32[]{:S(2)}, u32[]{:S(2)}) collective-permute-start(bf16[384,128]{1,0:T(8,128)(2,1)S(1)} %get-tuple-element.17.refs_0_), channel_id=1, source_target_pairs={{0,2},{1,3},{2,0},{3,1},{4,6},{5,7},{6,4},{7,5},{8,10},{9,11},{10,... | collective-permute-start | bytes 294920 | tf_op jit(solution)/shard_map/ppermute | solution.py:297
  57.0 2.1 %collective-permute-done.17.refs_3_ = bf16[384,128]{1,0:T(8,128)(2,1)S(1)} collective-permute-done((bf16[384,128]{1,0:T(8,128)(2,1)S(1)}, bf16[384,128]{1,0:T(8,128)(2,1)S(1)}, u32[]{:S(2)}, u32[]{:S(2)}) %collective-permute-start.17) | collective-permute-done | bytes 98336 | tf_op jit(solution)/shard_map/ppermute | solution.py:297
  59.0 1.0 %collective-permute-done.16.refs_2_ = bf16[384,128]{1,0:T(8,128)(2,1)S(1)} collective-permute-done((bf16[384,128]{1,0:T(8,128)(2,1)S(1)}, bf16[384,128]{1,0:T(8,128)(2,1)S(1)}, u32[]{:S(2)}, u32[]{:S(2)}) %collective-permute-start.16) | collective-permute-done | bytes 98336 | tf_op jit(solution)/shard_map/ppermute | solution.py:297
  60.1 0.6 collective-permute-done.15.refs_1_
  60.7 0.1 pad_maximum_fusion.1
  60.7 0.1 collective-permute-start.18
  60.8 0.6 unpack.1
  61.4 1.1 %collective-permute-done.18.refs_4_ = bf16[4,384,128]{2,1,0:T(8,128)(2,1)S(1)} collective-permute-done((bf16[4,384,128]{2,1,0:T(8,128)(2,1)S(1)}, bf16[4,384,128]{2,1,0:T(8,128)(2,1)S(1)}, u32[]{:S(2)}, u32[]{:S(2)}) %collective-permute-start.18) | collective-permute-done | bytes 393248 | tf_op jit(solution)/shard_map/ppermute | solution.py:297
  62.5 9.0 %backward.1 = f32[2,12,256,128]{3,2,1,0:T(8,128)} custom-call(s32[1,2]{1,0:T(1,128)S(1)} %bitcast.30, s32[32,128]{1,0:T(8,128)S(1)} %get-tuple-element.16.codes_in, bf16[10752,128]{1,0:T(8,128)(2,1)S(1)} %table.1.tab_ref, bf16[384,128]{1,0:T(8,128)(2,1)S(1)} %get-tuple-element.17.refs_0_, bf16[384,128]{1,0:T(8,128)(2,1)S(1)} %collective-permute-done.15.refs_1_, ...), custom_call_target="tpu_custom_call" | custom-call | tf_op jit(solution)/shard_map/backward/pallas_call | solution.py:413
  (9 shorter events, 0.2 us)
Async XLA Ops:
  0.6 1.2 %copy-start.3 = (s32[2,1]{0,1:T(1,128)S(1)}, s32[2,1]{0,1:T(1,128)}, u32[]{:S(2)}) copy-start(s32[2,1]{0,1:T(1,128)} %param.14) | copy-start | bytes 28
  0.6 1.2 %copy-start.8 = (s32[2,512]{1,0:T(2,128)S(1)}, s32[2,512]{1,0:T(2,128)}, u32[]{:S(2)}) copy-start(s32[2,512]{1,0:T(2,128)} %seed_ref.1) | copy-start | bytes 12292
  0.7 1.2 %copy-start.6 = (s32[2,512]{1,0:T(2,128)S(1)}, s32[2,512]{1,0:T(2,128)}, u32[]{:S(2)}) copy-start(s32[2,512]{1,0:T(2,128)} %target_ref.1) | copy-start | bytes 12292
  0.7 1.2 %copy-start.7 = (s32[2,512]{1,0:T(2,128)S(1)}, s32[2,512]{1,0:T(2,128)}, u32[]{:S(2)}) copy-start(s32[2,512]{1,0:T(2,128)} %source_ref.1) | copy-start | bytes 12292
  0.7 1.2 %copy-start.5 = (s32[2,512,1]{1,2,0:T(1,128)S(1)}, s32[2,512,1]{1,2,0:T(1,128)}, u32[]{:S(2)}) copy-start(s32[2,512,1]{1,2,0:T(1,128)} %param.10) | copy-start | bytes 12292
  0.7 1.4 %copy-start.4 = (bf16[2,12,256,128]{3,2,1,0:T(8,128)(2,1)S(1)}, bf16[2,12,256,128]{3,2,1,0:T(8,128)(2,1)}, u32[]{:S(2)}) copy-start(bf16[2,12,256,128]{3,2,1,0:T(8,128)(2,1)} %field_ref.1) | copy-start | bytes 4718596
  9.9 1.2 %copy-start = (f32[12,1,8,128]{3,2,1,0:T(8,128)S(1)}, f32[12,1,8,128]{3,2,1,0:T(8,128)}, u32[]{:S(2)}) copy-start(f32[12,1,8,128]{3,2,1,0:T(8,128)} %refs_0_.1) | copy-start | bytes 147460
  9.9 1.2 %copy-start.1 = (f32[12,1,8,128]{3,2,1,0:T(8,128)S(1)}, f32[12,1,8,128]{3,2,1,0:T(8,128)}, u32[]{:S(2)}) copy-start(f32[12,1,8,128]{3,2,1,0:T(8,128)} %refs_1_.1) | copy-start | bytes 147460
  9.9 1.2 %copy-start.2 = (f32[12,1,8,128]{3,2,1,0:T(8,128)S(1)}, f32[12,1,8,128]{3,2,1,0:T(8,128)}, u32[]{:S(2)}) copy-start(f32[12,1,8,128]{3,2,1,0:T(8,128)} %refs_2_.1) | copy-start | bytes 147460
  9.9 11.1 %collective-permute-start = (f32[4,384,128]{2,1,0:T(8,128)S(1)}, f32[4,384,128]{2,1,0:T(8,128)S(1)}, u32[]{:S(2)}, u32[]{:S(2)}) collective-permute-start(f32[4,384,128]{2,1,0:T(8,128)S(1)} %bitcast.32), channel_id=1, source_target_pairs={{0,1},{1,0},{2,3},{3,2},{4,5},{5,4},{6,7},{7,6},{8,9},{9,8},{10,11... | collective-permute-start | bytes 2359304 | tf_op jit(solution)/shard_map/ppermute | solution.py:297
  11.1 7.1 %collective-permute-start.6 = (f32[1,3,96,128]{3,2,1,0:T(8,128)S(1)}, f32[1,3,96,128]{3,2,1,0:T(8,128)S(1)}, u32[]{:S(2)}, u32[]{:S(2)}) collective-permute-start(f32[1,3,96,128]{3,2,1,0:T(8,128)S(1)} %bitcast.22), channel_id=1, source_target_pairs={{0,8},{8,0},{16,24},{24,16},{1,9},{9,1},{17,25},{25,17},{2,10},{10... | collective-permute-start | bytes 442376 | tf_op jit(solution)/shard_map/ppermute | solution.py:297
  18.2 19.1 %collective-permute-start.7 = (f32[2,3,96,128]{3,2,1,0:T(8,128)S(1)}, f32[2,3,96,128]{3,2,1,0:T(8,128)S(1)}, u32[]{:S(2)}, u32[]{:S(2)}) collective-permute-start(f32[2,3,96,128]{3,2,1,0:T(8,128)S(1)} %pad_maximum_fusion.2), channel_id=1, source_target_pairs={{0,16},{8,24},{16,0},{24,8},{1,17},{9,25},{17,1},{25,9},{2,18},{10... | collective-permute-start | bytes 884744 | tf_op jit(solution)/shard_map/ppermute | solution.py:297
  21.2 8.6 %collective-permute-start.3 = (f32[384,128]{1,0:T(8,128)S(1)}, f32[384,128]{1,0:T(8,128)S(1)}, u32[]{:S(2)}, u32[]{:S(2)}) collective-permute-start(f32[384,128]{1,0:T(8,128)S(1)} %get-tuple-element.18), channel_id=1, source_target_pairs={{0,6},{1,7},{2,4},{3,5},{4,2},{5,3},{6,0},{7,1},{8,14},{9,15},{10,... | collective-permute-start | bytes 589832 | tf_op jit(solution)/shard_map/ppermute | solution.py:297
  23.7 8.2 %collective-permute-start.2 = (f32[384,128]{1,0:T(8,128)S(1)}, f32[384,128]{1,0:T(8,128)S(1)}, u32[]{:S(2)}, u32[]{:S(2)}) collective-permute-start(f32[384,128]{1,0:T(8,128)S(1)} %get-tuple-element.19), channel_id=1, source_target_pairs={{0,4},{1,5},{2,6},{3,7},{4,0},{5,1},{6,2},{7,3},{8,12},{9,13},{10,... | collective-permute-start | bytes 589832 | tf_op jit(solution)/shard_map/ppermute | solution.py:297
  24.1 7.8 %collective-permute-start.1 = (f32[384,128]{1,0:T(8,128)S(1)}, f32[384,128]{1,0:T(8,128)S(1)}, u32[]{:S(2)}, u32[]{:S(2)}) collective-permute-start(f32[384,128]{1,0:T(8,128)S(1)} %get-tuple-element.20), channel_id=1, source_target_pairs={{0,2},{1,3},{2,0},{3,1},{4,6},{5,7},{6,4},{7,5},{8,10},{9,11},{10,... | collective-permute-start | bytes 589832 | tf_op jit(solution)/shard_map/ppermute | solution.py:297
  31.9 4.7 %collective-permute-start.4 = (f32[192,128]{1,0:T(8,128)S(1)}, f32[192,128]{1,0:T(8,128)S(1)}, u32[]{:S(2)}, u32[]{:S(2)}) collective-permute-start(f32[192,128]{1,0:T(8,128)S(1)} %get-tuple-element.12), channel_id=1, source_target_pairs={{0,8},{8,0},{16,24},{24,16},{1,9},{9,1},{17,25},{25,17},{2,10},{10... | collective-permute-start | bytes 294920 | tf_op jit(solution)/shard_map/ppermute | solution.py:297
  36.6 5.7 %collective-permute-start.5 = (f32[192,128]{1,0:T(8,128)S(1)}, f32[192,128]{1,0:T(8,128)S(1)}, u32[]{:S(2)}, u32[]{:S(2)}) collective-permute-start(f32[192,128]{1,0:T(8,128)S(1)} %add.24.a_ref), channel_id=1, source_target_pairs={{0,16},{8,24},{16,0},{24,8},{1,17},{9,25},{17,1},{25,9},{2,18},{10... | collective-permute-start | bytes 294920 | tf_op jit(solution)/shard_map/ppermute | solution.py:297
  42.3 3.5 %collective-permute-start.11 = (f32[8,128]{1,0:T(8,128)S(1)}, f32[8,128]{1,0:T(8,128)S(1)}, u32[]{:S(2)}, u32[]{:S(2)}) collective-permute-start(f32[8,128]{1,0:T(8,128)S(1)} %get-tuple-element.14), channel_id=1, source_target_pairs={{0,9},{1,8},{2,11},{3,10},{4,13},{5,12},{6,15},{7,14},{8,1},{9,0},... | collective-permute-start | bytes 12296 | tf_op jit(solution)/shard_map/ppermute | solution.py:384
  42.9 3.6 %collective-permute-start.10 = (f32[8,128]{1,0:T(8,128)S(1)}, f32[8,128]{1,0:T(8,128)S(1)}, u32[]{:S(2)}, u32[]{:S(2)}) collective-permute-start(f32[8,128]{1,0:T(8,128)S(1)} %get-tuple-element.14), channel_id=1, source_target_pairs={{0,8},{8,0},{16,24},{24,16},{1,9},{9,1},{17,25},{25,17},{2,10},{10... | collective-permute-start | bytes 12296 | tf_op jit(solution)/shard_map/ppermute | solution.py:297
  44.1 2.5 %collective-permute-start.9 = (f32[8,128]{1,0:T(8,128)S(1)}, f32[8,128]{1,0:T(8,128)S(1)}, u32[]{:S(2)}, u32[]{:S(2)}) collective-permute-start(f32[8,128]{1,0:T(8,128)S(1)} %get-tuple-element.14), channel_id=1, source_target_pairs={{0,1},{1,0},{2,3},{3,2},{4,5},{5,4},{6,7},{7,6},{8,9},{9,8},{10,11... | collective-permute-start | bytes 12296 | tf_op jit(solution)/shard_map/ppermute | solution.py:297
  44.3 9.0 %collective-permute-start.8 = (f32[192,128]{1,0:T(8,128)S(1)}, f32[192,128]{1,0:T(8,128)S(1)}, u32[]{:S(2)}, u32[]{:S(2)}) collective-permute-start(f32[192,128]{1,0:T(8,128)S(1)} %get-tuple-element.13.mine_ref), channel_id=1, source_target_pairs={{0,8},{8,0},{16,24},{24,16},{1,9},{9,1},{17,25},{25,17},{2,10},{10... | collective-permute-start | bytes 294920 | tf_op jit(solution)/shard_map/ppermute | solution.py:297
  46.5 4.7 %collective-permute-start.14 = (f32[8,128]{1,0:T(8,128)S(1)}, f32[8,128]{1,0:T(8,128)S(1)}, u32[]{:S(2)}, u32[]{:S(2)}) collective-permute-start(f32[8,128]{1,0:T(8,128)S(1)} %add_add_fusion.refs_0_), channel_id=1, source_target_pairs={{0,6},{1,7},{2,4},{3,5},{4,2},{5,3},{6,0},{7,1},{8,14},{9,15},{10,... | collective-permute-start | bytes 12296 | tf_op jit(solution)/shard_map/ppermute | solution.py:297
  49.6 3.6 %collective-permute-start.13 = (f32[8,128]{1,0:T(8,128)S(1)}, f32[8,128]{1,0:T(8,128)S(1)}, u32[]{:S(2)}, u32[]{:S(2)}) collective-permute-start(f32[8,128]{1,0:T(8,128)S(1)} %add_add_fusion.refs_0_), channel_id=1, source_target_pairs={{0,4},{1,5},{2,6},{3,7},{4,0},{5,1},{6,2},{7,3},{8,12},{9,13},{10,... | collective-permute-start | bytes 12296 | tf_op jit(solution)/shard_map/ppermute | solution.py:297
  49.6 3.6 %collective-permute-start.12 = (f32[8,128]{1,0:T(8,128)S(1)}, f32[8,128]{1,0:T(8,128)S(1)}, u32[]{:S(2)}, u32[]{:S(2)}) collective-permute-start(f32[8,128]{1,0:T(8,128)S(1)} %add_add_fusion.refs_0_), channel_id=1, source_target_pairs={{0,2},{1,3},{2,0},{3,1},{4,6},{5,7},{6,4},{7,5},{8,10},{9,11},{10,... | collective-permute-start | bytes 12296 | tf_op jit(solution)/shard_map/ppermute | solution.py:297
  53.4 5.6 %collective-permute-start.17 = (bf16[384,128]{1,0:T(8,128)(2,1)S(1)}, bf16[384,128]{1,0:T(8,128)(2,1)S(1)}, u32[]{:S(2)}, u32[]{:S(2)}) collective-permute-start(bf16[384,128]{1,0:T(8,128)(2,1)S(1)} %get-tuple-element.17.refs_0_), channel_id=1, source_target_pairs={{0,6},{1,7},{2,4},{3,5},{4,2},{5,3},{6,0},{7,1},{8,14},{9,15},{10,... | collective-permute-start | bytes 294920 | tf_op jit(solution)/shard_map/ppermute | solution.py:297
  54.9 5.1 %collective-permute-start.16 = (bf16[384,128]{1,0:T(8,128)(2,1)S(1)}, bf16[384,128]{1,0:T(8,128)(2,1)S(1)}, u32[]{:S(2)}, u32[]{:S(2)}) collective-permute-start(bf16[384,128]{1,0:T(8,128)(2,1)S(1)} %get-tuple-element.17.refs_0_), channel_id=1, source_target_pairs={{0,4},{1,5},{2,6},{3,7},{4,0},{5,1},{6,2},{7,3},{8,12},{9,13},{10,... | collective-permute-start | bytes 294920 | tf_op jit(solution)/shard_map/ppermute | solution.py:297
  55.6 5.1 %collective-permute-start.15 = (bf16[384,128]{1,0:T(8,128)(2,1)S(1)}, bf16[384,128]{1,0:T(8,128)(2,1)S(1)}, u32[]{:S(2)}, u32[]{:S(2)}) collective-permute-start(bf16[384,128]{1,0:T(8,128)(2,1)S(1)} %get-tuple-element.17.refs_0_), channel_id=1, source_target_pairs={{0,2},{1,3},{2,0},{3,1},{4,6},{5,7},{6,4},{7,5},{8,10},{9,11},{10,... | collective-permute-start | bytes 294920 | tf_op jit(solution)/shard_map/ppermute | solution.py:297
  60.7 1.8 %collective-permute-start.18 = (bf16[4,384,128]{2,1,0:T(8,128)(2,1)S(1)}, bf16[4,384,128]{2,1,0:T(8,128)(2,1)S(1)}, u32[]{:S(2)}, u32[]{:S(2)}) collective-permute-start(bf16[4,384,128]{2,1,0:T(8,128)(2,1)S(1)} %pad_maximum_fusion.1), channel_id=1, source_target_pairs={{0,1},{1,0},{2,3},{3,2},{4,5},{5,4},{6,7},{7,6},{8,9},{9,8},{10,11... | collective-permute-start | bytes 1179656 | tf_op jit(solution)/shard_map/ppermute | solution.py:297

commit v10 on v9

--- a/solution.py
+++ b/solution.py
@@ -51,6 +51,10 @@
     lax.fori_loop(0, SPREADS, one, 0)
 
 
+def turn(j, half):
+    return (j & ~3) | ((j & 1) << 1) | ((j >> 1) & 1) if half > 2 else j
+
+
 def fill_codes(dims, counts, owner_ref, target_ref, source_ref, seed_ref, codes_ref):
     events, comps, eblocks, nodes = dims["field"]
     half, subs, blocks = dims["half"], dims["subs"], dims["blocks"]
@@ -63,7 +67,8 @@
             at = pl.ds(g * LANES, LANES)
             live = lane + g * LANES < counts[v]
             r = owner_ref[v, :, at] ^ me
-            slot = ((r & 1) * half + (r >> 1)) * subs + target_ref[pl.ds(v, 1), at]
+            place = jnp.where(((r ^ me) & 1) == 1, turn(r >> 1, half), r >> 1)
+            slot = ((r & 1) * half + place) * subs + target_ref[pl.ds(v, 1), at]
             source = source_ref[pl.ds(v, 1), at] + v * eblocks
             seed = seed_ref[pl.ds(v, 1), at]
             turned = 2 * OFFSETS * ((seed * 9363) >> 16) - seed + (OFFSETS - 1)
@@ -184,6 +189,16 @@
 
 def fold_kernel(a_ref, b_ref, out_ref):
     out_ref[...] = a_ref[...] + b_ref[...]
+
+
+def add_kernel_call(a, b):
+    return pl.pallas_call(
+        fold_kernel,
+        out_shape=f32(*a.shape),
+        in_specs=[in_vmem()] * 2,
+        out_specs=in_vmem(),
+        compiler_params=limit(2),
+    )(a, b)
 
 
 def merge_kernel(*refs):
@@ -314,6 +329,10 @@
     hist = packed[None]
     for bit in range(evs.bit_length() - 1):
         hist = jnp.concatenate([hist, swap(hist, "ev", 1 << bit)], axis=0)
+
+    def along(x, j):
+        pairs = [(i, i ^ 2 * (turn(j, half) if i & 1 else j)) for i in range(parts)]
+        return lax.ppermute(x, "mesh", pairs)
 
     tab = pl.pallas_call(
         functools.partial(table_kernel, nodes),
@@ -346,22 +365,24 @@
     send = sums[half * part_rows : 2 * half * part_rows].reshape(half, part_rows, nodes)
     got = swap(send, "mesh", 1)
     held = [None] + [keep[j] + got[j] for j in range(1, half)]
+    for h in range(4, half, 4):
+        far = swap(jnp.stack(held[h : h + 4]), "mesh", 2 * h)
+        held[1:4] = [held[j] + far[j] for j in range(1, 4)]
+        keep = keep.at[0].add(far[0])
     arrived = []
-    for j in range(1, half):
-        arrived.append(swap(held[j], "mesh", 2 * j))
-    total = pl.pallas_call(
-        fold_kernel,
-        out_shape=f32(part_rows, nodes),
-        in_specs=[in_vmem()] * 2,
-        out_specs=in_vmem(),
-        compiler_params=limit(2),
-        name="fold",
-    )(keep[0], got[0])
+    if half > 2:
+        corner = along(held[3], 1)
+        arrived.append(along(held[1], 1))
+        relay = add_kernel_call(held[2], corner)
+        arrived.append(along(relay, 2))
+    else:
+        arrived += [along(held[j], j) for j in range(1, half)]
+    total = add_kernel_call(keep[0], got[0])
     half_rows = part_rows // 2
     stay, go = pl.pallas_call(
         merge_kernel,
         out_shape=[f32(half_rows, nodes)] * 2,
-        in_specs=[in_vmem()] * half,
+        in_specs=[in_vmem()] * (1 + len(arrived)),
         out_specs=[in_vmem()] * 2,
         compiler_params=limit(4),
         name="merge",
@@ -407,7 +428,7 @@
 
     mine = [rounded]
     for j in range(1, half):
-        mine.append(swap(rounded, "mesh", 2 * j))
+        mine.append(along(rounded, j))
     other = swap(jnp.stack(mine), "mesh", 1)
 
     event_direction = pl.pallas_call(

time: 71.9 us -> 72.2 us (level)
    ppermute x0 -> x6, starting transfers between devices: none -> 8 us  [along(): return lax.ppermute(x, 'mesh', pairs)]
    ppermute x18 -> x12, waiting for transfers between devices: 27.1 us -> 19.5 us  [swap(): return lax.ppermute(x, axis, [(i, i ^ k) for i in range(size)])]
    ppermute x18 -> x12, starting transfers between devices: 23.5 us -> 16.1 us  [swap(): return lax.ppermute(x, axis, [(i, i ^ k) for i in range(size)])]
    ppermute x0 -> x6, waiting for transfers between devices: none -> 7.02 us  [along(): return lax.ppermute(x, 'mesh', pairs)]
    ppermute x1, waiting for transfers between devices: 0.01 us -> 0.89 us  [body(): by_both = lax.ppermute(local, ('ev', 'mesh'), across_both)]
  transfers between devices with their start and end apart: 19 -> 19, of which waited for: 12 -> 13; matrix products, arithmetic and copies ran while one was open for 0% -> 0% of each run, Pallas kernels for 1% -> 1%
where the time goes in v10:
time: 72.2 us; the launch traced here: 71.8 us
  waiting for transfers between devices  27.4 us (38%)
  starting transfers between devices  24.1 us (33%)
  Pallas kernels  18.9 us (26%)
  between operations  0.85 us (1%)
    ppermute x12, waiting for transfers between devices, swap(): return lax.ppermute(x, axis, [(i, i ^ k) for i in range(size)])  19.5 us
    ppermute x12, starting transfers between devices, swap(): return lax.ppermute(x, axis, [(i, i ^ k) for i in range(size)])  16.1 us
    pallas_call x1, Pallas kernels, body(): pl.pallas_call(functools.partial(backward_kernel, dims), out_shape=f32(*k...  9.04 us
    ppermute x6, starting transfers between devices, along(): return lax.ppermute(x, 'mesh', pairs)  8 us
    pallas_call x1, Pallas kernels, body(): pl.pallas_call(functools.partial(forward_kernel, dims), out_shape=[f32(bl...  7.74 us
    ppermute x6, waiting for transfers between devices, along(): return lax.ppermute(x, 'mesh', pairs)  7.02 us
  transfers between devices with their start and end apart: 19, of which 13 were waited for; matrix products, arithmetic and copies ran while one was open for 0% of the time, Pallas kernels for 1%

profile of v10, /device:TPU:0, one launch (start us, length us, event | category | flops | bytes accessed | tf_op | source)
XLA Modules:
  0.0 71.8 jit_solution(401148346791905564)
XLA Ops:
  0.6 0.0 copy-start.3
  0.6 0.0 copy-start.8
  0.7 0.0 copy-start.6
  0.7 0.0 copy-start.7
  0.7 0.0 copy-start.5
  0.7 0.0 copy-start.4
  0.7 1.2 %table.1.tab_ref = bf16[10752,128]{1,0:T(8,128)(2,1)S(1)} custom-call(), custom_call_target="tpu_custom_call" | custom-call | flops 268435456 | bytes 4194304 | tf_op jit(solution)/shard_map/table/pallas_call | solution.py:337
  1.9 0.0 copy-done.3
  1.9 0.0 copy-done.8
  1.9 0.0 copy-done.6
  1.9 0.0 copy-done.7
  1.9 0.0 copy-done.5
  1.9 0.2 copy-done.4
  2.1 7.7 %forward.1 = (f32[3088,128]{1,0:T(8,128)S(1)}, s32[32,128]{1,0:T(8,128)S(1)}) custom-call(s32[1,2]{1,0:T(1,128)S(1)} %bitcast.29, s32[2,1,512]{2,1,0:T(1,128)S(1)} %bitcast.31, s32[2,512]{1,0:T(2,128)S(1)} %copy-done.6, s32[2,512]{1,0:T(2,128)S(1)} %copy-done.7, s32[2,512]{1,0:T(2,128)S(1)} %copy-done.8, bf16[2,12,256,128]{3,2,1,0:T(8,128)(2,1)S(1)} %copy-done.4, ...), custom_call_target="tpu_custom_call" | custom-call | flops 34359738368 | bytes 16777216 | tf_op jit(solution)/shard_map/forward/pallas_call | solution.py:345
  9.9 0.0 copy-start
  9.9 0.0 copy-start.1
  9.9 0.0 copy-start.2
  9.9 0.1 slice.37
  10.0 1.1 %collective-permute-start = (f32[4,384,128]{2,1,0:T(8,128)S(1)}, f32[4,384,128]{2,1,0:T(8,128)S(1)}, u32[]{:S(2)}, u32[]{:S(2)}) collective-permute-start(f32[4,384,128]{2,1,0:T(8,128)S(1)} %bitcast.32), channel_id=1, source_target_pairs={{0,1},{1,0},{2,3},{3,2},{4,5},{5,4},{6,7},{7,6},{8,9},{9,8},{10,11... | collective-permute-start | bytes 2359304 | tf_op jit(solution)/shard_map/ppermute | solution.py:312
  11.0 0.0 copy-done
  11.0 0.0 copy-done.1
  11.1 3.3 %collective-permute-start.6 = (f32[1,3,96,128]{3,2,1,0:T(8,128)S(1)}, f32[1,3,96,128]{3,2,1,0:T(8,128)S(1)}, u32[]{:S(2)}, u32[]{:S(2)}) collective-permute-start(f32[1,3,96,128]{3,2,1,0:T(8,128)S(1)} %bitcast.22), channel_id=1, source_target_pairs={{0,8},{8,0},{16,24},{24,16},{1,9},{9,1},{17,25},{25,17},{2,10},{10... | collective-permute-start | bytes 442376 | tf_op jit(solution)/shard_map/ppermute | solution.py:312
  14.4 0.0 collective-permute-done
  14.4 0.1 fusion
  14.5 1.4 %collective-permute-start.2 = (f32[384,128]{1,0:T(8,128)S(1)}, f32[384,128]{1,0:T(8,128)S(1)}, u32[]{:S(2)}, u32[]{:S(2)}) collective-permute-start(f32[384,128]{1,0:T(8,128)S(1)} %get-tuple-element.18), channel_id=1, source_target_pairs={{0,2},{1,5},{2,0},{3,7},{4,6},{5,1},{6,4},{7,3},{8,10},{9,13},{10,... | collective-permute-start | bytes 589832 | tf_op jit(solution)/shard_map/ppermute | solution.py:335
  15.9 2.3 %collective-permute-done.6 = f32[1,3,96,128]{3,2,1,0:T(8,128)S(1)} collective-permute-done((f32[1,3,96,128]{3,2,1,0:T(8,128)S(1)}, f32[1,3,96,128]{3,2,1,0:T(8,128)S(1)}, u32[]{:S(2)}, u32[]{:S(2)}) %collective-permute-start.6) | collective-permute-done | bytes 147488 | tf_op jit(solution)/shard_map/ppermute | solution.py:312
  18.3 2.8 %collective-permute-start.7 = (f32[2,3,96,128]{3,2,1,0:T(8,128)S(1)}, f32[2,3,96,128]{3,2,1,0:T(8,128)S(1)}, u32[]{:S(2)}, u32[]{:S(2)}) collective-permute-start(f32[2,3,96,128]{3,2,1,0:T(8,128)S(1)} %pad_maximum_fusion.2), channel_id=1, source_target_pairs={{0,16},{8,24},{16,0},{24,8},{1,17},{9,25},{17,1},{25,9},{2,18},{10... | collective-permute-start | bytes 884744 | tf_op jit(solution)/shard_map/ppermute | solution.py:312
  21.1 1.4 %collective-permute-start.1 = (f32[384,128]{1,0:T(8,128)S(1)}, f32[384,128]{1,0:T(8,128)S(1)}, u32[]{:S(2)}, u32[]{:S(2)}) collective-permute-start(f32[384,128]{1,0:T(8,128)S(1)} %get-tuple-element.20), channel_id=1, source_target_pairs={{0,2},{1,5},{2,0},{3,7},{4,6},{5,1},{6,4},{7,3},{8,10},{9,13},{10,... | collective-permute-start | bytes 589832 | tf_op jit(solution)/shard_map/ppermute | solution.py:335
  22.5 0.0 collective-permute-done.2.b_ref
  22.5 1.7 %collective-permute-start.3 = (f32[384,128]{1,0:T(8,128)S(1)}, f32[384,128]{1,0:T(8,128)S(1)}, u32[]{:S(2)}, u32[]{:S(2)}) collective-permute-start(f32[384,128]{1,0:T(8,128)S(1)} %shard_map.105), channel_id=1, source_target_pairs={{0,4},{1,3},{2,6},{3,1},{4,0},{5,7},{6,2},{7,5},{8,12},{9,11},{10,... | collective-permute-start | bytes 589832 | tf_op jit(solution)/shard_map/ppermute | solution.py:335
  24.2 3.4 %collective-permute-done.1.refs_1_ = f32[384,128]{1,0:T(8,128)S(1)} collective-permute-done((f32[384,128]{1,0:T(8,128)S(1)}, f32[384,128]{1,0:T(8,128)S(1)}, u32[]{:S(2)}, u32[]{:S(2)}) %collective-permute-start.1) | collective-permute-done | bytes 196640 | tf_op jit(solution)/shard_map/ppermute | solution.py:335
  27.7 0.6 collective-permute-done.3.refs_2_
  28.3 1.5 %collective-permute-start.4 = (f32[192,128]{1,0:T(8,128)S(1)}, f32[192,128]{1,0:T(8,128)S(1)}, u32[]{:S(2)}, u32[]{:S(2)}) collective-permute-start(f32[192,128]{1,0:T(8,128)S(1)} %get-tuple-element.12), channel_id=1, source_target_pairs={{0,8},{8,0},{16,24},{24,16},{1,9},{9,1},{17,25},{25,17},{2,10},{10... | collective-permute-start | bytes 294920 | tf_op jit(solution)/shard_map/ppermute | solution.py:312
  29.8 6.0 %collective-permute-done.4 = f32[192,128]{1,0:T(8,128)S(1)} collective-permute-done((f32[192,128]{1,0:T(8,128)S(1)}, f32[192,128]{1,0:T(8,128)S(1)}, u32[]{:S(2)}, u32[]{:S(2)}) %collective-permute-start.4) | collective-permute-done | bytes 98336 | tf_op jit(solution)/shard_map/ppermute | solution.py:312
  35.8 1.5 %collective-permute-start.5 = (f32[192,128]{1,0:T(8,128)S(1)}, f32[192,128]{1,0:T(8,128)S(1)}, u32[]{:S(2)}, u32[]{:S(2)}) collective-permute-start(f32[192,128]{1,0:T(8,128)S(1)} %add.24.a_ref), channel_id=1, source_target_pairs={{0,16},{8,24},{16,0},{24,8},{1,17},{9,25},{17,1},{25,9},{2,18},{10... | collective-permute-start | bytes 294920 | tf_op jit(solution)/shard_map/ppermute | solution.py:312
  37.4 0.0 collective-permute-done.7
  37.4 6.2 %collective-permute-done.5.b_ref = f32[192,128]{1,0:T(8,128)S(1)} collective-permute-done((f32[192,128]{1,0:T(8,128)S(1)}, f32[192,128]{1,0:T(8,128)S(1)}, u32[]{:S(2)}, u32[]{:S(2)}) %collective-permute-start.5) | collective-permute-done | bytes 98336 | tf_op jit(solution)/shard_map/ppermute | solution.py:312
  43.6 0.1 sums.1
  43.7 0.1 collective-permute-start.11
  43.8 0.9 %collective-permute-start.10 = (f32[8,128]{1,0:T(8,128)S(1)}, f32[8,128]{1,0:T(8,128)S(1)}, u32[]{:S(2)}, u32[]{:S(2)}) collective-permute-start(f32[8,128]{1,0:T(8,128)S(1)} %get-tuple-element.14), channel_id=1, source_target_pairs={{0,8},{8,0},{16,24},{24,16},{1,9},{9,1},{17,25},{25,17},{2,10},{10... | collective-permute-start | bytes 12296 | tf_op jit(solution)/shard_map/ppermute | solution.py:312
  44.6 1.0 %collective-permute-start.9 = (f32[8,128]{1,0:T(8,128)S(1)}, f32[8,128]{1,0:T(8,128)S(1)}, u32[]{:S(2)}, u32[]{:S(2)}) collective-permute-start(f32[8,128]{1,0:T(8,128)S(1)} %get-tuple-element.14), channel_id=1, source_target_pairs={{0,1},{1,0},{2,3},{3,2},{4,5},{5,4},{6,7},{7,6},{8,9},{9,8},{10,11... | collective-permute-start | bytes 12296 | tf_op jit(solution)/shard_map/ppermute | solution.py:312
  45.6 0.3 collective-permute-start.8
  45.9 0.9 %collective-permute-done.11 = f32[8,128]{1,0:T(8,128)S(1)} collective-permute-done((f32[8,128]{1,0:T(8,128)S(1)}, f32[8,128]{1,0:T(8,128)S(1)}, u32[]{:S(2)}, u32[]{:S(2)}) %collective-permute-start.11) | collective-permute-done | bytes 4128 | tf_op jit(solution)/shard_map/ppermute | solution.py:405
  46.8 0.7 collective-permute-done.10
  47.4 0.0 collective-permute-done.9
  47.4 2.0 %collective-permute-start.14 = (f32[8,128]{1,0:T(8,128)S(1)}, f32[8,128]{1,0:T(8,128)S(1)}, u32[]{:S(2)}, u32[]{:S(2)}) collective-permute-start(f32[8,128]{1,0:T(8,128)S(1)} %add_add_fusion.refs_0_), channel_id=1, source_target_pairs={{0,6},{1,7},{2,4},{3,5},{4,2},{5,3},{6,0},{7,1},{8,14},{9,15},{10,... | collective-permute-start | bytes 12296 | tf_op jit(solution)/shard_map/ppermute | solution.py:312
  49.4 1.2 %collective-permute-start.13 = (f32[8,128]{1,0:T(8,128)S(1)}, f32[8,128]{1,0:T(8,128)S(1)}, u32[]{:S(2)}, u32[]{:S(2)}) collective-permute-start(f32[8,128]{1,0:T(8,128)S(1)} %add_add_fusion.refs_0_), channel_id=1, source_target_pairs={{0,4},{1,5},{2,6},{3,7},{4,0},{5,1},{6,2},{7,3},{8,12},{9,13},{10,... | collective-permute-start | bytes 12296 | tf_op jit(solution)/shard_map/ppermute | solution.py:312
  50.6 0.4 collective-permute-start.12
  51.0 1.0 %collective-permute-done.14.refs_3_ = f32[8,128]{1,0:T(8,128)S(1)} collective-permute-done((f32[8,128]{1,0:T(8,128)S(1)}, f32[8,128]{1,0:T(8,128)S(1)}, u32[]{:S(2)}, u32[]{:S(2)}) %collective-permute-start.14) | collective-permute-done | bytes 4128 | tf_op jit(solution)/shard_map/ppermute | solution.py:312
  52.0 1.0 %collective-permute-done.13.refs_2_ = f32[8,128]{1,0:T(8,128)S(1)} collective-permute-done((f32[8,128]{1,0:T(8,128)S(1)}, f32[8,128]{1,0:T(8,128)S(1)}, u32[]{:S(2)}, u32[]{:S(2)}) %collective-permute-start.13) | collective-permute-done | bytes 4128 | tf_op jit(solution)/shard_map/ppermute | solution.py:312
  53.0 1.2 %collective-permute-done.12.refs_1_ = f32[8,128]{1,0:T(8,128)S(1)} collective-permute-done((f32[8,128]{1,0:T(8,128)S(1)}, f32[8,128]{1,0:T(8,128)S(1)}, u32[]{:S(2)}, u32[]{:S(2)}) %collective-permute-start.12) | collective-permute-done | bytes 4128 | tf_op jit(solution)/shard_map/ppermute | solution.py:312
  54.2 0.0 collective-permute-done.8.other_ref
  54.2 0.2 direction.1
  54.4 0.9 %collective-permute-start.17 = (bf16[384,128]{1,0:T(8,128)(2,1)S(1)}, bf16[384,128]{1,0:T(8,128)(2,1)S(1)}, u32[]{:S(2)}, u32[]{:S(2)}) collective-permute-start(bf16[384,128]{1,0:T(8,128)(2,1)S(1)} %get-tuple-element.17.refs_0_), channel_id=1, source_target_pairs={{0,6},{1,7},{2,4},{3,5},{4,2},{5,3},{6,0},{7,1},{8,14},{9,15},{10,... | collective-permute-start | bytes 294920 | tf_op jit(solution)/shard_map/ppermute | solution.py:335
  55.3 1.1 %collective-permute-start.16 = (bf16[384,128]{1,0:T(8,128)(2,1)S(1)}, bf16[384,128]{1,0:T(8,128)(2,1)S(1)}, u32[]{:S(2)}, u32[]{:S(2)}) collective-permute-start(bf16[384,128]{1,0:T(8,128)(2,1)S(1)} %get-tuple-element.17.refs_0_), channel_id=1, source_target_pairs={{0,4},{1,3},{2,6},{3,1},{4,0},{5,7},{6,2},{7,5},{8,12},{9,11},{10,... | collective-permute-start | bytes 294920 | tf_op jit(solution)/shard_map/ppermute | solution.py:335
  56.3 1.6 %collective-permute-start.15 = (bf16[384,128]{1,0:T(8,128)(2,1)S(1)}, bf16[384,128]{1,0:T(8,128)(2,1)S(1)}, u32[]{:S(2)}, u32[]{:S(2)}) collective-permute-start(bf16[384,128]{1,0:T(8,128)(2,1)S(1)} %get-tuple-element.17.refs_0_), channel_id=1, source_target_pairs={{0,2},{1,5},{2,0},{3,7},{4,6},{5,1},{6,4},{7,3},{8,10},{9,13},{10,... | collective-permute-start | bytes 294920 | tf_op jit(solution)/shard_map/ppermute | solution.py:335
  58.0 2.1 %collective-permute-done.17.refs_3_ = bf16[384,128]{1,0:T(8,128)(2,1)S(1)} collective-permute-done((bf16[384,128]{1,0:T(8,128)(2,1)S(1)}, bf16[384,128]{1,0:T(8,128)(2,1)S(1)}, u32[]{:S(2)}, u32[]{:S(2)}) %collective-permute-start.17) | collective-permute-done | bytes 98336 | tf_op jit(solution)/shard_map/ppermute | solution.py:335
  60.1 0.8 %collective-permute-done.16.refs_2_ = bf16[384,128]{1,0:T(8,128)(2,1)S(1)} collective-permute-done((bf16[384,128]{1,0:T(8,128)(2,1)S(1)}, bf16[384,128]{1,0:T(8,128)(2,1)S(1)}, u32[]{:S(2)}, u32[]{:S(2)}) %collective-permute-start.16) | collective-permute-done | bytes 98336 | tf_op jit(solution)/shard_map/ppermute | solution.py:335
  60.9 0.0 collective-permute-done.15.refs_1_
  60.9 0.1 pad_maximum_fusion.1
  61.0 0.1 collective-permute-start.18
  61.1 0.6 unpack.1
  61.7 1.1 %collective-permute-done.18.refs_4_ = bf16[4,384,128]{2,1,0:T(8,128)(2,1)S(1)} collective-permute-done((bf16[4,384,128]{2,1,0:T(8,128)(2,1)S(1)}, bf16[4,384,128]{2,1,0:T(8,128)(2,1)S(1)}, u32[]{:S(2)}, u32[]{:S(2)}) %collective-permute-start.18) | collective-permute-done | bytes 393248 | tf_op jit(solution)/shard_map/ppermute | solution.py:312
  62.8 9.0 %backward.1 = f32[2,12,256,128]{3,2,1,0:T(8,128)} custom-call(s32[1,2]{1,0:T(1,128)S(1)} %bitcast.30, s32[32,128]{1,0:T(8,128)S(1)} %get-tuple-element.16.codes_in, bf16[10752,128]{1,0:T(8,128)(2,1)S(1)} %table.1.tab_ref, bf16[384,128]{1,0:T(8,128)(2,1)S(1)} %get-tuple-element.17.refs_0_, bf16[384,128]{1,0:T(8,128)(2,1)S(1)} %collective-permute-done.15.refs_1_, ...), custom_call_target="tpu_custom_call" | custom-call | tf_op jit(solution)/shard_map/backward/pallas_call | solution.py:434
  (10 shorter events, 0.2 us)
Async XLA Ops:
  0.6 1.2 %copy-start.3 = (s32[2,1]{0,1:T(1,128)S(1)}, s32[2,1]{0,1:T(1,128)}, u32[]{:S(2)}) copy-start(s32[2,1]{0,1:T(1,128)} %param.14) | copy-start | bytes 28
  0.6 1.2 %copy-start.8 = (s32[2,512]{1,0:T(2,128)S(1)}, s32[2,512]{1,0:T(2,128)}, u32[]{:S(2)}) copy-start(s32[2,512]{1,0:T(2,128)} %seed_ref.1) | copy-start | bytes 12292
  0.7 1.2 %copy-start.6 = (s32[2,512]{1,0:T(2,128)S(1)}, s32[2,512]{1,0:T(2,128)}, u32[]{:S(2)}) copy-start(s32[2,512]{1,0:T(2,128)} %target_ref.1) | copy-start | bytes 12292
  0.7 1.2 %copy-start.7 = (s32[2,512]{1,0:T(2,128)S(1)}, s32[2,512]{1,0:T(2,128)}, u32[]{:S(2)}) copy-start(s32[2,512]{1,0:T(2,128)} %source_ref.1) | copy-start | bytes 12292
  0.7 1.2 %copy-start.5 = (s32[2,512,1]{1,2,0:T(1,128)S(1)}, s32[2,512,1]{1,2,0:T(1,128)}, u32[]{:S(2)}) copy-start(s32[2,512,1]{1,2,0:T(1,128)} %param.10) | copy-start | bytes 12292
  0.7 1.4 %copy-start.4 = (bf16[2,12,256,128]{3,2,1,0:T(8,128)(2,1)S(1)}, bf16[2,12,256,128]{3,2,1,0:T(8,128)(2,1)}, u32[]{:S(2)}) copy-start(bf16[2,12,256,128]{3,2,1,0:T(8,128)(2,1)} %field_ref.1) | copy-start | bytes 4718596
  9.9 1.2 %copy-start = (f32[12,1,8,128]{3,2,1,0:T(8,128)S(1)}, f32[12,1,8,128]{3,2,1,0:T(8,128)}, u32[]{:S(2)}) copy-start(f32[12,1,8,128]{3,2,1,0:T(8,128)} %refs_0_.1) | copy-start | bytes 147460
  9.9 1.2 %copy-start.1 = (f32[12,1,8,128]{3,2,1,0:T(8,128)S(1)}, f32[12,1,8,128]{3,2,1,0:T(8,128)}, u32[]{:S(2)}) copy-start(f32[12,1,8,128]{3,2,1,0:T(8,128)} %refs_1_.1) | copy-start | bytes 147460
  9.9 1.2 %copy-start.2 = (f32[12,1,8,128]{3,2,1,0:T(8,128)S(1)}, f32[12,1,8,128]{3,2,1,0:T(8,128)}, u32[]{:S(2)}) copy-start(f32[12,1,8,128]{3,2,1,0:T(8,128)} %refs_2_.1) | copy-start | bytes 147460
  10.0 4.4 %collective-permute-start = (f32[4,384,128]{2,1,0:T(8,128)S(1)}, f32[4,384,128]{2,1,0:T(8,128)S(1)}, u32[]{:S(2)}, u32[]{:S(2)}) collective-permute-start(f32[4,384,128]{2,1,0:T(8,128)S(1)} %bitcast.32), channel_id=1, source_target_pairs={{0,1},{1,0},{2,3},{3,2},{4,5},{5,4},{6,7},{7,6},{8,9},{9,8},{10,11... | collective-permute-start | bytes 2359304 | tf_op jit(solution)/shard_map/ppermute | solution.py:312
  11.1 7.2 %collective-permute-start.6 = (f32[1,3,96,128]{3,2,1,0:T(8,128)S(1)}, f32[1,3,96,128]{3,2,1,0:T(8,128)S(1)}, u32[]{:S(2)}, u32[]{:S(2)}) collective-permute-start(f32[1,3,96,128]{3,2,1,0:T(8,128)S(1)} %bitcast.22), channel_id=1, source_target_pairs={{0,8},{8,0},{16,24},{24,16},{1,9},{9,1},{17,25},{25,17},{2,10},{10... | collective-permute-start | bytes 442376 | tf_op jit(solution)/shard_map/ppermute | solution.py:312
  14.5 8.0 %collective-permute-start.2 = (f32[384,128]{1,0:T(8,128)S(1)}, f32[384,128]{1,0:T(8,128)S(1)}, u32[]{:S(2)}, u32[]{:S(2)}) collective-permute-start(f32[384,128]{1,0:T(8,128)S(1)} %get-tuple-element.18), channel_id=1, source_target_pairs={{0,2},{1,5},{2,0},{3,7},{4,6},{5,1},{6,4},{7,3},{8,10},{9,13},{10,... | collective-permute-start | bytes 589832 | tf_op jit(solution)/shard_map/ppermute | solution.py:335
  18.3 19.1 %collective-permute-start.7 = (f32[2,3,96,128]{3,2,1,0:T(8,128)S(1)}, f32[2,3,96,128]{3,2,1,0:T(8,128)S(1)}, u32[]{:S(2)}, u32[]{:S(2)}) collective-permute-start(f32[2,3,96,128]{3,2,1,0:T(8,128)S(1)} %pad_maximum_fusion.2), channel_id=1, source_target_pairs={{0,16},{8,24},{16,0},{24,8},{1,17},{9,25},{17,1},{25,9},{2,18},{10... | collective-permute-start | bytes 884744 | tf_op jit(solution)/shard_map/ppermute | solution.py:312
  21.1 6.6 %collective-permute-start.1 = (f32[384,128]{1,0:T(8,128)S(1)}, f32[384,128]{1,0:T(8,128)S(1)}, u32[]{:S(2)}, u32[]{:S(2)}) collective-permute-start(f32[384,128]{1,0:T(8,128)S(1)} %get-tuple-element.20), channel_id=1, source_target_pairs={{0,2},{1,5},{2,0},{3,7},{4,6},{5,1},{6,4},{7,3},{8,10},{9,13},{10,... | collective-permute-start | bytes 589832 | tf_op jit(solution)/shard_map/ppermute | solution.py:335
  22.5 5.7 %collective-permute-start.3 = (f32[384,128]{1,0:T(8,128)S(1)}, f32[384,128]{1,0:T(8,128)S(1)}, u32[]{:S(2)}, u32[]{:S(2)}) collective-permute-start(f32[384,128]{1,0:T(8,128)S(1)} %shard_map.105), channel_id=1, source_target_pairs={{0,4},{1,3},{2,6},{3,1},{4,0},{5,7},{6,2},{7,5},{8,12},{9,11},{10,... | collective-permute-start | bytes 589832 | tf_op jit(solution)/shard_map/ppermute | solution.py:335
  28.3 7.5 %collective-permute-start.4 = (f32[192,128]{1,0:T(8,128)S(1)}, f32[192,128]{1,0:T(8,128)S(1)}, u32[]{:S(2)}, u32[]{:S(2)}) collective-permute-start(f32[192,128]{1,0:T(8,128)S(1)} %get-tuple-element.12), channel_id=1, source_target_pairs={{0,8},{8,0},{16,24},{24,16},{1,9},{9,1},{17,25},{25,17},{2,10},{10... | collective-permute-start | bytes 294920 | tf_op jit(solution)/shard_map/ppermute | solution.py:312
  35.8 7.8 %collective-permute-start.5 = (f32[192,128]{1,0:T(8,128)S(1)}, f32[192,128]{1,0:T(8,128)S(1)}, u32[]{:S(2)}, u32[]{:S(2)}) collective-permute-start(f32[192,128]{1,0:T(8,128)S(1)} %add.24.a_ref), channel_id=1, source_target_pairs={{0,16},{8,24},{16,0},{24,8},{1,17},{9,25},{17,1},{25,9},{2,18},{10... | collective-permute-start | bytes 294920 | tf_op jit(solution)/shard_map/ppermute | solution.py:312
  43.7 3.1 %collective-permute-start.11 = (f32[8,128]{1,0:T(8,128)S(1)}, f32[8,128]{1,0:T(8,128)S(1)}, u32[]{:S(2)}, u32[]{:S(2)}) collective-permute-start(f32[8,128]{1,0:T(8,128)S(1)} %get-tuple-element.14), channel_id=1, source_target_pairs={{0,9},{1,8},{2,11},{3,10},{4,13},{5,12},{6,15},{7,14},{8,1},{9,0},... | collective-permute-start | bytes 12296 | tf_op jit(solution)/shard_map/ppermute | solution.py:405
  43.8 3.7 %collective-permute-start.10 = (f32[8,128]{1,0:T(8,128)S(1)}, f32[8,128]{1,0:T(8,128)S(1)}, u32[]{:S(2)}, u32[]{:S(2)}) collective-permute-start(f32[8,128]{1,0:T(8,128)S(1)} %get-tuple-element.14), channel_id=1, source_target_pairs={{0,8},{8,0},{16,24},{24,16},{1,9},{9,1},{17,25},{25,17},{2,10},{10... | collective-permute-start | bytes 12296 | tf_op jit(solution)/shard_map/ppermute | solution.py:312
  44.6 2.8 %collective-permute-start.9 = (f32[8,128]{1,0:T(8,128)S(1)}, f32[8,128]{1,0:T(8,128)S(1)}, u32[]{:S(2)}, u32[]{:S(2)}) collective-permute-start(f32[8,128]{1,0:T(8,128)S(1)} %get-tuple-element.14), channel_id=1, source_target_pairs={{0,1},{1,0},{2,3},{3,2},{4,5},{5,4},{6,7},{7,6},{8,9},{9,8},{10,11... | collective-permute-start | bytes 12296 | tf_op jit(solution)/shard_map/ppermute | solution.py:312
  45.6 8.6 %collective-permute-start.8 = (f32[192,128]{1,0:T(8,128)S(1)}, f32[192,128]{1,0:T(8,128)S(1)}, u32[]{:S(2)}, u32[]{:S(2)}) collective-permute-start(f32[192,128]{1,0:T(8,128)S(1)} %get-tuple-element.13.mine_ref), channel_id=1, source_target_pairs={{0,8},{8,0},{16,24},{24,16},{1,9},{9,1},{17,25},{25,17},{2,10},{10... | collective-permute-start | bytes 294920 | tf_op jit(solution)/shard_map/ppermute | solution.py:312
  47.4 4.6 %collective-permute-start.14 = (f32[8,128]{1,0:T(8,128)S(1)}, f32[8,128]{1,0:T(8,128)S(1)}, u32[]{:S(2)}, u32[]{:S(2)}) collective-permute-start(f32[8,128]{1,0:T(8,128)S(1)} %add_add_fusion.refs_0_), channel_id=1, source_target_pairs={{0,6},{1,7},{2,4},{3,5},{4,2},{5,3},{6,0},{7,1},{8,14},{9,15},{10,... | collective-permute-start | bytes 12296 | tf_op jit(solution)/shard_map/ppermute | solution.py:312
  49.4 3.6 %collective-permute-start.13 = (f32[8,128]{1,0:T(8,128)S(1)}, f32[8,128]{1,0:T(8,128)S(1)}, u32[]{:S(2)}, u32[]{:S(2)}) collective-permute-start(f32[8,128]{1,0:T(8,128)S(1)} %add_add_fusion.refs_0_), channel_id=1, source_target_pairs={{0,4},{1,5},{2,6},{3,7},{4,0},{5,1},{6,2},{7,3},{8,12},{9,13},{10,... | collective-permute-start | bytes 12296 | tf_op jit(solution)/shard_map/ppermute | solution.py:312
  50.6 3.6 %collective-permute-start.12 = (f32[8,128]{1,0:T(8,128)S(1)}, f32[8,128]{1,0:T(8,128)S(1)}, u32[]{:S(2)}, u32[]{:S(2)}) collective-permute-start(f32[8,128]{1,0:T(8,128)S(1)} %add_add_fusion.refs_0_), channel_id=1, source_target_pairs={{0,2},{1,3},{2,0},{3,1},{4,6},{5,7},{6,4},{7,5},{8,10},{9,11},{10,... | collective-permute-start | bytes 12296 | tf_op jit(solution)/shard_map/ppermute | solution.py:312
  54.4 5.7 %collective-permute-start.17 = (bf16[384,128]{1,0:T(8,128)(2,1)S(1)}, bf16[384,128]{1,0:T(8,128)(2,1)S(1)}, u32[]{:S(2)}, u32[]{:S(2)}) collective-permute-start(bf16[384,128]{1,0:T(8,128)(2,1)S(1)} %get-tuple-element.17.refs_0_), channel_id=1, source_target_pairs={{0,6},{1,7},{2,4},{3,5},{4,2},{5,3},{6,0},{7,1},{8,14},{9,15},{10,... | collective-permute-start | bytes 294920 | tf_op jit(solution)/shard_map/ppermute | solution.py:335
  55.3 5.7 %collective-permute-start.16 = (bf16[384,128]{1,0:T(8,128)(2,1)S(1)}, bf16[384,128]{1,0:T(8,128)(2,1)S(1)}, u32[]{:S(2)}, u32[]{:S(2)}) collective-permute-start(bf16[384,128]{1,0:T(8,128)(2,1)S(1)} %get-tuple-element.17.refs_0_), channel_id=1, source_target_pairs={{0,4},{1,3},{2,6},{3,1},{4,0},{5,7},{6,2},{7,5},{8,12},{9,11},{10,... | collective-permute-start | bytes 294920 | tf_op jit(solution)/shard_map/ppermute | solution.py:335
  56.3 4.6 %collective-permute-start.15 = (bf16[384,128]{1,0:T(8,128)(2,1)S(1)}, bf16[384,128]{1,0:T(8,128)(2,1)S(1)}, u32[]{:S(2)}, u32[]{:S(2)}) collective-permute-start(bf16[384,128]{1,0:T(8,128)(2,1)S(1)} %get-tuple-element.17.refs_0_), channel_id=1, source_target_pairs={{0,2},{1,5},{2,0},{3,7},{4,6},{5,1},{6,4},{7,3},{8,10},{9,13},{10,... | collective-permute-start | bytes 294920 | tf_op jit(solution)/shard_map/ppermute | solution.py:335
  61.0 1.8 %collective-permute-start.18 = (bf16[4,384,128]{2,1,0:T(8,128)(2,1)S(1)}, bf16[4,384,128]{2,1,0:T(8,128)(2,1)S(1)}, u32[]{:S(2)}, u32[]{:S(2)}) collective-permute-start(bf16[4,384,128]{2,1,0:T(8,128)(2,1)S(1)} %pad_maximum_fusion.1), channel_id=1, source_target_pairs={{0,1},{1,0},{2,3},{3,2},{4,5},{5,4},{6,7},{7,6},{8,9},{9,8},{10,11... | collective-permute-start | bytes 1179656 | tf_op jit(solution)/shard_map/ppermute | solution.py:312

commit v11 on v10

--- a/solution.py
+++ b/solution.py
@@ -189,6 +189,12 @@
 
 def fold_kernel(a_ref, b_ref, out_ref):
     out_ref[...] = a_ref[...] + b_ref[...]
+
+
+def slots_kernel(first, sum_ref, got_ref, *out_refs):
+    for n, out_ref in enumerate(out_refs):
+        rows = out_ref.shape[0]
+        out_ref[...] = sum_ref[pl.ds((first + n) * rows, rows), :] + got_ref[n]
 
 
 def add_kernel_call(a, b):
@@ -363,12 +369,30 @@
 
     keep = sums[: half * part_rows].reshape(half, part_rows, nodes)
     send = sums[half * part_rows : 2 * half * part_rows].reshape(half, part_rows, nodes)
-    got = swap(send, "mesh", 1)
-    held = [None] + [keep[j] + got[j] for j in range(1, half)]
-    for h in range(4, half, 4):
-        far = swap(jnp.stack(held[h : h + 4]), "mesh", 2 * h)
-        held[1:4] = [held[j] + far[j] for j in range(1, 4)]
-        keep = keep.at[0].add(far[0])
+
+    def slots_plus(got, first):
+        count = got.shape[0]
+        return pl.pallas_call(
+            functools.partial(slots_kernel, first),
+            out_shape=[f32(part_rows, nodes)] * count,
+            in_specs=[in_vmem()] * 2,
+            out_specs=[in_vmem()] * count,
+            compiler_params=limit(4),
+        )(sums, got)
+
+    if half == 4:
+        first = swap(send[3:], "mesh", 1)
+        got = swap(send[:3], "mesh", 1)
+        held = slots_plus(got, 0) + slots_plus(first, 3)
+        base = held[0]
+    else:
+        got = swap(send, "mesh", 1)
+        held = [None] + [keep[j] + got[j] for j in range(1, half)]
+        for h in range(4, half, 4):
+            far = swap(jnp.stack(held[h : h + 4]), "mesh", 2 * h)
+            held[1:4] = [held[j] + far[j] for j in range(1, 4)]
+            keep = keep.at[0].add(far[0])
+        base = add_kernel_call(keep[0], got[0])
     arrived = []
     if half > 2:
         corner = along(held[3], 1)
@@ -377,7 +401,7 @@
         arrived.append(along(relay, 2))
     else:
         arrived += [along(held[j], j) for j in range(1, half)]
-    total = add_kernel_call(keep[0], got[0])
+    total = base
     half_rows = part_rows // 2
     stay, go = pl.pallas_call(
         merge_kernel,
@@ -463,4 +487,6 @@
     )
     out_specs = (P(None, "mesh", "ev", None), P("ev", None, "mesh", None))
 
-    return jax.shard_map(body, mesh=mesh, in_specs=in_specs, out_specs=out_specs, check_vma=False)
+    return jax.shard_map(
+        body, mesh=mesh, in_specs=in_specs, out_specs=out_specs, check_vma=False
+    )

time: 72.2 us -> 70.5 us (0.976)
  waiting for transfers between devices: 27.4 us -> 23.6 us
  starting transfers between devices: 24.1 us -> 26.1 us
    ppermute x12 -> x13, waiting for transfers between devices: 19.5 us -> 17.7 us  [swap(): return lax.ppermute(x, axis, [(i, i ^ k) for i in range(size)])]
    ppermute x6, waiting for transfers between devices: 7.02 us -> 5.3 us  [along(): return lax.ppermute(x, 'mesh', pairs)]
    ppermute x6, starting transfers between devices: 8 us -> 9.38 us  [along(): return lax.ppermute(x, 'mesh', pairs)]
    ppermute x12 -> x13, starting transfers between devices: 16.1 us -> 16.5 us  [swap(): return lax.ppermute(x, axis, [(i, i ^ k) for i in range(size)])]
  transfers between devices with their start and end apart: 19 -> 20, of which waited for: 13 -> 16; matrix products, arithmetic and copies ran while one was open for 0% -> 0% of each run, Pallas kernels for 1% -> 1%
where the time goes in v11:
time: 70.5 us; the launch traced here: 70 us
  starting transfers between devices  26.1 us (37%)
  waiting for transfers between devices  23.6 us (33%)
  Pallas kernels  19 us (27%)
  between operations  0.84 us (1%)
    ppermute x13, waiting for transfers between devices, swap(): return lax.ppermute(x, axis, [(i, i ^ k) for i in range(size)])  17.7 us
    ppermute x13, starting transfers between devices, swap(): return lax.ppermute(x, axis, [(i, i ^ k) for i in range(size)])  16.5 us
    ppermute x6, starting transfers between devices, along(): return lax.ppermute(x, 'mesh', pairs)  9.38 us
    pallas_call x1, Pallas kernels, body(): pl.pallas_call(functools.partial(backward_kernel, dims), out_shape=f32(*k...  9.04 us
    pallas_call x1, Pallas kernels, body(): pl.pallas_call(functools.partial(forward_kernel, dims), out_shape=[f32(bl...  7.74 us
    ppermute x6, waiting for transfers between devices, along(): return lax.ppermute(x, 'mesh', pairs)  5.3 us
  transfers between devices with their start and end apart: 20, of which 16 were waited for; matrix products, arithmetic and copies ran while one was open for 0% of the time, Pallas kernels for 1%

profile of v11, /device:TPU:0, one launch (start us, length us, event | category | flops | bytes accessed | tf_op | source)
XLA Modules:
  0.0 70.0 jit_solution(8434796558678776540)
XLA Ops:
  0.6 0.0 copy-start.3
  0.6 0.0 copy-start.8
  0.7 0.0 copy-start.6
  0.7 0.0 copy-start.7
  0.7 0.0 copy-start.5
  0.7 0.0 copy-start.4
  0.7 1.2 %table.1.tab_ref = bf16[10752,128]{1,0:T(8,128)(2,1)S(1)} custom-call(), custom_call_target="tpu_custom_call" | custom-call | flops 268435456 | bytes 4194304 | tf_op jit(solution)/shard_map/table/pallas_call | solution.py:343
  1.9 0.0 copy-done.3
  1.9 0.0 copy-done.8
  1.9 0.0 copy-done.6
  1.9 0.0 copy-done.7
  1.9 0.0 copy-done.5
  1.9 0.2 copy-done.4
  2.1 7.7 %forward.1 = (f32[3088,128]{1,0:T(8,128)S(1)}, s32[32,128]{1,0:T(8,128)S(1)}) custom-call(s32[1,2]{1,0:T(1,128)S(1)} %bitcast.17, s32[2,1,512]{2,1,0:T(1,128)S(1)} %bitcast.19, s32[2,512]{1,0:T(2,128)S(1)} %copy-done.6, s32[2,512]{1,0:T(2,128)S(1)} %copy-done.7, s32[2,512]{1,0:T(2,128)S(1)} %copy-done.8, bf16[2,12,256,128]{3,2,1,0:T(8,128)(2,1)S(1)} %copy-done.4, ...), custom_call_target="tpu_custom_call" | custom-call | flops 34359738368 | bytes 16777216 | tf_op jit(solution)/shard_map/forward/pallas_call | solution.py:351
  9.9 0.0 copy-start
  9.9 0.0 copy-start.1
  9.9 0.0 copy-start.2
  10.0 1.1 %collective-permute-start = (f32[3,384,128]{2,1,0:T(8,128)S(1)}, f32[3,384,128]{2,1,0:T(8,128)S(1)}, u32[]{:S(2)}, u32[]{:S(2)}) collective-permute-start(f32[3,384,128]{2,1,0:T(8,128)S(1)} %bitcast.20), channel_id=1, source_target_pairs={{0,1},{1,0},{2,3},{3,2},{4,5},{5,4},{6,7},{7,6},{8,9},{9,8},{10,11... | collective-permute-start | bytes 1769480 | tf_op jit(solution)/shard_map/ppermute | solution.py:318
  11.0 0.1 collective-permute-start.2
  11.1 1.8 %collective-permute-done.2.got_ref = f32[1,384,128]{2,1,0:T(8,128)S(1)} collective-permute-done((f32[1,384,128]{2,1,0:T(8,128)S(1)}, f32[1,384,128]{2,1,0:T(8,128)S(1)}, u32[]{:S(2)}, u32[]{:S(2)}) %collective-permute-start.2) | collective-permute-done | bytes 196640 | tf_op jit(solution)/shard_map/ppermute | solution.py:318
  13.0 2.9 %collective-permute-start.3 = (f32[384,128]{1,0:T(8,128)S(1)}, f32[384,128]{1,0:T(8,128)S(1)}, u32[]{:S(2)}, u32[]{:S(2)}) collective-permute-start(f32[384,128]{1,0:T(8,128)S(1)} %shard_map.105), channel_id=1, source_target_pairs={{0,2},{1,5},{2,0},{3,7},{4,6},{5,1},{6,4},{7,3},{8,10},{9,13},{10,... | collective-permute-start | bytes 589832 | tf_op jit(solution)/shard_map/ppermute | solution.py:341
  15.8 0.0 copy-done.2
  15.9 1.4 %collective-permute-start.7 = (f32[1,3,96,128]{3,2,1,0:T(8,128)S(1)}, f32[1,3,96,128]{3,2,1,0:T(8,128)S(1)}, u32[]{:S(2)}, u32[]{:S(2)}) collective-permute-start(f32[1,3,96,128]{3,2,1,0:T(8,128)S(1)} %bitcast.10), channel_id=1, source_target_pairs={{0,8},{8,0},{16,24},{24,16},{1,9},{9,1},{17,25},{25,17},{2,10},{10... | collective-permute-start | bytes 442376 | tf_op jit(solution)/shard_map/ppermute | solution.py:318
  17.2 0.0 collective-permute-done.got_ref
  17.2 0.1 shard_map.104
  17.3 0.9 %collective-permute-start.1 = (f32[384,128]{1,0:T(8,128)S(1)}, f32[384,128]{1,0:T(8,128)S(1)}, u32[]{:S(2)}, u32[]{:S(2)}) collective-permute-start(f32[384,128]{1,0:T(8,128)S(1)} %get-tuple-element.15), channel_id=1, source_target_pairs={{0,2},{1,5},{2,0},{3,7},{4,6},{5,1},{6,4},{7,3},{8,10},{9,13},{10,... | collective-permute-start | bytes 589832 | tf_op jit(solution)/shard_map/ppermute | solution.py:341
  18.2 1.2 %collective-permute-done.3.b_ref = f32[384,128]{1,0:T(8,128)S(1)} collective-permute-done((f32[384,128]{1,0:T(8,128)S(1)}, f32[384,128]{1,0:T(8,128)S(1)}, u32[]{:S(2)}, u32[]{:S(2)}) %collective-permute-start.3) | collective-permute-done | bytes 196640 | tf_op jit(solution)/shard_map/ppermute | solution.py:341
  19.5 2.0 %collective-permute-start.4 = (f32[384,128]{1,0:T(8,128)S(1)}, f32[384,128]{1,0:T(8,128)S(1)}, u32[]{:S(2)}, u32[]{:S(2)}) collective-permute-start(f32[384,128]{1,0:T(8,128)S(1)} %shard_map.106), channel_id=1, source_target_pairs={{0,4},{1,3},{2,6},{3,1},{4,0},{5,7},{6,2},{7,5},{8,12},{9,11},{10,... | collective-permute-start | bytes 589832 | tf_op jit(solution)/shard_map/ppermute | solution.py:341
  21.5 0.1 collective-permute-done.7
  21.6 2.4 %collective-permute-start.8 = (f32[2,3,96,128]{3,2,1,0:T(8,128)S(1)}, f32[2,3,96,128]{3,2,1,0:T(8,128)S(1)}, u32[]{:S(2)}, u32[]{:S(2)}) collective-permute-start(f32[2,3,96,128]{3,2,1,0:T(8,128)S(1)} %pad_maximum_fusion.2), channel_id=1, source_target_pairs={{0,16},{8,24},{16,0},{24,8},{1,17},{9,25},{17,1},{25,9},{2,18},{10... | collective-permute-start | bytes 884744 | tf_op jit(solution)/shard_map/ppermute | solution.py:318
  24.0 0.4 collective-permute-done.1.refs_1_
  24.4 0.8 %collective-permute-done.4.refs_2_ = f32[384,128]{1,0:T(8,128)S(1)} collective-permute-done((f32[384,128]{1,0:T(8,128)S(1)}, f32[384,128]{1,0:T(8,128)S(1)}, u32[]{:S(2)}, u32[]{:S(2)}) %collective-permute-start.4) | collective-permute-done | bytes 196640 | tf_op jit(solution)/shard_map/ppermute | solution.py:341
  25.3 2.2 %collective-permute-start.5 = (f32[192,128]{1,0:T(8,128)S(1)}, f32[192,128]{1,0:T(8,128)S(1)}, u32[]{:S(2)}, u32[]{:S(2)}) collective-permute-start(f32[192,128]{1,0:T(8,128)S(1)} %get-tuple-element.18), channel_id=1, source_target_pairs={{0,8},{8,0},{16,24},{24,16},{1,9},{9,1},{17,25},{25,17},{2,10},{10... | collective-permute-start | bytes 294920 | tf_op jit(solution)/shard_map/ppermute | solution.py:318
  27.5 4.3 %collective-permute-done.5 = f32[192,128]{1,0:T(8,128)S(1)} collective-permute-done((f32[192,128]{1,0:T(8,128)S(1)}, f32[192,128]{1,0:T(8,128)S(1)}, u32[]{:S(2)}, u32[]{:S(2)}) %collective-permute-start.5) | collective-permute-done | bytes 98336 | tf_op jit(solution)/shard_map/ppermute | solution.py:318
  31.8 3.2 %collective-permute-start.6 = (f32[192,128]{1,0:T(8,128)S(1)}, f32[192,128]{1,0:T(8,128)S(1)}, u32[]{:S(2)}, u32[]{:S(2)}) collective-permute-start(f32[192,128]{1,0:T(8,128)S(1)} %add.12.a_ref), channel_id=1, source_target_pairs={{0,16},{8,24},{16,0},{24,8},{1,17},{9,25},{17,1},{25,9},{2,18},{10... | collective-permute-start | bytes 294920 | tf_op jit(solution)/shard_map/ppermute | solution.py:318
  35.0 5.1 %collective-permute-done.8 = f32[2,3,96,128]{3,2,1,0:T(8,128)S(1)} collective-permute-done((f32[2,3,96,128]{3,2,1,0:T(8,128)S(1)}, f32[2,3,96,128]{3,2,1,0:T(8,128)S(1)}, u32[]{:S(2)}, u32[]{:S(2)}) %collective-permute-start.8) | collective-permute-done | bytes 294944 | tf_op jit(solution)/shard_map/ppermute | solution.py:318
  40.1 1.0 %collective-permute-done.6.b_ref = f32[192,128]{1,0:T(8,128)S(1)} collective-permute-done((f32[192,128]{1,0:T(8,128)S(1)}, f32[192,128]{1,0:T(8,128)S(1)}, u32[]{:S(2)}, u32[]{:S(2)}) %collective-permute-start.6) | collective-permute-done | bytes 98336 | tf_op jit(solution)/shard_map/ppermute | solution.py:318
  41.1 0.1 sums.1
  41.2 0.2 collective-permute-start.12
  41.4 0.5 collective-permute-start.11
  41.9 1.3 %collective-permute-start.10 = (f32[8,128]{1,0:T(8,128)S(1)}, f32[8,128]{1,0:T(8,128)S(1)}, u32[]{:S(2)}, u32[]{:S(2)}) collective-permute-start(f32[8,128]{1,0:T(8,128)S(1)} %get-tuple-element.20), channel_id=1, source_target_pairs={{0,1},{1,0},{2,3},{3,2},{4,5},{5,4},{6,7},{7,6},{8,9},{9,8},{10,11... | collective-permute-start | bytes 12296 | tf_op jit(solution)/shard_map/ppermute | solution.py:318
  43.1 0.5 collective-permute-start.9
  43.6 0.6 collective-permute-done.12
  44.3 0.7 %collective-permute-done.11 = f32[8,128]{1,0:T(8,128)S(1)} collective-permute-done((f32[8,128]{1,0:T(8,128)S(1)}, f32[8,128]{1,0:T(8,128)S(1)}, u32[]{:S(2)}, u32[]{:S(2)}) %collective-permute-start.11) | collective-permute-done | bytes 4128 | tf_op jit(solution)/shard_map/ppermute | solution.py:318
  45.0 0.0 collective-permute-done.10
  45.0 1.5 %collective-permute-start.15 = (f32[8,128]{1,0:T(8,128)S(1)}, f32[8,128]{1,0:T(8,128)S(1)}, u32[]{:S(2)}, u32[]{:S(2)}) collective-permute-start(f32[8,128]{1,0:T(8,128)S(1)} %add_add_fusion.refs_0_), channel_id=1, source_target_pairs={{0,6},{1,7},{2,4},{3,5},{4,2},{5,3},{6,0},{7,1},{8,14},{9,15},{10,... | collective-permute-start | bytes 12296 | tf_op jit(solution)/shard_map/ppermute | solution.py:318
  46.5 2.4 %collective-permute-start.14 = (f32[8,128]{1,0:T(8,128)S(1)}, f32[8,128]{1,0:T(8,128)S(1)}, u32[]{:S(2)}, u32[]{:S(2)}) collective-permute-start(f32[8,128]{1,0:T(8,128)S(1)} %add_add_fusion.refs_0_), channel_id=1, source_target_pairs={{0,4},{1,5},{2,6},{3,7},{4,0},{5,1},{6,2},{7,3},{8,12},{9,13},{10,... | collective-permute-start | bytes 12296 | tf_op jit(solution)/shard_map/ppermute | solution.py:318
  48.9 0.0 collective-permute-start.13
  48.9 0.7 collective-permute-done.15.refs_3_
  49.6 0.9 %collective-permute-done.14.refs_2_ = f32[8,128]{1,0:T(8,128)S(1)} collective-permute-done((f32[8,128]{1,0:T(8,128)S(1)}, f32[8,128]{1,0:T(8,128)S(1)}, u32[]{:S(2)}, u32[]{:S(2)}) %collective-permute-start.14) | collective-permute-done | bytes 4128 | tf_op jit(solution)/shard_map/ppermute | solution.py:318
  50.5 2.0 %collective-permute-done.13.refs_1_ = f32[8,128]{1,0:T(8,128)S(1)} collective-permute-done((f32[8,128]{1,0:T(8,128)S(1)}, f32[8,128]{1,0:T(8,128)S(1)}, u32[]{:S(2)}, u32[]{:S(2)}) %collective-permute-start.13) | collective-permute-done | bytes 4128 | tf_op jit(solution)/shard_map/ppermute | solution.py:318
  52.5 0.0 collective-permute-done.9.other_ref
  52.5 0.2 direction.1
  52.7 0.8 %collective-permute-start.18 = (bf16[384,128]{1,0:T(8,128)(2,1)S(1)}, bf16[384,128]{1,0:T(8,128)(2,1)S(1)}, u32[]{:S(2)}, u32[]{:S(2)}) collective-permute-start(bf16[384,128]{1,0:T(8,128)(2,1)S(1)} %get-tuple-element.23.refs_0_), channel_id=1, source_target_pairs={{0,6},{1,7},{2,4},{3,5},{4,2},{5,3},{6,0},{7,1},{8,14},{9,15},{10,... | collective-permute-start | bytes 294920 | tf_op jit(solution)/shard_map/ppermute | solution.py:341
  53.5 0.8 %collective-permute-start.17 = (bf16[384,128]{1,0:T(8,128)(2,1)S(1)}, bf16[384,128]{1,0:T(8,128)(2,1)S(1)}, u32[]{:S(2)}, u32[]{:S(2)}) collective-permute-start(bf16[384,128]{1,0:T(8,128)(2,1)S(1)} %get-tuple-element.23.refs_0_), channel_id=1, source_target_pairs={{0,4},{1,3},{2,6},{3,1},{4,0},{5,7},{6,2},{7,5},{8,12},{9,11},{10,... | collective-permute-start | bytes 294920 | tf_op jit(solution)/shard_map/ppermute | solution.py:341
  54.3 2.0 %collective-permute-start.16 = (bf16[384,128]{1,0:T(8,128)(2,1)S(1)}, bf16[384,128]{1,0:T(8,128)(2,1)S(1)}, u32[]{:S(2)}, u32[]{:S(2)}) collective-permute-start(bf16[384,128]{1,0:T(8,128)(2,1)S(1)} %get-tuple-element.23.refs_0_), channel_id=1, source_target_pairs={{0,2},{1,5},{2,0},{3,7},{4,6},{5,1},{6,4},{7,3},{8,10},{9,13},{10,... | collective-permute-start | bytes 294920 | tf_op jit(solution)/shard_map/ppermute | solution.py:341
  56.3 2.1 %collective-permute-done.18.refs_3_ = bf16[384,128]{1,0:T(8,128)(2,1)S(1)} collective-permute-done((bf16[384,128]{1,0:T(8,128)(2,1)S(1)}, bf16[384,128]{1,0:T(8,128)(2,1)S(1)}, u32[]{:S(2)}, u32[]{:S(2)}) %collective-permute-start.18) | collective-permute-done | bytes 98336 | tf_op jit(solution)/shard_map/ppermute | solution.py:341
  58.4 0.8 %collective-permute-done.17.refs_2_ = bf16[384,128]{1,0:T(8,128)(2,1)S(1)} collective-permute-done((bf16[384,128]{1,0:T(8,128)(2,1)S(1)}, bf16[384,128]{1,0:T(8,128)(2,1)S(1)}, u32[]{:S(2)}, u32[]{:S(2)}) %collective-permute-start.17) | collective-permute-done | bytes 98336 | tf_op jit(solution)/shard_map/ppermute | solution.py:341
  59.2 0.0 collective-permute-done.16.refs_1_
  59.2 0.1 pad_maximum_fusion.1
  59.2 0.1 collective-permute-start.19
  59.3 0.6 unpack.1
  59.9 1.1 %collective-permute-done.19.refs_4_ = bf16[4,384,128]{2,1,0:T(8,128)(2,1)S(1)} collective-permute-done((bf16[4,384,128]{2,1,0:T(8,128)(2,1)S(1)}, bf16[4,384,128]{2,1,0:T(8,128)(2,1)S(1)}, u32[]{:S(2)}, u32[]{:S(2)}) %collective-permute-start.19) | collective-permute-done | bytes 393248 | tf_op jit(solution)/shard_map/ppermute | solution.py:318
  61.0 9.0 %backward.1 = f32[2,12,256,128]{3,2,1,0:T(8,128)} custom-call(s32[1,2]{1,0:T(1,128)S(1)} %bitcast.18, s32[32,128]{1,0:T(8,128)S(1)} %get-tuple-element.22.codes_in, bf16[10752,128]{1,0:T(8,128)(2,1)S(1)} %table.1.tab_ref, bf16[384,128]{1,0:T(8,128)(2,1)S(1)} %get-tuple-element.23.refs_0_, bf16[384,128]{1,0:T(8,128)(2,1)S(1)} %collective-permute-done.16.refs_1_, ...), custom_call_target="tpu_custom_call" | custom-call | tf_op jit(solution)/shard_map/backward/pallas_call | solution.py:458
  (12 shorter events, 0.3 us)
Async XLA Ops:
  0.6 1.2 %copy-start.3 = (s32[2,1]{0,1:T(1,128)S(1)}, s32[2,1]{0,1:T(1,128)}, u32[]{:S(2)}) copy-start(s32[2,1]{0,1:T(1,128)} %param.14) | copy-start | bytes 28
  0.6 1.2 %copy-start.8 = (s32[2,512]{1,0:T(2,128)S(1)}, s32[2,512]{1,0:T(2,128)}, u32[]{:S(2)}) copy-start(s32[2,512]{1,0:T(2,128)} %seed_ref.1) | copy-start | bytes 12292
  0.7 1.2 %copy-start.6 = (s32[2,512]{1,0:T(2,128)S(1)}, s32[2,512]{1,0:T(2,128)}, u32[]{:S(2)}) copy-start(s32[2,512]{1,0:T(2,128)} %target_ref.1) | copy-start | bytes 12292
  0.7 1.2 %copy-start.7 = (s32[2,512]{1,0:T(2,128)S(1)}, s32[2,512]{1,0:T(2,128)}, u32[]{:S(2)}) copy-start(s32[2,512]{1,0:T(2,128)} %source_ref.1) | copy-start | bytes 12292
  0.7 1.2 %copy-start.5 = (s32[2,512,1]{1,2,0:T(1,128)S(1)}, s32[2,512,1]{1,2,0:T(1,128)}, u32[]{:S(2)}) copy-start(s32[2,512,1]{1,2,0:T(1,128)} %param.10) | copy-start | bytes 12292
  0.7 1.4 %copy-start.4 = (bf16[2,12,256,128]{3,2,1,0:T(8,128)(2,1)S(1)}, bf16[2,12,256,128]{3,2,1,0:T(8,128)(2,1)}, u32[]{:S(2)}) copy-start(bf16[2,12,256,128]{3,2,1,0:T(8,128)(2,1)} %field_ref.1) | copy-start | bytes 4718596
  9.9 6.0 %copy-start = (f32[12,1,8,128]{3,2,1,0:T(8,128)S(1)}, f32[12,1,8,128]{3,2,1,0:T(8,128)}, u32[]{:S(2)}) copy-start(f32[12,1,8,128]{3,2,1,0:T(8,128)} %refs_0_.1) | copy-start | bytes 147460
  9.9 5.9 %copy-start.1 = (f32[12,1,8,128]{3,2,1,0:T(8,128)S(1)}, f32[12,1,8,128]{3,2,1,0:T(8,128)}, u32[]{:S(2)}) copy-start(f32[12,1,8,128]{3,2,1,0:T(8,128)} %refs_1_.1) | copy-start | bytes 147460
  9.9 5.9 %copy-start.2 = (f32[12,1,8,128]{3,2,1,0:T(8,128)S(1)}, f32[12,1,8,128]{3,2,1,0:T(8,128)}, u32[]{:S(2)}) copy-start(f32[12,1,8,128]{3,2,1,0:T(8,128)} %refs_2_.1) | copy-start | bytes 147460
  10.0 7.3 %collective-permute-start = (f32[3,384,128]{2,1,0:T(8,128)S(1)}, f32[3,384,128]{2,1,0:T(8,128)S(1)}, u32[]{:S(2)}, u32[]{:S(2)}) collective-permute-start(f32[3,384,128]{2,1,0:T(8,128)S(1)} %bitcast.20), channel_id=1, source_target_pairs={{0,1},{1,0},{2,3},{3,2},{4,5},{5,4},{6,7},{7,6},{8,9},{9,8},{10,11... | collective-permute-start | bytes 1769480 | tf_op jit(solution)/shard_map/ppermute | solution.py:318
  11.0 1.9 %collective-permute-start.2 = (f32[1,384,128]{2,1,0:T(8,128)S(1)}, f32[1,384,128]{2,1,0:T(8,128)S(1)}, u32[]{:S(2)}, u32[]{:S(2)}) collective-permute-start(f32[1,384,128]{2,1,0:T(8,128)S(1)} %slice_bitcast_fusion), channel_id=1, source_target_pairs={{0,1},{1,0},{2,3},{3,2},{4,5},{5,4},{6,7},{7,6},{8,9},{9,8},{10,11... | collective-permute-start | bytes 589832 | tf_op jit(solution)/shard_map/ppermute | solution.py:318
  13.0 6.5 %collective-permute-start.3 = (f32[384,128]{1,0:T(8,128)S(1)}, f32[384,128]{1,0:T(8,128)S(1)}, u32[]{:S(2)}, u32[]{:S(2)}) collective-permute-start(f32[384,128]{1,0:T(8,128)S(1)} %shard_map.105), channel_id=1, source_target_pairs={{0,2},{1,5},{2,0},{3,7},{4,6},{5,1},{6,4},{7,3},{8,10},{9,13},{10,... | collective-permute-start | bytes 589832 | tf_op jit(solution)/shard_map/ppermute | solution.py:341
  15.9 5.7 %collective-permute-start.7 = (f32[1,3,96,128]{3,2,1,0:T(8,128)S(1)}, f32[1,3,96,128]{3,2,1,0:T(8,128)S(1)}, u32[]{:S(2)}, u32[]{:S(2)}) collective-permute-start(f32[1,3,96,128]{3,2,1,0:T(8,128)S(1)} %bitcast.10), channel_id=1, source_target_pairs={{0,8},{8,0},{16,24},{24,16},{1,9},{9,1},{17,25},{25,17},{2,10},{10... | collective-permute-start | bytes 442376 | tf_op jit(solution)/shard_map/ppermute | solution.py:318
  17.3 7.1 %collective-permute-start.1 = (f32[384,128]{1,0:T(8,128)S(1)}, f32[384,128]{1,0:T(8,128)S(1)}, u32[]{:S(2)}, u32[]{:S(2)}) collective-permute-start(f32[384,128]{1,0:T(8,128)S(1)} %get-tuple-element.15), channel_id=1, source_target_pairs={{0,2},{1,5},{2,0},{3,7},{4,6},{5,1},{6,4},{7,3},{8,10},{9,13},{10,... | collective-permute-start | bytes 589832 | tf_op jit(solution)/shard_map/ppermute | solution.py:341
  19.5 5.7 %collective-permute-start.4 = (f32[384,128]{1,0:T(8,128)S(1)}, f32[384,128]{1,0:T(8,128)S(1)}, u32[]{:S(2)}, u32[]{:S(2)}) collective-permute-start(f32[384,128]{1,0:T(8,128)S(1)} %shard_map.106), channel_id=1, source_target_pairs={{0,4},{1,3},{2,6},{3,1},{4,0},{5,7},{6,2},{7,5},{8,12},{9,11},{10,... | collective-permute-start | bytes 589832 | tf_op jit(solution)/shard_map/ppermute | solution.py:341
  21.6 18.4 %collective-permute-start.8 = (f32[2,3,96,128]{3,2,1,0:T(8,128)S(1)}, f32[2,3,96,128]{3,2,1,0:T(8,128)S(1)}, u32[]{:S(2)}, u32[]{:S(2)}) collective-permute-start(f32[2,3,96,128]{3,2,1,0:T(8,128)S(1)} %pad_maximum_fusion.2), channel_id=1, source_target_pairs={{0,16},{8,24},{16,0},{24,8},{1,17},{9,25},{17,1},{25,9},{2,18},{10... | collective-permute-start | bytes 884744 | tf_op jit(solution)/shard_map/ppermute | solution.py:318
  25.3 6.5 %collective-permute-start.5 = (f32[192,128]{1,0:T(8,128)S(1)}, f32[192,128]{1,0:T(8,128)S(1)}, u32[]{:S(2)}, u32[]{:S(2)}) collective-permute-start(f32[192,128]{1,0:T(8,128)S(1)} %get-tuple-element.18), channel_id=1, source_target_pairs={{0,8},{8,0},{16,24},{24,16},{1,9},{9,1},{17,25},{25,17},{2,10},{10... | collective-permute-start | bytes 294920 | tf_op jit(solution)/shard_map/ppermute | solution.py:318
  31.8 9.3 %collective-permute-start.6 = (f32[192,128]{1,0:T(8,128)S(1)}, f32[192,128]{1,0:T(8,128)S(1)}, u32[]{:S(2)}, u32[]{:S(2)}) collective-permute-start(f32[192,128]{1,0:T(8,128)S(1)} %add.12.a_ref), channel_id=1, source_target_pairs={{0,16},{8,24},{16,0},{24,8},{1,17},{9,25},{17,1},{25,9},{2,18},{10... | collective-permute-start | bytes 294920 | tf_op jit(solution)/shard_map/ppermute | solution.py:318
  41.2 3.1 %collective-permute-start.12 = (f32[8,128]{1,0:T(8,128)S(1)}, f32[8,128]{1,0:T(8,128)S(1)}, u32[]{:S(2)}, u32[]{:S(2)}) collective-permute-start(f32[8,128]{1,0:T(8,128)S(1)} %get-tuple-element.20), channel_id=1, source_target_pairs={{0,9},{1,8},{2,11},{3,10},{4,13},{5,12},{6,15},{7,14},{8,1},{9,0},... | collective-permute-start | bytes 12296 | tf_op jit(solution)/shard_map/ppermute | solution.py:429
  41.4 3.6 %collective-permute-start.11 = (f32[8,128]{1,0:T(8,128)S(1)}, f32[8,128]{1,0:T(8,128)S(1)}, u32[]{:S(2)}, u32[]{:S(2)}) collective-permute-start(f32[8,128]{1,0:T(8,128)S(1)} %get-tuple-element.20), channel_id=1, source_target_pairs={{0,8},{8,0},{16,24},{24,16},{1,9},{9,1},{17,25},{25,17},{2,10},{10... | collective-permute-start | bytes 12296 | tf_op jit(solution)/shard_map/ppermute | solution.py:318
  41.9 3.2 %collective-permute-start.10 = (f32[8,128]{1,0:T(8,128)S(1)}, f32[8,128]{1,0:T(8,128)S(1)}, u32[]{:S(2)}, u32[]{:S(2)}) collective-permute-start(f32[8,128]{1,0:T(8,128)S(1)} %get-tuple-element.20), channel_id=1, source_target_pairs={{0,1},{1,0},{2,3},{3,2},{4,5},{5,4},{6,7},{7,6},{8,9},{9,8},{10,11... | collective-permute-start | bytes 12296 | tf_op jit(solution)/shard_map/ppermute | solution.py:318
  43.1 9.4 %collective-permute-start.9 = (f32[192,128]{1,0:T(8,128)S(1)}, f32[192,128]{1,0:T(8,128)S(1)}, u32[]{:S(2)}, u32[]{:S(2)}) collective-permute-start(f32[192,128]{1,0:T(8,128)S(1)} %get-tuple-element.19.mine_ref), channel_id=1, source_target_pairs={{0,8},{8,0},{16,24},{24,16},{1,9},{9,1},{17,25},{25,17},{2,10},{10... | collective-permute-start | bytes 294920 | tf_op jit(solution)/shard_map/ppermute | solution.py:318
  45.0 4.6 %collective-permute-start.15 = (f32[8,128]{1,0:T(8,128)S(1)}, f32[8,128]{1,0:T(8,128)S(1)}, u32[]{:S(2)}, u32[]{:S(2)}) collective-permute-start(f32[8,128]{1,0:T(8,128)S(1)} %add_add_fusion.refs_0_), channel_id=1, source_target_pairs={{0,6},{1,7},{2,4},{3,5},{4,2},{5,3},{6,0},{7,1},{8,14},{9,15},{10,... | collective-permute-start | bytes 12296 | tf_op jit(solution)/shard_map/ppermute | solution.py:318
  46.5 4.0 %collective-permute-start.14 = (f32[8,128]{1,0:T(8,128)S(1)}, f32[8,128]{1,0:T(8,128)S(1)}, u32[]{:S(2)}, u32[]{:S(2)}) collective-permute-start(f32[8,128]{1,0:T(8,128)S(1)} %add_add_fusion.refs_0_), channel_id=1, source_target_pairs={{0,4},{1,5},{2,6},{3,7},{4,0},{5,1},{6,2},{7,3},{8,12},{9,13},{10,... | collective-permute-start | bytes 12296 | tf_op jit(solution)/shard_map/ppermute | solution.py:318
  48.9 3.6 %collective-permute-start.13 = (f32[8,128]{1,0:T(8,128)S(1)}, f32[8,128]{1,0:T(8,128)S(1)}, u32[]{:S(2)}, u32[]{:S(2)}) collective-permute-start(f32[8,128]{1,0:T(8,128)S(1)} %add_add_fusion.refs_0_), channel_id=1, source_target_pairs={{0,2},{1,3},{2,0},{3,1},{4,6},{5,7},{6,4},{7,5},{8,10},{9,11},{10,... | collective-permute-start | bytes 12296 | tf_op jit(solution)/shard_map/ppermute | solution.py:318
  52.7 5.7 %collective-permute-start.18 = (bf16[384,128]{1,0:T(8,128)(2,1)S(1)}, bf16[384,128]{1,0:T(8,128)(2,1)S(1)}, u32[]{:S(2)}, u32[]{:S(2)}) collective-permute-start(bf16[384,128]{1,0:T(8,128)(2,1)S(1)} %get-tuple-element.23.refs_0_), channel_id=1, source_target_pairs={{0,6},{1,7},{2,4},{3,5},{4,2},{5,3},{6,0},{7,1},{8,14},{9,15},{10,... | collective-permute-start | bytes 294920 | tf_op jit(solution)/shard_map/ppermute | solution.py:341
  53.5 5.7 %collective-permute-start.17 = (bf16[384,128]{1,0:T(8,128)(2,1)S(1)}, bf16[384,128]{1,0:T(8,128)(2,1)S(1)}, u32[]{:S(2)}, u32[]{:S(2)}) collective-permute-start(bf16[384,128]{1,0:T(8,128)(2,1)S(1)} %get-tuple-element.23.refs_0_), channel_id=1, source_target_pairs={{0,4},{1,3},{2,6},{3,1},{4,0},{5,7},{6,2},{7,5},{8,12},{9,11},{10,... | collective-permute-start | bytes 294920 | tf_op jit(solution)/shard_map/ppermute | solution.py:341
  54.3 4.9 %collective-permute-start.16 = (bf16[384,128]{1,0:T(8,128)(2,1)S(1)}, bf16[384,128]{1,0:T(8,128)(2,1)S(1)}, u32[]{:S(2)}, u32[]{:S(2)}) collective-permute-start(bf16[384,128]{1,0:T(8,128)(2,1)S(1)} %get-tuple-element.23.refs_0_), channel_id=1, source_target_pairs={{0,2},{1,5},{2,0},{3,7},{4,6},{5,1},{6,4},{7,3},{8,10},{9,13},{10,... | collective-permute-start | bytes 294920 | tf_op jit(solution)/shard_map/ppermute | solution.py:341
  59.2 1.8 %collective-permute-start.19 = (bf16[4,384,128]{2,1,0:T(8,128)(2,1)S(1)}, bf16[4,384,128]{2,1,0:T(8,128)(2,1)S(1)}, u32[]{:S(2)}, u32[]{:S(2)}) collective-permute-start(bf16[4,384,128]{2,1,0:T(8,128)(2,1)S(1)} %pad_maximum_fusion.1), channel_id=1, source_target_pairs={{0,1},{1,0},{2,3},{3,2},{4,5},{5,4},{6,7},{7,6},{8,9},{9,8},{10,11... | collective-permute-start | bytes 1179656 | tf_op jit(solution)/shard_map/ppermute | solution.py:318
